TPU v7x, 32 devices: a whole 2x2x4 slice. The times are simulated.
32 devices in a mesh: ctx: 8 (over z, y), head: 4 (over x, core).
Axes of the slice: x: 2, y: 2, z: 4, core: 2. Of those that a mesh axis runs over, the one named last changes fastest.
Arguments:
- queries: bfloat16 [8192, 1024], P('ctx', 'head'), may hold values from -6 to 6
- keys: bfloat16 [8192, 1024], P('ctx', 'head'), may hold values from -1.7 to 1.7
- values: bfloat16 [8192, 1024], P('ctx', 'head'), may hold values from -6 to 6
- w_out: bfloat16 [1024, 2048], P('head'), may hold values from -0.1875 to 0.1875
- cotangent: bfloat16 [8192, 2048], P('ctx', 'head'), may hold values from -6 to 6
Outputs:
- layer_out: bfloat16 [8192, 2048], P('ctx', 'head')
- grad_queries: bfloat16 [8192, 1024], P('ctx', 'head')
- grad_keys: bfloat16 [8192, 1024], P('ctx', 'head')
- grad_values: bfloat16 [8192, 1024], P('ctx', 'head')
- grad_weight: float32 [1024, 2048], P('head', 'ctx')
All inputs are finite; a program needn't handle non-finite values.
Results may differ from a plain program's by a relative error of at most 0.014.
Values may be sent and summed in bfloat16 or wider, within the bound.
No kernel may reach another device: no remote copies, remote signals or barrier semaphores. Data moves between devices by JAX's collectives and lax.ppermute only.
A program may use at most 128 MiB of HBM per device.

v0:
```python
import functools

import jax
import jax.numpy as jnp
from jax import lax
from jax.experimental import pallas as pl
from jax.experimental.pallas import tpu as pltpu
from jax.sharding import PartitionSpec as P

HDIM = 128
SPAN = 256
NEWTON = 8
RIDGE = 1.0
F32 = jnp.float32
BF16 = jnp.bfloat16
VMEM_SPEC = pl.BlockSpec(memory_space=pltpu.VMEM)
SMEM_SPEC = pl.BlockSpec(memory_space=pltpu.SMEM)


def dot(left, right, axes=(1, 0)):
    return lax.dot_general(
        left, right, (((axes[0],), (axes[1],)), ((), ())), preferred_element_type=F32
    )


def split(value):
    high = value.astype(BF16)
    return high, (value - high.astype(F32)).astype(BF16)


def cat(parts, axis):
    return jnp.concatenate(parts, axis=axis)


def params(limit=60):
    return pltpu.CompilerParams(vmem_limit_bytes=limit * 1024 * 1024)


def cost(flops, size):
    return pl.CostEstimate(flops=flops, bytes_accessed=size, transcendentals=0)


def shape(dims, dtype=F32):
    return jax.ShapeDtypeStruct(dims, dtype)


def unit():
    rows = lax.broadcasted_iota(jnp.int32, (HDIM, HDIM), 0)
    cols = lax.broadcasted_iota(jnp.int32, (HDIM, HDIM), 1)
    return rows == cols


def causal():
    rows = lax.broadcasted_iota(jnp.int32, (SPAN, SPAN), 0)
    cols = lax.broadcasted_iota(jnp.int32, (SPAN, SPAN), 1)
    return rows >= cols


def totals_kernel(k_ref, v_ref, g_ref, n_ref):
    for h in range(g_ref.shape[0]):
        cols = slice(h * HDIM, (h + 1) * HDIM)
        k = k_ref[:, cols]
        both = dot(k, cat([k, v_ref[:, cols]], 1), (0, 0))
        g_ref[h] = both[:, :HDIM]
        n_ref[h] = both[:, HDIM:]


def totals(keys, values, heads):
    state = shape((heads, HDIM, HDIM))
    return pl.pallas_call(
        totals_kernel,
        out_shape=(state, state),
        in_specs=[VMEM_SPEC] * 2,
        out_specs=(VMEM_SPEC, VMEM_SPEC),
        compiler_params=params(),
        cost_estimate=cost(2 * 2 * keys.size * HDIM, 4 * keys.size),
    )(keys, values)


def primal_kernel(
    q_ref, k_ref, v_ref, g_ref, n_ref, out_ref, e_ref, x_ref, last_ref, a_ref, pre_ref, es, xs
):
    blocks = a_ref.shape[1]
    eye = unit()
    gram, pair = g_ref[0], n_ref[0]
    for b in range(blocks):
        rows = slice(b * SPAN, (b + 1) * SPAN)
        ridged = gram + jnp.where(eye, RIDGE, 0.0)
        scale = 1.0 / jnp.sqrt(jnp.sum(ridged * ridged, keepdims=True))
        a_ref[0, b] = ridged
        pre_ref[0, b] = pair
        es[b] = ridged * scale
        xs[b] = jnp.where(eye, scale, 0.0)
        if b < blocks - 1:
            k = k_ref[rows, :]
            both = dot(k, cat([k, v_ref[rows, :]], 1), (0, 0))
            gram = gram + both[:, :HDIM]
            pair = pair + both[:, HDIM:]
    nil = jnp.zeros((HDIM, HDIM), BF16)

    def step(j, carry):
        for b in range(blocks):
            e, x = es[b], xs[b]
            eh, el = split(e)
            xh, xl = split(x)
            e_ref[0, j, b] = eh
            x_ref[0, j, b] = xh
            left = cat([cat([eh, el], 1), cat([xh, xl], 1)], 0)
            right = cat([cat([eh, el], 1), cat([eh, nil], 1)], 0)
            both = dot(left, right)
            both = both[:, :HDIM] + both[:, HDIM:]
            es[b] = 2.0 * e - both[:HDIM]
            xs[b] = 2.0 * x - both[HDIM:]
        return carry

    lax.fori_loop(0, NEWTON, step, 0)
    keep = causal()
    for b in range(blocks):
        rows = slice(b * SPAN, (b + 1) * SPAN)
        q, k, v = q_ref[rows, :], k_ref[rows, :], v_ref[rows, :]
        x = xs[b]
        last_ref[0, b] = x
        xh, xl = split(x)
        sh, sl = split(dot(cat([q, q], 1), cat([xh, xl], 0)))
        scores = dot(cat([sh, sl], 1), cat([k, k], 1), (1, 1))
        scores = jnp.where(keep, scores, 0.0).astype(BF16)
        nh, nl = split(pre_ref[0, b])
        out = dot(scores, v) + dot(cat([sh, sl], 1), cat([nh, nh], 0)) + dot(sh, nl)
        out_ref[rows, :] = out.astype(BF16)


def column(tok, index=0):
    return pl.BlockSpec((tok, HDIM), lambda h: (0, h))


def per_head(*dims):
    return pl.BlockSpec((1,) + dims, lambda h: (h,) + (0,) * len(dims))


def primal(queries, keys, values, gram, pair, heads, blocks):
    tok = queries.shape[0]
    stash = shape((heads, NEWTON, blocks, HDIM, HDIM), BF16)
    state = shape((heads, blocks, HDIM, HDIM))
    return pl.pallas_call(
        primal_kernel,
        grid=(heads,),
        out_shape=(shape(queries.shape, BF16), stash, stash, state, state, state),
        in_specs=[column(tok)] * 3 + [per_head(HDIM, HDIM)] * 2,
        out_specs=(column(tok),)
        + (per_head(NEWTON, blocks, HDIM, HDIM),) * 2
        + (per_head(blocks, HDIM, HDIM),) * 3,
        scratch_shapes=[pltpu.VMEM((blocks, HDIM, HDIM), F32)] * 2,
        compiler_params=params(),
        cost_estimate=cost(4_000_000_000, 8_000_000),
    )(queries, keys, values, gram, pair)


def tangent_kernel(
    q_ref, k_ref, v_ref, do_ref, e_ref, x_ref, last_ref, a_ref, pre_ref,
    dq_ref, dk_ref, dv_ref, da_ref, dn_ref, ga_ref, gn_ref, des, dxs, first,
):
    blocks = a_ref.shape[1]
    keep = causal()
    nil = jnp.zeros((HDIM, HDIM), BF16)
    for b in range(blocks):
        rows = slice(b * SPAN, (b + 1) * SPAN)
        q, k, v, do = q_ref[rows, :], k_ref[rows, :], v_ref[rows, :], do_ref[rows, :]
        weights = jnp.where(keep, dot(do, v, (1, 1)), 0.0).astype(BF16)
        nh, nl = split(pre_ref[0, b])
        ds = dot(weights, k) + dot(cat([do, do], 1), cat([nh, nl], 1), (1, 1))
        ds = ds.astype(BF16)
        xh, xl = split(last_ref[0, b])
        inverse = cat([xh, xl], 0)
        sh, sl = split(dot(cat([q, q], 1), inverse))
        scores = dot(cat([sh, sl], 1), cat([k, k], 1), (1, 1))
        scores = jnp.where(keep, scores, 0.0).astype(BF16)
        dv_ref[rows, :] = dot(scores, do, (0, 0))
        dk_ref[rows, :] = dot(weights, sh, (0, 0))
        dn_ref[0, b] = dot(sh, do, (0, 0)) + dot(sl, do, (0, 0))
        dq_ref[rows, :] = dot(cat([ds, ds], 1), inverse).astype(BF16)
        bar = dot(q, ds, (0, 0))
        bar = bar + bar.T
        ridged = a_ref[0, b]
        scale = 1.0 / jnp.sqrt(jnp.sum(ridged * ridged, keepdims=True))
        first[b] = bar
        des[b] = bar * scale
        dxs[b] = jnp.zeros((HDIM, HDIM), F32)

    def step(j, carry):
        for b in range(blocks):
            e, x = e_ref[0, j, b], x_ref[0, j, b]
            de, dx = des[b], dxs[b]
            left = cat([cat([dx.astype(BF16), x], 1), cat([nil, e], 1)], 0)
            both = dot(left, cat([e, de.astype(BF16)], 0))
            turned = both[HDIM:]
            dxs[b] = 2.0 * dx - both[:HDIM]
            des[b] = 2.0 * de - (turned + turned.T)
        return carry

    lax.fori_loop(0, NEWTON, step, 0)
    sum_a = jnp.zeros((HDIM, HDIM), F32)
    sum_n = jnp.zeros((HDIM, HDIM), F32)
    for b in range(blocks):
        ridged, dx = a_ref[0, b], dxs[b]
        square = jnp.sum(ridged * ridged, keepdims=True)
        along = jnp.sum(first[b] * last_ref[0, b] + dx * ridged, keepdims=True)
        da = dx - (along / square) * ridged
        da_ref[0, b] = da
        sum_a = sum_a + da
        sum_n = sum_n + dn_ref[0, b]
    ga_ref[0] = sum_a
    gn_ref[0] = sum_n


def tangent(queries, keys, values, grads, stash, heads, blocks):
    tok = queries.shape[0]
    state = shape((heads, blocks, HDIM, HDIM))
    total = shape((heads, HDIM, HDIM))
    wide = shape(queries.shape)
    return pl.pallas_call(
        tangent_kernel,
        grid=(heads,),
        out_shape=(shape(queries.shape, BF16), wide, wide, state, state, total, total),
        in_specs=[column(tok)] * 4
        + [per_head(NEWTON, blocks, HDIM, HDIM)] * 2
        + [per_head(blocks, HDIM, HDIM)] * 3,
        out_specs=(column(tok),) * 3
        + (per_head(blocks, HDIM, HDIM),) * 2
        + (per_head(HDIM, HDIM),) * 2,
        scratch_shapes=[pltpu.VMEM((blocks, HDIM, HDIM), F32)] * 3,
        compiler_params=params(),
        cost_estimate=cost(4_000_000_000, 8_000_000),
    )(queries, keys, values, grads, *stash)


def finish_kernel(k_ref, v_ref, dk_ref, dv_ref, da_ref, dn_ref, sa_ref, sn_ref, gk_ref, gv_ref):
    blocks = da_ref.shape[1]
    sa, sn = sa_ref[0], sn_ref[0]
    for b in reversed(range(blocks)):
        rows = slice(b * SPAN, (b + 1) * SPAN)
        k, v = k_ref[rows, :], v_ref[rows, :]
        nh, nl = split(sn)
        grad_k = dk_ref[rows, :] + dot(k, sa.astype(BF16)) + dot(cat([v, v], 1), cat([nh, nl], 1), (1, 1))
        grad_v = dv_ref[rows, :] + dot(cat([k, k], 1), cat([nh, nl], 0))
        gk_ref[rows, :] = grad_k.astype(BF16)
        gv_ref[rows, :] = grad_v.astype(BF16)
        if b:
            sa = sa + da_ref[0, b]
            sn = sn + dn_ref[0, b]


def finish(keys, values, dk, dv, da, dn, sa, sn, heads, blocks):
    tok = keys.shape[0]
    return pl.pallas_call(
        finish_kernel,
        grid=(heads,),
        out_shape=(shape(keys.shape, BF16),) * 2,
        in_specs=[column(tok)] * 4
        + [per_head(blocks, HDIM, HDIM)] * 2
        + [per_head(HDIM, HDIM)] * 2,
        out_specs=(column(tok),) * 2,
        compiler_params=params(),
        cost_estimate=cost(1_000_000_000, 6_000_000),
    )(keys, values, dk, dv, da, dn, sa, sn)


def grads_kernel(me_ref, w_ref, *refs):
    parts, out_ref = refs[:-1], refs[-1]
    me = me_ref[0]
    width = parts[0].shape[1]
    total = None
    for s, part in enumerate(parts):
        cols = pl.ds(pl.multiple_of((me ^ s) * width, width), width)
        term = dot(part[...], w_ref[:, cols], (1, 1))
        total = term if total is None else total + term
    out_ref[...] = total.astype(BF16)


def head_grads(me, w_out, parts):
    rows = parts[0].shape[0]
    return pl.pallas_call(
        grads_kernel,
        out_shape=shape((rows, w_out.shape[0]), BF16),
        in_specs=[SMEM_SPEC] + [VMEM_SPEC] * (1 + len(parts)),
        out_specs=VMEM_SPEC,
        compiler_params=params(),
        cost_estimate=cost(2 * rows * w_out.size, 6_000_000),
    )(me, w_out, *parts)


def weights_kernel(count, me_ref, h_ref, *refs):
    parts, out_ref = refs[:-1], refs[-1]
    me, mine = me_ref[0], me_ref[1]
    width = out_ref.shape[2]
    fold = parts[0].shape[1] // width
    for s, part in enumerate(parts):
        for f in range(fold):
            target = (me ^ s) * fold + f
            term = dot(h_ref[...], part[:, f * width : (f + 1) * width], (0, 0))
            out_ref[target ^ mine] = term.astype(BF16)


def weight_terms(me, heads_out, parts, count):
    feats = sum(part.shape[1] for part in parts)
    return pl.pallas_call(
        functools.partial(weights_kernel, count),
        out_shape=shape((count, heads_out.shape[1], feats // count), BF16),
        in_specs=[SMEM_SPEC] + [VMEM_SPEC] * (1 + len(parts)),
        out_specs=VMEM_SPEC,
        compiler_params=params(),
        cost_estimate=cost(2 * heads_out.size * feats, 6_000_000),
    )(me, heads_out, *parts)


def layer_kernel(*refs):
    count = (len(refs) - 1) // 2
    total = None
    for s in range(count):
        term = dot(refs[s][...], refs[count + s][...])
        total = term if total is None else total + term
    refs[-1][...] = total.astype(BF16)


def layer(parts, blocks):
    rows, cols = parts[0].shape[0], blocks[0].shape[1]
    return pl.pallas_call(
        layer_kernel,
        out_shape=shape((rows, cols), BF16),
        in_specs=[VMEM_SPEC] * (len(parts) + len(blocks)),
        out_specs=VMEM_SPEC,
        compiler_params=params(),
        cost_estimate=cost(2 * rows * cols * sum(p.shape[1] for p in parts), 6_000_000),
    )(*parts, *blocks)


def swap(value, axis, distance):
    count = lax.axis_size(axis)
    return lax.ppermute(value, axis, [(i, i ^ distance) for i in range(count)])


def gather_relative(value, axis):
    count = lax.axis_size(axis)
    near = {s: value if s == 0 else swap(value, axis, s) for s in range(0, count, 2)}
    out = []
    for s in range(0, count, 2):
        out += [near[s], swap(near[s], axis, 1)]
    return out


def before(value, axis, backward):
    count, mine = lax.axis_size(axis), lax.axis_index(axis)
    prefix = jax.tree.map(jnp.zeros_like, value)
    distance = 1
    while distance < count:
        other = jax.tree.map(lambda part: swap(part, axis, distance), value)
        upper = (mine & distance) != 0
        take = jnp.logical_not(upper) if backward else upper
        prefix = jax.tree.map(lambda p, o: p + jnp.where(take, o, 0.0), prefix, other)
        value = jax.tree.map(jnp.add, value, other)
        distance *= 2
    return prefix


def scatter_sum(terms, axis):
    count = lax.axis_size(axis)
    pairs = terms.reshape((count // 2, 2) + terms.shape[1:])
    other = swap(pairs[:, 1], axis, 1)
    half = pairs[:, 0].astype(F32) + other.astype(F32)
    total = half[0]
    for u in range(1, count // 2):
        total = total + swap(half[u].astype(BF16), axis, 2 * u).astype(F32)
    return total


def shards(queries, keys, values, w_out, cotangent):
    heads = queries.shape[1] // HDIM
    blocks = queries.shape[0] // SPAN
    head_count, ctx_count = lax.axis_size("head"), lax.axis_size("ctx")
    me_head, me_ctx = lax.axis_index("head"), lax.axis_index("ctx")
    me = jnp.stack([me_head, me_ctx]).astype(jnp.int32)

    grad_parts = gather_relative(cotangent, "head")
    gram, pair = totals(keys, values, heads)
    gram, pair = before((gram, pair), "ctx", False)
    heads_out, *stash = primal(queries, keys, values, gram, pair, heads, blocks)
    grads = head_grads(me, w_out, grad_parts)
    grad_queries, dk, dv, da, dn, sum_a, sum_n = tangent(
        queries, keys, values, grads, stash, heads, blocks
    )
    sum_a, sum_n = before((sum_a, sum_n), "ctx", True)
    grad_keys, grad_values = finish(keys, values, dk, dv, da, dn, sum_a, sum_n, heads, blocks)

    terms = weight_terms(me, heads_out, grad_parts, ctx_count)
    grad_weight = scatter_sum(terms, "ctx")

    width = w_out.shape[1] // head_count
    columns = []
    for s in range(head_count):
        mine = lax.dynamic_slice_in_dim(w_out, (me_head ^ s) * width, width, axis=1)
        columns.append(swap(mine, "head", s) if s else mine)
    layer_out = layer(gather_relative(heads_out, "head"), columns)
    return (layer_out, grad_queries, grad_keys, grad_values, grad_weight)


def solution(mesh):
    in_specs = (
        P("ctx", "head"),
        P("ctx", "head"),
        P("ctx", "head"),
        P("head", None),
        P("ctx", "head"),
    )
    out_specs = (
        P("ctx", "head"),
        P("ctx", "head"),
        P("ctx", "head"),
        P("ctx", "head"),
        P("head", "ctx"),
    )
    return jax.shard_map(shards, mesh=mesh, in_specs=in_specs, out_specs=out_specs, check_vma=False)
```

profile of v0, /device:TPU:0, one launch (start us, length us, event | category | flops | bytes accessed | tf_op | source)
XLA Modules:
  0.0 125.8 jit_solution(6107741993044518397)
XLA Ops:
  0.6 0.0 copy-start.2
  0.6 3.0 %collective-permute-start.13 = (bf16[1024,512]{1,0:T(8,128)(2,1)}, bf16[1024,512]{1,0:T(8,128)(2,1)S(1)}, u32[]{:S(2)}, u32[]{:S(2)}) collective-permute-start(bf16[1024,512]{1,0:T(8,128)(2,1)} %refs_0_.3), channel_id=1, source_target_pairs={{0,2},{1,3},{2,0},{3,1},{4,6},{5,7},{6,4},{7,5},{8,10},{9,11},{10,... | collective-permute-start | bytes 3145736 | tf_op jit(solution)/shard_map/ppermute | solution.py:338
  3.7 2.2 %shard_map.92 = (f32[2,128,128]{2,1,0:T(8,128)}, f32[2,128,128]{2,1,0:T(8,128)}) custom-call(bf16[1024,256]{1,0:T(8,128)(2,1)} %k_ref.7, bf16[1024,256]{1,0:T(8,128)(2,1)} %v_ref.7), custom_call_target="tpu_custom_call" | custom-call | flops 134217728 | bytes 1048576 | tf_op jit(solution)/shard_map/pallas_call | solution.py:70
  5.9 1.5 %collective-permute-start.3 = (f32[2,128,128]{2,1,0:T(8,128)}, f32[2,128,128]{2,1,0:T(8,128)S(1)}, u32[]{:S(2)}, u32[]{:S(2)}) collective-permute-start(f32[2,128,128]{2,1,0:T(8,128)} %get-tuple-element.23), channel_id=1, source_target_pairs={{0,4},{4,0},{8,12},{12,8},{16,20},{20,16},{24,28},{28,24},{1,5},{5... | collective-permute-start | bytes 393224 | tf_op jit(solution)/shard_map/ppermute | solution.py:338
  7.4 0.5 collective-permute-start
  7.9 4.5 %collective-permute-done.3 = f32[2,128,128]{2,1,0:T(8,128)S(1)} collective-permute-done((f32[2,128,128]{2,1,0:T(8,128)}, f32[2,128,128]{2,1,0:T(8,128)S(1)}, u32[]{:S(2)}, u32[]{:S(2)}) %collective-permute-start.3) | collective-permute-done | bytes 131104 | tf_op jit(solution)/shard_map/ppermute | solution.py:338
  12.5 0.9 add.76
  13.4 1.6 %collective-permute-start.4 = (f32[2,128,128]{2,1,0:T(8,128)S(1)}, f32[2,128,128]{2,1,0:T(8,128)S(1)}, u32[]{:S(2)}, u32[]{:S(2)}) collective-permute-start(f32[2,128,128]{2,1,0:T(8,128)S(1)} %add.76), channel_id=1, source_target_pairs={{0,8},{4,12},{8,0},{12,4},{16,24},{20,28},{24,16},{28,20},{1,9},{5... | collective-permute-start | bytes 393224 | tf_op jit(solution)/shard_map/ppermute | solution.py:338
  15.1 0.9 add.72
  16.0 0.5 collective-permute-start.1
  16.5 3.9 %collective-permute-done.4 = f32[2,128,128]{2,1,0:T(8,128)S(1)} collective-permute-done((f32[2,128,128]{2,1,0:T(8,128)S(1)}, f32[2,128,128]{2,1,0:T(8,128)S(1)}, u32[]{:S(2)}, u32[]{:S(2)}) %collective-permute-start.4) | collective-permute-done | bytes 131104 | tf_op jit(solution)/shard_map/ppermute | solution.py:338
  20.4 2.1 %collective-permute-start.5 = (f32[2,128,128]{2,1,0:T(8,128)S(1)}, f32[2,128,128]{2,1,0:T(8,128)S(1)}, u32[]{:S(2)}, u32[]{:S(2)}) collective-permute-start(f32[2,128,128]{2,1,0:T(8,128)S(1)} %add.78), channel_id=1, source_target_pairs={{0,16},{4,20},{8,24},{12,28},{16,0},{20,4},{24,8},{28,12},{1,17},{... | collective-permute-start | bytes 393224 | tf_op jit(solution)/shard_map/ppermute | solution.py:338
  22.6 1.9 %collective-permute-start.2 = (f32[2,128,128]{2,1,0:T(8,128)S(1)}, f32[2,128,128]{2,1,0:T(8,128)S(1)}, u32[]{:S(2)}, u32[]{:S(2)}) collective-permute-start(f32[2,128,128]{2,1,0:T(8,128)S(1)} %add.74), channel_id=1, source_target_pairs={{0,16},{4,20},{8,24},{12,28},{16,0},{20,4},{24,8},{28,12},{1,17},{... | collective-permute-start | bytes 393224 | tf_op jit(solution)/shard_map/ppermute | solution.py:338
  24.5 7.2 %collective-permute-done.5 = f32[2,128,128]{2,1,0:T(8,128)S(1)} collective-permute-done((f32[2,128,128]{2,1,0:T(8,128)S(1)}, f32[2,128,128]{2,1,0:T(8,128)S(1)}, u32[]{:S(2)}, u32[]{:S(2)}) %collective-permute-start.5) | collective-permute-done | bytes 131104 | tf_op jit(solution)/shard_map/ppermute | solution.py:338
  31.7 0.7 select_add_fusion.2.n_ref
  32.4 1.0 collective-permute-done.2
  33.4 0.7 select_add_fusion.3.g_ref
  34.1 10.7 %shard_map.93 = (bf16[1024,256]{1,0:T(8,128)(2,1)}, bf16[2,8,4,128,128]{4,3,2,1,0:T(8,128)(2,1)}, bf16[2,8,4,128,128]{4,3,2,1,0:T(8,128)(2,1)}, f32[2,4,128,128]...) custom-call(bf16[1024,256]{1,0:T(8,128)(2,1)} %q_ref.3, bf16[1024,256]{1,0:T(8,128)(2,1)} %k_ref.7, ...), custom_call_target="tpu_custom_call" | custom-call | flops 4000000000 | bytes 8000000 | tf_op jit(solution)/shard_map/pallas_call | solution.py:144
  44.8 0.6 collective-permute-start.7
  45.4 0.9 constant_dynamic-slice_fusion
  46.3 1.5 %collective-permute-start.10 = (bf16[256,512]{1,0:T(8,128)(2,1)}, bf16[256,512]{1,0:T(8,128)(2,1)S(1)}, u32[]{:S(2)}, u32[]{:S(2)}) collective-permute-start(bf16[256,512]{1,0:T(8,128)(2,1)} %get-tuple-element.42), channel_id=1, source_target_pairs={{0,2},{1,3},{2,0},{3,1},{4,6},{5,7},{6,4},{7,5},{8,10},{9,11},{10,... | collective-permute-start | bytes 786440 | tf_op jit(solution)/shard_map/ppermute | solution.py:338
  47.8 0.6 pad_add_fusion.me_ref
  48.4 11.6 %collective-permute-done.7.refs_2_ = bf16[1024,256]{1,0:T(8,128)(2,1)} collective-permute-done((bf16[1024,256]{1,0:T(8,128)(2,1)}, bf16[1024,256]{1,0:T(8,128)(2,1)}, u32[]{:S(2)}, u32[]{:S(2)}) %collective-permute-start.7) | collective-permute-done | bytes 524320 | tf_op jit(solution)/shard_map/ppermute | solution.py:338
  60.0 0.5 collective-permute-start.6
  60.5 0.1 collective-permute-start.8
  60.6 4.6 %shard_map.95.do_ref = bf16[1024,256]{1,0:T(8,128)(2,1)} custom-call(s32[2]{0:T(128)} %pad_add_fusion.me_ref, bf16[256,2048]{1,0:T(8,128)(2,1)} %w_ref.1, bf16[1024,512]{1,0:T(8,128)(2,1)} %refs_0_.3, bf16[1024,512]{1,0:T(8,128)(2,1)} %collective-permute-done.12.refs_1_, bf16[1024,512]{1,0:T(8,128)(2,1)} %copy-done.3, ...), custom_call_target="tpu_custom_call" | custom-call | flops 1073741824 | bytes 6000000 | tf_op jit(solution)/shard_map/pallas_call | solution.py:281
  65.2 14.5 %shard_map.96 = (bf16[1024,256]{1,0:T(8,128)(2,1)}, f32[1024,256]{1,0:T(8,128)}, f32[1024,256]{1,0:T(8,128)}, f32[2,4,128,128]{3,2,1,0:T(8,128)}, f32[2,4,128,12...) custom-call(bf16[1024,256]{1,0:T(8,128)(2,1)} %q_ref.3, bf16[1024,256]{1,0:T(8,128)(2,1)} %k_ref.7, ...), custom_call_target="tpu_custom_call" | custom-call | flops 4000000000 | bytes 8000000 | tf_op jit(solution)/shard_map/pallas_call | solution.py:220
  79.7 4.7 %shard_map.98 = bf16[8,256,256]{2,1,0:T(8,128)(2,1)} custom-call(s32[2]{0:T(128)} %pad_add_fusion.me_ref, bf16[1024,256]{1,0:T(8,128)(2,1)} %get-tuple-element.24.refs_0_.h_ref, bf16[1024,512]{1,0:T(8,128)(2,1)} %refs_0_.3, bf16[1024,512]{1,0:T(8,128)(2,1)} %collective-permute-done.12.refs_1_, bf16[1024,512]{1,0:T(8,128)(2,1)} %copy-done.3, ...), custom_call_target="tpu_custom_call" | custom-call | flops 1073741824 | bytes 6000000 | tf_op jit(solution)/shard_map/pallas_call | solution.py:305
  84.4 1.6 %collective-permute-start.18 = (f32[2,128,128]{2,1,0:T(8,128)S(1)}, f32[2,128,128]{2,1,0:T(8,128)S(1)}, u32[]{:S(2)}, u32[]{:S(2)}) collective-permute-start(f32[2,128,128]{2,1,0:T(8,128)S(1)} %copy-done.8), channel_id=1, source_target_pairs={{0,4},{4,0},{8,12},{12,8},{16,20},{20,16},{24,28},{28,24},{1,5},{5... | collective-permute-start | bytes 393224 | tf_op jit(solution)/shard_map/ppermute | solution.py:338
  86.0 0.6 collective-permute-start.15
  86.6 1.1 slice_bitcast_fusion
  87.6 3.2 %collective-permute-done.18 = f32[2,128,128]{2,1,0:T(8,128)S(1)} collective-permute-done((f32[2,128,128]{2,1,0:T(8,128)S(1)}, f32[2,128,128]{2,1,0:T(8,128)S(1)}, u32[]{:S(2)}, u32[]{:S(2)}) %collective-permute-start.18) | collective-permute-done | bytes 131104 | tf_op jit(solution)/shard_map/ppermute | solution.py:338
  90.8 1.5 %collective-permute-start.21 = (bf16[4,256,256]{2,1,0:T(8,128)(2,1)S(1)}, bf16[4,256,256]{2,1,0:T(8,128)(2,1)S(1)}, u32[]{:S(2)}, u32[]{:S(2)}) collective-permute-start(bf16[4,256,256]{2,1,0:T(8,128)(2,1)S(1)} %slice_bitcast_fusion), channel_id=1, source_target_pairs={{0,4},{4,0},{8,12},{12,8},{16,20},{20,16},{24,28},{28,24},{1,5},{5... | collective-permute-start | bytes 1572872 | tf_op jit(solution)/shard_map/ppermute | solution.py:338
  92.4 1.2 collective-permute-done.15
  93.7 4.9 %collective-permute-done.19 = f32[2,128,128]{2,1,0:T(8,128)S(1)} collective-permute-done((f32[2,128,128]{2,1,0:T(8,128)S(1)}, f32[2,128,128]{2,1,0:T(8,128)S(1)}, u32[]{:S(2)}, u32[]{:S(2)}) %collective-permute-start.19) | collective-permute-done | bytes 131104 | tf_op jit(solution)/shard_map/ppermute | solution.py:338
  98.6 3.2 %collective-permute-start.20 = (f32[2,128,128]{2,1,0:T(8,128)S(1)}, f32[2,128,128]{2,1,0:T(8,128)S(1)}, u32[]{:S(2)}, u32[]{:S(2)}) collective-permute-start(f32[2,128,128]{2,1,0:T(8,128)S(1)} %add.90), channel_id=1, source_target_pairs={{0,16},{4,20},{8,24},{12,28},{16,0},{20,4},{24,8},{28,12},{1,17},{... | collective-permute-start | bytes 393224 | tf_op jit(solution)/shard_map/ppermute | solution.py:338
  101.9 0.8 copy-done.4
  102.7 4.1 %shard_map.94 = bf16[1024,512]{1,0:T(8,128)(2,1)} custom-call(bf16[1024,256]{1,0:T(8,128)(2,1)} %get-tuple-element.24.refs_0_.h_ref, bf16[1024,256]{1,0:T(8,128)(2,1)} %collective-permute-done.6.refs_1_, bf16[1024,256]{1,0:T(8,128)(2,1)} %collective-permute-done.7.refs_2_, bf16[1024,256]{1,0:T(8,128)(2,1)} %copy-done.4, ...), custom_call_target="tpu_custom_call" | custom-call | flops 1073741824 | bytes 6000000 | tf_op jit(solution)/shard_map/pallas_call | solution.py:326
  106.8 0.1 collective-permute-start.17
  106.9 0.7 select_add_fusion.sn_ref
  107.6 0.1 fusion.3
  107.8 1.8 %collective-permute-start.22 = (bf16[256,256]{1,0:T(8,128)(2,1)S(1)}, bf16[256,256]{1,0:T(8,128)(2,1)S(1)}, u32[]{:S(2)}, u32[]{:S(2)}) collective-permute-start(bf16[256,256]{1,0:T(8,128)(2,1)S(1)} %get-tuple-element.45), channel_id=1, source_target_pairs={{0,8},{4,12},{8,0},{12,4},{16,24},{20,28},{24,16},{28,20},{1,9},{5... | collective-permute-start | bytes 393224 | tf_op jit(solution)/shard_map/ppermute | solution.py:338
  109.6 1.2 collective-permute-start.23
  110.8 1.4 %collective-permute-start.24 = (bf16[256,256]{1,0:T(8,128)(2,1)S(1)}, bf16[256,256]{1,0:T(8,128)(2,1)S(1)}, u32[]{:S(2)}, u32[]{:S(2)}) collective-permute-start(bf16[256,256]{1,0:T(8,128)(2,1)S(1)} %get-tuple-element.46), channel_id=1, source_target_pairs={{0,24},{4,28},{8,16},{12,20},{16,8},{20,12},{24,0},{28,4},{1,25},{... | collective-permute-start | bytes 393224 | tf_op jit(solution)/shard_map/ppermute | solution.py:338
  112.3 8.7 %collective-permute-done.17 = f32[2,128,128]{2,1,0:T(8,128)S(1)} collective-permute-done((f32[2,128,128]{2,1,0:T(8,128)S(1)}, f32[2,128,128]{2,1,0:T(8,128)S(1)}, u32[]{:S(2)}, u32[]{:S(2)}) %collective-permute-start.17) | collective-permute-done | bytes 131104 | tf_op jit(solution)/shard_map/ppermute | solution.py:338
  120.9 0.7 select_add_fusion.1.sa_ref
  121.6 3.5 %shard_map.97 = (bf16[1024,256]{1,0:T(8,128)(2,1)}, bf16[1024,256]{1,0:T(8,128)(2,1)}) custom-call(bf16[1024,256]{1,0:T(8,128)(2,1)} %k_ref.7, bf16[1024,256]{1,0:T(8,128)(2,1)} %v_ref.7, f32[1024,256]{1,0:T(8,128)} %get-tuple-element.31.dk_ref, f32[1024,256]{1,0:T(8,128)} %get-tuple-element.32.dv_ref, f32[2,4,128,128]{3,2,1,0:T(8,128)} %get-tuple-element.33.da_ref, ...), custom_call_target="tpu_custom_call" | custom-call | flops 1000000000 | bytes 6000000 | tf_op jit(solution)/shard_map/pallas_call | solution.py:254
  125.1 0.8 fusion.2
  (45 shorter events, 0.2 us)
Async XLA Ops:
  0.6 21.9 %copy-start.2 = (bf16[1024,512]{1,0:T(8,128)(2,1)S(1)}, bf16[1024,512]{1,0:T(8,128)(2,1)}, u32[]{:S(2)}) copy-start(bf16[1024,512]{1,0:T(8,128)(2,1)} %refs_0_.3) | copy-start | bytes 3145732
  0.6 31.7 %collective-permute-start.13 = (bf16[1024,512]{1,0:T(8,128)(2,1)}, bf16[1024,512]{1,0:T(8,128)(2,1)S(1)}, u32[]{:S(2)}, u32[]{:S(2)}) collective-permute-start(bf16[1024,512]{1,0:T(8,128)(2,1)} %refs_0_.3), channel_id=1, source_target_pairs={{0,2},{1,3},{2,0},{3,1},{4,6},{5,7},{6,4},{7,5},{8,10},{9,11},{10,... | collective-permute-start | bytes 3145736 | tf_op jit(solution)/shard_map/ppermute | solution.py:338
  5.9 6.6 %collective-permute-start.3 = (f32[2,128,128]{2,1,0:T(8,128)}, f32[2,128,128]{2,1,0:T(8,128)S(1)}, u32[]{:S(2)}, u32[]{:S(2)}) collective-permute-start(f32[2,128,128]{2,1,0:T(8,128)} %get-tuple-element.23), channel_id=1, source_target_pairs={{0,4},{4,0},{8,12},{12,8},{16,20},{20,16},{24,28},{28,24},{1,5},{5... | collective-permute-start | bytes 393224 | tf_op jit(solution)/shard_map/ppermute | solution.py:338
  7.4 7.6 %collective-permute-start = (f32[2,128,128]{2,1,0:T(8,128)}, f32[2,128,128]{2,1,0:T(8,128)S(1)}, u32[]{:S(2)}, u32[]{:S(2)}) collective-permute-start(f32[2,128,128]{2,1,0:T(8,128)} %get-tuple-element.22), channel_id=1, source_target_pairs={{0,4},{4,0},{8,12},{12,8},{16,20},{20,16},{24,28},{28,24},{1,5},{5... | collective-permute-start | bytes 393224 | tf_op jit(solution)/shard_map/ppermute | solution.py:338
  13.4 7.0 %collective-permute-start.4 = (f32[2,128,128]{2,1,0:T(8,128)S(1)}, f32[2,128,128]{2,1,0:T(8,128)S(1)}, u32[]{:S(2)}, u32[]{:S(2)}) collective-permute-start(f32[2,128,128]{2,1,0:T(8,128)S(1)} %add.76), channel_id=1, source_target_pairs={{0,8},{4,12},{8,0},{12,4},{16,24},{20,28},{24,16},{28,20},{1,9},{5... | collective-permute-start | bytes 393224 | tf_op jit(solution)/shard_map/ppermute | solution.py:338
  16.0 6.5 %collective-permute-start.1 = (f32[2,128,128]{2,1,0:T(8,128)S(1)}, f32[2,128,128]{2,1,0:T(8,128)S(1)}, u32[]{:S(2)}, u32[]{:S(2)}) collective-permute-start(f32[2,128,128]{2,1,0:T(8,128)S(1)} %add.72), channel_id=1, source_target_pairs={{0,8},{4,12},{8,0},{12,4},{16,24},{20,28},{24,16},{28,20},{1,9},{5... | collective-permute-start | bytes 393224 | tf_op jit(solution)/shard_map/ppermute | solution.py:338
  20.4 11.3 %collective-permute-start.5 = (f32[2,128,128]{2,1,0:T(8,128)S(1)}, f32[2,128,128]{2,1,0:T(8,128)S(1)}, u32[]{:S(2)}, u32[]{:S(2)}) collective-permute-start(f32[2,128,128]{2,1,0:T(8,128)S(1)} %add.78), channel_id=1, source_target_pairs={{0,16},{4,20},{8,24},{12,28},{16,0},{20,4},{24,8},{28,12},{1,17},{... | collective-permute-start | bytes 393224 | tf_op jit(solution)/shard_map/ppermute | solution.py:338
  22.5 37.5 %collective-permute-start.12 = (bf16[1024,512]{1,0:T(8,128)(2,1)S(1)}, bf16[1024,512]{1,0:T(8,128)(2,1)}, u32[]{:S(2)}, u32[]{:S(2)}) collective-permute-start(bf16[1024,512]{1,0:T(8,128)(2,1)S(1)} %copy-done.2), channel_id=1, source_target_pairs={{0,1},{1,0},{2,3},{3,2},{4,5},{5,4},{6,7},{7,6},{8,9},{9,8},{10,11... | collective-permute-start | bytes 3145736 | tf_op jit(solution)/shard_map/ppermute | solution.py:338
  22.6 10.8 %collective-permute-start.2 = (f32[2,128,128]{2,1,0:T(8,128)S(1)}, f32[2,128,128]{2,1,0:T(8,128)S(1)}, u32[]{:S(2)}, u32[]{:S(2)}) collective-permute-start(f32[2,128,128]{2,1,0:T(8,128)S(1)} %add.74), channel_id=1, source_target_pairs={{0,16},{4,20},{8,24},{12,28},{16,0},{20,4},{24,8},{28,12},{1,17},{... | collective-permute-start | bytes 393224 | tf_op jit(solution)/shard_map/ppermute | solution.py:338
  32.4 12.4 %copy-start.3 = (bf16[1024,512]{1,0:T(8,128)(2,1)}, bf16[1024,512]{1,0:T(8,128)(2,1)S(1)}, u32[]{:S(2)}) copy-start(bf16[1024,512]{1,0:T(8,128)(2,1)S(1)} %collective-permute-done.13.refs_2_) | copy-start | bytes 3145732
  32.4 28.1 %collective-permute-start.14 = (bf16[1024,512]{1,0:T(8,128)(2,1)S(1)}, bf16[1024,512]{1,0:T(8,128)(2,1)}, u32[]{:S(2)}, u32[]{:S(2)}) collective-permute-start(bf16[1024,512]{1,0:T(8,128)(2,1)S(1)} %collective-permute-done.13.refs_2_), channel_id=1, source_target_pairs={{0,1},{1,0},{2,3},{3,2},{4,5},{5,4},{6,7},{7,6},{8,9},{9,8},{10,11... | collective-permute-start | bytes 3145736 | tf_op jit(solution)/shard_map/ppermute | solution.py:338
  34.0 11.4 %copy-start = (bf16[256,2048]{1,0:T(8,128)(2,1)S(1)}, bf16[256,2048]{1,0:T(8,128)(2,1)}, u32[]{:S(2)}) copy-start(bf16[256,2048]{1,0:T(8,128)(2,1)} %w_ref.1) | copy-start | bytes 3145732
  44.8 15.2 %collective-permute-start.7 = (bf16[1024,256]{1,0:T(8,128)(2,1)}, bf16[1024,256]{1,0:T(8,128)(2,1)}, u32[]{:S(2)}, u32[]{:S(2)}) collective-permute-start(bf16[1024,256]{1,0:T(8,128)(2,1)} %get-tuple-element.24.refs_0_.h_ref), channel_id=1, source_target_pairs={{0,2},{1,3},{2,0},{3,1},{4,6},{5,7},{6,4},{7,5},{8,10},{9,11},{10,... | collective-permute-start | bytes 1572872 | tf_op jit(solution)/shard_map/ppermute | solution.py:338
  46.3 38.1 %collective-permute-start.10 = (bf16[256,512]{1,0:T(8,128)(2,1)}, bf16[256,512]{1,0:T(8,128)(2,1)S(1)}, u32[]{:S(2)}, u32[]{:S(2)}) collective-permute-start(bf16[256,512]{1,0:T(8,128)(2,1)} %get-tuple-element.42), channel_id=1, source_target_pairs={{0,2},{1,3},{2,0},{3,1},{4,6},{5,7},{6,4},{7,5},{8,10},{9,11},{10,... | collective-permute-start | bytes 786440 | tf_op jit(solution)/shard_map/ppermute | solution.py:338
  47.8 38.2 %collective-permute-start.11 = (bf16[256,512]{1,0:T(8,128)(2,1)S(1)}, bf16[256,512]{1,0:T(8,128)(2,1)S(1)}, u32[]{:S(2)}, u32[]{:S(2)}) collective-permute-start(bf16[256,512]{1,0:T(8,128)(2,1)S(1)} %get-tuple-element.41), channel_id=1, source_target_pairs={{0,3},{1,2},{2,1},{3,0},{4,7},{5,6},{6,5},{7,4},{8,11},{9,10},{10,... | collective-permute-start | bytes 786440 | tf_op jit(solution)/shard_map/ppermute | solution.py:338
  60.0 38.6 %collective-permute-start.9 = (bf16[256,512]{1,0:T(8,128)(2,1)S(1)}, bf16[256,512]{1,0:T(8,128)(2,1)}, u32[]{:S(2)}, u32[]{:S(2)}) collective-permute-start(bf16[256,512]{1,0:T(8,128)(2,1)S(1)} %get-tuple-element.43), channel_id=1, source_target_pairs={{0,1},{1,0},{2,3},{3,2},{4,5},{5,4},{6,7},{7,6},{8,9},{9,8},{10,11... | collective-permute-start | bytes 786440 | tf_op jit(solution)/shard_map/ppermute | solution.py:338
  60.0 41.9 %collective-permute-start.6 = (bf16[1024,256]{1,0:T(8,128)(2,1)}, bf16[1024,256]{1,0:T(8,128)(2,1)}, u32[]{:S(2)}, u32[]{:S(2)}) collective-permute-start(bf16[1024,256]{1,0:T(8,128)(2,1)} %get-tuple-element.24.refs_0_.h_ref), channel_id=1, source_target_pairs={{0,1},{1,0},{2,3},{3,2},{4,5},{5,4},{6,7},{7,6},{8,9},{9,8},{10,11... | collective-permute-start | bytes 1572872 | tf_op jit(solution)/shard_map/ppermute | solution.py:338
  60.5 41.4 %collective-permute-start.8 = (bf16[1024,256]{1,0:T(8,128)(2,1)}, bf16[1024,256]{1,0:T(8,128)(2,1)S(1)}, u32[]{:S(2)}, u32[]{:S(2)}) collective-permute-start(bf16[1024,256]{1,0:T(8,128)(2,1)} %collective-permute-done.7.refs_2_), channel_id=1, source_target_pairs={{0,1},{1,0},{2,3},{3,2},{4,5},{5,4},{6,7},{7,6},{8,9},{9,8},{10,11... | collective-permute-start | bytes 1572872 | tf_op jit(solution)/shard_map/ppermute | solution.py:338
  79.7 4.7 %copy-start.8 = (f32[2,128,128]{2,1,0:T(8,128)S(1)}, f32[2,128,128]{2,1,0:T(8,128)}, u32[]{:S(2)}) copy-start(f32[2,128,128]{2,1,0:T(8,128)} %get-tuple-element.36) | copy-start | bytes 393220
  79.7 6.3 %copy-start.7 = (f32[2,128,128]{2,1,0:T(8,128)S(1)}, f32[2,128,128]{2,1,0:T(8,128)}, u32[]{:S(2)}) copy-start(f32[2,128,128]{2,1,0:T(8,128)} %get-tuple-element.35) | copy-start | bytes 393220
  84.4 17.5 %copy-start.5 = (bf16[256,512]{1,0:T(8,128)(2,1)}, bf16[256,512]{1,0:T(8,128)(2,1)S(1)}, u32[]{:S(2)}) copy-start(bf16[256,512]{1,0:T(8,128)(2,1)S(1)} %collective-permute-done.10.refs_6_) | copy-start | bytes 786436
  84.4 6.4 %collective-permute-start.18 = (f32[2,128,128]{2,1,0:T(8,128)S(1)}, f32[2,128,128]{2,1,0:T(8,128)S(1)}, u32[]{:S(2)}, u32[]{:S(2)}) collective-permute-start(f32[2,128,128]{2,1,0:T(8,128)S(1)} %copy-done.8), channel_id=1, source_target_pairs={{0,4},{4,0},{8,12},{12,8},{16,20},{20,16},{24,28},{28,24},{1,5},{5... | collective-permute-start | bytes 393224 | tf_op jit(solution)/shard_map/ppermute | solution.py:338
  86.0 6.4 %copy-start.6 = (bf16[256,512]{1,0:T(8,128)(2,1)}, bf16[256,512]{1,0:T(8,128)(2,1)S(1)}, u32[]{:S(2)}) copy-start(bf16[256,512]{1,0:T(8,128)(2,1)S(1)} %collective-permute-done.11.refs_7_) | copy-start | bytes 786436
  86.0 7.6 %collective-permute-start.15 = (f32[2,128,128]{2,1,0:T(8,128)S(1)}, f32[2,128,128]{2,1,0:T(8,128)S(1)}, u32[]{:S(2)}, u32[]{:S(2)}) collective-permute-start(f32[2,128,128]{2,1,0:T(8,128)S(1)} %copy-done.7), channel_id=1, source_target_pairs={{0,4},{4,0},{8,12},{12,8},{16,20},{20,16},{24,28},{28,24},{1,5},{5... | collective-permute-start | bytes 393224 | tf_op jit(solution)/shard_map/ppermute | solution.py:338
  90.8 16.8 %collective-permute-start.21 = (bf16[4,256,256]{2,1,0:T(8,128)(2,1)S(1)}, bf16[4,256,256]{2,1,0:T(8,128)(2,1)S(1)}, u32[]{:S(2)}, u32[]{:S(2)}) collective-permute-start(bf16[4,256,256]{2,1,0:T(8,128)(2,1)S(1)} %slice_bitcast_fusion), channel_id=1, source_target_pairs={{0,4},{4,0},{8,12},{12,8},{16,20},{20,16},{24,28},{28,24},{1,5},{5... | collective-permute-start | bytes 1572872 | tf_op jit(solution)/shard_map/ppermute | solution.py:338
  93.6 5.0 %collective-permute-start.19 = (f32[2,128,128]{2,1,0:T(8,128)S(1)}, f32[2,128,128]{2,1,0:T(8,128)S(1)}, u32[]{:S(2)}, u32[]{:S(2)}) collective-permute-start(f32[2,128,128]{2,1,0:T(8,128)S(1)} %add.88), channel_id=1, source_target_pairs={{0,8},{4,12},{8,0},{12,4},{16,24},{20,28},{24,16},{28,20},{1,9},{5... | collective-permute-start | bytes 393224 | tf_op jit(solution)/shard_map/ppermute | solution.py:338
  98.6 8.2 %collective-permute-start.16 = (f32[2,128,128]{2,1,0:T(8,128)S(1)}, f32[2,128,128]{2,1,0:T(8,128)S(1)}, u32[]{:S(2)}, u32[]{:S(2)}) collective-permute-start(f32[2,128,128]{2,1,0:T(8,128)S(1)} %add.84), channel_id=1, source_target_pairs={{0,8},{4,12},{8,0},{12,4},{16,24},{20,28},{24,16},{28,20},{1,9},{5... | collective-permute-start | bytes 393224 | tf_op jit(solution)/shard_map/ppermute | solution.py:338
  98.6 8.3 %collective-permute-start.20 = (f32[2,128,128]{2,1,0:T(8,128)S(1)}, f32[2,128,128]{2,1,0:T(8,128)S(1)}, u32[]{:S(2)}, u32[]{:S(2)}) collective-permute-start(f32[2,128,128]{2,1,0:T(8,128)S(1)} %add.90), channel_id=1, source_target_pairs={{0,16},{4,20},{8,24},{12,28},{16,0},{20,4},{24,8},{28,12},{1,17},{... | collective-permute-start | bytes 393224 | tf_op jit(solution)/shard_map/ppermute | solution.py:338
  101.9 0.8 copy-start.4
  102.7 4.9 %copy-start.1 = (bf16[8,256,256]{2,1,0:T(8,128)(2,1)S(1)}, bf16[8,256,256]{2,1,0:T(8,128)(2,1)}, u32[]{:S(2)}) copy-start(bf16[8,256,256]{2,1,0:T(8,128)(2,1)} %shard_map.98) | copy-start | bytes 3145732
  106.8 14.1 %collective-permute-start.17 = (f32[2,128,128]{2,1,0:T(8,128)S(1)}, f32[2,128,128]{2,1,0:T(8,128)S(1)}, u32[]{:S(2)}, u32[]{:S(2)}) collective-permute-start(f32[2,128,128]{2,1,0:T(8,128)S(1)} %add.86), channel_id=1, source_target_pairs={{0,16},{4,20},{8,24},{12,28},{16,0},{20,4},{24,8},{28,12},{1,17},{... | collective-permute-start | bytes 393224 | tf_op jit(solution)/shard_map/ppermute | solution.py:338
  107.8 17.3 %collective-permute-start.22 = (bf16[256,256]{1,0:T(8,128)(2,1)S(1)}, bf16[256,256]{1,0:T(8,128)(2,1)S(1)}, u32[]{:S(2)}, u32[]{:S(2)}) collective-permute-start(bf16[256,256]{1,0:T(8,128)(2,1)S(1)} %get-tuple-element.45), channel_id=1, source_target_pairs={{0,8},{4,12},{8,0},{12,4},{16,24},{20,28},{24,16},{28,20},{1,9},{5... | collective-permute-start | bytes 393224 | tf_op jit(solution)/shard_map/ppermute | solution.py:338
  109.6 15.5 %collective-permute-start.23 = (bf16[256,256]{1,0:T(8,128)(2,1)S(1)}, bf16[256,256]{1,0:T(8,128)(2,1)S(1)}, u32[]{:S(2)}, u32[]{:S(2)}) collective-permute-start(bf16[256,256]{1,0:T(8,128)(2,1)S(1)} %get-tuple-element.47), channel_id=1, source_target_pairs={{0,16},{4,20},{8,24},{12,28},{16,0},{20,4},{24,8},{28,12},{1,17},{... | collective-permute-start | bytes 393224 | tf_op jit(solution)/shard_map/ppermute | solution.py:338
  110.8 14.2 %collective-permute-start.24 = (bf16[256,256]{1,0:T(8,128)(2,1)S(1)}, bf16[256,256]{1,0:T(8,128)(2,1)S(1)}, u32[]{:S(2)}, u32[]{:S(2)}) collective-permute-start(bf16[256,256]{1,0:T(8,128)(2,1)S(1)} %get-tuple-element.46), channel_id=1, source_target_pairs={{0,24},{4,28},{8,16},{12,20},{16,8},{20,12},{24,0},{28,4},{1,25},{... | collective-permute-start | bytes 393224 | tf_op jit(solution)/shard_map/ppermute | solution.py:338
where the time goes:
time: 126 us
  waiting for transfers between devices  46.3 us (37%)
  Pallas kernels  44.4 us (35%)
  starting transfers between devices  25.4 us (20%)
  other arithmetic  6.13 us (5%)
  local copies, waits for them, and re-layouts  2.82 us (2%)
    ppermute x25, waiting for transfers between devices, swap(): return lax.ppermute(value, axis, [(i, i ^ distance) for i in range(count)])  46.3 us
    ppermute x25, starting transfers between devices, swap(): return lax.ppermute(value, axis, [(i, i ^ distance) for i in range(count)])  25.4 us
    pallas_call x1, Pallas kernels, tangent(): pl.pallas_call(tangent_kernel, grid=(heads,), out_shape=(shape(queries.sh...  14.5 us
    pallas_call x1, Pallas kernels, primal(): pl.pallas_call(primal_kernel, grid=(heads,), out_shape=(shape(queries.sha...  10.7 us
    pallas_call x1, Pallas kernels, weight_terms(): pl.pallas_call(functools.partial(weights_kernel, count), out_shape=shape(...  4.65 us
    pallas_call x1, Pallas kernels, head_grads(): pl.pallas_call(grads_kernel, out_shape=shape((rows, w_out.shape[0]), BF16...  4.58 us
    pallas_call x1, Pallas kernels, layer(): pl.pallas_call(layer_kernel, out_shape=shape((rows, cols), BF16), in_spec...  4.12 us
    pallas_call x1, Pallas kernels, finish(): pl.pallas_call(finish_kernel, grid=(heads,), out_shape=(shape(keys.shape,...  3.46 us
  transfers between devices with their start and end apart: 25, of which 9 were waited for; matrix products, arithmetic and copies ran while one was open for 6% of the time, Pallas kernels for 35%

commit v1 on v0

v1 whole, which is shorter than its diff:
```python
import functools

import jax
import jax.numpy as jnp
from jax import lax
from jax.experimental import pallas as pl
from jax.experimental.pallas import tpu as pltpu
from jax.sharding import PartitionSpec as P

HDIM = 128
SPAN = 256
NEWTON = 8
RIDGE = 1.0
F32 = jnp.float32
BF16 = jnp.bfloat16
VMEM_SPEC = pl.BlockSpec(memory_space=pltpu.VMEM)
SMEM_SPEC = pl.BlockSpec(memory_space=pltpu.SMEM)


def dot(left, right, axes=(1, 0)):
    return lax.dot_general(
        left, right, (((axes[0],), (axes[1],)), ((), ())), preferred_element_type=F32
    )


def split(value):
    high = value.astype(BF16)
    return high, (value - high.astype(F32)).astype(BF16)


def cat(parts, axis):
    return jnp.concatenate(parts, axis=axis)


def params(limit=16):
    return pltpu.CompilerParams(vmem_limit_bytes=limit * 1024 * 1024)


def cost(flops, size):
    return pl.CostEstimate(flops=flops, bytes_accessed=size, transcendentals=0)


def shape(dims, dtype=F32):
    return jax.ShapeDtypeStruct(dims, dtype)


def unit():
    rows = lax.broadcasted_iota(jnp.int32, (HDIM, HDIM), 0)
    cols = lax.broadcasted_iota(jnp.int32, (HDIM, HDIM), 1)
    return rows == cols


def causal():
    rows = lax.broadcasted_iota(jnp.int32, (SPAN, SPAN), 0)
    cols = lax.broadcasted_iota(jnp.int32, (SPAN, SPAN), 1)
    return rows >= cols


def corner():
    rows = lax.broadcasted_iota(jnp.int32, (HDIM, HDIM), 0)
    cols = lax.broadcasted_iota(jnp.int32, (HDIM, HDIM), 1)
    return rows, cols


def fold(one, two):
    rows, cols = corner()
    both = jnp.where(rows <= cols, one, two)
    line = jnp.sum(jnp.where(rows == cols, two, 0.0), axis=0, keepdims=True)
    return both, jnp.broadcast_to(line, (8, HDIM))


def unfold(both, line):
    rows, cols = corner()
    turned = both.T
    one = jnp.where(rows <= cols, both, turned)
    two = jnp.where(rows > cols, both, turned)
    two = jnp.where(rows == cols, line[:1], two)
    return one, two


def folded(heads):
    return (heads + 1) // 2


def fold_into(ref, mats, base=0):
    for i in range(folded(len(mats))):
        one, two = mats[2 * i], mats[min(2 * i + 1, len(mats) - 1)]
        both, line = fold(one, two)
        top = base + i * (HDIM + 8)
        ref[top : top + HDIM, :] = both
        ref[top + HDIM : top + HDIM + 8, :] = line


def unfold_from(ref, heads, base=0):
    mats = []
    for i in range(folded(heads)):
        top = base + i * (HDIM + 8)
        mats += unfold(ref[top : top + HDIM, :], ref[top + HDIM : top + HDIM + 8, :])
    return mats[:heads]


def totals_kernel(k_ref, v_ref, g_ref, n_ref):
    grams = []
    for h in range(k_ref.shape[1] // HDIM):
        cols = slice(h * HDIM, (h + 1) * HDIM)
        k = k_ref[:, cols]
        both = dot(k, cat([k, v_ref[:, cols]], 1), (0, 0))
        grams.append(both[:, :HDIM])
        n_ref[cols, :] = both[:, HDIM:]
    fold_into(g_ref, grams)


def totals(keys, values, heads):
    return pl.pallas_call(
        totals_kernel,
        out_shape=(shape((folded(heads) * (HDIM + 8), HDIM)), shape((heads * HDIM, HDIM))),
        in_specs=[VMEM_SPEC] * 2,
        out_specs=(VMEM_SPEC, VMEM_SPEC),
        compiler_params=params(),
        cost_estimate=cost(2 * 2 * keys.size * HDIM, 4 * keys.size),
    )(keys, values)


def places(q_ref, heads):
    blocks = q_ref.shape[0] // SPAN
    for h in range(heads):
        for b in range(blocks):
            yield h, b, h * blocks + b, slice(b * SPAN, (b + 1) * SPAN), slice(h * HDIM, (h + 1) * HDIM)


def primal_kernel(
    q_ref, k_ref, v_ref, g_ref, n_ref, out_ref, e_ref, x_ref, last_ref, a_ref, pre_ref, es, xs
):
    heads = q_ref.shape[1] // HDIM
    eye = unit()
    grams = unfold_from(g_ref, heads)
    pairs = [n_ref[h * HDIM : (h + 1) * HDIM, :] for h in range(heads)]
    for h, b, i, rows, cols in places(q_ref, heads):
        ridged = grams[h] + jnp.where(eye, RIDGE, 0.0)
        scale = 1.0 / jnp.sqrt(jnp.sum(ridged * ridged, keepdims=True))
        a_ref[i] = ridged
        pre_ref[i] = pairs[h]
        es[i] = ridged * scale
        xs[i] = jnp.where(eye, scale, 0.0)
        k = k_ref[rows, cols]
        both = dot(k, cat([k, v_ref[rows, cols]], 1), (0, 0))
        grams[h] = grams[h] + both[:, :HDIM]
        pairs[h] = pairs[h] + both[:, HDIM:]
    nil = jnp.zeros((HDIM, HDIM), BF16)

    def step(j, carry):
        for i in range(es.shape[0]):
            e, x = es[i], xs[i]
            eh, el = split(e)
            xh, xl = split(x)
            e_ref[j, i] = eh
            x_ref[j, i] = xh
            left = cat([cat([eh, el], 1), cat([xh, xl], 1)], 0)
            right = cat([cat([eh, el], 1), cat([eh, nil], 1)], 0)
            both = dot(left, right)
            both = both[:, :HDIM] + both[:, HDIM:]
            es[i] = 2.0 * e - both[:HDIM]
            xs[i] = 2.0 * x - both[HDIM:]
        return carry

    lax.fori_loop(0, NEWTON, step, 0)
    keep = causal()
    for h, b, i, rows, cols in places(q_ref, heads):
        q, k, v = q_ref[rows, cols], k_ref[rows, cols], v_ref[rows, cols]
        x = xs[i]
        last_ref[i] = x
        xh, xl = split(x)
        sh, sl = split(dot(cat([q, q], 1), cat([xh, xl], 0)))
        both = cat([sh, sl], 1)
        scores = dot(both, cat([k, k], 1), (1, 1))
        scores = jnp.where(keep, scores, 0.0).astype(BF16)
        nh, nl = split(pre_ref[i])
        state = dot(both, cat([cat([nh, nl], 1), cat([nh, nil], 1)], 0))
        out = dot(scores, v) + state[:, :HDIM] + state[:, HDIM:]
        out_ref[rows, cols] = out.astype(BF16)


def primal(queries, keys, values, gram, pair, heads, blocks):
    count = heads * blocks
    stash = shape((NEWTON, count, HDIM, HDIM), BF16)
    state = shape((count, HDIM, HDIM))
    return pl.pallas_call(
        primal_kernel,
        out_shape=(shape(queries.shape, BF16), stash, stash, state, state, state),
        in_specs=[VMEM_SPEC] * 5,
        out_specs=(VMEM_SPEC,) * 6,
        scratch_shapes=[pltpu.VMEM((count, HDIM, HDIM), F32)] * 2,
        compiler_params=params(24),
        cost_estimate=cost(4_000_000_000, 8_000_000),
    )(queries, keys, values, gram, pair)


def tangent_kernel(
    q_ref, k_ref, v_ref, do_ref, e_ref, x_ref, last_ref, a_ref, pre_ref,
    dq_ref, dk_ref, dv_ref, da_ref, dn_ref, sum_ref, des, dxs, first,
):
    heads = q_ref.shape[1] // HDIM
    keep = causal()
    nil = jnp.zeros((HDIM, HDIM), BF16)
    for h, b, i, rows, cols in places(q_ref, heads):
        q, k, v, do = q_ref[rows, cols], k_ref[rows, cols], v_ref[rows, cols], do_ref[rows, cols]
        weights = jnp.where(keep, dot(do, v, (1, 1)), 0.0).astype(BF16)
        nh, nl = split(pre_ref[i])
        ds = dot(weights, k) + dot(cat([do, do], 1), cat([nh, nl], 1), (1, 1))
        ds = ds.astype(BF16)
        xh, xl = split(last_ref[i])
        inverse = cat([xh, xl], 0)
        sh, sl = split(dot(cat([q, q], 1), inverse))
        both = cat([sh, sl], 1)
        scores = dot(both, cat([k, k], 1), (1, 1))
        scores = jnp.where(keep, scores, 0.0).astype(BF16)
        dv_ref[rows, cols] = dot(scores, do, (0, 0))
        dk_ref[rows, cols] = dot(weights, sh, (0, 0))
        state = dot(both, do, (0, 0))
        dn_ref[i] = state[:HDIM] + state[HDIM:]
        dq_ref[rows, cols] = dot(cat([ds, ds], 1), inverse).astype(BF16)
        bar = dot(q, ds, (0, 0))
        bar = bar + bar.T
        ridged = a_ref[i]
        scale = 1.0 / jnp.sqrt(jnp.sum(ridged * ridged, keepdims=True))
        first[i] = bar
        des[i] = bar * scale
        dxs[i] = jnp.zeros((HDIM, HDIM), F32)

    def step(j, carry):
        for i in range(des.shape[0]):
            e, x = e_ref[j, i], x_ref[j, i]
            de, dx = des[i], dxs[i]
            left = cat([cat([dx.astype(BF16), x], 1), cat([nil, e], 1)], 0)
            both = dot(left, cat([e, de.astype(BF16)], 0))
            turned = both[HDIM:]
            dxs[i] = 2.0 * dx - both[:HDIM]
            des[i] = 2.0 * de - (turned + turned.T)
        return carry

    lax.fori_loop(0, NEWTON, step, 0)
    sum_a = [jnp.zeros((HDIM, HDIM), F32) for _ in range(heads)]
    sum_n = [jnp.zeros((HDIM, HDIM), F32) for _ in range(heads)]
    for h, b, i, rows, cols in places(q_ref, heads):
        ridged, dx = a_ref[i], dxs[i]
        square = jnp.sum(ridged * ridged, keepdims=True)
        along = jnp.sum(first[i] * last_ref[i] + dx * ridged, keepdims=True)
        da = dx - (along / square) * ridged
        da_ref[i] = da
        sum_a[h] = sum_a[h] + da
        sum_n[h] = sum_n[h] + dn_ref[i]
    for h in range(heads):
        sum_ref[h * HDIM : (h + 1) * HDIM, :] = sum_n[h]
    fold_into(sum_ref, sum_a, heads * HDIM)


def tangent(queries, keys, values, grads, stash, heads, blocks):
    count = heads * blocks
    state = shape((count, HDIM, HDIM))
    wide = shape(queries.shape)
    rows = heads * HDIM + folded(heads) * (HDIM + 8)
    return pl.pallas_call(
        tangent_kernel,
        out_shape=(shape(queries.shape, BF16), wide, wide, state, state, shape((rows, HDIM))),
        in_specs=[VMEM_SPEC] * 9,
        out_specs=(VMEM_SPEC,) * 6,
        scratch_shapes=[pltpu.VMEM((count, HDIM, HDIM), F32)] * 3,
        compiler_params=params(24),
        cost_estimate=cost(4_000_000_000, 8_000_000),
    )(queries, keys, values, grads, *stash)


def finish_kernel(k_ref, v_ref, dk_ref, dv_ref, da_ref, dn_ref, sum_ref, gk_ref, gv_ref):
    heads = k_ref.shape[1] // HDIM
    sa = unfold_from(sum_ref, heads, heads * HDIM)
    sn = [sum_ref[h * HDIM : (h + 1) * HDIM, :] for h in range(heads)]
    for h, b, i, rows, cols in reversed(list(places(k_ref, heads))):
        k, v = k_ref[rows, cols], v_ref[rows, cols]
        nh, nl = split(sn[h])
        grad_k = dk_ref[rows, cols] + dot(k, sa[h].astype(BF16))
        grad_k = grad_k + dot(cat([v, v], 1), cat([nh, nl], 1), (1, 1))
        grad_v = dv_ref[rows, cols] + dot(cat([k, k], 1), cat([nh, nl], 0))
        gk_ref[rows, cols] = grad_k.astype(BF16)
        gv_ref[rows, cols] = grad_v.astype(BF16)
        sa[h] = sa[h] + da_ref[i]
        sn[h] = sn[h] + dn_ref[i]


def finish(keys, values, dk, dv, da, dn, sums):
    return pl.pallas_call(
        finish_kernel,
        out_shape=(shape(keys.shape, BF16),) * 2,
        in_specs=[VMEM_SPEC] * 7,
        out_specs=(VMEM_SPEC,) * 2,
        compiler_params=params(),
        cost_estimate=cost(1_000_000_000, 6_000_000),
    )(keys, values, dk, dv, da, dn, sums)


def grads_kernel(first, me_ref, w_ref, *refs):
    out_ref = refs[-1]
    me = me_ref[0]
    rest = refs[:-1]
    total = None
    if first:
        total, rest = rest[0][...], rest[1:]
    for s, part in enumerate(rest):
        width = part.shape[1]
        cols = pl.ds(pl.multiple_of((me ^ (first + s)) * width, width), width)
        term = dot(part[...], w_ref[:, cols], (1, 1))
        total = term if total is None else total + term
    out_ref[...] = total.astype(out_ref.dtype)


def head_grads(me, w_out, parts, first, begun=None):
    rows = parts[0].shape[0]
    begun = [] if begun is None else [begun]
    return pl.pallas_call(
        functools.partial(grads_kernel, first),
        out_shape=shape((rows, w_out.shape[0]), BF16 if begun else F32),
        in_specs=[SMEM_SPEC] + [VMEM_SPEC] * (1 + len(parts) + len(begun)),
        out_specs=VMEM_SPEC,
        compiler_params=params(),
        cost_estimate=cost(rows * w_out.size, 4_000_000),
    )(me, w_out, *begun, *parts)


def weights_kernel(count, me_ref, h_ref, *refs):
    parts, out_ref = refs[:-1], refs[-1]
    me, mine = me_ref[0], me_ref[1]
    width = out_ref.shape[2]
    fold = parts[0].shape[1] // width
    for s, part in enumerate(parts):
        for f in range(fold):
            target = (me ^ s) * fold + f
            term = dot(h_ref[...], part[:, f * width : (f + 1) * width], (0, 0))
            out_ref[target ^ mine] = term.astype(BF16)


def weight_terms(me, heads_out, parts, count):
    feats = sum(part.shape[1] for part in parts)
    return pl.pallas_call(
        functools.partial(weights_kernel, count),
        out_shape=shape((count, heads_out.shape[1], feats // count), BF16),
        in_specs=[SMEM_SPEC] + [VMEM_SPEC] * (1 + len(parts)),
        out_specs=VMEM_SPEC,
        compiler_params=params(),
        cost_estimate=cost(2 * heads_out.size * feats, 6_000_000),
    )(me, heads_out, *parts)


def layer_kernel(*refs):
    count = (len(refs) - 1) // 2
    total = None
    for s in range(count):
        term = dot(refs[s][...], refs[count + s][...])
        total = term if total is None else total + term
    refs[-1][...] = total.astype(BF16)


def layer(parts, blocks):
    rows, cols = parts[0].shape[0], blocks[0].shape[1]
    return pl.pallas_call(
        layer_kernel,
        out_shape=shape((rows, cols), BF16),
        in_specs=[VMEM_SPEC] * (len(parts) + len(blocks)),
        out_specs=VMEM_SPEC,
        compiler_params=params(),
        cost_estimate=cost(2 * rows * cols * sum(p.shape[1] for p in parts), 6_000_000),
    )(*parts, *blocks)


def swap(value, axis, distance):
    count = lax.axis_size(axis)
    return lax.ppermute(value, axis, [(i, i ^ distance) for i in range(count)])


def after(value, *others):
    return lax.optimization_barrier((value,) + others)[0]


def before(value, axis, backward, kind):
    count, mine = lax.axis_size(axis), lax.axis_index(axis)
    prefix = jnp.zeros_like(value)
    distance = 1
    while distance < count:
        other = swap(value.astype(kind), axis, distance).astype(F32)
        upper = (mine & distance) != 0
        take = jnp.logical_not(upper) if backward else upper
        prefix = prefix + jnp.where(take, other, 0.0)
        value = value + other
        distance *= 2
    return prefix


def shards(queries, keys, values, w_out, cotangent):
    heads = queries.shape[1] // HDIM
    blocks = queries.shape[0] // SPAN
    head_count, ctx_count = lax.axis_size("head"), lax.axis_size("ctx")
    me_head, me_ctx = lax.axis_index("head"), lax.axis_index("ctx")
    me = jnp.stack([me_head, me_ctx]).astype(jnp.int32)
    evens = range(2, head_count, 2)

    far = [swap(cotangent, "head", s) for s in evens]
    near = swap(cotangent, "head", 1)
    gram, pair = totals(keys, values, heads)
    gram = before(gram, "ctx", False, F32)
    pair = before(pair, "ctx", False, F32)
    begun = head_grads(me, w_out, [cotangent, near], 0)
    gram = after(gram, begun)
    heads_out, *stash = primal(queries, keys, values, gram, pair, heads, blocks)
    grad_parts = [cotangent, near]
    for part in far:
        grad_parts += [part, swap(part, "head", 1)]
    begun = after(begun, heads_out)
    grads = head_grads(me, w_out, grad_parts[2:], 2, begun)

    outs_far = [swap(after(heads_out, grads), "head", s) for s in evens]
    outs_near = swap(after(heads_out, grads), "head", 1)
    terms = weight_terms(me, after(heads_out, grads), grad_parts, ctx_count)
    pairs = terms.reshape((ctx_count // 2, 2) + terms.shape[1:])
    other = swap(pairs[:, 1], "ctx", 1)

    width = w_out.shape[1] // head_count
    late = after(w_out, terms)
    columns = []
    for s in range(head_count):
        mine = lax.dynamic_slice_in_dim(late, (me_head ^ s) * width, width, axis=1)
        columns.append(swap(mine, "head", s) if s else mine)

    grad_queries, dk, dv, da, dn, sums = tangent(
        queries, keys, values, after(grads, terms), stash, heads, blocks
    )
    sums = before(sums, "ctx", True, BF16)

    half = pairs[:, 0].astype(F32) + after(other, grad_queries).astype(F32)
    grad_weight = half[0]
    for u in range(1, ctx_count // 2):
        grad_weight = grad_weight + swap(half[u].astype(BF16), "ctx", 2 * u).astype(F32)

    outs = [heads_out, outs_near]
    for part in outs_far:
        outs += [part, swap(after(part, grad_queries), "head", 1)]
    layer_out = layer(outs, columns)
    grad_keys, grad_values = finish(keys, values, dk, dv, da, dn, sums)
    return (layer_out, grad_queries, grad_keys, grad_values, grad_weight)


def solution(mesh):
    in_specs = (
        P("ctx", "head"),
        P("ctx", "head"),
        P("ctx", "head"),
        P("head", None),
        P("ctx", "head"),
    )
    out_specs = (
        P("ctx", "head"),
        P("ctx", "head"),
        P("ctx", "head"),
        P("ctx", "head"),
        P("head", "ctx"),
    )
    return jax.shard_map(shards, mesh=mesh, in_specs=in_specs, out_specs=out_specs, check_vma=False)
```

time: 126 us -> 112 us (0.89); the launches traced: 126 us -> 110 us
  Pallas kernels: 44.4 us -> 27.3 us
  waiting for transfers between devices: 46.3 us -> 51.2 us
  other arithmetic: 6.13 us -> 2.79 us
    pallas_call x5 -> x6, Pallas kernels: 35.6 us -> 22.3 us  [the longest x1 9.95 us: tangent(): pl.pallas_call(tangent_kernel, out_shape=(shape(queries.shape, BF16), wid...]
    ppermute x25 -> x22, waiting for transfers between devices: 46.3 us -> 51.2 us  [swap(): return lax.ppermute(value, axis, [(i, i ^ distance) for i in range(count)])]
    add x13 -> x8, other arithmetic: 5.4 us -> 2.49 us  [the longest x4 1.61 us: before(): value = value + other]
    pallas_call x1, Pallas kernels: 4.12 us -> 2.21 us  [layer(): pl.pallas_call(layer_kernel, out_shape=shape((rows, cols), BF16), in_spec...]
    pallas_call x1, Pallas kernels: 4.65 us -> 2.84 us  [weight_terms(): pl.pallas_call(functools.partial(weights_kernel, count), out_shape=shape(...]
    unnamed x18 -> x16, local copies, waits for them, and re-layouts: 0.81 us -> 2.11 us
    ppermute x25 -> x22, starting transfers between devices: 25.4 us -> 25.5 us  [swap(): return lax.ppermute(value, axis, [(i, i ^ distance) for i in range(count)])]
  transfers between devices with their start and end apart: 25 -> 22, of which waited for: 9 -> 11; matrix products, arithmetic and copies ran while one was open for 6% -> 3% of each run, Pallas kernels for 35% -> 21%
where the time goes in v1:
time: 112 us; the launch traced here: 110 us
  waiting for transfers between devices  51.2 us (46%)
  Pallas kernels  27.3 us (24%)
  starting transfers between devices  25.5 us (23%)
  other arithmetic  2.79 us (2%)
  local copies, waits for them, and re-layouts  2.28 us (2%)
    ppermute x22, waiting for transfers between devices, swap(): return lax.ppermute(value, axis, [(i, i ^ distance) for i in range(count)])  51.2 us
    ppermute x22, starting transfers between devices, swap(): return lax.ppermute(value, axis, [(i, i ^ distance) for i in range(count)])  25.5 us
    pallas_call x1, Pallas kernels, tangent(): pl.pallas_call(tangent_kernel, out_shape=(shape(queries.shape, BF16), wid...  9.95 us
    pallas_call x1, Pallas kernels, primal(): pl.pallas_call(primal_kernel, out_shape=(shape(queries.shape, BF16), stas...  6.02 us
    pallas_call x2, Pallas kernels, head_grads(): pl.pallas_call(functools.partial(grads_kernel, first), out_shape=shape((r...  4.07 us
    pallas_call x1, Pallas kernels, weight_terms(): pl.pallas_call(functools.partial(weights_kernel, count), out_shape=shape(...  2.84 us
  transfers between devices with their start and end apart: 22, of which 11 were waited for; matrix products, arithmetic and copies ran while one was open for 3% of the time, Pallas kernels for 21%

profile of v1, /device:TPU:0, one launch (start us, length us, event | category | flops | bytes accessed | tf_op | source)
XLA Modules:
  0.0 109.9 jit_solution(5437938144138800499)
XLA Ops:
  0.7 3.0 %collective-permute-start.7 = (bf16[1024,512]{1,0:T(8,128)(2,1)}, bf16[1024,512]{1,0:T(8,128)(2,1)S(1)}, u32[]{:S(2)}, u32[]{:S(2)}) collective-permute-start(bf16[1024,512]{1,0:T(8,128)(2,1)} %refs_0_.3), channel_id=1, source_target_pairs={{0,2},{1,3},{2,0},{3,1},{4,6},{5,7},{6,4},{7,5},{8,10},{9,11},{10,... | collective-permute-start | bytes 3145736 | tf_op jit(solution)/shard_map/ppermute | solution.py:375
  3.7 1.0 copy-done.2
  4.7 1.0 copy-done.4
  5.8 0.3 shard_map.92
  6.1 1.6 %collective-permute-start.4 = (f32[256,128]{1,0:T(8,128)S(1)}, f32[256,128]{1,0:T(8,128)S(1)}, u32[]{:S(2)}, u32[]{:S(2)}) collective-permute-start(f32[256,128]{1,0:T(8,128)S(1)} %get-tuple-element.30), channel_id=1, source_target_pairs={{0,4},{4,0},{8,12},{12,8},{16,20},{20,16},{24,28},{28,24},{1,5},{5... | collective-permute-start | bytes 393224 | tf_op jit(solution)/shard_map/ppermute | solution.py:375
  7.7 0.5 collective-permute-start
  8.2 5.4 %collective-permute-done = f32[136,128]{1,0:T(8,128)S(1)} collective-permute-done((f32[136,128]{1,0:T(8,128)S(1)}, f32[136,128]{1,0:T(8,128)S(1)}, u32[]{:S(2)}, u32[]{:S(2)}) %collective-permute-start) | collective-permute-done | bytes 69664 | tf_op jit(solution)/shard_map/ppermute | solution.py:375
  13.6 0.7 add.60
  14.2 1.6 %collective-permute-start.1 = (f32[136,128]{1,0:T(8,128)}, f32[136,128]{1,0:T(8,128)}, u32[]{:S(2)}, u32[]{:S(2)}) collective-permute-start(f32[136,128]{1,0:T(8,128)} %add.60), channel_id=1, source_target_pairs={{0,8},{4,12},{8,0},{12,4},{16,24},{20,28},{24,16},{28,20},{1,9},{5... | collective-permute-start | bytes 208904 | tf_op jit(solution)/shard_map/ppermute | solution.py:375
  15.8 11.2 %collective-permute-done.7.refs_1_.refs_2_ = bf16[1024,512]{1,0:T(8,128)(2,1)S(1)} collective-permute-done((bf16[1024,512]{1,0:T(8,128)(2,1)}, bf16[1024,512]{1,0:T(8,128)(2,1)S(1)}, u32[]{:S(2)}, u32[]{:S(2)}) %collective-permute-start.7) | collective-permute-done | bytes 1048608 | tf_op jit(solution)/shard_map/ppermute | solution.py:375
  27.1 1.9 %collective-permute-start.5 = (f32[256,128]{1,0:T(8,128)S(1)}, f32[256,128]{1,0:T(8,128)S(1)}, u32[]{:S(2)}, u32[]{:S(2)}) collective-permute-start(f32[256,128]{1,0:T(8,128)S(1)} %add.64), channel_id=1, source_target_pairs={{0,8},{4,12},{8,0},{12,4},{16,24},{20,28},{24,16},{28,20},{1,9},{5... | collective-permute-start | bytes 393224 | tf_op jit(solution)/shard_map/ppermute | solution.py:375
  29.0 0.9 add.62
  29.9 2.7 %collective-permute-start.2 = (f32[136,128]{1,0:T(8,128)S(1)}, f32[136,128]{1,0:T(8,128)S(1)}, u32[]{:S(2)}, u32[]{:S(2)}) collective-permute-start(f32[136,128]{1,0:T(8,128)S(1)} %add.62), channel_id=1, source_target_pairs={{0,16},{4,20},{8,24},{12,28},{16,0},{20,4},{24,8},{28,12},{1,17},{... | collective-permute-start | bytes 208904 | tf_op jit(solution)/shard_map/ppermute | solution.py:375
  32.6 0.1 pad_add_fusion.me_ref
  32.6 0.5 collective-permute-done.5
  33.2 3.3 %collective-permute-start.6 = (f32[256,128]{1,0:T(8,128)S(1)}, f32[256,128]{1,0:T(8,128)S(1)}, u32[]{:S(2)}, u32[]{:S(2)}) collective-permute-start(f32[256,128]{1,0:T(8,128)S(1)} %add.66), channel_id=1, source_target_pairs={{0,16},{4,20},{8,24},{12,28},{16,0},{20,4},{24,8},{28,12},{1,17},{... | collective-permute-start | bytes 393224 | tf_op jit(solution)/shard_map/ppermute | solution.py:375
  36.5 6.0 %collective-permute-done.6 = f32[256,128]{1,0:T(8,128)S(1)} collective-permute-done((f32[256,128]{1,0:T(8,128)S(1)}, f32[256,128]{1,0:T(8,128)S(1)}, u32[]{:S(2)}, u32[]{:S(2)}) %collective-permute-start.6) | collective-permute-done | bytes 131104 | tf_op jit(solution)/shard_map/ppermute | solution.py:375
  42.5 0.0 copy-start.3
  42.5 0.0 copy-start.5
  42.5 0.0 copy-start.6
  42.6 2.1 %shard_map.93.refs_0_ = f32[1024,256]{1,0:T(8,128)S(1)} custom-call(s32[2]{0:T(128)S(1)} %pad_add_fusion.me_ref, bf16[256,2048]{1,0:T(8,128)(2,1)S(1)} %copy-done, bf16[1024,512]{1,0:T(8,128)(2,1)S(1)} %copy-done.1, bf16[1024,512]{1,0:T(8,128)(2,1)} %collective-permute-done.3.refs_1_), custom_call_target="tpu_custom_call" | custom-call | flops 536870912 | bytes 4000000 | tf_op jit(solution)/shard_map/pallas_call | solution.py:318
  44.7 6.0 %shard_map.94 = (bf16[1024,256]{1,0:T(8,128)(2,1)S(1)}, bf16[8,8,128,128]{3,2,1,0:T(8,128)(2,1)S(1)}, bf16[8,8,128,128]{3,2,1,0:T(8,128)(2,1)S(1)}, f32[8,128,12...) custom-call(bf16[1024,256]{1,0:T(8,128)(2,1)S(1)} %copy-done.6, ...), custom_call_target="tpu_custom_call" | custom-call | flops 4000000000 | bytes 8000000 | tf_op jit(solution)/shard_map/pallas_call | solution.py:187
  50.7 2.0 %shard_map.95.do_ref = bf16[1024,256]{1,0:T(8,128)(2,1)S(1)} custom-call(s32[2]{0:T(128)S(1)} %pad_add_fusion.me_ref, bf16[256,2048]{1,0:T(8,128)(2,1)S(1)} %copy-done, f32[1024,256]{1,0:T(8,128)S(1)} %shard_map.93.refs_0_, bf16[1024,512]{1,0:T(8,128)(2,1)S(1)} %collective-permute-done.7.refs_1_.refs_2_, bf16[1024,512]{1,0:T(8,128)(2,1)} %collective-permute-done.8.refs_2_.refs_3_), custom_call_target="tpu_custom_call" | custom-call | flops 536870912 | bytes 4000000 | tf_op jit(solution)/shard_map/pallas_call | solution.py:318
  52.7 1.6 %collective-permute-start.10 = (bf16[1024,256]{1,0:T(8,128)(2,1)S(1)}, bf16[1024,256]{1,0:T(8,128)(2,1)S(1)}, u32[]{:S(2)}, u32[]{:S(2)}) collective-permute-start(bf16[1024,256]{1,0:T(8,128)(2,1)S(1)} %get-tuple-element.33.h_ref.refs_0_), channel_id=1, source_target_pairs={{0,2},{1,3},{2,0},{3,1},{4,6},{5,7},{6,4},{7,5},{8,10},{9,11},{10,... | collective-permute-start | bytes 1572872 | tf_op jit(solution)/shard_map/ppermute | solution.py:375
  54.3 2.8 %shard_map.96 = bf16[8,256,256]{2,1,0:T(8,128)(2,1)S(1)} custom-call(s32[2]{0:T(128)S(1)} %pad_add_fusion.me_ref, bf16[1024,256]{1,0:T(8,128)(2,1)S(1)} %get-tuple-element.33.h_ref.refs_0_, bf16[1024,512]{1,0:T(8,128)(2,1)S(1)} %copy-done.1, bf16[1024,512]{1,0:T(8,128)(2,1)} %collective-permute-done.3.refs_1_, ...), custom_call_target="tpu_custom_call" | custom-call | flops 1073741824 | bytes 6000000 | tf_op jit(solution)/shard_map/pallas_call | solution.py:342
  57.1 0.1 collective-permute-start.9
  57.2 10.0 %shard_map.97 = (bf16[1024,256]{1,0:T(8,128)(2,1)}, f32[1024,256]{1,0:T(8,128)S(1)}, f32[1024,256]{1,0:T(8,128)S(1)}, f32[8,128,128]{2,1,0:T(8,128)S(1)}, f32[8,...) custom-call(bf16[1024,256]{1,0:T(8,128)(2,1)S(1)} %copy-done.6, bf16[1024,256]{1,0:T(8,128)(2,1)S(1)} %copy-done.3, ...), custom_call_target="tpu_custom_call" | custom-call | flops 4000000000 | bytes 8000000 | tf_op jit(solution)/shard_map/pallas_call | solution.py:262
  67.2 1.6 %collective-permute-start.15 = (bf16[392,128]{1,0:T(8,128)(2,1)S(1)}, bf16[392,128]{1,0:T(8,128)(2,1)S(1)}, u32[]{:S(2)}, u32[]{:S(2)}) collective-permute-start(bf16[392,128]{1,0:T(8,128)(2,1)S(1)} %convert_element_type.48), channel_id=1, source_target_pairs={{0,4},{4,0},{8,12},{12,8},{16,20},{20,16},{24,28},{28,24},{1,5},{5... | collective-permute-start | bytes 301064 | tf_op jit(solution)/shard_map/ppermute | solution.py:375
  68.8 0.6 collective-permute-start.18
  69.4 3.6 %collective-permute-done.15 = bf16[392,128]{1,0:T(8,128)(2,1)S(1)} collective-permute-done((bf16[392,128]{1,0:T(8,128)(2,1)S(1)}, bf16[392,128]{1,0:T(8,128)(2,1)S(1)}, u32[]{:S(2)}, u32[]{:S(2)}) %collective-permute-start.15) | collective-permute-done | bytes 100384 | tf_op jit(solution)/shard_map/ppermute | solution.py:375
  73.0 0.4 collective-permute-start.16
  73.4 0.1 constant_dynamic-slice_fusion
  73.5 4.2 %collective-permute-done.16 = bf16[392,128]{1,0:T(8,128)(2,1)S(1)} collective-permute-done((bf16[392,128]{1,0:T(8,128)(2,1)S(1)}, bf16[392,128]{1,0:T(8,128)(2,1)S(1)}, u32[]{:S(2)}, u32[]{:S(2)}) %collective-permute-start.16) | collective-permute-done | bytes 100384 | tf_op jit(solution)/shard_map/ppermute | solution.py:375
  77.7 1.8 %collective-permute-start.17 = (bf16[392,128]{1,0:T(8,128)(2,1)S(1)}, bf16[392,128]{1,0:T(8,128)(2,1)S(1)}, u32[]{:S(2)}, u32[]{:S(2)}) collective-permute-start(bf16[392,128]{1,0:T(8,128)(2,1)S(1)} %fusion.5), channel_id=1, source_target_pairs={{0,16},{4,20},{8,24},{12,28},{16,0},{20,4},{24,8},{28,12},{1,17},{... | collective-permute-start | bytes 301064 | tf_op jit(solution)/shard_map/ppermute | solution.py:375
  79.5 4.2 %collective-permute-done.18 = bf16[4,256,256]{2,1,0:T(8,128)(2,1)S(1)} collective-permute-done((bf16[4,256,256]{2,1,0:T(8,128)(2,1)S(1)}, bf16[4,256,256]{2,1,0:T(8,128)(2,1)S(1)}, u32[]{:S(2)}, u32[]{:S(2)}) %collective-permute-start.18) | collective-permute-done | bytes 524320 | tf_op jit(solution)/shard_map/ppermute | solution.py:375
  83.7 0.1 fusion.7
  83.9 0.4 collective-permute-start.19
  84.3 3.4 %collective-permute-start.20 = (bf16[256,256]{1,0:T(8,128)(2,1)S(1)}, bf16[256,256]{1,0:T(8,128)(2,1)S(1)}, u32[]{:S(2)}, u32[]{:S(2)}) collective-permute-start(bf16[256,256]{1,0:T(8,128)(2,1)S(1)} %get-tuple-element.59), channel_id=1, source_target_pairs={{0,16},{4,20},{8,24},{12,28},{16,0},{20,4},{24,8},{28,12},{1,17},{... | collective-permute-start | bytes 393224 | tf_op jit(solution)/shard_map/ppermute | solution.py:375
  87.7 0.6 collective-permute-start.21
  88.4 0.1 fusion.4.sum_ref
  88.4 2.4 %collective-permute-done.19 = bf16[256,256]{1,0:T(8,128)(2,1)S(1)} collective-permute-done((bf16[256,256]{1,0:T(8,128)(2,1)S(1)}, bf16[256,256]{1,0:T(8,128)(2,1)S(1)}, u32[]{:S(2)}, u32[]{:S(2)}) %collective-permute-start.19) | collective-permute-done | bytes 131104 | tf_op jit(solution)/shard_map/ppermute | solution.py:375
  90.8 6.8 %collective-permute-done.20 = bf16[256,256]{1,0:T(8,128)(2,1)S(1)} collective-permute-done((bf16[256,256]{1,0:T(8,128)(2,1)S(1)}, bf16[256,256]{1,0:T(8,128)(2,1)S(1)}, u32[]{:S(2)}, u32[]{:S(2)}) %collective-permute-start.20) | collective-permute-done | bytes 131104 | tf_op jit(solution)/shard_map/ppermute | solution.py:375
  97.7 0.5 collective-permute-start.13
  98.2 1.9 %shard_map.99 = (bf16[1024,256]{1,0:T(8,128)(2,1)}, bf16[1024,256]{1,0:T(8,128)(2,1)}) custom-call(bf16[1024,256]{1,0:T(8,128)(2,1)S(1)} %copy-done.3, bf16[1024,256]{1,0:T(8,128)(2,1)S(1)} %copy-done.5, f32[1024,256]{1,0:T(8,128)S(1)} %get-tuple-element.43.dk_ref, f32[1024,256]{1,0:T(8,128)S(1)} %get-tuple-element.44.dv_ref, ...), custom_call_target="tpu_custom_call" | custom-call | flops 1000000000 | bytes 6000000 | tf_op jit(solution)/shard_map/pallas_call | solution.py:290
  100.1 0.8 fusion.2
  100.8 6.0 %collective-permute-done.13.refs_6_ = bf16[256,512]{1,0:T(8,128)(2,1)S(1)} collective-permute-done((bf16[256,512]{1,0:T(8,128)(2,1)S(1)}, bf16[256,512]{1,0:T(8,128)(2,1)S(1)}, u32[]{:S(2)}, u32[]{:S(2)}) %collective-permute-start.13) | collective-permute-done | bytes 262176 | tf_op jit(solution)/shard_map/ppermute | solution.py:375
  106.8 0.9 collective-permute-done.14.refs_7_
  107.7 2.2 %shard_map.98 = bf16[1024,512]{1,0:T(8,128)(2,1)} custom-call(bf16[1024,256]{1,0:T(8,128)(2,1)S(1)} %get-tuple-element.33.h_ref.refs_0_, bf16[1024,256]{1,0:T(8,128)(2,1)S(1)} %collective-permute-done.9.refs_1_, bf16[1024,256]{1,0:T(8,128)(2,1)S(1)} %collective-permute-done.10.refs_2_, bf16[1024,256]{1,0:T(8,128)(2,1)S(1)} %collective-permute-done.11.refs_3_, ...), custom_call_target="tpu_custom_call" | custom-call | flops 1073741824 | bytes 6000000 | tf_op jit(solution)/shard_map/pallas_call | solution.py:363
  (36 shorter events, 0.3 us)
Async XLA Ops:
  0.6 41.9 %copy-start.1 = (bf16[1024,512]{1,0:T(8,128)(2,1)S(1)}, bf16[1024,512]{1,0:T(8,128)(2,1)}, u32[]{:S(2)}) copy-start(bf16[1024,512]{1,0:T(8,128)(2,1)} %refs_0_.3) | copy-start | bytes 3145732
  0.6 41.9 %copy-start = (bf16[256,2048]{1,0:T(8,128)(2,1)S(1)}, bf16[256,2048]{1,0:T(8,128)(2,1)}, u32[]{:S(2)}) copy-start(bf16[256,2048]{1,0:T(8,128)(2,1)} %w_ref.3) | copy-start | bytes 3145732
  0.7 26.4 %collective-permute-start.7 = (bf16[1024,512]{1,0:T(8,128)(2,1)}, bf16[1024,512]{1,0:T(8,128)(2,1)S(1)}, u32[]{:S(2)}, u32[]{:S(2)}) collective-permute-start(bf16[1024,512]{1,0:T(8,128)(2,1)} %refs_0_.3), channel_id=1, source_target_pairs={{0,2},{1,3},{2,0},{3,1},{4,6},{5,7},{6,4},{7,5},{8,10},{9,11},{10,... | collective-permute-start | bytes 3145736 | tf_op jit(solution)/shard_map/ppermute | solution.py:375
  3.7 38.8 %collective-permute-start.3 = (bf16[1024,512]{1,0:T(8,128)(2,1)}, bf16[1024,512]{1,0:T(8,128)(2,1)}, u32[]{:S(2)}, u32[]{:S(2)}) collective-permute-start(bf16[1024,512]{1,0:T(8,128)(2,1)} %refs_0_.3), channel_id=1, source_target_pairs={{0,1},{1,0},{2,3},{3,2},{4,5},{5,4},{6,7},{7,6},{8,9},{9,8},{10,11... | collective-permute-start | bytes 3145736 | tf_op jit(solution)/shard_map/ppermute | solution.py:375
  3.7 1.0 copy-start.2
  4.7 1.0 copy-start.4
  6.1 21.0 %collective-permute-start.4 = (f32[256,128]{1,0:T(8,128)S(1)}, f32[256,128]{1,0:T(8,128)S(1)}, u32[]{:S(2)}, u32[]{:S(2)}) collective-permute-start(f32[256,128]{1,0:T(8,128)S(1)} %get-tuple-element.30), channel_id=1, source_target_pairs={{0,4},{4,0},{8,12},{12,8},{16,20},{20,16},{24,28},{28,24},{1,5},{5... | collective-permute-start | bytes 393224 | tf_op jit(solution)/shard_map/ppermute | solution.py:375
  7.7 5.9 %collective-permute-start = (f32[136,128]{1,0:T(8,128)S(1)}, f32[136,128]{1,0:T(8,128)S(1)}, u32[]{:S(2)}, u32[]{:S(2)}) collective-permute-start(f32[136,128]{1,0:T(8,128)S(1)} %get-tuple-element.28), channel_id=1, source_target_pairs={{0,4},{4,0},{8,12},{12,8},{16,20},{20,16},{24,28},{28,24},{1,5},{5... | collective-permute-start | bytes 208904 | tf_op jit(solution)/shard_map/ppermute | solution.py:375
  13.6 13.5 %copy-start.7 = (f32[136,128]{1,0:T(8,128)}, f32[136,128]{1,0:T(8,128)S(1)}, u32[]{:S(2)}) copy-start(f32[136,128]{1,0:T(8,128)S(1)} %collective-permute-done) | copy-start | bytes 208900
  14.2 14.8 %collective-permute-start.1 = (f32[136,128]{1,0:T(8,128)}, f32[136,128]{1,0:T(8,128)}, u32[]{:S(2)}, u32[]{:S(2)}) collective-permute-start(f32[136,128]{1,0:T(8,128)} %add.60), channel_id=1, source_target_pairs={{0,8},{4,12},{8,0},{12,4},{16,24},{20,28},{24,16},{28,20},{1,9},{5... | collective-permute-start | bytes 208904 | tf_op jit(solution)/shard_map/ppermute | solution.py:375
  27.1 23.7 %collective-permute-start.8 = (bf16[1024,512]{1,0:T(8,128)(2,1)S(1)}, bf16[1024,512]{1,0:T(8,128)(2,1)}, u32[]{:S(2)}, u32[]{:S(2)}) collective-permute-start(bf16[1024,512]{1,0:T(8,128)(2,1)S(1)} %collective-permute-done.7.refs_1_.refs_2_), channel_id=1, source_target_pairs={{0,1},{1,0},{2,3},{3,2},{4,5},{5,4},{6,7},{7,6},{8,9},{9,8},{10,11... | collective-permute-start | bytes 3145736 | tf_op jit(solution)/shard_map/ppermute | solution.py:375
  27.1 6.1 %collective-permute-start.5 = (f32[256,128]{1,0:T(8,128)S(1)}, f32[256,128]{1,0:T(8,128)S(1)}, u32[]{:S(2)}, u32[]{:S(2)}) collective-permute-start(f32[256,128]{1,0:T(8,128)S(1)} %add.64), channel_id=1, source_target_pairs={{0,8},{4,12},{8,0},{12,4},{16,24},{20,28},{24,16},{28,20},{1,9},{5... | collective-permute-start | bytes 393224 | tf_op jit(solution)/shard_map/ppermute | solution.py:375
  29.9 6.5 %collective-permute-start.2 = (f32[136,128]{1,0:T(8,128)S(1)}, f32[136,128]{1,0:T(8,128)S(1)}, u32[]{:S(2)}, u32[]{:S(2)}) collective-permute-start(f32[136,128]{1,0:T(8,128)S(1)} %add.62), channel_id=1, source_target_pairs={{0,16},{4,20},{8,24},{12,28},{16,0},{20,4},{24,8},{28,12},{1,17},{... | collective-permute-start | bytes 208904 | tf_op jit(solution)/shard_map/ppermute | solution.py:375
  33.2 9.3 %collective-permute-start.6 = (f32[256,128]{1,0:T(8,128)S(1)}, f32[256,128]{1,0:T(8,128)S(1)}, u32[]{:S(2)}, u32[]{:S(2)}) collective-permute-start(f32[256,128]{1,0:T(8,128)S(1)} %add.66), channel_id=1, source_target_pairs={{0,16},{4,20},{8,24},{12,28},{16,0},{20,4},{24,8},{28,12},{1,17},{... | collective-permute-start | bytes 393224 | tf_op jit(solution)/shard_map/ppermute | solution.py:375
  42.5 2.2 %copy-start.3 = (bf16[1024,256]{1,0:T(8,128)(2,1)S(1)}, bf16[1024,256]{1,0:T(8,128)(2,1)}, u32[]{:S(2)}) copy-start(bf16[1024,256]{1,0:T(8,128)(2,1)} %k_ref.7) | copy-start | bytes 1572868
  42.5 2.2 %copy-start.5 = (bf16[1024,256]{1,0:T(8,128)(2,1)S(1)}, bf16[1024,256]{1,0:T(8,128)(2,1)}, u32[]{:S(2)}) copy-start(bf16[1024,256]{1,0:T(8,128)(2,1)} %v_ref.7) | copy-start | bytes 1572868
  42.5 2.2 %copy-start.6 = (bf16[1024,256]{1,0:T(8,128)(2,1)S(1)}, bf16[1024,256]{1,0:T(8,128)(2,1)}, u32[]{:S(2)}) copy-start(bf16[1024,256]{1,0:T(8,128)(2,1)} %q_ref.3) | copy-start | bytes 1572868
  52.7 35.0 %collective-permute-start.10 = (bf16[1024,256]{1,0:T(8,128)(2,1)S(1)}, bf16[1024,256]{1,0:T(8,128)(2,1)S(1)}, u32[]{:S(2)}, u32[]{:S(2)}) collective-permute-start(bf16[1024,256]{1,0:T(8,128)(2,1)S(1)} %get-tuple-element.33.h_ref.refs_0_), channel_id=1, source_target_pairs={{0,2},{1,3},{2,0},{3,1},{4,6},{5,7},{6,4},{7,5},{8,10},{9,11},{10,... | collective-permute-start | bytes 1572872 | tf_op jit(solution)/shard_map/ppermute | solution.py:375
  57.1 50.6 %collective-permute-start.9 = (bf16[1024,256]{1,0:T(8,128)(2,1)S(1)}, bf16[1024,256]{1,0:T(8,128)(2,1)S(1)}, u32[]{:S(2)}, u32[]{:S(2)}) collective-permute-start(bf16[1024,256]{1,0:T(8,128)(2,1)S(1)} %get-tuple-element.33.h_ref.refs_0_), channel_id=1, source_target_pairs={{0,1},{1,0},{2,3},{3,2},{4,5},{5,4},{6,7},{7,6},{8,9},{9,8},{10,11... | collective-permute-start | bytes 1572872 | tf_op jit(solution)/shard_map/ppermute | solution.py:375
  67.2 5.8 %collective-permute-start.15 = (bf16[392,128]{1,0:T(8,128)(2,1)S(1)}, bf16[392,128]{1,0:T(8,128)(2,1)S(1)}, u32[]{:S(2)}, u32[]{:S(2)}) collective-permute-start(bf16[392,128]{1,0:T(8,128)(2,1)S(1)} %convert_element_type.48), channel_id=1, source_target_pairs={{0,4},{4,0},{8,12},{12,8},{16,20},{20,16},{24,28},{28,24},{1,5},{5... | collective-permute-start | bytes 301064 | tf_op jit(solution)/shard_map/ppermute | solution.py:375
  68.8 14.9 %collective-permute-start.18 = (bf16[4,256,256]{2,1,0:T(8,128)(2,1)S(1)}, bf16[4,256,256]{2,1,0:T(8,128)(2,1)S(1)}, u32[]{:S(2)}, u32[]{:S(2)}) collective-permute-start(bf16[4,256,256]{2,1,0:T(8,128)(2,1)S(1)} %slice_bitcast_fusion), channel_id=1, source_target_pairs={{0,4},{4,0},{8,12},{12,8},{16,20},{20,16},{24,28},{28,24},{1,5},{5... | collective-permute-start | bytes 1572872 | tf_op jit(solution)/shard_map/ppermute | solution.py:375
  73.0 4.7 %collective-permute-start.16 = (bf16[392,128]{1,0:T(8,128)(2,1)S(1)}, bf16[392,128]{1,0:T(8,128)(2,1)S(1)}, u32[]{:S(2)}, u32[]{:S(2)}) collective-permute-start(bf16[392,128]{1,0:T(8,128)(2,1)S(1)} %fusion.6), channel_id=1, source_target_pairs={{0,8},{4,12},{8,0},{12,4},{16,24},{20,28},{24,16},{28,20},{1,9},{5... | collective-permute-start | bytes 301064 | tf_op jit(solution)/shard_map/ppermute | solution.py:375
  77.7 10.6 %collective-permute-start.17 = (bf16[392,128]{1,0:T(8,128)(2,1)S(1)}, bf16[392,128]{1,0:T(8,128)(2,1)S(1)}, u32[]{:S(2)}, u32[]{:S(2)}) collective-permute-start(bf16[392,128]{1,0:T(8,128)(2,1)S(1)} %fusion.5), channel_id=1, source_target_pairs={{0,16},{4,20},{8,24},{12,28},{16,0},{20,4},{24,8},{28,12},{1,17},{... | collective-permute-start | bytes 301064 | tf_op jit(solution)/shard_map/ppermute | solution.py:375
  83.9 6.9 %collective-permute-start.19 = (bf16[256,256]{1,0:T(8,128)(2,1)S(1)}, bf16[256,256]{1,0:T(8,128)(2,1)S(1)}, u32[]{:S(2)}, u32[]{:S(2)}) collective-permute-start(bf16[256,256]{1,0:T(8,128)(2,1)S(1)} %get-tuple-element.57), channel_id=1, source_target_pairs={{0,8},{4,12},{8,0},{12,4},{16,24},{20,28},{24,16},{28,20},{1,9},{5... | collective-permute-start | bytes 393224 | tf_op jit(solution)/shard_map/ppermute | solution.py:375
  84.3 13.3 %collective-permute-start.20 = (bf16[256,256]{1,0:T(8,128)(2,1)S(1)}, bf16[256,256]{1,0:T(8,128)(2,1)S(1)}, u32[]{:S(2)}, u32[]{:S(2)}) collective-permute-start(bf16[256,256]{1,0:T(8,128)(2,1)S(1)} %get-tuple-element.59), channel_id=1, source_target_pairs={{0,16},{4,20},{8,24},{12,28},{16,0},{20,4},{24,8},{28,12},{1,17},{... | collective-permute-start | bytes 393224 | tf_op jit(solution)/shard_map/ppermute | solution.py:375
  87.7 10.5 %collective-permute-start.21 = (bf16[256,256]{1,0:T(8,128)(2,1)S(1)}, bf16[256,256]{1,0:T(8,128)(2,1)S(1)}, u32[]{:S(2)}, u32[]{:S(2)}) collective-permute-start(bf16[256,256]{1,0:T(8,128)(2,1)S(1)} %get-tuple-element.58), channel_id=1, source_target_pairs={{0,24},{4,28},{8,16},{12,20},{16,8},{20,12},{24,0},{28,4},{1,25},{... | collective-permute-start | bytes 393224 | tf_op jit(solution)/shard_map/ppermute | solution.py:375
  88.4 19.4 %collective-permute-start.11 = (bf16[1024,256]{1,0:T(8,128)(2,1)S(1)}, bf16[1024,256]{1,0:T(8,128)(2,1)S(1)}, u32[]{:S(2)}, u32[]{:S(2)}) collective-permute-start(bf16[1024,256]{1,0:T(8,128)(2,1)S(1)} %collective-permute-done.10.refs_2_), channel_id=1, source_target_pairs={{0,1},{1,0},{2,3},{3,2},{4,5},{5,4},{6,7},{7,6},{8,9},{9,8},{10,11... | collective-permute-start | bytes 1572872 | tf_op jit(solution)/shard_map/ppermute | solution.py:375
  90.8 10.0 %collective-permute-start.12 = (bf16[256,512]{1,0:T(8,128)(2,1)S(1)}, bf16[256,512]{1,0:T(8,128)(2,1)S(1)}, u32[]{:S(2)}, u32[]{:S(2)}) collective-permute-start(bf16[256,512]{1,0:T(8,128)(2,1)S(1)} %get-tuple-element.55), channel_id=1, source_target_pairs={{0,1},{1,0},{2,3},{3,2},{4,5},{5,4},{6,7},{7,6},{8,9},{9,8},{10,11... | collective-permute-start | bytes 786440 | tf_op jit(solution)/shard_map/ppermute | solution.py:375
  97.7 9.1 %collective-permute-start.13 = (bf16[256,512]{1,0:T(8,128)(2,1)S(1)}, bf16[256,512]{1,0:T(8,128)(2,1)S(1)}, u32[]{:S(2)}, u32[]{:S(2)}) collective-permute-start(bf16[256,512]{1,0:T(8,128)(2,1)S(1)} %get-tuple-element.54), channel_id=1, source_target_pairs={{0,2},{1,3},{2,0},{3,1},{4,6},{5,7},{6,4},{7,5},{8,10},{9,11},{10,... | collective-permute-start | bytes 786440 | tf_op jit(solution)/shard_map/ppermute | solution.py:375
  98.2 9.5 %collective-permute-start.14 = (bf16[256,512]{1,0:T(8,128)(2,1)S(1)}, bf16[256,512]{1,0:T(8,128)(2,1)S(1)}, u32[]{:S(2)}, u32[]{:S(2)}) collective-permute-start(bf16[256,512]{1,0:T(8,128)(2,1)S(1)} %get-tuple-element.53), channel_id=1, source_target_pairs={{0,3},{1,2},{2,1},{3,0},{4,7},{5,6},{6,5},{7,4},{8,11},{9,10},{10,... | collective-permute-start | bytes 786440 | tf_op jit(solution)/shard_map/ppermute | solution.py:375

commit v2 on v1

--- a/solution.py
+++ b/solution.py
@@ -6,6 +6,7 @@
 from jax.experimental import pallas as pl
 from jax.experimental.pallas import tpu as pltpu
 from jax.sharding import PartitionSpec as P
+
 
 HDIM = 128
 SPAN = 256
@@ -128,24 +129,18 @@
             yield h, b, h * blocks + b, slice(b * SPAN, (b + 1) * SPAN), slice(h * HDIM, (h + 1) * HDIM)
 
 
-def primal_kernel(
-    q_ref, k_ref, v_ref, g_ref, n_ref, out_ref, e_ref, x_ref, last_ref, a_ref, pre_ref, es, xs
-):
-    heads = q_ref.shape[1] // HDIM
+def inverse_kernel(k_ref, g_ref, e_ref, x_ref, last_ref, a_ref, es, xs):
+    heads = k_ref.shape[1] // HDIM
     eye = unit()
     grams = unfold_from(g_ref, heads)
-    pairs = [n_ref[h * HDIM : (h + 1) * HDIM, :] for h in range(heads)]
-    for h, b, i, rows, cols in places(q_ref, heads):
+    for h, b, i, rows, cols in places(k_ref, heads):
         ridged = grams[h] + jnp.where(eye, RIDGE, 0.0)
         scale = 1.0 / jnp.sqrt(jnp.sum(ridged * ridged, keepdims=True))
         a_ref[i] = ridged
-        pre_ref[i] = pairs[h]
         es[i] = ridged * scale
         xs[i] = jnp.where(eye, scale, 0.0)
         k = k_ref[rows, cols]
-        both = dot(k, cat([k, v_ref[rows, cols]], 1), (0, 0))
-        grams[h] = grams[h] + both[:, :HDIM]
-        pairs[h] = pairs[h] + both[:, HDIM:]
+        grams[h] = grams[h] + dot(k, k, (0, 0))
     nil = jnp.zeros((HDIM, HDIM), BF16)
 
     def step(j, carry):
@@ -164,39 +159,65 @@
         return carry
 
     lax.fori_loop(0, NEWTON, step, 0)
+    for i in range(xs.shape[0]):
+        last_ref[i] = xs[i]
+
+
+def inverses(keys, gram, count):
+    stash = shape((NEWTON, count, HDIM, HDIM), BF16)
+    state = shape((count, HDIM, HDIM))
+    return pl.pallas_call(
+        inverse_kernel,
+        out_shape=(stash, stash, state, state),
+        in_specs=[VMEM_SPEC] * 2,
+        out_specs=(VMEM_SPEC,) * 4,
+        scratch_shapes=[pltpu.VMEM((count, HDIM, HDIM), F32)] * 2,
+        compiler_params=params(),
+        cost_estimate=cost(2_000_000_000, 8_000_000),
+    )(keys, gram)
+
+
+def outputs_kernel(q_ref, k_ref, v_ref, n_ref, last_ref, out_ref, pre_ref, s_ref, w_ref):
+    heads = q_ref.shape[1] // HDIM
     keep = causal()
+    nil = jnp.zeros((HDIM, HDIM), BF16)
+    pairs = [n_ref[h * HDIM : (h + 1) * HDIM, :] for h in range(heads)]
     for h, b, i, rows, cols in places(q_ref, heads):
         q, k, v = q_ref[rows, cols], k_ref[rows, cols], v_ref[rows, cols]
-        x = xs[i]
-        last_ref[i] = x
-        xh, xl = split(x)
+        xh, xl = split(last_ref[i])
         sh, sl = split(dot(cat([q, q], 1), cat([xh, xl], 0)))
         both = cat([sh, sl], 1)
+        s_ref[i] = both
         scores = dot(both, cat([k, k], 1), (1, 1))
         scores = jnp.where(keep, scores, 0.0).astype(BF16)
-        nh, nl = split(pre_ref[i])
+        w_ref[i] = scores
+        nh, nl = split(pairs[h])
+        pre_ref[i] = cat([nh, nl], 1)
         state = dot(both, cat([cat([nh, nl], 1), cat([nh, nil], 1)], 0))
         out = dot(scores, v) + state[:, :HDIM] + state[:, HDIM:]
         out_ref[rows, cols] = out.astype(BF16)
-
-
-def primal(queries, keys, values, gram, pair, heads, blocks):
-    count = heads * blocks
-    stash = shape((NEWTON, count, HDIM, HDIM), BF16)
-    state = shape((count, HDIM, HDIM))
-    return pl.pallas_call(
-        primal_kernel,
-        out_shape=(shape(queries.shape, BF16), stash, stash, state, state, state),
+        pairs[h] = pairs[h] + dot(k, v, (0, 0))
+
+
+def outputs(queries, keys, values, pair, last):
+    count = last.shape[0]
+    return pl.pallas_call(
+        outputs_kernel,
+        out_shape=(
+            shape(queries.shape, BF16),
+            shape((count, HDIM, 2 * HDIM), BF16),
+            shape((count, SPAN, 2 * HDIM), BF16),
+            shape((count, SPAN, SPAN), BF16),
+        ),
         in_specs=[VMEM_SPEC] * 5,
-        out_specs=(VMEM_SPEC,) * 6,
-        scratch_shapes=[pltpu.VMEM((count, HDIM, HDIM), F32)] * 2,
-        compiler_params=params(24),
-        cost_estimate=cost(4_000_000_000, 8_000_000),
-    )(queries, keys, values, gram, pair)
+        out_specs=(VMEM_SPEC,) * 4,
+        compiler_params=params(),
+        cost_estimate=cost(2_000_000_000, 8_000_000),
+    )(queries, keys, values, pair, last)
 
 
 def tangent_kernel(
-    q_ref, k_ref, v_ref, do_ref, e_ref, x_ref, last_ref, a_ref, pre_ref,
+    q_ref, k_ref, v_ref, do_ref, e_ref, x_ref, last_ref, a_ref, pre_ref, s_ref, w_ref,
     dq_ref, dk_ref, dv_ref, da_ref, dn_ref, sum_ref, des, dxs, first,
 ):
     heads = q_ref.shape[1] // HDIM
@@ -205,15 +226,13 @@
     for h, b, i, rows, cols in places(q_ref, heads):
         q, k, v, do = q_ref[rows, cols], k_ref[rows, cols], v_ref[rows, cols], do_ref[rows, cols]
         weights = jnp.where(keep, dot(do, v, (1, 1)), 0.0).astype(BF16)
-        nh, nl = split(pre_ref[i])
-        ds = dot(weights, k) + dot(cat([do, do], 1), cat([nh, nl], 1), (1, 1))
+        ds = dot(weights, k) + dot(cat([do, do], 1), pre_ref[i], (1, 1))
         ds = ds.astype(BF16)
         xh, xl = split(last_ref[i])
         inverse = cat([xh, xl], 0)
-        sh, sl = split(dot(cat([q, q], 1), inverse))
-        both = cat([sh, sl], 1)
-        scores = dot(both, cat([k, k], 1), (1, 1))
-        scores = jnp.where(keep, scores, 0.0).astype(BF16)
+        both = s_ref[i]
+        sh = both[:, :HDIM]
+        scores = w_ref[i]
         dv_ref[rows, cols] = dot(scores, do, (0, 0))
         dk_ref[rows, cols] = dot(weights, sh, (0, 0))
         state = dot(both, do, (0, 0))
@@ -254,15 +273,16 @@
     fold_into(sum_ref, sum_a, heads * HDIM)
 
 
-def tangent(queries, keys, values, grads, stash, heads, blocks):
-    count = heads * blocks
+def tangent(queries, keys, values, grads, stash):
+    heads = queries.shape[1] // HDIM
+    count = stash[-1].shape[0]
     state = shape((count, HDIM, HDIM))
     wide = shape(queries.shape)
     rows = heads * HDIM + folded(heads) * (HDIM + 8)
     return pl.pallas_call(
         tangent_kernel,
         out_shape=(shape(queries.shape, BF16), wide, wide, state, state, shape((rows, HDIM))),
-        in_specs=[VMEM_SPEC] * 9,
+        in_specs=[VMEM_SPEC] * 11,
         out_specs=(VMEM_SPEC,) * 6,
         scratch_shapes=[pltpu.VMEM((count, HDIM, HDIM), F32)] * 3,
         compiler_params=params(24),
@@ -297,56 +317,77 @@
     )(keys, values, dk, dv, da, dn, sums)
 
 
-def grads_kernel(first, me_ref, w_ref, *refs):
+def spans(pieces):
+    out, top = [], 0
+    for piece in pieces:
+        out.append(slice(top, top + piece.shape[0]))
+        top += piece.shape[0]
+    return out
+
+
+def groups(refs, cuts):
+    out, at = [], 0
+    for cut in cuts:
+        out.append(refs[at : at + cut])
+        at += cut
+    return out
+
+
+def grads_kernel(first, cuts, me_ref, w_ref, *refs):
     out_ref = refs[-1]
     me = me_ref[0]
-    rest = refs[:-1]
-    total = None
-    if first:
-        total, rest = rest[0][...], rest[1:]
-    for s, part in enumerate(rest):
-        width = part.shape[1]
-        cols = pl.ds(pl.multiple_of((me ^ (first + s)) * width, width), width)
-        term = dot(part[...], w_ref[:, cols], (1, 1))
-        total = term if total is None else total + term
-    out_ref[...] = total.astype(out_ref.dtype)
+    parts = groups(refs[1:-1] if first else refs[:-1], cuts)
+    for c, rows in enumerate(spans(parts[0])):
+        total = refs[0][rows, :] if first else None
+        for s, part in enumerate(parts):
+            width = part[c].shape[1]
+            cols = pl.ds(pl.multiple_of((me ^ (first + s)) * width, width), width)
+            term = dot(part[c][...], w_ref[:, cols], (1, 1))
+            total = term if total is None else total + term
+        out_ref[rows, :] = total.astype(out_ref.dtype)
 
 
 def head_grads(me, w_out, parts, first, begun=None):
-    rows = parts[0].shape[0]
+    flat = [piece for part in parts for piece in part]
+    rows = sum(piece.shape[0] for piece in parts[0])
     begun = [] if begun is None else [begun]
     return pl.pallas_call(
-        functools.partial(grads_kernel, first),
+        functools.partial(grads_kernel, first, [len(part) for part in parts]),
         out_shape=shape((rows, w_out.shape[0]), BF16 if begun else F32),
-        in_specs=[SMEM_SPEC] + [VMEM_SPEC] * (1 + len(parts) + len(begun)),
+        in_specs=[SMEM_SPEC] + [VMEM_SPEC] * (1 + len(flat) + len(begun)),
         out_specs=VMEM_SPEC,
         compiler_params=params(),
         cost_estimate=cost(rows * w_out.size, 4_000_000),
-    )(me, w_out, *begun, *parts)
-
-
-def weights_kernel(count, me_ref, h_ref, *refs):
-    parts, out_ref = refs[:-1], refs[-1]
+    )(me, w_out, *begun, *flat)
+
+
+def weights_kernel(cuts, me_ref, h_ref, *refs):
+    parts, out_ref = groups(refs[:-1], cuts), refs[-1]
     me, mine = me_ref[0], me_ref[1]
     width = out_ref.shape[2]
-    fold = parts[0].shape[1] // width
+    fold = parts[0][0].shape[1] // width
     for s, part in enumerate(parts):
         for f in range(fold):
             target = (me ^ s) * fold + f
-            term = dot(h_ref[...], part[:, f * width : (f + 1) * width], (0, 0))
-            out_ref[target ^ mine] = term.astype(BF16)
+            cols = slice(f * width, (f + 1) * width)
+            total = None
+            for piece, rows in zip(part, spans(part)):
+                term = dot(h_ref[rows, :], piece[:, cols], (0, 0))
+                total = term if total is None else total + term
+            out_ref[target ^ mine] = total.astype(BF16)
 
 
 def weight_terms(me, heads_out, parts, count):
-    feats = sum(part.shape[1] for part in parts)
-    return pl.pallas_call(
-        functools.partial(weights_kernel, count),
+    flat = [piece for part in parts for piece in part]
+    feats = sum(part[0].shape[1] for part in parts)
+    return pl.pallas_call(
+        functools.partial(weights_kernel, [len(part) for part in parts]),
         out_shape=shape((count, heads_out.shape[1], feats // count), BF16),
-        in_specs=[SMEM_SPEC] + [VMEM_SPEC] * (1 + len(parts)),
+        in_specs=[SMEM_SPEC] + [VMEM_SPEC] * (1 + len(flat)),
         out_specs=VMEM_SPEC,
         compiler_params=params(),
         cost_estimate=cost(2 * heads_out.size * feats, 6_000_000),
-    )(me, heads_out, *parts)
+    )(me, heads_out, *flat)
 
 
 def layer_kernel(*refs):
@@ -379,47 +420,62 @@
     return lax.optimization_barrier((value,) + others)[0]
 
 
-def before(value, axis, backward, kind):
-    count, mine = lax.axis_size(axis), lax.axis_index(axis)
-    prefix = jnp.zeros_like(value)
-    distance = 1
-    while distance < count:
-        other = swap(value.astype(kind), axis, distance).astype(F32)
-        upper = (mine & distance) != 0
-        take = jnp.logical_not(upper) if backward else upper
-        prefix = prefix + jnp.where(take, other, 0.0)
-        value = value + other
-        distance *= 2
-    return prefix
+def take(prefix, other, axis, distance, backward):
+    upper = (lax.axis_index(axis) & distance) != 0
+    wanted = jnp.logical_not(upper) if backward else upper
+    return prefix + jnp.where(wanted, other, 0.0)
+
+
+def doublings(axis):
+    return [1 << i for i in range((lax.axis_size(axis) - 1).bit_length())]
 
 
 def shards(queries, keys, values, w_out, cotangent):
     heads = queries.shape[1] // HDIM
-    blocks = queries.shape[0] // SPAN
+    count = heads * (queries.shape[0] // SPAN)
     head_count, ctx_count = lax.axis_size("head"), lax.axis_size("ctx")
     me_head, me_ctx = lax.axis_index("head"), lax.axis_index("ctx")
     me = jnp.stack([me_head, me_ctx]).astype(jnp.int32)
     evens = range(2, head_count, 2)
-
-    far = [swap(cotangent, "head", s) for s in evens]
-    near = swap(cotangent, "head", 1)
+    middle = cotangent.shape[0] // 2
+
     gram, pair = totals(keys, values, heads)
-    gram = before(gram, "ctx", False, F32)
-    pair = before(pair, "ctx", False, F32)
-    begun = head_grads(me, w_out, [cotangent, near], 0)
-    gram = after(gram, begun)
-    heads_out, *stash = primal(queries, keys, values, gram, pair, heads, blocks)
-    grad_parts = [cotangent, near]
-    for part in far:
-        grad_parts += [part, swap(part, "head", 1)]
-    begun = after(begun, heads_out)
-    grads = head_grads(me, w_out, grad_parts[2:], 2, begun)
-
-    outs_far = [swap(after(heads_out, grads), "head", s) for s in evens]
-    outs_near = swap(after(heads_out, grads), "head", 1)
-    terms = weight_terms(me, after(heads_out, grads), grad_parts, ctx_count)
-    pairs = terms.reshape((ctx_count // 2, 2) + terms.shape[1:])
-    other = swap(pairs[:, 1], "ctx", 1)
+    cot = after(cotangent, gram, pair)
+    pieces = (cot[:middle], cot[middle:])
+    far = {s: [swap(p, "head", s) for p in pieces] for s in evens}
+    near = swap(cot, "head", 1)
+
+    grams, pairs = jnp.zeros_like(gram), jnp.zeros_like(pair)
+    begun = None
+    crossed = {s: [] for s in evens}
+    for distance in doublings("ctx"):
+        if distance == ctx_count // 2:
+            gram = after(gram, begun)
+            for s in evens:
+                crossed[s].append(swap(after(far[s][0], gram), "head", 1))
+        other_gram = swap(gram, "ctx", distance)
+        other_pair = swap(pair, "ctx", distance)
+        grams = take(grams, other_gram, "ctx", distance, False)
+        pairs = take(pairs, other_pair, "ctx", distance, False)
+        if begun is None:
+            begun = head_grads(me, w_out, [[cotangent], [after(near, grams)]], 0)
+        gram, pair = gram + other_gram, pair + other_pair
+    *stash, last, ridged = inverses(keys, grams, count)
+    pairs = after(pairs, last)
+    for s in evens:
+        crossed[s].append(swap(after(far[s][1], pairs), "head", 1))
+    heads_out, states, solved, scores = outputs(queries, keys, values, pairs, last)
+
+    parts = []
+    for s in evens:
+        parts += [far[s], crossed[s]]
+    grads = head_grads(me, w_out, parts, 2, after(begun, heads_out))
+    parts = [[cotangent], [near]] + parts
+
+    terms = weight_terms(me, after(heads_out, grads), parts, ctx_count)
+    halves = terms.reshape((ctx_count // 2, 2) + terms.shape[1:])
+    cut = ctx_count // 4
+    sent = [swap(halves[cut:, 1], "ctx", 1), swap(halves[:cut, 1], "ctx", 1)]
 
     width = w_out.shape[1] // head_count
     late = after(w_out, terms)
@@ -427,22 +483,35 @@
     for s in range(head_count):
         mine = lax.dynamic_slice_in_dim(late, (me_head ^ s) * width, width, axis=1)
         columns.append(swap(mine, "head", s) if s else mine)
+    outs_out = after(heads_out, terms)
+    outs_far = [swap(outs_out, "head", s) for s in evens]
+    outs_near = swap(outs_out, "head", 1)
 
     grad_queries, dk, dv, da, dn, sums = tangent(
-        queries, keys, values, after(grads, terms), stash, heads, blocks
+        queries, keys, values, after(grads, terms), [*stash, last, ridged, states, solved, scores]
     )
-    sums = before(sums, "ctx", True, BF16)
-
-    half = pairs[:, 0].astype(F32) + after(other, grad_queries).astype(F32)
-    grad_weight = half[0]
-    for u in range(1, ctx_count // 2):
-        grad_weight = grad_weight + swap(half[u].astype(BF16), "ctx", 2 * u).astype(F32)
+
+    sent = after(sent[0], grad_queries), sent[1]
+    high = halves[cut:, 0].astype(F32) + sent[0].astype(F32)
+    moved = [swap(high[u].astype(BF16), "ctx", 2 * (cut + u)) for u in range(high.shape[0])]
+
+    later = jnp.zeros_like(sums)
+    for distance in doublings("ctx"):
+        other = swap(sums.astype(BF16), "ctx", distance).astype(F32)
+        later = take(later, other, "ctx", distance, True)
+        sums = sums + other
+
+    low = halves[:cut, 0].astype(F32) + after(sent[1], grad_queries).astype(F32)
+    moved += [swap(low[u].astype(BF16), "ctx", 2 * u) for u in range(1, cut)]
+    grad_weight = low[0]
+    for part in moved:
+        grad_weight = grad_weight + part.astype(F32)
 
     outs = [heads_out, outs_near]
     for part in outs_far:
         outs += [part, swap(after(part, grad_queries), "head", 1)]
     layer_out = layer(outs, columns)
-    grad_keys, grad_values = finish(keys, values, dk, dv, da, dn, sums)
+    grad_keys, grad_values = finish(keys, values, dk, dv, da, dn, later)
     return (layer_out, grad_queries, grad_keys, grad_values, grad_weight)
 
 

time: 112 us -> 111 us (level); the launches traced: 110 us -> 111 us
  local copies, waits for them, and re-layouts: 2.28 us -> 15.3 us
  waiting for transfers between devices: 51.2 us -> 40.1 us
  starting transfers between devices: 25.5 us -> 27.4 us
  other arithmetic: 2.79 us -> 1.21 us
  Pallas kernels: 27.3 us -> 25.9 us
    ppermute x22 -> x25, waiting for transfers between devices: 51.2 us -> 40.1 us  [swap(): return lax.ppermute(value, axis, [(i, i ^ distance) for i in range(count)])]
    unnamed x16 -> x46, local copies, waits for them, and re-layouts: 2.11 us -> 12.9 us
    slice x0 -> x1, local copies, waits for them, and re-layouts: none -> 2.23 us  [shards(): pieces = (cot[:middle], cot[middle:])]
    pallas_call x1, Pallas kernels: 9.95 us -> 8.03 us  [tangent(): pl.pallas_call(tangent_kernel, out_shape=(shape(queries.shape, BF16), wid...]
    ppermute x22 -> x25, starting transfers between devices: 25.5 us -> 27.4 us  [swap(): return lax.ppermute(value, axis, [(i, i ^ distance) for i in range(count)])]
    add x8 -> x7, other arithmetic: 2.49 us -> 0.91 us  [the longest x1 0.76 us: shards(): grad_weight = grad_weight + part.astype(F32)]
    pallas_call x4 -> x5, Pallas kernels: 12.9 us -> 13.4 us  [the longest x1 4.38 us: inverses(): pl.pallas_call(inverse_kernel, out_shape=(stash, stash, state, state), in...]
  transfers between devices with their start and end apart: 22 -> 25, of which waited for: 11 -> 10; matrix products, arithmetic and copies ran while one was open for 3% -> 3% of each run, Pallas kernels for 21% -> 16%
where the time goes in v2:
time: 111 us
  waiting for transfers between devices  40.1 us (36%)
  starting transfers between devices  27.4 us (25%)
  Pallas kernels  25.9 us (23%)
  local copies, waits for them, and re-layouts  15.3 us (14%)
  other arithmetic  1.21 us (1%)
    ppermute x25, waiting for transfers between devices, swap(): return lax.ppermute(value, axis, [(i, i ^ distance) for i in range(count)])  40.1 us
    ppermute x25, starting transfers between devices, swap(): return lax.ppermute(value, axis, [(i, i ^ distance) for i in range(count)])  27.4 us
    unnamed x46, local copies, waits for them, and re-layouts  12.9 us
    pallas_call x1, Pallas kernels, tangent(): pl.pallas_call(tangent_kernel, out_shape=(shape(queries.shape, BF16), wid...  8.03 us
    pallas_call x1, Pallas kernels, inverses(): pl.pallas_call(inverse_kernel, out_shape=(stash, stash, state, state), in...  4.38 us
    pallas_call x2, Pallas kernels, head_grads(): pl.pallas_call(functools.partial(grads_kernel, first, [len(part) for part...  3.69 us
    pallas_call x1, Pallas kernels, weight_terms(): pl.pallas_call(functools.partial(weights_kernel, [len(part) for part in p...  2.97 us
    pallas_call x1, Pallas kernels, outputs(): pl.pallas_call(outputs_kernel, out_shape=(shape(queries.shape, BF16), sha...  2.39 us
  transfers between devices with their start and end apart: 25, of which 10 were waited for; matrix products, arithmetic and copies ran while one was open for 3% of the time, Pallas kernels for 16%

profile of v2, /device:TPU:0, one launch (start us, length us, event | category | flops | bytes accessed | tf_op | source)
XLA Modules:
  0.0 110.9 jit_solution(8639262265151424314)
XLA Ops:
  0.7 1.2 %copy-done.5 = bf16[1024,256]{1,0:T(8,128)(2,1)S(1)} copy-done((bf16[1024,256]{1,0:T(8,128)(2,1)S(1)}, bf16[1024,256]{1,0:T(8,128)(2,1)}, u32[]{:S(2)}) %copy-start.5) | copy-done | bytes 524312
  1.8 1.0 copy-done.9
  3.2 0.6 collective-permute-start.5
  3.8 2.6 %collective-permute-start.3 = (f32[136,128]{1,0:T(8,128)S(1)}, f32[136,128]{1,0:T(8,128)S(1)}, u32[]{:S(2)}, u32[]{:S(2)}) collective-permute-start(f32[136,128]{1,0:T(8,128)S(1)} %get-tuple-element.38), channel_id=1, source_target_pairs={{0,4},{4,0},{8,12},{12,8},{16,20},{20,16},{24,28},{28,24},{1,5},{5... | collective-permute-start | bytes 208904 | tf_op jit(solution)/shard_map/ppermute | solution.py:416
  6.4 2.2 %fusion.9 = (bf16[512,512]{1,0:T(8,128)(2,1)}, bf16[512,512]{1,0:T(8,128)(2,1)}) fusion(bf16[1024,512]{1,0:T(8,128)(2,1)} %refs_0_.3), kind=kLoop, calls=%fused_computation.31 | loop fusion | bytes 2097152 | tf_op jit(solution)/shard_map/slice | solution.py:444
  8.7 1.9 %collective-permute-start.8 = (bf16[512,512]{1,0:T(8,128)(2,1)}, bf16[512,512]{1,0:T(8,128)(2,1)}, u32[]{:S(2)}, u32[]{:S(2)}) collective-permute-start(bf16[512,512]{1,0:T(8,128)(2,1)} %get-tuple-element.77), channel_id=1, source_target_pairs={{0,2},{1,3},{2,0},{3,1},{4,6},{5,7},{6,4},{7,5},{8,10},{9,11},{10,... | collective-permute-start | bytes 1572872 | tf_op jit(solution)/shard_map/ppermute | solution.py:416
  10.7 1.2 %collective-permute-done = f32[256,128]{1,0:T(8,128)S(1)} collective-permute-done((f32[256,128]{1,0:T(8,128)S(1)}, f32[256,128]{1,0:T(8,128)S(1)}, u32[]{:S(2)}, u32[]{:S(2)}) %collective-permute-start) | collective-permute-done | bytes 131104 | tf_op jit(solution)/shard_map/ppermute | solution.py:416
  12.0 1.9 %collective-permute-start.1 = (f32[256,128]{1,0:T(8,128)S(1)}, f32[256,128]{1,0:T(8,128)S(1)}, u32[]{:S(2)}, u32[]{:S(2)}) collective-permute-start(f32[256,128]{1,0:T(8,128)S(1)} %add.63), channel_id=1, source_target_pairs={{0,8},{4,12},{8,0},{12,4},{16,24},{20,28},{24,16},{28,20},{1,9},{5... | collective-permute-start | bytes 393224 | tf_op jit(solution)/shard_map/ppermute | solution.py:416
  14.1 3.6 %collective-permute-done.1 = f32[256,128]{1,0:T(8,128)S(1)} collective-permute-done((f32[256,128]{1,0:T(8,128)S(1)}, f32[256,128]{1,0:T(8,128)S(1)}, u32[]{:S(2)}, u32[]{:S(2)}) %collective-permute-start.1) | collective-permute-done | bytes 131104 | tf_op jit(solution)/shard_map/ppermute | solution.py:416
  17.8 2.8 %collective-permute-start.2 = (f32[256,128]{1,0:T(8,128)S(1)}, f32[256,128]{1,0:T(8,128)S(1)}, u32[]{:S(2)}, u32[]{:S(2)}) collective-permute-start(f32[256,128]{1,0:T(8,128)S(1)} %add.65), channel_id=1, source_target_pairs={{0,16},{4,20},{8,24},{12,28},{16,0},{20,4},{24,8},{28,12},{1,17},{... | collective-permute-start | bytes 393224 | tf_op jit(solution)/shard_map/ppermute | solution.py:416
  20.7 1.0 copy-done.2
  21.7 1.2 %copy-done.3 = bf16[1024,512]{1,0:T(8,128)(2,1)S(1)} copy-done((bf16[1024,512]{1,0:T(8,128)(2,1)S(1)}, bf16[1024,512]{1,0:T(8,128)(2,1)}, u32[]{:S(2)}) %copy-start.3) | copy-done | bytes 1048600
  22.9 1.3 %shard_map.93.refs_0_ = f32[1024,256]{1,0:T(8,128)S(1)} custom-call(s32[2]{0:T(128)S(1)} %pad_add_fusion.me_ref, bf16[256,2048]{1,0:T(8,128)(2,1)S(1)} %copy-done, bf16[1024,512]{1,0:T(8,128)(2,1)S(1)} %copy-done.1, bf16[1024,512]{1,0:T(8,128)(2,1)S(1)} %copy-done.3), custom_call_target="tpu_custom_call" | custom-call | flops 536870912 | bytes 4000000 | tf_op jit(solution)/shard_map/pallas_call | solution.py:354
  24.2 0.8 collective-permute-start.6
  25.2 8.9 %collective-permute-done.7.refs_1_.refs_2_ = bf16[512,512]{1,0:T(8,128)(2,1)} collective-permute-done((bf16[512,512]{1,0:T(8,128)(2,1)}, bf16[512,512]{1,0:T(8,128)(2,1)}, u32[]{:S(2)}, u32[]{:S(2)}) %collective-permute-start.7) | collective-permute-done | bytes 524320 | tf_op jit(solution)/shard_map/ppermute | solution.py:416
  34.2 4.4 %shard_map.94 = (bf16[8,8,128,128]{3,2,1,0:T(8,128)(2,1)S(1)}, bf16[8,8,128,128]{3,2,1,0:T(8,128)(2,1)S(1)}, f32[8,128,128]{2,1,0:T(8,128)S(1)}, f32[8,128,128]{2,1,0:T(8,128)S(1)}) custom-call(bf16[1024,256]{1,0:T(8,128)(2,1)S(1)} %copy-done.6, f32[136,128]{1,0:T(8,128)S(1)} %select_add_fusion.1.g_ref), custom_call_target="tpu_custom_call" | custom-call | flops 2000000000 | bytes 8000000 | tf_op jit(solution)/shard_map/pallas_call | solution.py:169
  38.6 1.3 %copy-done.14 = bf16[8,8,128,128]{3,2,1,0:T(8,128)(2,1)} copy-done((bf16[8,8,128,128]{3,2,1,0:T(8,128)(2,1)}, bf16[8,8,128,128]{3,2,1,0:T(8,128)(2,1)S(1)}, u32[]{:S(2)}) %copy-start.14) | copy-done | bytes 2097176
  39.9 1.4 %copy-done.16 = bf16[8,8,128,128]{3,2,1,0:T(8,128)(2,1)} copy-done((bf16[8,8,128,128]{3,2,1,0:T(8,128)(2,1)}, bf16[8,8,128,128]{3,2,1,0:T(8,128)(2,1)S(1)}, u32[]{:S(2)}) %copy-start.16) | copy-done | bytes 2097176
  41.3 0.8 copy-done.18
  42.1 0.8 copy-done.21
  42.9 0.5 collective-permute-start.10
  43.4 1.0 copy-done.7
  44.4 1.0 copy-done.10
  45.5 1.0 copy-done.12
  46.5 1.0 copy-done.19
  47.5 2.4 %shard_map.95 = (bf16[1024,256]{1,0:T(8,128)(2,1)S(1)}, bf16[8,128,256]{2,1,0:T(8,128)(2,1)S(1)}, bf16[8,256,256]{2,1,0:T(8,128)(2,1)S(1)}, bf16[8,256,256]{2,1,0:T(8,128)(2,1)S(1)}) custom-call(bf16[1024,256]{1,0:T(8,128)(2,1)S(1)} %copy-done.12, bf16[1024,256]{1,0:T(8,128)(2,1)S(1)} %copy-done.7, bf16[1024,256]{1,0:T(8,128)(2,1)S(1)} %copy-done.10, ...), custom_call_target="tpu_custom_call" | custom-call | flops 2000000000 | bytes 8000000 | tf_op jit(solution)/shard_map/pallas_call | solution.py:204
  50.0 2.4 %shard_map.96.do_ref = bf16[1024,256]{1,0:T(8,128)(2,1)S(1)} custom-call(s32[2]{0:T(128)S(1)} %pad_add_fusion.me_ref, bf16[256,2048]{1,0:T(8,128)(2,1)S(1)} %copy-done, f32[1024,256]{1,0:T(8,128)S(1)} %shard_map.93.refs_0_, bf16[512,512]{1,0:T(8,128)(2,1)} %collective-permute-done.7.refs_1_.refs_2_, bf16[512,512]{1,0:T(8,128)(2,1)} %collective-permute-done.8.refs_2_.refs_3_, ...), custom_call_target="tpu_custom_call" | custom-call | flops 536870912 | bytes 4000000 | tf_op jit(solution)/shard_map/pallas_call | solution.py:354
  52.5 3.0 %shard_map.97 = bf16[8,256,256]{2,1,0:T(8,128)(2,1)S(1)} custom-call(s32[2]{0:T(128)S(1)} %pad_add_fusion.me_ref, bf16[1024,256]{1,0:T(8,128)(2,1)S(1)} %get-tuple-element.49.h_ref.refs_0_, bf16[1024,512]{1,0:T(8,128)(2,1)S(1)} %copy-done.1, bf16[1024,512]{1,0:T(8,128)(2,1)S(1)} %copy-done.4, bf16[512,512]{1,0:T(8,128)(2,1)} %collective-permute-done.7.refs_1_.refs_2_, ...), custom_call_target="tpu_custom_call" | custom-call | flops 1073741824 | bytes 6000000 | tf_op jit(solution)/shard_map/pallas_call | solution.py:383
  55.4 1.8 %collective-permute-start.12 = (bf16[1024,256]{1,0:T(8,128)(2,1)S(1)}, bf16[1024,256]{1,0:T(8,128)(2,1)S(1)}, u32[]{:S(2)}, u32[]{:S(2)}) collective-permute-start(bf16[1024,256]{1,0:T(8,128)(2,1)S(1)} %get-tuple-element.49.h_ref.refs_0_), channel_id=1, source_target_pairs={{0,2},{1,3},{2,0},{3,1},{4,6},{5,7},{6,4},{7,5},{8,10},{9,11},{10,... | collective-permute-start | bytes 1572872 | tf_op jit(solution)/shard_map/ppermute | solution.py:416
  57.3 8.0 %shard_map.98 = (bf16[1024,256]{1,0:T(8,128)(2,1)}, f32[1024,256]{1,0:T(8,128)S(1)}, f32[1024,256]{1,0:T(8,128)S(1)}, f32[8,128,128]{2,1,0:T(8,128)S(1)}, f32[8,...) custom-call(bf16[1024,256]{1,0:T(8,128)(2,1)S(1)} %copy-done.13, bf16[1024,256]{1,0:T(8,128)(2,1)S(1)} %copy-done.8, ...), custom_call_target="tpu_custom_call" | custom-call | flops 4000000000 | bytes 8000000 | tf_op jit(solution)/shard_map/pallas_call | solution.py:282
  65.3 1.6 %collective-permute-start.17 = (bf16[392,128]{1,0:T(8,128)(2,1)S(1)}, bf16[392,128]{1,0:T(8,128)(2,1)S(1)}, u32[]{:S(2)}, u32[]{:S(2)}) collective-permute-start(bf16[392,128]{1,0:T(8,128)(2,1)S(1)} %convert_element_type.57), channel_id=1, source_target_pairs={{0,4},{4,0},{8,12},{12,8},{16,20},{20,16},{24,28},{28,24},{1,5},{5... | collective-permute-start | bytes 301064 | tf_op jit(solution)/shard_map/ppermute | solution.py:416
  66.9 0.6 collective-permute-start.20
  67.5 1.5 %collective-permute-start.21 = (bf16[2,256,256]{2,1,0:T(8,128)(2,1)S(1)}, bf16[2,256,256]{2,1,0:T(8,128)(2,1)S(1)}, u32[]{:S(2)}, u32[]{:S(2)}) collective-permute-start(bf16[2,256,256]{2,1,0:T(8,128)(2,1)S(1)} %get-tuple-element.71), channel_id=1, source_target_pairs={{0,4},{4,0},{8,12},{12,8},{16,20},{20,16},{24,28},{28,24},{1,5},{5... | collective-permute-start | bytes 786440 | tf_op jit(solution)/shard_map/ppermute | solution.py:416
  69.0 2.1 %collective-permute-done.17 = bf16[392,128]{1,0:T(8,128)(2,1)S(1)} collective-permute-done((bf16[392,128]{1,0:T(8,128)(2,1)S(1)}, bf16[392,128]{1,0:T(8,128)(2,1)S(1)}, u32[]{:S(2)}, u32[]{:S(2)}) %collective-permute-start.17) | collective-permute-done | bytes 100384 | tf_op jit(solution)/shard_map/ppermute | solution.py:416
  71.1 1.6 %collective-permute-start.18 = (bf16[392,128]{1,0:T(8,128)(2,1)S(1)}, bf16[392,128]{1,0:T(8,128)(2,1)S(1)}, u32[]{:S(2)}, u32[]{:S(2)}) collective-permute-start(bf16[392,128]{1,0:T(8,128)(2,1)S(1)} %fusion.7), channel_id=1, source_target_pairs={{0,8},{4,12},{8,0},{12,4},{16,24},{20,28},{24,16},{28,20},{1,9},{5... | collective-permute-start | bytes 301064 | tf_op jit(solution)/shard_map/ppermute | solution.py:416
  72.9 3.0 %collective-permute-done.18 = bf16[392,128]{1,0:T(8,128)(2,1)S(1)} collective-permute-done((bf16[392,128]{1,0:T(8,128)(2,1)S(1)}, bf16[392,128]{1,0:T(8,128)(2,1)S(1)}, u32[]{:S(2)}, u32[]{:S(2)}) %collective-permute-start.18) | collective-permute-done | bytes 100384 | tf_op jit(solution)/shard_map/ppermute | solution.py:416
  75.9 2.7 %collective-permute-start.19 = (bf16[392,128]{1,0:T(8,128)(2,1)S(1)}, bf16[392,128]{1,0:T(8,128)(2,1)S(1)}, u32[]{:S(2)}, u32[]{:S(2)}) collective-permute-start(bf16[392,128]{1,0:T(8,128)(2,1)S(1)} %fusion.6), channel_id=1, source_target_pairs={{0,16},{4,20},{8,24},{12,28},{16,0},{20,4},{24,8},{28,12},{1,17},{... | collective-permute-start | bytes 301064 | tf_op jit(solution)/shard_map/ppermute | solution.py:416
  78.5 3.3 %collective-permute-done.21 = bf16[2,256,256]{2,1,0:T(8,128)(2,1)S(1)} collective-permute-done((bf16[2,256,256]{2,1,0:T(8,128)(2,1)S(1)}, bf16[2,256,256]{2,1,0:T(8,128)(2,1)S(1)}, u32[]{:S(2)}, u32[]{:S(2)}) %collective-permute-start.21) | collective-permute-done | bytes 262176 | tf_op jit(solution)/shard_map/ppermute | solution.py:416
  82.0 2.6 %collective-permute-start.22 = (bf16[256,256]{1,0:T(8,128)(2,1)S(1)}, bf16[256,256]{1,0:T(8,128)(2,1)S(1)}, u32[]{:S(2)}, u32[]{:S(2)}) collective-permute-start(bf16[256,256]{1,0:T(8,128)(2,1)S(1)} %get-tuple-element.79), channel_id=1, source_target_pairs={{0,16},{4,20},{8,24},{12,28},{16,0},{20,4},{24,8},{28,12},{1,17},{... | collective-permute-start | bytes 393224 | tf_op jit(solution)/shard_map/ppermute | solution.py:416
  84.7 1.4 %collective-permute-start.23 = (bf16[256,256]{1,0:T(8,128)(2,1)S(1)}, bf16[256,256]{1,0:T(8,128)(2,1)S(1)}, u32[]{:S(2)}, u32[]{:S(2)}) collective-permute-start(bf16[256,256]{1,0:T(8,128)(2,1)S(1)} %get-tuple-element.80), channel_id=1, source_target_pairs={{0,24},{4,28},{8,16},{12,20},{16,8},{20,12},{24,0},{28,4},{1,25},{... | collective-permute-start | bytes 393224 | tf_op jit(solution)/shard_map/ppermute | solution.py:416
  86.4 8.4 %collective-permute-done.22 = bf16[256,256]{1,0:T(8,128)(2,1)S(1)} collective-permute-done((bf16[256,256]{1,0:T(8,128)(2,1)S(1)}, bf16[256,256]{1,0:T(8,128)(2,1)S(1)}, u32[]{:S(2)}, u32[]{:S(2)}) %collective-permute-start.22) | collective-permute-done | bytes 131104 | tf_op jit(solution)/shard_map/ppermute | solution.py:416
  94.8 0.5 collective-permute-start.15
  95.3 1.3 %collective-permute-start.16 = (bf16[256,512]{1,0:T(8,128)(2,1)S(1)}, bf16[256,512]{1,0:T(8,128)(2,1)S(1)}, u32[]{:S(2)}, u32[]{:S(2)}) collective-permute-start(bf16[256,512]{1,0:T(8,128)(2,1)S(1)} %get-tuple-element.73), channel_id=1, source_target_pairs={{0,3},{1,2},{2,1},{3,0},{4,7},{5,6},{6,5},{7,4},{8,11},{9,10},{10,... | collective-permute-start | bytes 786440 | tf_op jit(solution)/shard_map/ppermute | solution.py:416
  96.7 1.9 %shard_map.100 = (bf16[1024,256]{1,0:T(8,128)(2,1)}, bf16[1024,256]{1,0:T(8,128)(2,1)}) custom-call(bf16[1024,256]{1,0:T(8,128)(2,1)S(1)} %copy-done.8, bf16[1024,256]{1,0:T(8,128)(2,1)S(1)} %copy-done.11, f32[1024,256]{1,0:T(8,128)S(1)} %get-tuple-element.60.dk_ref, f32[1024,256]{1,0:T(8,128)S(1)} %get-tuple-element.61.dv_ref, ...), custom_call_target="tpu_custom_call" | custom-call | flops 1000000000 | bytes 6000000 | tf_op jit(solution)/shard_map/pallas_call | solution.py:310
  98.5 0.8 fusion.3
  99.3 4.7 %collective-permute-done.15.refs_6_ = bf16[256,512]{1,0:T(8,128)(2,1)S(1)} collective-permute-done((bf16[256,512]{1,0:T(8,128)(2,1)S(1)}, bf16[256,512]{1,0:T(8,128)(2,1)S(1)}, u32[]{:S(2)}, u32[]{:S(2)}) %collective-permute-start.15) | collective-permute-done | bytes 262176 | tf_op jit(solution)/shard_map/ppermute | solution.py:416
  104.0 4.7 %collective-permute-done.16.refs_7_ = bf16[256,512]{1,0:T(8,128)(2,1)S(1)} collective-permute-done((bf16[256,512]{1,0:T(8,128)(2,1)S(1)}, bf16[256,512]{1,0:T(8,128)(2,1)S(1)}, u32[]{:S(2)}, u32[]{:S(2)}) %collective-permute-start.16) | collective-permute-done | bytes 262176 | tf_op jit(solution)/shard_map/ppermute | solution.py:416
  108.7 2.2 %shard_map.99 = bf16[1024,512]{1,0:T(8,128)(2,1)} custom-call(bf16[1024,256]{1,0:T(8,128)(2,1)S(1)} %get-tuple-element.49.h_ref.refs_0_, bf16[1024,256]{1,0:T(8,128)(2,1)S(1)} %collective-permute-done.11.refs_1_, bf16[1024,256]{1,0:T(8,128)(2,1)S(1)} %collective-permute-done.12.refs_2_, bf16[1024,256]{1,0:T(8,128)(2,1)S(1)} %collective-permute-done.13.refs_3_, ...), custom_call_target="tpu_custom_call" | custom-call | flops 1073741824 | bytes 6000000 | tf_op jit(solution)/shard_map/pallas_call | solution.py:404
  (75 shorter events, 2.0 us)
Async XLA Ops:
  0.6 21.1 %copy-start.1 = (bf16[1024,512]{1,0:T(8,128)(2,1)S(1)}, bf16[1024,512]{1,0:T(8,128)(2,1)}, u32[]{:S(2)}) copy-start(bf16[1024,512]{1,0:T(8,128)(2,1)} %refs_0_.3) | copy-start | bytes 3145732
  0.6 21.1 %copy-start = (bf16[256,2048]{1,0:T(8,128)(2,1)S(1)}, bf16[256,2048]{1,0:T(8,128)(2,1)}, u32[]{:S(2)}) copy-start(bf16[256,2048]{1,0:T(8,128)(2,1)} %w_ref.3) | copy-start | bytes 3145732
  0.7 1.2 %copy-start.5 = (bf16[1024,256]{1,0:T(8,128)(2,1)S(1)}, bf16[1024,256]{1,0:T(8,128)(2,1)}, u32[]{:S(2)}) copy-start(bf16[1024,256]{1,0:T(8,128)(2,1)} %k_ref.9) | copy-start | bytes 1572868
  1.8 1.0 copy-start.9
  3.2 17.5 %collective-permute-start.5 = (bf16[1024,512]{1,0:T(8,128)(2,1)}, bf16[1024,512]{1,0:T(8,128)(2,1)S(1)}, u32[]{:S(2)}, u32[]{:S(2)}) collective-permute-start(bf16[1024,512]{1,0:T(8,128)(2,1)} %refs_0_.3), channel_id=1, source_target_pairs={{0,1},{1,0},{2,3},{3,2},{4,5},{5,4},{6,7},{7,6},{8,9},{9,8},{10,11... | collective-permute-start | bytes 3145736 | tf_op jit(solution)/shard_map/ppermute | solution.py:416
  3.8 10.1 %collective-permute-start.3 = (f32[136,128]{1,0:T(8,128)S(1)}, f32[136,128]{1,0:T(8,128)S(1)}, u32[]{:S(2)}, u32[]{:S(2)}) collective-permute-start(f32[136,128]{1,0:T(8,128)S(1)} %get-tuple-element.38), channel_id=1, source_target_pairs={{0,4},{4,0},{8,12},{12,8},{16,20},{20,16},{24,28},{28,24},{1,5},{5... | collective-permute-start | bytes 208904 | tf_op jit(solution)/shard_map/ppermute | solution.py:416
  6.4 5.6 %collective-permute-start = (f32[256,128]{1,0:T(8,128)S(1)}, f32[256,128]{1,0:T(8,128)S(1)}, u32[]{:S(2)}, u32[]{:S(2)}) collective-permute-start(f32[256,128]{1,0:T(8,128)S(1)} %get-tuple-element.37), channel_id=1, source_target_pairs={{0,4},{4,0},{8,12},{12,8},{16,20},{20,16},{24,28},{28,24},{1,5},{5... | collective-permute-start | bytes 393224 | tf_op jit(solution)/shard_map/ppermute | solution.py:416
  8.7 34.2 %collective-permute-start.8 = (bf16[512,512]{1,0:T(8,128)(2,1)}, bf16[512,512]{1,0:T(8,128)(2,1)}, u32[]{:S(2)}, u32[]{:S(2)}) collective-permute-start(bf16[512,512]{1,0:T(8,128)(2,1)} %get-tuple-element.77), channel_id=1, source_target_pairs={{0,2},{1,3},{2,0},{3,1},{4,6},{5,7},{6,4},{7,5},{8,10},{9,11},{10,... | collective-permute-start | bytes 1572872 | tf_op jit(solution)/shard_map/ppermute | solution.py:416
  10.6 23.5 %collective-permute-start.7 = (bf16[512,512]{1,0:T(8,128)(2,1)}, bf16[512,512]{1,0:T(8,128)(2,1)}, u32[]{:S(2)}, u32[]{:S(2)}) collective-permute-start(bf16[512,512]{1,0:T(8,128)(2,1)} %get-tuple-element.78), channel_id=1, source_target_pairs={{0,2},{1,3},{2,0},{3,1},{4,6},{5,7},{6,4},{7,5},{8,10},{9,11},{10,... | collective-permute-start | bytes 1572872 | tf_op jit(solution)/shard_map/ppermute | solution.py:416
  12.0 5.8 %collective-permute-start.1 = (f32[256,128]{1,0:T(8,128)S(1)}, f32[256,128]{1,0:T(8,128)S(1)}, u32[]{:S(2)}, u32[]{:S(2)}) collective-permute-start(f32[256,128]{1,0:T(8,128)S(1)} %add.63), channel_id=1, source_target_pairs={{0,8},{4,12},{8,0},{12,4},{16,24},{20,28},{24,16},{28,20},{1,9},{5... | collective-permute-start | bytes 393224 | tf_op jit(solution)/shard_map/ppermute | solution.py:416
  13.9 6.8 %collective-permute-start.4 = (f32[136,128]{1,0:T(8,128)S(1)}, f32[136,128]{1,0:T(8,128)S(1)}, u32[]{:S(2)}, u32[]{:S(2)}) collective-permute-start(f32[136,128]{1,0:T(8,128)S(1)} %get-tuple-element.82), channel_id=1, source_target_pairs={{0,8},{4,12},{8,0},{12,4},{16,24},{20,28},{24,16},{28,20},{1,9},{5... | collective-permute-start | bytes 208904 | tf_op jit(solution)/shard_map/ppermute | solution.py:416
  17.8 7.4 %collective-permute-start.2 = (f32[256,128]{1,0:T(8,128)S(1)}, f32[256,128]{1,0:T(8,128)S(1)}, u32[]{:S(2)}, u32[]{:S(2)}) collective-permute-start(f32[256,128]{1,0:T(8,128)S(1)} %add.65), channel_id=1, source_target_pairs={{0,16},{4,20},{8,24},{12,28},{16,0},{20,4},{24,8},{28,12},{1,17},{... | collective-permute-start | bytes 393224 | tf_op jit(solution)/shard_map/ppermute | solution.py:416
  20.7 1.0 copy-start.2
  21.7 1.2 %copy-start.3 = (bf16[1024,512]{1,0:T(8,128)(2,1)S(1)}, bf16[1024,512]{1,0:T(8,128)(2,1)}, u32[]{:S(2)}) copy-start(bf16[1024,512]{1,0:T(8,128)(2,1)} %copy-done.2) | copy-start | bytes 3145732
  22.9 11.2 %copy-start.6 = (bf16[1024,256]{1,0:T(8,128)(2,1)S(1)}, bf16[1024,256]{1,0:T(8,128)(2,1)}, u32[]{:S(2)}) copy-start(bf16[1024,256]{1,0:T(8,128)(2,1)} %k_ref.9) | copy-start | bytes 1572868
  24.2 9.9 %collective-permute-start.6 = (f32[136,128]{1,0:T(8,128)S(1)}, f32[136,128]{1,0:T(8,128)S(1)}, u32[]{:S(2)}, u32[]{:S(2)}) collective-permute-start(f32[136,128]{1,0:T(8,128)S(1)} %add.69), channel_id=1, source_target_pairs={{0,16},{4,20},{8,24},{12,28},{16,0},{20,4},{24,8},{28,12},{1,17},{... | collective-permute-start | bytes 208904 | tf_op jit(solution)/shard_map/ppermute | solution.py:416
  34.1 15.8 %collective-permute-start.9 = (bf16[512,512]{1,0:T(8,128)(2,1)}, bf16[512,512]{1,0:T(8,128)(2,1)}, u32[]{:S(2)}, u32[]{:S(2)}) collective-permute-start(bf16[512,512]{1,0:T(8,128)(2,1)} %collective-permute-done.7.refs_1_.refs_2_), channel_id=1, source_target_pairs={{0,1},{1,0},{2,3},{3,2},{4,5},{5,4},{6,7},{7,6},{8,9},{9,8},{10,11... | collective-permute-start | bytes 1572872 | tf_op jit(solution)/shard_map/ppermute | solution.py:416
  38.6 1.3 %copy-start.14 = (bf16[8,8,128,128]{3,2,1,0:T(8,128)(2,1)}, bf16[8,8,128,128]{3,2,1,0:T(8,128)(2,1)S(1)}, u32[]{:S(2)}) copy-start(bf16[8,8,128,128]{3,2,1,0:T(8,128)(2,1)S(1)} %get-tuple-element.51.e_ref) | copy-start | bytes 6291460
  39.9 1.4 %copy-start.16 = (bf16[8,8,128,128]{3,2,1,0:T(8,128)(2,1)}, bf16[8,8,128,128]{3,2,1,0:T(8,128)(2,1)S(1)}, u32[]{:S(2)}) copy-start(bf16[8,8,128,128]{3,2,1,0:T(8,128)(2,1)S(1)} %get-tuple-element.52.x_ref) | copy-start | bytes 6291460
  41.3 0.8 copy-start.18
  42.1 0.8 copy-start.21
  42.9 7.1 %collective-permute-start.10 = (bf16[512,512]{1,0:T(8,128)(2,1)}, bf16[512,512]{1,0:T(8,128)(2,1)}, u32[]{:S(2)}, u32[]{:S(2)}) collective-permute-start(bf16[512,512]{1,0:T(8,128)(2,1)} %collective-permute-done.8.refs_2_.refs_3_), channel_id=1, source_target_pairs={{0,1},{1,0},{2,3},{3,2},{4,5},{5,4},{6,7},{7,6},{8,9},{9,8},{10,11... | collective-permute-start | bytes 1572872 | tf_op jit(solution)/shard_map/ppermute | solution.py:416
  43.4 1.0 copy-start.7
  44.4 1.0 copy-start.10
  45.5 1.0 copy-start.12
  46.5 1.0 copy-start.19
  49.9 2.5 %copy-start.4 = (bf16[1024,512]{1,0:T(8,128)(2,1)S(1)}, bf16[1024,512]{1,0:T(8,128)(2,1)}, u32[]{:S(2)}) copy-start(bf16[1024,512]{1,0:T(8,128)(2,1)} %copy-done.2) | copy-start | bytes 3145732
  50.0 7.2 %copy-start.20 = (f32[8,128,128]{2,1,0:T(8,128)S(1)}, f32[8,128,128]{2,1,0:T(8,128)}, u32[]{:S(2)}) copy-start(f32[8,128,128]{2,1,0:T(8,128)} %copy-done.18) | copy-start | bytes 1572868
  50.0 7.2 %copy-start.22 = (f32[8,128,128]{2,1,0:T(8,128)S(1)}, f32[8,128,128]{2,1,0:T(8,128)}, u32[]{:S(2)}) copy-start(f32[8,128,128]{2,1,0:T(8,128)} %copy-done.21) | copy-start | bytes 1572868
  52.4 4.8 %copy-start.8 = (bf16[1024,256]{1,0:T(8,128)(2,1)S(1)}, bf16[1024,256]{1,0:T(8,128)(2,1)}, u32[]{:S(2)}) copy-start(bf16[1024,256]{1,0:T(8,128)(2,1)} %k_ref.9) | copy-start | bytes 1572868
  52.4 4.8 %copy-start.11 = (bf16[1024,256]{1,0:T(8,128)(2,1)S(1)}, bf16[1024,256]{1,0:T(8,128)(2,1)}, u32[]{:S(2)}) copy-start(bf16[1024,256]{1,0:T(8,128)(2,1)} %v_ref.7) | copy-start | bytes 1572868
  52.4 4.8 %copy-start.13 = (bf16[1024,256]{1,0:T(8,128)(2,1)S(1)}, bf16[1024,256]{1,0:T(8,128)(2,1)}, u32[]{:S(2)}) copy-start(bf16[1024,256]{1,0:T(8,128)(2,1)} %q_ref.3) | copy-start | bytes 1572868
  52.4 4.8 %copy-start.15 = (bf16[8,8,128,128]{3,2,1,0:T(8,128)(2,1)S(1)}, bf16[8,8,128,128]{3,2,1,0:T(8,128)(2,1)}, u32[]{:S(2)}) copy-start(bf16[8,8,128,128]{3,2,1,0:T(8,128)(2,1)} %copy-done.14) | copy-start | bytes 6291460
  52.5 4.8 %copy-start.17 = (bf16[8,8,128,128]{3,2,1,0:T(8,128)(2,1)S(1)}, bf16[8,8,128,128]{3,2,1,0:T(8,128)(2,1)}, u32[]{:S(2)}) copy-start(bf16[8,8,128,128]{3,2,1,0:T(8,128)(2,1)} %copy-done.16) | copy-start | bytes 6291460
  55.4 30.6 %collective-permute-start.12 = (bf16[1024,256]{1,0:T(8,128)(2,1)S(1)}, bf16[1024,256]{1,0:T(8,128)(2,1)S(1)}, u32[]{:S(2)}, u32[]{:S(2)}) collective-permute-start(bf16[1024,256]{1,0:T(8,128)(2,1)S(1)} %get-tuple-element.49.h_ref.refs_0_), channel_id=1, source_target_pairs={{0,2},{1,3},{2,0},{3,1},{4,6},{5,7},{6,4},{7,5},{8,10},{9,11},{10,... | collective-permute-start | bytes 1572872 | tf_op jit(solution)/shard_map/ppermute | solution.py:416
  57.2 51.5 %collective-permute-start.11 = (bf16[1024,256]{1,0:T(8,128)(2,1)S(1)}, bf16[1024,256]{1,0:T(8,128)(2,1)S(1)}, u32[]{:S(2)}, u32[]{:S(2)}) collective-permute-start(bf16[1024,256]{1,0:T(8,128)(2,1)S(1)} %get-tuple-element.49.h_ref.refs_0_), channel_id=1, source_target_pairs={{0,1},{1,0},{2,3},{3,2},{4,5},{5,4},{6,7},{7,6},{8,9},{9,8},{10,11... | collective-permute-start | bytes 1572872 | tf_op jit(solution)/shard_map/ppermute | solution.py:416
  65.3 5.8 %collective-permute-start.17 = (bf16[392,128]{1,0:T(8,128)(2,1)S(1)}, bf16[392,128]{1,0:T(8,128)(2,1)S(1)}, u32[]{:S(2)}, u32[]{:S(2)}) collective-permute-start(bf16[392,128]{1,0:T(8,128)(2,1)S(1)} %convert_element_type.57), channel_id=1, source_target_pairs={{0,4},{4,0},{8,12},{12,8},{16,20},{20,16},{24,28},{28,24},{1,5},{5... | collective-permute-start | bytes 301064 | tf_op jit(solution)/shard_map/ppermute | solution.py:416
  66.9 11.6 %collective-permute-start.20 = (bf16[2,256,256]{2,1,0:T(8,128)(2,1)S(1)}, bf16[2,256,256]{2,1,0:T(8,128)(2,1)S(1)}, u32[]{:S(2)}, u32[]{:S(2)}) collective-permute-start(bf16[2,256,256]{2,1,0:T(8,128)(2,1)S(1)} %get-tuple-element.72), channel_id=1, source_target_pairs={{0,4},{4,0},{8,12},{12,8},{16,20},{20,16},{24,28},{28,24},{1,5},{5... | collective-permute-start | bytes 786440 | tf_op jit(solution)/shard_map/ppermute | solution.py:416
  67.5 14.3 %collective-permute-start.21 = (bf16[2,256,256]{2,1,0:T(8,128)(2,1)S(1)}, bf16[2,256,256]{2,1,0:T(8,128)(2,1)S(1)}, u32[]{:S(2)}, u32[]{:S(2)}) collective-permute-start(bf16[2,256,256]{2,1,0:T(8,128)(2,1)S(1)} %get-tuple-element.71), channel_id=1, source_target_pairs={{0,4},{4,0},{8,12},{12,8},{16,20},{20,16},{24,28},{28,24},{1,5},{5... | collective-permute-start | bytes 786440 | tf_op jit(solution)/shard_map/ppermute | solution.py:416
  71.1 4.7 %collective-permute-start.18 = (bf16[392,128]{1,0:T(8,128)(2,1)S(1)}, bf16[392,128]{1,0:T(8,128)(2,1)S(1)}, u32[]{:S(2)}, u32[]{:S(2)}) collective-permute-start(bf16[392,128]{1,0:T(8,128)(2,1)S(1)} %fusion.7), channel_id=1, source_target_pairs={{0,8},{4,12},{8,0},{12,4},{16,24},{20,28},{24,16},{28,20},{1,9},{5... | collective-permute-start | bytes 301064 | tf_op jit(solution)/shard_map/ppermute | solution.py:416
  75.9 10.5 %collective-permute-start.19 = (bf16[392,128]{1,0:T(8,128)(2,1)S(1)}, bf16[392,128]{1,0:T(8,128)(2,1)S(1)}, u32[]{:S(2)}, u32[]{:S(2)}) collective-permute-start(bf16[392,128]{1,0:T(8,128)(2,1)S(1)} %fusion.6), channel_id=1, source_target_pairs={{0,16},{4,20},{8,24},{12,28},{16,0},{20,4},{24,8},{28,12},{1,17},{... | collective-permute-start | bytes 301064 | tf_op jit(solution)/shard_map/ppermute | solution.py:416
  82.0 12.8 %collective-permute-start.22 = (bf16[256,256]{1,0:T(8,128)(2,1)S(1)}, bf16[256,256]{1,0:T(8,128)(2,1)S(1)}, u32[]{:S(2)}, u32[]{:S(2)}) collective-permute-start(bf16[256,256]{1,0:T(8,128)(2,1)S(1)} %get-tuple-element.79), channel_id=1, source_target_pairs={{0,16},{4,20},{8,24},{12,28},{16,0},{20,4},{24,8},{28,12},{1,17},{... | collective-permute-start | bytes 393224 | tf_op jit(solution)/shard_map/ppermute | solution.py:416
  84.7 10.1 %collective-permute-start.23 = (bf16[256,256]{1,0:T(8,128)(2,1)S(1)}, bf16[256,256]{1,0:T(8,128)(2,1)S(1)}, u32[]{:S(2)}, u32[]{:S(2)}) collective-permute-start(bf16[256,256]{1,0:T(8,128)(2,1)S(1)} %get-tuple-element.80), channel_id=1, source_target_pairs={{0,24},{4,28},{8,16},{12,20},{16,8},{20,12},{24,0},{28,4},{1,25},{... | collective-permute-start | bytes 393224 | tf_op jit(solution)/shard_map/ppermute | solution.py:416
  86.0 9.3 %collective-permute-start.24 = (bf16[256,256]{1,0:T(8,128)(2,1)S(1)}, bf16[256,256]{1,0:T(8,128)(2,1)S(1)}, u32[]{:S(2)}, u32[]{:S(2)}) collective-permute-start(bf16[256,256]{1,0:T(8,128)(2,1)S(1)} %fusion.8), channel_id=1, source_target_pairs={{0,8},{4,12},{8,0},{12,4},{16,24},{20,28},{24,16},{28,20},{1,9},{5... | collective-permute-start | bytes 393224 | tf_op jit(solution)/shard_map/ppermute | solution.py:416
  86.3 22.3 %collective-permute-start.13 = (bf16[1024,256]{1,0:T(8,128)(2,1)S(1)}, bf16[1024,256]{1,0:T(8,128)(2,1)S(1)}, u32[]{:S(2)}, u32[]{:S(2)}) collective-permute-start(bf16[1024,256]{1,0:T(8,128)(2,1)S(1)} %collective-permute-done.12.refs_2_), channel_id=1, source_target_pairs={{0,1},{1,0},{2,3},{3,2},{4,5},{5,4},{6,7},{7,6},{8,9},{9,8},{10,11... | collective-permute-start | bytes 1572872 | tf_op jit(solution)/shard_map/ppermute | solution.py:416
  94.8 4.5 %collective-permute-start.14 = (bf16[256,512]{1,0:T(8,128)(2,1)S(1)}, bf16[256,512]{1,0:T(8,128)(2,1)S(1)}, u32[]{:S(2)}, u32[]{:S(2)}) collective-permute-start(bf16[256,512]{1,0:T(8,128)(2,1)S(1)} %get-tuple-element.75), channel_id=1, source_target_pairs={{0,1},{1,0},{2,3},{3,2},{4,5},{5,4},{6,7},{7,6},{8,9},{9,8},{10,11... | collective-permute-start | bytes 786440 | tf_op jit(solution)/shard_map/ppermute | solution.py:416
  94.8 9.2 %collective-permute-start.15 = (bf16[256,512]{1,0:T(8,128)(2,1)S(1)}, bf16[256,512]{1,0:T(8,128)(2,1)S(1)}, u32[]{:S(2)}, u32[]{:S(2)}) collective-permute-start(bf16[256,512]{1,0:T(8,128)(2,1)S(1)} %get-tuple-element.74), channel_id=1, source_target_pairs={{0,2},{1,3},{2,0},{3,1},{4,6},{5,7},{6,4},{7,5},{8,10},{9,11},{10,... | collective-permute-start | bytes 786440 | tf_op jit(solution)/shard_map/ppermute | solution.py:416
  95.3 13.3 %collective-permute-start.16 = (bf16[256,512]{1,0:T(8,128)(2,1)S(1)}, bf16[256,512]{1,0:T(8,128)(2,1)S(1)}, u32[]{:S(2)}, u32[]{:S(2)}) collective-permute-start(bf16[256,512]{1,0:T(8,128)(2,1)S(1)} %get-tuple-element.73), channel_id=1, source_target_pairs={{0,3},{1,2},{2,1},{3,0},{4,7},{5,6},{6,5},{7,4},{8,11},{9,10},{10,... | collective-permute-start | bytes 786440 | tf_op jit(solution)/shard_map/ppermute | solution.py:416

commit v3 on v2

--- a/solution.py
+++ b/solution.py
@@ -15,6 +15,7 @@
 F32 = jnp.float32
 BF16 = jnp.bfloat16
 VMEM_SPEC = pl.BlockSpec(memory_space=pltpu.VMEM)
+HBM_SPEC = pl.BlockSpec(memory_space=pltpu.HBM)
 SMEM_SPEC = pl.BlockSpec(memory_space=pltpu.SMEM)
 
 
@@ -33,7 +34,7 @@
     return jnp.concatenate(parts, axis=axis)
 
 
-def params(limit=16):
+def params(limit=8):
     return pltpu.CompilerParams(vmem_limit_bytes=limit * 1024 * 1024)
 
 
@@ -100,7 +101,15 @@
     return mats[:heads]
 
 
-def totals_kernel(k_ref, v_ref, g_ref, n_ref):
+def totals_kernel(me_ref, k_hbm, v_hbm, g_ref, n_ref, k_ref, v_ref, sem):
+    copies = [
+        pltpu.make_async_copy(k_hbm, k_ref, sem.at[0]),
+        pltpu.make_async_copy(v_hbm, v_ref, sem.at[1]),
+    ]
+    for copy in copies:
+        copy.start()
+    for copy in copies:
+        copy.wait()
     grams = []
     for h in range(k_ref.shape[1] // HDIM):
         cols = slice(h * HDIM, (h + 1) * HDIM)
@@ -111,15 +120,26 @@
     fold_into(g_ref, grams)
 
 
-def totals(keys, values, heads):
+def totals(me, keys, values, heads):
     return pl.pallas_call(
         totals_kernel,
         out_shape=(shape((folded(heads) * (HDIM + 8), HDIM)), shape((heads * HDIM, HDIM))),
-        in_specs=[VMEM_SPEC] * 2,
+        in_specs=[SMEM_SPEC, HBM_SPEC, HBM_SPEC],
         out_specs=(VMEM_SPEC, VMEM_SPEC),
-        compiler_params=params(),
+        scratch_shapes=[pltpu.VMEM(keys.shape, BF16)] * 2 + [pltpu.SemaphoreType.DMA((2,))],
+        compiler_params=params(60),
         cost_estimate=cost(2 * 2 * keys.size * HDIM, 4 * keys.size),
-    )(keys, values)
+    )(me, keys, values)
+
+
+def taken(me_ref, refs, backward):
+    total = None
+    for r, ref in enumerate(refs):
+        bit = (me_ref[1] >> r) & 1
+        wanted = jnp.where(bit == (0 if backward else 1), 1.0, 0.0)
+        part = ref[...].astype(F32) * wanted
+        total = part if total is None else total + part
+    return total
 
 
 def places(q_ref, heads):
@@ -129,10 +149,11 @@
             yield h, b, h * blocks + b, slice(b * SPAN, (b + 1) * SPAN), slice(h * HDIM, (h + 1) * HDIM)
 
 
-def inverse_kernel(k_ref, g_ref, e_ref, x_ref, last_ref, a_ref, es, xs):
+def inverse_kernel(rounds, me_ref, k_ref, *refs):
+    e_ref, x_ref, last_ref, a_ref, es, xs = refs[rounds:]
     heads = k_ref.shape[1] // HDIM
     eye = unit()
-    grams = unfold_from(g_ref, heads)
+    grams = unfold_from(taken(me_ref, refs[:rounds], False), heads)
     for h, b, i, rows, cols in places(k_ref, heads):
         ridged = grams[h] + jnp.where(eye, RIDGE, 0.0)
         scale = 1.0 / jnp.sqrt(jnp.sum(ridged * ridged, keepdims=True))
@@ -163,25 +184,27 @@
         last_ref[i] = xs[i]
 
 
-def inverses(keys, gram, count):
+def inverses(me, keys, grams, count):
     stash = shape((NEWTON, count, HDIM, HDIM), BF16)
     state = shape((count, HDIM, HDIM))
     return pl.pallas_call(
-        inverse_kernel,
+        functools.partial(inverse_kernel, len(grams)),
         out_shape=(stash, stash, state, state),
-        in_specs=[VMEM_SPEC] * 2,
+        in_specs=[SMEM_SPEC] + [VMEM_SPEC] * (1 + len(grams)),
         out_specs=(VMEM_SPEC,) * 4,
         scratch_shapes=[pltpu.VMEM((count, HDIM, HDIM), F32)] * 2,
         compiler_params=params(),
         cost_estimate=cost(2_000_000_000, 8_000_000),
-    )(keys, gram)
-
-
-def outputs_kernel(q_ref, k_ref, v_ref, n_ref, last_ref, out_ref, pre_ref, s_ref, w_ref):
+    )(me, keys, *grams)
+
+
+def outputs_kernel(rounds, me_ref, q_ref, k_ref, v_ref, last_ref, *refs):
+    out_ref, pre_ref, s_ref, w_ref = refs[rounds:]
+    prefix = taken(me_ref, refs[:rounds], False)
     heads = q_ref.shape[1] // HDIM
     keep = causal()
     nil = jnp.zeros((HDIM, HDIM), BF16)
-    pairs = [n_ref[h * HDIM : (h + 1) * HDIM, :] for h in range(heads)]
+    pairs = [prefix[h * HDIM : (h + 1) * HDIM, :] for h in range(heads)]
     for h, b, i, rows, cols in places(q_ref, heads):
         q, k, v = q_ref[rows, cols], k_ref[rows, cols], v_ref[rows, cols]
         xh, xl = split(last_ref[i])
@@ -199,26 +222,26 @@
         pairs[h] = pairs[h] + dot(k, v, (0, 0))
 
 
-def outputs(queries, keys, values, pair, last):
+def outputs(me, queries, keys, values, last, pairs):
     count = last.shape[0]
     return pl.pallas_call(
-        outputs_kernel,
+        functools.partial(outputs_kernel, len(pairs)),
         out_shape=(
             shape(queries.shape, BF16),
             shape((count, HDIM, 2 * HDIM), BF16),
             shape((count, SPAN, 2 * HDIM), BF16),
             shape((count, SPAN, SPAN), BF16),
         ),
-        in_specs=[VMEM_SPEC] * 5,
+        in_specs=[SMEM_SPEC] + [VMEM_SPEC] * (4 + len(pairs)),
         out_specs=(VMEM_SPEC,) * 4,
         compiler_params=params(),
         cost_estimate=cost(2_000_000_000, 8_000_000),
-    )(queries, keys, values, pair, last)
+    )(me, queries, keys, values, last, *pairs)
 
 
 def tangent_kernel(
     q_ref, k_ref, v_ref, do_ref, e_ref, x_ref, last_ref, a_ref, pre_ref, s_ref, w_ref,
-    dq_ref, dk_ref, dv_ref, da_ref, dn_ref, sum_ref, des, dxs, first,
+    dq_ref, dk_ref, dv_ref, da_ref, dn_ref, sum_ref, send_ref, des, dxs, first,
 ):
     heads = q_ref.shape[1] // HDIM
     keep = causal()
@@ -271,6 +294,7 @@
     for h in range(heads):
         sum_ref[h * HDIM : (h + 1) * HDIM, :] = sum_n[h]
     fold_into(sum_ref, sum_a, heads * HDIM)
+    send_ref[...] = sum_ref[...].astype(BF16)
 
 
 def tangent(queries, keys, values, grads, stash):
@@ -281,16 +305,21 @@
     rows = heads * HDIM + folded(heads) * (HDIM + 8)
     return pl.pallas_call(
         tangent_kernel,
-        out_shape=(shape(queries.shape, BF16), wide, wide, state, state, shape((rows, HDIM))),
+        out_shape=(
+            shape(queries.shape, BF16), wide, wide, state, state,
+            shape((rows, HDIM)), shape((rows, HDIM), BF16),
+        ),
         in_specs=[VMEM_SPEC] * 11,
-        out_specs=(VMEM_SPEC,) * 6,
+        out_specs=(VMEM_SPEC,) * 7,
         scratch_shapes=[pltpu.VMEM((count, HDIM, HDIM), F32)] * 3,
-        compiler_params=params(24),
+        compiler_params=params(),
         cost_estimate=cost(4_000_000_000, 8_000_000),
     )(queries, keys, values, grads, *stash)
 
 
-def finish_kernel(k_ref, v_ref, dk_ref, dv_ref, da_ref, dn_ref, sum_ref, gk_ref, gv_ref):
+def finish_kernel(rounds, me_ref, k_ref, v_ref, dk_ref, dv_ref, da_ref, dn_ref, *refs):
+    gk_ref, gv_ref = refs[rounds:]
+    sum_ref = taken(me_ref, refs[:rounds], True)
     heads = k_ref.shape[1] // HDIM
     sa = unfold_from(sum_ref, heads, heads * HDIM)
     sn = [sum_ref[h * HDIM : (h + 1) * HDIM, :] for h in range(heads)]
@@ -306,88 +335,88 @@
         sn[h] = sn[h] + dn_ref[i]
 
 
-def finish(keys, values, dk, dv, da, dn, sums):
-    return pl.pallas_call(
-        finish_kernel,
+def finish(me, keys, values, dk, dv, da, dn, sums):
+    return pl.pallas_call(
+        functools.partial(finish_kernel, len(sums)),
         out_shape=(shape(keys.shape, BF16),) * 2,
-        in_specs=[VMEM_SPEC] * 7,
+        in_specs=[SMEM_SPEC] + [VMEM_SPEC] * (6 + len(sums)),
         out_specs=(VMEM_SPEC,) * 2,
         compiler_params=params(),
         cost_estimate=cost(1_000_000_000, 6_000_000),
-    )(keys, values, dk, dv, da, dn, sums)
-
-
-def spans(pieces):
-    out, top = [], 0
-    for piece in pieces:
-        out.append(slice(top, top + piece.shape[0]))
-        top += piece.shape[0]
-    return out
-
-
-def groups(refs, cuts):
-    out, at = [], 0
-    for cut in cuts:
-        out.append(refs[at : at + cut])
-        at += cut
-    return out
-
-
-def grads_kernel(first, cuts, me_ref, w_ref, *refs):
+    )(me, keys, values, dk, dv, da, dn, *sums)
+
+
+def grads_kernel(first, me_ref, w_ref, *refs):
     out_ref = refs[-1]
     me = me_ref[0]
-    parts = groups(refs[1:-1] if first else refs[:-1], cuts)
-    for c, rows in enumerate(spans(parts[0])):
-        total = refs[0][rows, :] if first else None
-        for s, part in enumerate(parts):
-            width = part[c].shape[1]
-            cols = pl.ds(pl.multiple_of((me ^ (first + s)) * width, width), width)
-            term = dot(part[c][...], w_ref[:, cols], (1, 1))
-            total = term if total is None else total + term
-        out_ref[rows, :] = total.astype(out_ref.dtype)
+    total = refs[0][...] if first else None
+    for s, part in enumerate(refs[1:-1] if first else refs[:-1]):
+        width = part.shape[1]
+        cols = pl.ds(pl.multiple_of((me ^ (first + s)) * width, width), width)
+        term = dot(part[...], w_ref[:, cols], (1, 1))
+        total = term if total is None else total + term
+    out_ref[...] = total.astype(out_ref.dtype)
 
 
 def head_grads(me, w_out, parts, first, begun=None):
-    flat = [piece for part in parts for piece in part]
-    rows = sum(piece.shape[0] for piece in parts[0])
+    rows = parts[0].shape[0]
     begun = [] if begun is None else [begun]
     return pl.pallas_call(
-        functools.partial(grads_kernel, first, [len(part) for part in parts]),
+        functools.partial(grads_kernel, first),
         out_shape=shape((rows, w_out.shape[0]), BF16 if begun else F32),
-        in_specs=[SMEM_SPEC] + [VMEM_SPEC] * (1 + len(flat) + len(begun)),
+        in_specs=[SMEM_SPEC] + [VMEM_SPEC] * (1 + len(parts) + len(begun)),
         out_specs=VMEM_SPEC,
         compiler_params=params(),
         cost_estimate=cost(rows * w_out.size, 4_000_000),
-    )(me, w_out, *begun, *flat)
-
-
-def weights_kernel(cuts, me_ref, h_ref, *refs):
-    parts, out_ref = groups(refs[:-1], cuts), refs[-1]
+    )(me, w_out, *begun, *parts)
+
+
+def columns_kernel(me_ref, w_ref, *refs):
+    for s, out_ref in enumerate(refs):
+        width = out_ref.shape[1]
+        cols = pl.ds(pl.multiple_of((me_ref[0] ^ s) * width, width), width)
+        out_ref[...] = w_ref[:, cols]
+
+
+def column_pieces(me, w_out, count):
+    piece = shape((w_out.shape[0], w_out.shape[1] // count), BF16)
+    return pl.pallas_call(
+        columns_kernel,
+        out_shape=(piece,) * count,
+        in_specs=[SMEM_SPEC, VMEM_SPEC],
+        out_specs=(VMEM_SPEC,) * count,
+        compiler_params=params(),
+        cost_estimate=cost(0, 4 * w_out.size),
+    )(me, w_out)
+
+
+def weights_kernel(me_ref, h_ref, *refs):
+    parts, outs, all_ref = refs[:-5], refs[-5:-1], refs[-1]
     me, mine = me_ref[0], me_ref[1]
-    width = out_ref.shape[2]
-    fold = parts[0][0].shape[1] // width
+    count, _, width = all_ref.shape
+    fold = parts[0].shape[1] // width
     for s, part in enumerate(parts):
+        term = dot(h_ref[...], part[...], (0, 0)).astype(BF16)
         for f in range(fold):
             target = (me ^ s) * fold + f
-            cols = slice(f * width, (f + 1) * width)
-            total = None
-            for piece, rows in zip(part, spans(part)):
-                term = dot(h_ref[rows, :], piece[:, cols], (0, 0))
-                total = term if total is None else total + term
-            out_ref[target ^ mine] = total.astype(BF16)
+            all_ref[target ^ mine] = term[:, f * width : (f + 1) * width]
+    for t in range(count):
+        ref = outs[2 * (t % 2) + (t >= count // 2)]
+        ref[t % (count // 2) // 2] = all_ref[t]
 
 
 def weight_terms(me, heads_out, parts, count):
-    flat = [piece for part in parts for piece in part]
-    feats = sum(part[0].shape[1] for part in parts)
-    return pl.pallas_call(
-        functools.partial(weights_kernel, [len(part) for part in parts]),
-        out_shape=shape((count, heads_out.shape[1], feats // count), BF16),
-        in_specs=[SMEM_SPEC] + [VMEM_SPEC] * (1 + len(flat)),
-        out_specs=VMEM_SPEC,
+    feats = sum(part.shape[1] for part in parts)
+    piece = (heads_out.shape[1], feats // count)
+    return pl.pallas_call(
+        weights_kernel,
+        out_shape=(shape((count // 4,) + piece, BF16),) * 4,
+        in_specs=[SMEM_SPEC] + [VMEM_SPEC] * (1 + len(parts)),
+        out_specs=(VMEM_SPEC,) * 4,
+        scratch_shapes=[pltpu.VMEM((count,) + piece, BF16)],
         compiler_params=params(),
         cost_estimate=cost(2 * heads_out.size * feats, 6_000_000),
-    )(me, heads_out, *flat)
+    )(me, heads_out, *parts)
 
 
 def layer_kernel(*refs):
@@ -420,12 +449,6 @@
     return lax.optimization_barrier((value,) + others)[0]
 
 
-def take(prefix, other, axis, distance, backward):
-    upper = (lax.axis_index(axis) & distance) != 0
-    wanted = jnp.logical_not(upper) if backward else upper
-    return prefix + jnp.where(wanted, other, 0.0)
-
-
 def doublings(axis):
     return [1 << i for i in range((lax.axis_size(axis) - 1).bit_length())]
 
@@ -434,75 +457,63 @@
     heads = queries.shape[1] // HDIM
     count = heads * (queries.shape[0] // SPAN)
     head_count, ctx_count = lax.axis_size("head"), lax.axis_size("ctx")
-    me_head, me_ctx = lax.axis_index("head"), lax.axis_index("ctx")
-    me = jnp.stack([me_head, me_ctx]).astype(jnp.int32)
+    me = jnp.stack([lax.axis_index("head"), lax.axis_index("ctx")]).astype(jnp.int32)
     evens = range(2, head_count, 2)
-    middle = cotangent.shape[0] // 2
-
-    gram, pair = totals(keys, values, heads)
+
+    gram, pair = totals(me, keys, values, heads)
     cot = after(cotangent, gram, pair)
-    pieces = (cot[:middle], cot[middle:])
-    far = {s: [swap(p, "head", s) for p in pieces] for s in evens}
+    far = {s: swap(cot, "head", s) for s in evens}
     near = swap(cot, "head", 1)
 
-    grams, pairs = jnp.zeros_like(gram), jnp.zeros_like(pair)
+    grams, pairs = [], []
     begun = None
-    crossed = {s: [] for s in evens}
     for distance in doublings("ctx"):
         if distance == ctx_count // 2:
             gram = after(gram, begun)
-            for s in evens:
-                crossed[s].append(swap(after(far[s][0], gram), "head", 1))
-        other_gram = swap(gram, "ctx", distance)
-        other_pair = swap(pair, "ctx", distance)
-        grams = take(grams, other_gram, "ctx", distance, False)
-        pairs = take(pairs, other_pair, "ctx", distance, False)
+        grams.append(swap(gram, "ctx", distance))
+        pairs.append(swap(pair, "ctx", distance))
         if begun is None:
-            begun = head_grads(me, w_out, [[cotangent], [after(near, grams)]], 0)
-        gram, pair = gram + other_gram, pair + other_pair
-    *stash, last, ridged = inverses(keys, grams, count)
-    pairs = after(pairs, last)
-    for s in evens:
-        crossed[s].append(swap(after(far[s][1], pairs), "head", 1))
-    heads_out, states, solved, scores = outputs(queries, keys, values, pairs, last)
-
+            begun = head_grads(me, w_out, [cotangent, after(near, grams[0])], 0)
+        gram, pair = gram + grams[-1], pair + pairs[-1]
+    *stash, last, ridged = inverses(me, keys, grams, count)
+    pairs[-1] = after(pairs[-1], last)
     parts = []
     for s in evens:
-        parts += [far[s], crossed[s]]
+        parts += [far[s], swap(after(far[s], pairs[-1]), "head", 1)]
+    columns = column_pieces(me, after(w_out, begun), head_count)
+    columns = [after(c, pairs[-1], *far.values()) for c in columns]
+    columns = [swap(c, "head", s) if s else c for s, c in enumerate(columns)]
+    heads_out, states, solved, scores = outputs(me, queries, keys, values, last, pairs)
+
     grads = head_grads(me, w_out, parts, 2, after(begun, heads_out))
-    parts = [[cotangent], [near]] + parts
-
-    terms = weight_terms(me, after(heads_out, grads), parts, ctx_count)
-    halves = terms.reshape((ctx_count // 2, 2) + terms.shape[1:])
-    cut = ctx_count // 4
-    sent = [swap(halves[cut:, 1], "ctx", 1), swap(halves[:cut, 1], "ctx", 1)]
-
-    width = w_out.shape[1] // head_count
-    late = after(w_out, terms)
-    columns = []
-    for s in range(head_count):
-        mine = lax.dynamic_slice_in_dim(late, (me_head ^ s) * width, width, axis=1)
-        columns.append(swap(mine, "head", s) if s else mine)
-    outs_out = after(heads_out, terms)
+    parts = [cotangent, near] + parts
+    even_low, even_high, odd_low, odd_high = weight_terms(
+        me, after(heads_out, grads), parts, ctx_count
+    )
+    high = swap(odd_high, "ctx", 1)
+    low = swap(odd_low, "ctx", 1)
+
+    outs_out = after(heads_out, odd_low)
     outs_far = [swap(outs_out, "head", s) for s in evens]
     outs_near = swap(outs_out, "head", 1)
 
-    grad_queries, dk, dv, da, dn, sums = tangent(
-        queries, keys, values, after(grads, terms), [*stash, last, ridged, states, solved, scores]
+    grad_queries, dk, dv, da, dn, sums, send = tangent(
+        queries, keys, values, after(grads, odd_low), [*stash, last, ridged, states, solved, scores]
     )
 
-    sent = after(sent[0], grad_queries), sent[1]
-    high = halves[cut:, 0].astype(F32) + sent[0].astype(F32)
-    moved = [swap(high[u].astype(BF16), "ctx", 2 * (cut + u)) for u in range(high.shape[0])]
-
-    later = jnp.zeros_like(sums)
+    high, low = after(high, grad_queries), after(low, grad_queries)
+    high = even_high.astype(F32) + high.astype(F32)
+    half = ctx_count // 4
+    moved = [swap(high[u].astype(BF16), "ctx", 2 * (half + u)) for u in range(half)]
+
+    later = []
     for distance in doublings("ctx"):
-        other = swap(sums.astype(BF16), "ctx", distance).astype(F32)
-        later = take(later, other, "ctx", distance, True)
-        sums = sums + other
-
-    low = halves[:cut, 0].astype(F32) + after(sent[1], grad_queries).astype(F32)
-    moved += [swap(low[u].astype(BF16), "ctx", 2 * u) for u in range(1, cut)]
+        later.append(swap(send, "ctx", distance))
+        sums = sums + later[-1].astype(F32)
+        send = sums.astype(BF16)
+
+    low = even_low.astype(F32) + low.astype(F32)
+    moved += [swap(low[u].astype(BF16), "ctx", 2 * u) for u in range(1, half)]
     grad_weight = low[0]
     for part in moved:
         grad_weight = grad_weight + part.astype(F32)
@@ -511,7 +522,7 @@
     for part in outs_far:
         outs += [part, swap(after(part, grad_queries), "head", 1)]
     layer_out = layer(outs, columns)
-    grad_keys, grad_values = finish(keys, values, dk, dv, da, dn, later)
+    grad_keys, grad_values = finish(me, keys, values, dk, dv, da, dn, later)
     return (layer_out, grad_queries, grad_keys, grad_values, grad_weight)
 
 

time: 111 us -> 93.9 us (0.85)
  local copies, waits for them, and re-layouts: 15.3 us -> 1.94 us
  waiting for transfers between devices: 40.1 us -> 32.5 us
  Pallas kernels: 25.9 us -> 28.6 us
  other arithmetic: 1.21 us -> 3.39 us
    unnamed x46 -> x16, local copies, waits for them, and re-layouts: 12.9 us -> 1.91 us
    ppermute x25 -> x23, waiting for transfers between devices: 40.1 us -> 32.5 us  [swap(): return lax.ppermute(value, axis, [(i, i ^ distance) for i in range(count)])]
    pallas_call x1, Pallas kernels: 0.33 us -> 2.89 us  [totals(): pl.pallas_call(totals_kernel, out_shape=(shape((folded(heads) * (HDIM + 8...]
    slice x1 -> x0, local copies, waits for them, and re-layouts: 2.23 us -> none  [shards(): pieces = (cot[:middle], cot[middle:])]
    add x6 -> x5, other arithmetic: 0.15 us -> 1.9 us  [the longest x4 1.84 us: shards(): gram, pair = (gram + grams[-1], pair + pairs[-1])]
    ppermute x25 -> x23, starting transfers between devices: 27.4 us -> 26.4 us  [swap(): return lax.ppermute(value, axis, [(i, i ^ distance) for i in range(count)])]
    pallas_call x6 -> x7, Pallas kernels: 15.3 us -> 15.3 us  [the longest x1 4.75 us: inverses(): pl.pallas_call(functools.partial(inverse_kernel, len(grams)), out_shape=(...]
  transfers between devices with their start and end apart: 25 -> 23, of which waited for: 10 -> 11; matrix products, arithmetic and copies ran while one was open for 3% -> 3% of each run, Pallas kernels for 16% -> 13%
where the time goes in v3:
time: 93.9 us; the launch traced here: 93.7 us
  waiting for transfers between devices  32.5 us (35%)
  Pallas kernels  28.6 us (30%)
  starting transfers between devices  26.4 us (28%)
  other arithmetic  3.39 us (4%)
  local copies, waits for them, and re-layouts  1.94 us (2%)
    ppermute x23, waiting for transfers between devices, swap(): return lax.ppermute(value, axis, [(i, i ^ distance) for i in range(count)])  32.5 us
    ppermute x23, starting transfers between devices, swap(): return lax.ppermute(value, axis, [(i, i ^ distance) for i in range(count)])  26.4 us
    pallas_call x1, Pallas kernels, tangent(): pl.pallas_call(tangent_kernel, out_shape=(shape(queries.shape, BF16), wid...  8.18 us
    pallas_call x1, Pallas kernels, inverses(): pl.pallas_call(functools.partial(inverse_kernel, len(grams)), out_shape=(...  4.75 us
    pallas_call x1, Pallas kernels, outputs(): pl.pallas_call(functools.partial(outputs_kernel, len(pairs)), out_shape=(...  2.94 us
    pallas_call x1, Pallas kernels, totals(): pl.pallas_call(totals_kernel, out_shape=(shape((folded(heads) * (HDIM + 8...  2.89 us
    pallas_call x2, Pallas kernels, head_grads(): pl.pallas_call(functools.partial(grads_kernel, first), out_shape=shape((r...  2.58 us
    pallas_call x1, Pallas kernels, finish(): pl.pallas_call(functools.partial(finish_kernel, len(sums)), out_shape=(sh...  2.48 us
  transfers between devices with their start and end apart: 23, of which 11 were waited for; matrix products, arithmetic and copies ran while one was open for 3% of the time, Pallas kernels for 13%

profile of v3, /device:TPU:0, one launch (start us, length us, event | category | flops | bytes accessed | tf_op | source)
XLA Modules:
  0.0 93.7 jit_solution(13477171940176404640)
XLA Ops:
  0.6 0.6 pad_add_fusion.me_ref
  1.2 2.9 %shard_map.92 = (f32[136,128]{1,0:T(8,128)}, f32[256,128]{1,0:T(8,128)}) custom-call(s32[2]{0:T(128)} %pad_add_fusion.me_ref, bf16[1024,256]{1,0:T(8,128)(2,1)} %k_ref.7, bf16[1024,256]{1,0:T(8,128)(2,1)} %v_ref.5), custom_call_target="tpu_custom_call" | custom-call | flops 134217728 | bytes 1048576 | tf_op jit(solution)/shard_map/pallas_call | solution.py:124
  4.1 0.6 collective-permute-start.2
  4.7 2.6 %collective-permute-start.7 = (bf16[1024,512]{1,0:T(8,128)(2,1)}, bf16[1024,512]{1,0:T(8,128)(2,1)S(1)}, u32[]{:S(2)}, u32[]{:S(2)}) collective-permute-start(bf16[1024,512]{1,0:T(8,128)(2,1)} %refs_0_.3), channel_id=1, source_target_pairs={{0,2},{1,3},{2,0},{3,1},{4,6},{5,7},{6,4},{7,5},{8,10},{9,11},{10,... | collective-permute-start | bytes 3145736 | tf_op jit(solution)/shard_map/ppermute | solution.py:445
  7.2 1.5 %collective-permute-start.4 = (f32[256,128]{1,0:T(8,128)}, f32[256,128]{1,0:T(8,128)S(1)}, u32[]{:S(2)}, u32[]{:S(2)}) collective-permute-start(f32[256,128]{1,0:T(8,128)} %get-tuple-element.50), channel_id=1, source_target_pairs={{0,4},{4,0},{8,12},{12,8},{16,20},{20,16},{24,28},{28,24},{1,5},{5... | collective-permute-start | bytes 393224 | tf_op jit(solution)/shard_map/ppermute | solution.py:445
  8.8 0.5 collective-permute-start
  9.3 5.2 %collective-permute-done.refs_0_ = f32[136,128]{1,0:T(8,128)S(1)} collective-permute-done((f32[136,128]{1,0:T(8,128)}, f32[136,128]{1,0:T(8,128)S(1)}, u32[]{:S(2)}, u32[]{:S(2)}) %collective-permute-start) | collective-permute-done | bytes 69664 | tf_op jit(solution)/shard_map/ppermute | solution.py:445
  14.5 0.9 add.33
  15.4 1.6 %collective-permute-start.1 = (f32[136,128]{1,0:T(8,128)S(1)}, f32[136,128]{1,0:T(8,128)S(1)}, u32[]{:S(2)}, u32[]{:S(2)}) collective-permute-start(f32[136,128]{1,0:T(8,128)S(1)} %add.33), channel_id=1, source_target_pairs={{0,8},{4,12},{8,0},{12,4},{16,24},{20,28},{24,16},{28,20},{1,9},{5... | collective-permute-start | bytes 208904 | tf_op jit(solution)/shard_map/ppermute | solution.py:445
  17.0 0.9 add.35
  18.0 0.5 collective-permute-start.5
  18.5 1.4 %collective-permute-done.1.refs_1_ = f32[136,128]{1,0:T(8,128)S(1)} collective-permute-done((f32[136,128]{1,0:T(8,128)S(1)}, f32[136,128]{1,0:T(8,128)S(1)}, u32[]{:S(2)}, u32[]{:S(2)}) %collective-permute-start.1) | collective-permute-done | bytes 69664 | tf_op jit(solution)/shard_map/ppermute | solution.py:445
  19.9 1.2 %copy-done.1 = bf16[1024,512]{1,0:T(8,128)(2,1)S(1)} copy-done((bf16[1024,512]{1,0:T(8,128)(2,1)S(1)}, bf16[1024,512]{1,0:T(8,128)(2,1)}, u32[]{:S(2)}) %copy-start.1) | copy-done | bytes 1048600
  21.2 0.7 copy-done.5
  21.8 1.3 %shard_map.93.refs_0_ = f32[1024,256]{1,0:T(8,128)S(1)} custom-call(s32[2]{0:T(128)S(1)} %copy-done.5, bf16[256,2048]{1,0:T(8,128)(2,1)S(1)} %copy-done, bf16[1024,512]{1,0:T(8,128)(2,1)S(1)} %copy-done.1, bf16[1024,512]{1,0:T(8,128)(2,1)S(1)} %collective-permute-done.2.refs_1_), custom_call_target="tpu_custom_call" | custom-call | flops 536870912 | bytes 4000000 | tf_op jit(solution)/shard_map/pallas_call | solution.py:364
  23.1 2.6 %collective-permute-start.3 = (f32[136,128]{1,0:T(8,128)S(1)}, f32[136,128]{1,0:T(8,128)S(1)}, u32[]{:S(2)}, u32[]{:S(2)}) collective-permute-start(f32[136,128]{1,0:T(8,128)S(1)} %add.34), channel_id=1, source_target_pairs={{0,16},{4,20},{8,24},{12,28},{16,0},{20,4},{24,8},{28,12},{1,17},{... | collective-permute-start | bytes 208904 | tf_op jit(solution)/shard_map/ppermute | solution.py:445
  25.8 0.4 collective-permute-start.6
  26.2 5.1 %collective-permute-done.3.refs_2_ = f32[136,128]{1,0:T(8,128)S(1)} collective-permute-done((f32[136,128]{1,0:T(8,128)S(1)}, f32[136,128]{1,0:T(8,128)S(1)}, u32[]{:S(2)}, u32[]{:S(2)}) %collective-permute-start.3) | collective-permute-done | bytes 69664 | tf_op jit(solution)/shard_map/ppermute | solution.py:445
  31.3 4.7 %shard_map.94 = (bf16[8,8,128,128]{3,2,1,0:T(8,128)(2,1)S(1)}, bf16[8,8,128,128]{3,2,1,0:T(8,128)(2,1)S(1)}, f32[8,128,128]{2,1,0:T(8,128)S(1)}, f32[8,128,128]{2,1,0:T(8,128)S(1)}) custom-call(s32[2]{0:T(128)S(1)} %copy-done.6, bf16[1024,256]{1,0:T(8,128)(2,1)S(1)} %copy-done.3, f32[136,128]{1,0:T(8,128)S(1)} %collective-permute-done.refs_0_, ...), custom_call_target="tpu_custom_call" | custom-call | flops 2000000000 | bytes 8000000 | tf_op jit(solution)/shard_map/pallas_call | solution.py:190
  36.1 0.1 collective-permute-start.8
  36.2 2.9 %shard_map.95 = (bf16[1024,256]{1,0:T(8,128)(2,1)S(1)}, bf16[8,128,256]{2,1,0:T(8,128)(2,1)S(1)}, bf16[8,256,256]{2,1,0:T(8,128)(2,1)S(1)}, bf16[8,256,256]{2,1,0:T(8,128)(2,1)S(1)}) custom-call(s32[2]{0:T(128)S(1)} %copy-done.6, bf16[1024,256]{1,0:T(8,128)(2,1)S(1)} %copy-done.7, bf16[1024,256]{1,0:T(8,128)(2,1)S(1)} %copy-done.3, ...), custom_call_target="tpu_custom_call" | custom-call | flops 2000000000 | bytes 8000000 | tf_op jit(solution)/shard_map/pallas_call | solution.py:227
  39.1 1.3 %shard_map.96.do_ref = bf16[1024,256]{1,0:T(8,128)(2,1)S(1)} custom-call(s32[2]{0:T(128)S(1)} %copy-done.6, bf16[256,2048]{1,0:T(8,128)(2,1)S(1)} %copy-done, f32[1024,256]{1,0:T(8,128)S(1)} %shard_map.93.refs_0_, bf16[1024,512]{1,0:T(8,128)(2,1)S(1)} %collective-permute-done.7.refs_1_.refs_2_, bf16[1024,512]{1,0:T(8,128)(2,1)S(1)} %collective-permute-done.8.refs_2_.refs_3_), custom_call_target="tpu_custom_call" | custom-call | flops 536870912 | bytes 4000000 | tf_op jit(solution)/shard_map/pallas_call | solution.py:364
  40.4 1.9 %shard_map.97 = (bf16[2,256,256]{2,1,0:T(8,128)(2,1)S(1)}, bf16[2,256,256]{2,1,0:T(8,128)(2,1)S(1)}, bf16[2,256,256]{2,1,0:T(8,128)(2,1)S(1)}, bf16[2,256,256]{2,1,0:T(8,128)(2,1)S(1)}) custom-call(s32[2]{0:T(128)S(1)} %copy-done.6, bf16[1024,256]{1,0:T(8,128)(2,1)S(1)} %get-tuple-element.61.h_ref.refs_0_, bf16[1024,512]{1,0:T(8,128)(2,1)S(1)} %copy-done.2, ...), custom_call_target="tpu_custom_call" | custom-call | flops 1073741824 | bytes 6000000 | tf_op jit(solution)/shard_map/pallas_call | solution.py:411
  42.4 8.2 %shard_map.98 = (bf16[1024,256]{1,0:T(8,128)(2,1)}, f32[1024,256]{1,0:T(8,128)S(1)}, f32[1024,256]{1,0:T(8,128)S(1)}, f32[8,128,128]{2,1,0:T(8,128)S(1)}, f32[8,...) custom-call(bf16[1024,256]{1,0:T(8,128)(2,1)S(1)} %copy-done.7, ...), custom_call_target="tpu_custom_call" | custom-call | flops 4000000000 | bytes 8000000 | tf_op jit(solution)/shard_map/pallas_call | solution.py:306
  50.5 1.5 %collective-permute-start.15 = (bf16[392,128]{1,0:T(8,128)(2,1)S(1)}, bf16[392,128]{1,0:T(8,128)(2,1)S(1)}, u32[]{:S(2)}, u32[]{:S(2)}) collective-permute-start(bf16[392,128]{1,0:T(8,128)(2,1)S(1)} %get-tuple-element.84), channel_id=1, source_target_pairs={{0,4},{4,0},{8,12},{12,8},{16,20},{20,16},{24,28},{28,24},{1,5},{5... | collective-permute-start | bytes 301064 | tf_op jit(solution)/shard_map/ppermute | solution.py:445
  52.1 3.7 %collective-permute-done.15.refs_0_ = bf16[392,128]{1,0:T(8,128)(2,1)S(1)} collective-permute-done((bf16[392,128]{1,0:T(8,128)(2,1)S(1)}, bf16[392,128]{1,0:T(8,128)(2,1)S(1)}, u32[]{:S(2)}, u32[]{:S(2)}) %collective-permute-start.15) | collective-permute-done | bytes 100384 | tf_op jit(solution)/shard_map/ppermute | solution.py:445
  55.8 0.7 collective-permute-start.16
  56.5 1.5 %collective-permute-start.19 = (bf16[2,256,256]{2,1,0:T(8,128)(2,1)S(1)}, bf16[2,256,256]{2,1,0:T(8,128)(2,1)S(1)}, u32[]{:S(2)}, u32[]{:S(2)}) collective-permute-start(bf16[2,256,256]{2,1,0:T(8,128)(2,1)S(1)} %get-tuple-element.91), channel_id=1, source_target_pairs={{0,4},{4,0},{8,12},{12,8},{16,20},{20,16},{24,28},{28,24},{1,5},{5... | collective-permute-start | bytes 786440 | tf_op jit(solution)/shard_map/ppermute | solution.py:445
  58.0 0.5 collective-permute-start.18
  58.5 0.5 collective-permute-start.10
  59.1 1.4 %collective-permute-done.16.refs_1_ = bf16[392,128]{1,0:T(8,128)(2,1)S(1)} collective-permute-done((bf16[392,128]{1,0:T(8,128)(2,1)S(1)}, bf16[392,128]{1,0:T(8,128)(2,1)S(1)}, u32[]{:S(2)}, u32[]{:S(2)}) %collective-permute-start.16) | collective-permute-done | bytes 100384 | tf_op jit(solution)/shard_map/ppermute | solution.py:445
  60.5 2.1 %collective-permute-start.17 = (bf16[392,128]{1,0:T(8,128)(2,1)S(1)}, bf16[392,128]{1,0:T(8,128)(2,1)S(1)}, u32[]{:S(2)}, u32[]{:S(2)}) collective-permute-start(bf16[392,128]{1,0:T(8,128)(2,1)S(1)} %add_convert_fusion.1), channel_id=1, source_target_pairs={{0,16},{4,20},{8,24},{12,28},{16,0},{20,4},{24,8},{28,12},{1,17},{... | collective-permute-start | bytes 301064 | tf_op jit(solution)/shard_map/ppermute | solution.py:445
  62.6 3.1 %collective-permute-done.19 = bf16[2,256,256]{2,1,0:T(8,128)(2,1)S(1)} collective-permute-done((bf16[2,256,256]{2,1,0:T(8,128)(2,1)S(1)}, bf16[2,256,256]{2,1,0:T(8,128)(2,1)S(1)}, u32[]{:S(2)}, u32[]{:S(2)}) %collective-permute-start.19) | collective-permute-done | bytes 262176 | tf_op jit(solution)/shard_map/ppermute | solution.py:445
  65.8 3.4 %collective-permute-start.20 = (bf16[256,256]{1,0:T(8,128)(2,1)S(1)}, bf16[256,256]{1,0:T(8,128)(2,1)S(1)}, u32[]{:S(2)}, u32[]{:S(2)}) collective-permute-start(bf16[256,256]{1,0:T(8,128)(2,1)S(1)} %get-tuple-element.93), channel_id=1, source_target_pairs={{0,16},{4,20},{8,24},{12,28},{16,0},{20,4},{24,8},{28,12},{1,17},{... | collective-permute-start | bytes 393224 | tf_op jit(solution)/shard_map/ppermute | solution.py:445
  69.2 0.4 collective-permute-done.18
  69.7 3.2 %collective-permute-start.21 = (bf16[256,256]{1,0:T(8,128)(2,1)S(1)}, bf16[256,256]{1,0:T(8,128)(2,1)S(1)}, u32[]{:S(2)}, u32[]{:S(2)}) collective-permute-start(bf16[256,256]{1,0:T(8,128)(2,1)S(1)} %get-tuple-element.94), channel_id=1, source_target_pairs={{0,24},{4,28},{8,16},{12,20},{16,8},{20,12},{24,0},{28,4},{1,25},{... | collective-permute-start | bytes 393224 | tf_op jit(solution)/shard_map/ppermute | solution.py:445
  72.9 0.1 collective-permute-start.11
  73.1 0.8 collective-permute-start.22
  73.9 0.6 shard_map.99
  74.5 3.0 %collective-permute-done.20 = bf16[256,256]{1,0:T(8,128)(2,1)S(1)} collective-permute-done((bf16[256,256]{1,0:T(8,128)(2,1)S(1)}, bf16[256,256]{1,0:T(8,128)(2,1)S(1)}, u32[]{:S(2)}, u32[]{:S(2)}) %collective-permute-start.20) | collective-permute-done | bytes 131104 | tf_op jit(solution)/shard_map/ppermute | solution.py:445
  77.6 0.8 collective-permute-start.13
  78.4 1.5 %collective-permute-done.22 = bf16[256,256]{1,0:T(8,128)(2,1)S(1)} collective-permute-done((bf16[256,256]{1,0:T(8,128)(2,1)S(1)}, bf16[256,256]{1,0:T(8,128)(2,1)S(1)}, u32[]{:S(2)}, u32[]{:S(2)}) %collective-permute-start.22) | collective-permute-done | bytes 131104 | tf_op jit(solution)/shard_map/ppermute | solution.py:445
  79.9 0.8 collective-permute-start.14
  80.6 2.5 %shard_map.101 = (bf16[1024,256]{1,0:T(8,128)(2,1)}, bf16[1024,256]{1,0:T(8,128)(2,1)}) custom-call(s32[2]{0:T(128)S(1)} %copy-done.6, bf16[1024,256]{1,0:T(8,128)(2,1)S(1)} %copy-done.3, bf16[1024,256]{1,0:T(8,128)(2,1)S(1)} %copy-done.4, f32[1024,256]{1,0:T(8,128)S(1)} %get-tuple-element.80.dk_ref, f32[1024,256]{1,0:T(8,128)S(1)} %get-tuple-element.81.dv_ref, ...), custom_call_target="tpu_custom_call" | custom-call | flops 1000000000 | bytes 6000000 | tf_op jit(solution)/shard_map/pallas_call | solution.py:339
  83.1 0.8 fusion.2
  83.9 2.9 %collective-permute-done.13.refs_6_ = bf16[256,512]{1,0:T(8,128)(2,1)S(1)} collective-permute-done((bf16[256,512]{1,0:T(8,128)(2,1)S(1)}, bf16[256,512]{1,0:T(8,128)(2,1)S(1)}, u32[]{:S(2)}, u32[]{:S(2)}) %collective-permute-start.13) | collective-permute-done | bytes 262176 | tf_op jit(solution)/shard_map/ppermute | solution.py:445
  86.8 4.7 %collective-permute-done.14.refs_7_ = bf16[256,512]{1,0:T(8,128)(2,1)S(1)} collective-permute-done((bf16[256,512]{1,0:T(8,128)(2,1)S(1)}, bf16[256,512]{1,0:T(8,128)(2,1)S(1)}, u32[]{:S(2)}, u32[]{:S(2)}) %collective-permute-start.14) | collective-permute-done | bytes 262176 | tf_op jit(solution)/shard_map/ppermute | solution.py:445
  91.5 2.2 %shard_map.100 = bf16[1024,512]{1,0:T(8,128)(2,1)} custom-call(bf16[1024,256]{1,0:T(8,128)(2,1)S(1)} %get-tuple-element.61.h_ref.refs_0_, bf16[1024,256]{1,0:T(8,128)(2,1)S(1)} %collective-permute-done.9.refs_1_, bf16[1024,256]{1,0:T(8,128)(2,1)S(1)} %collective-permute-done.10.refs_2_, bf16[1024,256]{1,0:T(8,128)(2,1)S(1)} %collective-permute-done.11.refs_3_, ...), custom_call_target="tpu_custom_call" | custom-call | flops 1073741824 | bytes 6000000 | tf_op jit(solution)/shard_map/pallas_call | solution.py:433
  (36 shorter events, 0.3 us)
Async XLA Ops:
  0.6 19.3 %copy-start = (bf16[256,2048]{1,0:T(8,128)(2,1)S(1)}, bf16[256,2048]{1,0:T(8,128)(2,1)}, u32[]{:S(2)}) copy-start(bf16[256,2048]{1,0:T(8,128)(2,1)} %w_ref.4) | copy-start | bytes 3145732
  4.1 15.8 %collective-permute-start.2 = (bf16[1024,512]{1,0:T(8,128)(2,1)}, bf16[1024,512]{1,0:T(8,128)(2,1)S(1)}, u32[]{:S(2)}, u32[]{:S(2)}) collective-permute-start(bf16[1024,512]{1,0:T(8,128)(2,1)} %refs_0_.3), channel_id=1, source_target_pairs={{0,1},{1,0},{2,3},{3,2},{4,5},{5,4},{6,7},{7,6},{8,9},{9,8},{10,11... | collective-permute-start | bytes 3145736 | tf_op jit(solution)/shard_map/ppermute | solution.py:445
  4.7 31.4 %collective-permute-start.7 = (bf16[1024,512]{1,0:T(8,128)(2,1)}, bf16[1024,512]{1,0:T(8,128)(2,1)S(1)}, u32[]{:S(2)}, u32[]{:S(2)}) collective-permute-start(bf16[1024,512]{1,0:T(8,128)(2,1)} %refs_0_.3), channel_id=1, source_target_pairs={{0,2},{1,3},{2,0},{3,1},{4,6},{5,7},{6,4},{7,5},{8,10},{9,11},{10,... | collective-permute-start | bytes 3145736 | tf_op jit(solution)/shard_map/ppermute | solution.py:445
  7.2 9.8 %collective-permute-start.4 = (f32[256,128]{1,0:T(8,128)}, f32[256,128]{1,0:T(8,128)S(1)}, u32[]{:S(2)}, u32[]{:S(2)}) collective-permute-start(f32[256,128]{1,0:T(8,128)} %get-tuple-element.50), channel_id=1, source_target_pairs={{0,4},{4,0},{8,12},{12,8},{16,20},{20,16},{24,28},{28,24},{1,5},{5... | collective-permute-start | bytes 393224 | tf_op jit(solution)/shard_map/ppermute | solution.py:445
  8.8 5.7 %collective-permute-start = (f32[136,128]{1,0:T(8,128)}, f32[136,128]{1,0:T(8,128)S(1)}, u32[]{:S(2)}, u32[]{:S(2)}) collective-permute-start(f32[136,128]{1,0:T(8,128)} %get-tuple-element.49), channel_id=1, source_target_pairs={{0,4},{4,0},{8,12},{12,8},{16,20},{20,16},{24,28},{28,24},{1,5},{5... | collective-permute-start | bytes 208904 | tf_op jit(solution)/shard_map/ppermute | solution.py:445
  15.4 4.5 %collective-permute-start.1 = (f32[136,128]{1,0:T(8,128)S(1)}, f32[136,128]{1,0:T(8,128)S(1)}, u32[]{:S(2)}, u32[]{:S(2)}) collective-permute-start(f32[136,128]{1,0:T(8,128)S(1)} %add.33), channel_id=1, source_target_pairs={{0,8},{4,12},{8,0},{12,4},{16,24},{20,28},{24,16},{28,20},{1,9},{5... | collective-permute-start | bytes 208904 | tf_op jit(solution)/shard_map/ppermute | solution.py:445
  18.0 7.8 %collective-permute-start.5 = (f32[256,128]{1,0:T(8,128)S(1)}, f32[256,128]{1,0:T(8,128)S(1)}, u32[]{:S(2)}, u32[]{:S(2)}) collective-permute-start(f32[256,128]{1,0:T(8,128)S(1)} %add.35), channel_id=1, source_target_pairs={{0,8},{4,12},{8,0},{12,4},{16,24},{20,28},{24,16},{28,20},{1,9},{5... | collective-permute-start | bytes 393224 | tf_op jit(solution)/shard_map/ppermute | solution.py:445
  19.9 1.2 %copy-start.1 = (bf16[1024,512]{1,0:T(8,128)(2,1)S(1)}, bf16[1024,512]{1,0:T(8,128)(2,1)}, u32[]{:S(2)}) copy-start(bf16[1024,512]{1,0:T(8,128)(2,1)} %refs_0_.3) | copy-start | bytes 3145732
  21.2 0.7 copy-start.5
  21.8 9.5 %copy-start.3 = (bf16[1024,256]{1,0:T(8,128)(2,1)S(1)}, bf16[1024,256]{1,0:T(8,128)(2,1)}, u32[]{:S(2)}) copy-start(bf16[1024,256]{1,0:T(8,128)(2,1)} %k_ref.7) | copy-start | bytes 1572868
  21.8 9.5 %copy-start.6 = (s32[2]{0:T(128)S(1)}, s32[2]{0:T(128)}, u32[]{:S(2)}) copy-start(s32[2]{0:T(128)} %pad_add_fusion.me_ref) | copy-start | bytes 28
  23.1 8.2 %collective-permute-start.3 = (f32[136,128]{1,0:T(8,128)S(1)}, f32[136,128]{1,0:T(8,128)S(1)}, u32[]{:S(2)}, u32[]{:S(2)}) collective-permute-start(f32[136,128]{1,0:T(8,128)S(1)} %add.34), channel_id=1, source_target_pairs={{0,16},{4,20},{8,24},{12,28},{16,0},{20,4},{24,8},{28,12},{1,17},{... | collective-permute-start | bytes 208904 | tf_op jit(solution)/shard_map/ppermute | solution.py:445
  25.8 10.4 %copy-start.4 = (bf16[1024,256]{1,0:T(8,128)(2,1)S(1)}, bf16[1024,256]{1,0:T(8,128)(2,1)}, u32[]{:S(2)}) copy-start(bf16[1024,256]{1,0:T(8,128)(2,1)} %v_ref.5) | copy-start | bytes 1572868
  25.8 10.4 %copy-start.7 = (bf16[1024,256]{1,0:T(8,128)(2,1)S(1)}, bf16[1024,256]{1,0:T(8,128)(2,1)}, u32[]{:S(2)}) copy-start(bf16[1024,256]{1,0:T(8,128)(2,1)} %q_ref.3) | copy-start | bytes 1572868
  25.8 10.2 %collective-permute-start.6 = (f32[256,128]{1,0:T(8,128)S(1)}, f32[256,128]{1,0:T(8,128)S(1)}, u32[]{:S(2)}, u32[]{:S(2)}) collective-permute-start(f32[256,128]{1,0:T(8,128)S(1)} %add.36), channel_id=1, source_target_pairs={{0,16},{4,20},{8,24},{12,28},{16,0},{20,4},{24,8},{28,12},{1,17},{... | collective-permute-start | bytes 393224 | tf_op jit(solution)/shard_map/ppermute | solution.py:445
  36.1 3.1 %collective-permute-start.8 = (bf16[1024,512]{1,0:T(8,128)(2,1)S(1)}, bf16[1024,512]{1,0:T(8,128)(2,1)S(1)}, u32[]{:S(2)}, u32[]{:S(2)}) collective-permute-start(bf16[1024,512]{1,0:T(8,128)(2,1)S(1)} %collective-permute-done.7.refs_1_.refs_2_), channel_id=1, source_target_pairs={{0,1},{1,0},{2,3},{3,2},{4,5},{5,4},{6,7},{7,6},{8,9},{9,8},{10,11... | collective-permute-start | bytes 3145736 | tf_op jit(solution)/shard_map/ppermute | solution.py:445
  39.1 1.3 %copy-start.2 = (bf16[1024,512]{1,0:T(8,128)(2,1)S(1)}, bf16[1024,512]{1,0:T(8,128)(2,1)}, u32[]{:S(2)}) copy-start(bf16[1024,512]{1,0:T(8,128)(2,1)} %refs_0_.3) | copy-start | bytes 3145732
  50.5 5.2 %collective-permute-start.15 = (bf16[392,128]{1,0:T(8,128)(2,1)S(1)}, bf16[392,128]{1,0:T(8,128)(2,1)S(1)}, u32[]{:S(2)}, u32[]{:S(2)}) collective-permute-start(bf16[392,128]{1,0:T(8,128)(2,1)S(1)} %get-tuple-element.84), channel_id=1, source_target_pairs={{0,4},{4,0},{8,12},{12,8},{16,20},{20,16},{24,28},{28,24},{1,5},{5... | collective-permute-start | bytes 301064 | tf_op jit(solution)/shard_map/ppermute | solution.py:445
  55.8 4.7 %collective-permute-start.16 = (bf16[392,128]{1,0:T(8,128)(2,1)S(1)}, bf16[392,128]{1,0:T(8,128)(2,1)S(1)}, u32[]{:S(2)}, u32[]{:S(2)}) collective-permute-start(bf16[392,128]{1,0:T(8,128)(2,1)S(1)} %fusion.3), channel_id=1, source_target_pairs={{0,8},{4,12},{8,0},{12,4},{16,24},{20,28},{24,16},{28,20},{1,9},{5... | collective-permute-start | bytes 301064 | tf_op jit(solution)/shard_map/ppermute | solution.py:445
  56.5 9.2 %collective-permute-start.19 = (bf16[2,256,256]{2,1,0:T(8,128)(2,1)S(1)}, bf16[2,256,256]{2,1,0:T(8,128)(2,1)S(1)}, u32[]{:S(2)}, u32[]{:S(2)}) collective-permute-start(bf16[2,256,256]{2,1,0:T(8,128)(2,1)S(1)} %get-tuple-element.91), channel_id=1, source_target_pairs={{0,4},{4,0},{8,12},{12,8},{16,20},{20,16},{24,28},{28,24},{1,5},{5... | collective-permute-start | bytes 786440 | tf_op jit(solution)/shard_map/ppermute | solution.py:445
  58.0 11.6 %collective-permute-start.18 = (bf16[2,256,256]{2,1,0:T(8,128)(2,1)S(1)}, bf16[2,256,256]{2,1,0:T(8,128)(2,1)S(1)}, u32[]{:S(2)}, u32[]{:S(2)}) collective-permute-start(bf16[2,256,256]{2,1,0:T(8,128)(2,1)S(1)} %get-tuple-element.60), channel_id=1, source_target_pairs={{0,4},{4,0},{8,12},{12,8},{16,20},{20,16},{24,28},{28,24},{1,5},{5... | collective-permute-start | bytes 786440 | tf_op jit(solution)/shard_map/ppermute | solution.py:445
  58.5 14.4 %collective-permute-start.10 = (bf16[1024,256]{1,0:T(8,128)(2,1)S(1)}, bf16[1024,256]{1,0:T(8,128)(2,1)S(1)}, u32[]{:S(2)}, u32[]{:S(2)}) collective-permute-start(bf16[1024,256]{1,0:T(8,128)(2,1)S(1)} %get-tuple-element.61.h_ref.refs_0_), channel_id=1, source_target_pairs={{0,2},{1,3},{2,0},{3,1},{4,6},{5,7},{6,4},{7,5},{8,10},{9,11},{10,... | collective-permute-start | bytes 1572872 | tf_op jit(solution)/shard_map/ppermute | solution.py:445
  59.1 32.4 %collective-permute-start.9 = (bf16[1024,256]{1,0:T(8,128)(2,1)S(1)}, bf16[1024,256]{1,0:T(8,128)(2,1)S(1)}, u32[]{:S(2)}, u32[]{:S(2)}) collective-permute-start(bf16[1024,256]{1,0:T(8,128)(2,1)S(1)} %get-tuple-element.61.h_ref.refs_0_), channel_id=1, source_target_pairs={{0,1},{1,0},{2,3},{3,2},{4,5},{5,4},{6,7},{7,6},{8,9},{9,8},{10,11... | collective-permute-start | bytes 1572872 | tf_op jit(solution)/shard_map/ppermute | solution.py:445
  60.5 12.5 %collective-permute-start.17 = (bf16[392,128]{1,0:T(8,128)(2,1)S(1)}, bf16[392,128]{1,0:T(8,128)(2,1)S(1)}, u32[]{:S(2)}, u32[]{:S(2)}) collective-permute-start(bf16[392,128]{1,0:T(8,128)(2,1)S(1)} %add_convert_fusion.1), channel_id=1, source_target_pairs={{0,16},{4,20},{8,24},{12,28},{16,0},{20,4},{24,8},{28,12},{1,17},{... | collective-permute-start | bytes 301064 | tf_op jit(solution)/shard_map/ppermute | solution.py:445
  65.8 11.8 %collective-permute-start.20 = (bf16[256,256]{1,0:T(8,128)(2,1)S(1)}, bf16[256,256]{1,0:T(8,128)(2,1)S(1)}, u32[]{:S(2)}, u32[]{:S(2)}) collective-permute-start(bf16[256,256]{1,0:T(8,128)(2,1)S(1)} %get-tuple-element.93), channel_id=1, source_target_pairs={{0,16},{4,20},{8,24},{12,28},{16,0},{20,4},{24,8},{28,12},{1,17},{... | collective-permute-start | bytes 393224 | tf_op jit(solution)/shard_map/ppermute | solution.py:445
  69.7 7.9 %collective-permute-start.21 = (bf16[256,256]{1,0:T(8,128)(2,1)S(1)}, bf16[256,256]{1,0:T(8,128)(2,1)S(1)}, u32[]{:S(2)}, u32[]{:S(2)}) collective-permute-start(bf16[256,256]{1,0:T(8,128)(2,1)S(1)} %get-tuple-element.94), channel_id=1, source_target_pairs={{0,24},{4,28},{8,16},{12,20},{16,8},{20,12},{24,0},{28,4},{1,25},{... | collective-permute-start | bytes 393224 | tf_op jit(solution)/shard_map/ppermute | solution.py:445
  72.9 18.5 %collective-permute-start.11 = (bf16[1024,256]{1,0:T(8,128)(2,1)S(1)}, bf16[1024,256]{1,0:T(8,128)(2,1)S(1)}, u32[]{:S(2)}, u32[]{:S(2)}) collective-permute-start(bf16[1024,256]{1,0:T(8,128)(2,1)S(1)} %collective-permute-done.10.refs_2_), channel_id=1, source_target_pairs={{0,1},{1,0},{2,3},{3,2},{4,5},{5,4},{6,7},{7,6},{8,9},{9,8},{10,11... | collective-permute-start | bytes 1572872 | tf_op jit(solution)/shard_map/ppermute | solution.py:445
  73.1 6.8 %collective-permute-start.22 = (bf16[256,256]{1,0:T(8,128)(2,1)S(1)}, bf16[256,256]{1,0:T(8,128)(2,1)S(1)}, u32[]{:S(2)}, u32[]{:S(2)}) collective-permute-start(bf16[256,256]{1,0:T(8,128)(2,1)S(1)} %fusion.4), channel_id=1, source_target_pairs={{0,8},{4,12},{8,0},{12,4},{16,24},{20,28},{24,16},{28,20},{1,9},{5... | collective-permute-start | bytes 393224 | tf_op jit(solution)/shard_map/ppermute | solution.py:445
  77.6 6.3 %collective-permute-start.12 = (bf16[256,512]{1,0:T(8,128)(2,1)S(1)}, bf16[256,512]{1,0:T(8,128)(2,1)S(1)}, u32[]{:S(2)}, u32[]{:S(2)}) collective-permute-start(bf16[256,512]{1,0:T(8,128)(2,1)S(1)} %get-tuple-element.75), channel_id=1, source_target_pairs={{0,1},{1,0},{2,3},{3,2},{4,5},{5,4},{6,7},{7,6},{8,9},{9,8},{10,11... | collective-permute-start | bytes 786440 | tf_op jit(solution)/shard_map/ppermute | solution.py:445
  77.6 9.2 %collective-permute-start.13 = (bf16[256,512]{1,0:T(8,128)(2,1)S(1)}, bf16[256,512]{1,0:T(8,128)(2,1)S(1)}, u32[]{:S(2)}, u32[]{:S(2)}) collective-permute-start(bf16[256,512]{1,0:T(8,128)(2,1)S(1)} %get-tuple-element.77), channel_id=1, source_target_pairs={{0,2},{1,3},{2,0},{3,1},{4,6},{5,7},{6,4},{7,5},{8,10},{9,11},{10,... | collective-permute-start | bytes 786440 | tf_op jit(solution)/shard_map/ppermute | solution.py:445
  79.9 11.6 %collective-permute-start.14 = (bf16[256,512]{1,0:T(8,128)(2,1)S(1)}, bf16[256,512]{1,0:T(8,128)(2,1)S(1)}, u32[]{:S(2)}, u32[]{:S(2)}) collective-permute-start(bf16[256,512]{1,0:T(8,128)(2,1)S(1)} %get-tuple-element.79), channel_id=1, source_target_pairs={{0,3},{1,2},{2,1},{3,0},{4,7},{5,6},{6,5},{7,4},{8,11},{9,10},{10,... | collective-permute-start | bytes 786440 | tf_op jit(solution)/shard_map/ppermute | solution.py:445

commit v4 on v3

--- a/solution.py
+++ b/solution.py
@@ -15,8 +15,6 @@
 F32 = jnp.float32
 BF16 = jnp.bfloat16
 VMEM_SPEC = pl.BlockSpec(memory_space=pltpu.VMEM)
-HBM_SPEC = pl.BlockSpec(memory_space=pltpu.HBM)
-SMEM_SPEC = pl.BlockSpec(memory_space=pltpu.SMEM)
 
 
 def dot(left, right, axes=(1, 0)):
@@ -101,15 +99,7 @@
     return mats[:heads]
 
 
-def totals_kernel(me_ref, k_hbm, v_hbm, g_ref, n_ref, k_ref, v_ref, sem):
-    copies = [
-        pltpu.make_async_copy(k_hbm, k_ref, sem.at[0]),
-        pltpu.make_async_copy(v_hbm, v_ref, sem.at[1]),
-    ]
-    for copy in copies:
-        copy.start()
-    for copy in copies:
-        copy.wait()
+def totals_kernel(k_ref, v_ref, g_ref, n_ref):
     grams = []
     for h in range(k_ref.shape[1] // HDIM):
         cols = slice(h * HDIM, (h + 1) * HDIM)
@@ -120,22 +110,22 @@
     fold_into(g_ref, grams)
 
 
-def totals(me, keys, values, heads):
+def totals(keys, values, heads):
     return pl.pallas_call(
         totals_kernel,
         out_shape=(shape((folded(heads) * (HDIM + 8), HDIM)), shape((heads * HDIM, HDIM))),
-        in_specs=[SMEM_SPEC, HBM_SPEC, HBM_SPEC],
+        in_specs=[VMEM_SPEC] * 2,
         out_specs=(VMEM_SPEC, VMEM_SPEC),
-        scratch_shapes=[pltpu.VMEM(keys.shape, BF16)] * 2 + [pltpu.SemaphoreType.DMA((2,))],
-        compiler_params=params(60),
+        compiler_params=params(),
         cost_estimate=cost(2 * 2 * keys.size * HDIM, 4 * keys.size),
-    )(me, keys, values)
-
-
-def taken(me_ref, refs, backward):
+    )(keys, values)
+
+
+def taken(refs, backward):
     total = None
+    mine = lax.axis_index("ctx")
     for r, ref in enumerate(refs):
-        bit = (me_ref[1] >> r) & 1
+        bit = (mine >> r) & 1
         wanted = jnp.where(bit == (0 if backward else 1), 1.0, 0.0)
         part = ref[...].astype(F32) * wanted
         total = part if total is None else total + part
@@ -149,11 +139,11 @@
             yield h, b, h * blocks + b, slice(b * SPAN, (b + 1) * SPAN), slice(h * HDIM, (h + 1) * HDIM)
 
 
-def inverse_kernel(rounds, me_ref, k_ref, *refs):
+def inverse_kernel(rounds, k_ref, *refs):
     e_ref, x_ref, last_ref, a_ref, es, xs = refs[rounds:]
     heads = k_ref.shape[1] // HDIM
     eye = unit()
-    grams = unfold_from(taken(me_ref, refs[:rounds], False), heads)
+    grams = unfold_from(taken(refs[:rounds], False), heads)
     for h, b, i, rows, cols in places(k_ref, heads):
         ridged = grams[h] + jnp.where(eye, RIDGE, 0.0)
         scale = 1.0 / jnp.sqrt(jnp.sum(ridged * ridged, keepdims=True))
@@ -184,23 +174,23 @@
         last_ref[i] = xs[i]
 
 
-def inverses(me, keys, grams, count):
+def inverses(keys, grams, count):
     stash = shape((NEWTON, count, HDIM, HDIM), BF16)
     state = shape((count, HDIM, HDIM))
     return pl.pallas_call(
         functools.partial(inverse_kernel, len(grams)),
         out_shape=(stash, stash, state, state),
-        in_specs=[SMEM_SPEC] + [VMEM_SPEC] * (1 + len(grams)),
+        in_specs=[VMEM_SPEC] * (1 + len(grams)),
         out_specs=(VMEM_SPEC,) * 4,
         scratch_shapes=[pltpu.VMEM((count, HDIM, HDIM), F32)] * 2,
         compiler_params=params(),
         cost_estimate=cost(2_000_000_000, 8_000_000),
-    )(me, keys, *grams)
-
-
-def outputs_kernel(rounds, me_ref, q_ref, k_ref, v_ref, last_ref, *refs):
+    )(keys, *grams)
+
+
+def outputs_kernel(rounds, q_ref, k_ref, v_ref, last_ref, *refs):
     out_ref, pre_ref, s_ref, w_ref = refs[rounds:]
-    prefix = taken(me_ref, refs[:rounds], False)
+    prefix = taken(refs[:rounds], False)
     heads = q_ref.shape[1] // HDIM
     keep = causal()
     nil = jnp.zeros((HDIM, HDIM), BF16)
@@ -222,7 +212,7 @@
         pairs[h] = pairs[h] + dot(k, v, (0, 0))
 
 
-def outputs(me, queries, keys, values, last, pairs):
+def outputs(queries, keys, values, last, pairs):
     count = last.shape[0]
     return pl.pallas_call(
         functools.partial(outputs_kernel, len(pairs)),
@@ -232,11 +222,11 @@
             shape((count, SPAN, 2 * HDIM), BF16),
             shape((count, SPAN, SPAN), BF16),
         ),
-        in_specs=[SMEM_SPEC] + [VMEM_SPEC] * (4 + len(pairs)),
+        in_specs=[VMEM_SPEC] * (4 + len(pairs)),
         out_specs=(VMEM_SPEC,) * 4,
         compiler_params=params(),
         cost_estimate=cost(2_000_000_000, 8_000_000),
-    )(me, queries, keys, values, last, *pairs)
+    )(queries, keys, values, last, *pairs)
 
 
 def tangent_kernel(
@@ -317,9 +307,9 @@
     )(queries, keys, values, grads, *stash)
 
 
-def finish_kernel(rounds, me_ref, k_ref, v_ref, dk_ref, dv_ref, da_ref, dn_ref, *refs):
+def finish_kernel(rounds, k_ref, v_ref, dk_ref, dv_ref, da_ref, dn_ref, *refs):
     gk_ref, gv_ref = refs[rounds:]
-    sum_ref = taken(me_ref, refs[:rounds], True)
+    sum_ref = taken(refs[:rounds], True)
     heads = k_ref.shape[1] // HDIM
     sa = unfold_from(sum_ref, heads, heads * HDIM)
     sn = [sum_ref[h * HDIM : (h + 1) * HDIM, :] for h in range(heads)]
@@ -335,20 +325,20 @@
         sn[h] = sn[h] + dn_ref[i]
 
 
-def finish(me, keys, values, dk, dv, da, dn, sums):
+def finish(keys, values, dk, dv, da, dn, sums):
     return pl.pallas_call(
         functools.partial(finish_kernel, len(sums)),
         out_shape=(shape(keys.shape, BF16),) * 2,
-        in_specs=[SMEM_SPEC] + [VMEM_SPEC] * (6 + len(sums)),
+        in_specs=[VMEM_SPEC] * (6 + len(sums)),
         out_specs=(VMEM_SPEC,) * 2,
         compiler_params=params(),
         cost_estimate=cost(1_000_000_000, 6_000_000),
-    )(me, keys, values, dk, dv, da, dn, *sums)
-
-
-def grads_kernel(first, me_ref, w_ref, *refs):
+    )(keys, values, dk, dv, da, dn, *sums)
+
+
+def grads_kernel(first, w_ref, *refs):
     out_ref = refs[-1]
-    me = me_ref[0]
+    me = lax.axis_index("head")
     total = refs[0][...] if first else None
     for s, part in enumerate(refs[1:-1] if first else refs[:-1]):
         width = part.shape[1]
@@ -358,41 +348,41 @@
     out_ref[...] = total.astype(out_ref.dtype)
 
 
-def head_grads(me, w_out, parts, first, begun=None):
+def head_grads(w_out, parts, first, begun=None):
     rows = parts[0].shape[0]
     begun = [] if begun is None else [begun]
     return pl.pallas_call(
         functools.partial(grads_kernel, first),
         out_shape=shape((rows, w_out.shape[0]), BF16 if begun else F32),
-        in_specs=[SMEM_SPEC] + [VMEM_SPEC] * (1 + len(parts) + len(begun)),
+        in_specs=[VMEM_SPEC] * (1 + len(parts) + len(begun)),
         out_specs=VMEM_SPEC,
         compiler_params=params(),
         cost_estimate=cost(rows * w_out.size, 4_000_000),
-    )(me, w_out, *begun, *parts)
-
-
-def columns_kernel(me_ref, w_ref, *refs):
+    )(w_out, *begun, *parts)
+
+
+def columns_kernel(w_ref, *refs):
     for s, out_ref in enumerate(refs):
         width = out_ref.shape[1]
-        cols = pl.ds(pl.multiple_of((me_ref[0] ^ s) * width, width), width)
+        cols = pl.ds(pl.multiple_of((lax.axis_index("head") ^ s) * width, width), width)
         out_ref[...] = w_ref[:, cols]
 
 
-def column_pieces(me, w_out, count):
+def column_pieces(w_out, count):
     piece = shape((w_out.shape[0], w_out.shape[1] // count), BF16)
     return pl.pallas_call(
         columns_kernel,
         out_shape=(piece,) * count,
-        in_specs=[SMEM_SPEC, VMEM_SPEC],
+        in_specs=[VMEM_SPEC],
         out_specs=(VMEM_SPEC,) * count,
         compiler_params=params(),
         cost_estimate=cost(0, 4 * w_out.size),
-    )(me, w_out)
-
-
-def weights_kernel(me_ref, h_ref, *refs):
+    )(w_out)
+
+
+def weights_kernel(h_ref, *refs):
     parts, outs, all_ref = refs[:-5], refs[-5:-1], refs[-1]
-    me, mine = me_ref[0], me_ref[1]
+    me, mine = lax.axis_index("head"), lax.axis_index("ctx")
     count, _, width = all_ref.shape
     fold = parts[0].shape[1] // width
     for s, part in enumerate(parts):
@@ -405,18 +395,18 @@
         ref[t % (count // 2) // 2] = all_ref[t]
 
 
-def weight_terms(me, heads_out, parts, count):
+def weight_terms(heads_out, parts, count):
     feats = sum(part.shape[1] for part in parts)
     piece = (heads_out.shape[1], feats // count)
     return pl.pallas_call(
         weights_kernel,
         out_shape=(shape((count // 4,) + piece, BF16),) * 4,
-        in_specs=[SMEM_SPEC] + [VMEM_SPEC] * (1 + len(parts)),
+        in_specs=[VMEM_SPEC] * (1 + len(parts)),
         out_specs=(VMEM_SPEC,) * 4,
         scratch_shapes=[pltpu.VMEM((count,) + piece, BF16)],
         compiler_params=params(),
         cost_estimate=cost(2 * heads_out.size * feats, 6_000_000),
-    )(me, heads_out, *parts)
+    )(heads_out, *parts)
 
 
 def layer_kernel(*refs):
@@ -457,10 +447,9 @@
     heads = queries.shape[1] // HDIM
     count = heads * (queries.shape[0] // SPAN)
     head_count, ctx_count = lax.axis_size("head"), lax.axis_size("ctx")
-    me = jnp.stack([lax.axis_index("head"), lax.axis_index("ctx")]).astype(jnp.int32)
     evens = range(2, head_count, 2)
 
-    gram, pair = totals(me, keys, values, heads)
+    gram, pair = totals(keys, values, heads)
     cot = after(cotangent, gram, pair)
     far = {s: swap(cot, "head", s) for s in evens}
     near = swap(cot, "head", 1)
@@ -468,27 +457,26 @@
     grams, pairs = [], []
     begun = None
     for distance in doublings("ctx"):
-        if distance == ctx_count // 2:
-            gram = after(gram, begun)
         grams.append(swap(gram, "ctx", distance))
         pairs.append(swap(pair, "ctx", distance))
         if begun is None:
-            begun = head_grads(me, w_out, [cotangent, after(near, grams[0])], 0)
+            begun = head_grads(w_out, [cotangent, near], 0)
         gram, pair = gram + grams[-1], pair + pairs[-1]
-    *stash, last, ridged = inverses(me, keys, grams, count)
+    grams[-1] = after(grams[-1], begun)
+    *stash, last, ridged = inverses(keys, grams, count)
     pairs[-1] = after(pairs[-1], last)
     parts = []
     for s in evens:
         parts += [far[s], swap(after(far[s], pairs[-1]), "head", 1)]
-    columns = column_pieces(me, after(w_out, begun), head_count)
+    columns = column_pieces(after(w_out, begun), head_count)
     columns = [after(c, pairs[-1], *far.values()) for c in columns]
     columns = [swap(c, "head", s) if s else c for s, c in enumerate(columns)]
-    heads_out, states, solved, scores = outputs(me, queries, keys, values, last, pairs)
-
-    grads = head_grads(me, w_out, parts, 2, after(begun, heads_out))
+    heads_out, states, solved, scores = outputs(queries, keys, values, last, pairs)
+
+    grads = head_grads(w_out, parts, 2, after(begun, heads_out))
     parts = [cotangent, near] + parts
     even_low, even_high, odd_low, odd_high = weight_terms(
-        me, after(heads_out, grads), parts, ctx_count
+        after(heads_out, grads), parts, ctx_count
     )
     high = swap(odd_high, "ctx", 1)
     low = swap(odd_low, "ctx", 1)
@@ -501,8 +489,7 @@
         queries, keys, values, after(grads, odd_low), [*stash, last, ridged, states, solved, scores]
     )
 
-    high, low = after(high, grad_queries), after(low, grad_queries)
-    high = even_high.astype(F32) + high.astype(F32)
+    high = even_high.astype(F32) + after(high, grad_queries).astype(F32)
     half = ctx_count // 4
     moved = [swap(high[u].astype(BF16), "ctx", 2 * (half + u)) for u in range(half)]
 
@@ -512,17 +499,16 @@
         sums = sums + later[-1].astype(F32)
         send = sums.astype(BF16)
 
-    low = even_low.astype(F32) + low.astype(F32)
+    low = even_low.astype(F32) + after(low, *later[:2]).astype(F32)
     moved += [swap(low[u].astype(BF16), "ctx", 2 * u) for u in range(1, half)]
-    grad_weight = low[0]
-    for part in moved:
-        grad_weight = grad_weight + part.astype(F32)
-
     outs = [heads_out, outs_near]
     for part in outs_far:
         outs += [part, swap(after(part, grad_queries), "head", 1)]
     layer_out = layer(outs, columns)
-    grad_keys, grad_values = finish(me, keys, values, dk, dv, da, dn, later)
+    grad_weight = low[0]
+    for part in moved:
+        grad_weight = grad_weight + after(part, layer_out).astype(F32)
+    grad_keys, grad_values = finish(keys, values, dk, dv, da, dn, later)
     return (layer_out, grad_queries, grad_keys, grad_values, grad_weight)
 
 

time: 93.9 us -> 93.5 us (level)
  waiting for transfers between devices: 32.5 us -> 43.4 us
  Pallas kernels: 28.6 us -> 22.2 us
  starting transfers between devices: 26.4 us -> 23.6 us
  other arithmetic: 3.39 us -> 1.01 us
    ppermute x23, waiting for transfers between devices: 32.5 us -> 43.4 us  [swap(): return lax.ppermute(value, axis, [(i, i ^ distance) for i in range(count)])]
    ppermute x23, starting transfers between devices: 26.4 us -> 23.6 us  [swap(): return lax.ppermute(value, axis, [(i, i ^ distance) for i in range(count)])]
    pallas_call x1, Pallas kernels: 2.89 us -> 0.33 us  [totals(): pl.pallas_call(totals_kernel, out_shape=(shape((folded(heads) * (HDIM + 8...]
    add x4, other arithmetic: 1.84 us -> 0.05 us  [shards(): gram, pair = (gram + grams[-1], pair + pairs[-1])]
    pallas_call x2, Pallas kernels: 2.58 us -> 1.5 us  [head_grads(): pl.pallas_call(functools.partial(grads_kernel, first), out_shape=shape((r...]
    unnamed x16 -> x14, local copies, waits for them, and re-layouts: 1.91 us -> 2.25 us
  transfers between devices with their start and end apart: 23 -> 23, of which waited for: 11 -> 11; matrix products, arithmetic and copies ran while one was open for 3% -> 0% of each run, Pallas kernels for 13% -> 12%
where the time goes in v4:
time: 93.5 us; the launch traced here: 93.4 us
  waiting for transfers between devices  43.4 us (46%)
  starting transfers between devices  23.6 us (25%)
  Pallas kernels  22.2 us (24%)
  local copies, waits for them, and re-layouts  2.29 us (2%)
  other arithmetic  1.01 us (1%)
    ppermute x23, waiting for transfers between devices, swap(): return lax.ppermute(value, axis, [(i, i ^ distance) for i in range(count)])  43.4 us
    ppermute x23, starting transfers between devices, swap(): return lax.ppermute(value, axis, [(i, i ^ distance) for i in range(count)])  23.6 us
    pallas_call x1, Pallas kernels, tangent(): pl.pallas_call(tangent_kernel, out_shape=(shape(queries.shape, BF16), wid...  8.14 us
    pallas_call x1, Pallas kernels, inverses(): pl.pallas_call(functools.partial(inverse_kernel, len(grams)), out_shape=(...  4.21 us
    pallas_call x1, Pallas kernels, outputs(): pl.pallas_call(functools.partial(outputs_kernel, len(pairs)), out_shape=(...  2.4 us
    unnamed x14, local copies, waits for them, and re-layouts  2.25 us
    pallas_call x1, Pallas kernels, layer(): pl.pallas_call(layer_kernel, out_shape=shape((rows, cols), BF16), in_spec...  2.22 us
    pallas_call x1, Pallas kernels, finish(): pl.pallas_call(functools.partial(finish_kernel, len(sums)), out_shape=(sh...  1.94 us
  transfers between devices with their start and end apart: 23, of which 11 were waited for; matrix products, arithmetic and copies ran while one was open for 0% of the time, Pallas kernels for 12%

profile of v4, /device:TPU:0, one launch (start us, length us, event | category | flops | bytes accessed | tf_op | source)
XLA Modules:
  0.0 93.4 jit_solution(3951220100715579195)
XLA Ops:
  0.6 0.0 copy-start.1
  0.7 0.0 copy-start.2
  0.7 1.2 %copy-done.2 = bf16[1024,256]{1,0:T(8,128)(2,1)S(1)} copy-done((bf16[1024,256]{1,0:T(8,128)(2,1)S(1)}, bf16[1024,256]{1,0:T(8,128)(2,1)}, u32[]{:S(2)}) %copy-start.2) | copy-done | bytes 524312
  1.8 1.0 %copy-done.4 = bf16[1024,256]{1,0:T(8,128)(2,1)S(1)} copy-done((bf16[1024,256]{1,0:T(8,128)(2,1)S(1)}, bf16[1024,256]{1,0:T(8,128)(2,1)}, u32[]{:S(2)}) %copy-start.4) | copy-done | bytes 524312
  2.9 0.3 shard_map.92
  3.2 0.6 collective-permute-start.3
  3.8 2.6 %collective-permute-start.7 = (bf16[1024,512]{1,0:T(8,128)(2,1)}, bf16[1024,512]{1,0:T(8,128)(2,1)S(1)}, u32[]{:S(2)}, u32[]{:S(2)}) collective-permute-start(bf16[1024,512]{1,0:T(8,128)(2,1)} %refs_0_.3), channel_id=1, source_target_pairs={{0,2},{1,3},{2,0},{3,1},{4,6},{5,7},{6,4},{7,5},{8,10},{9,11},{10,... | collective-permute-start | bytes 3145736 | tf_op jit(solution)/shard_map/ppermute | solution.py:435
  6.3 1.5 %collective-permute-start.4 = (f32[256,128]{1,0:T(8,128)S(1)}, f32[256,128]{1,0:T(8,128)S(1)}, u32[]{:S(2)}, u32[]{:S(2)}) collective-permute-start(f32[256,128]{1,0:T(8,128)S(1)} %get-tuple-element.52), channel_id=1, source_target_pairs={{0,4},{4,0},{8,12},{12,8},{16,20},{20,16},{24,28},{28,24},{1,5},{5... | collective-permute-start | bytes 393224 | tf_op jit(solution)/shard_map/ppermute | solution.py:435
  7.9 0.5 collective-permute-start
  8.4 4.3 %collective-permute-done.4.refs_0_ = f32[256,128]{1,0:T(8,128)S(1)} collective-permute-done((f32[256,128]{1,0:T(8,128)S(1)}, f32[256,128]{1,0:T(8,128)S(1)}, u32[]{:S(2)}, u32[]{:S(2)}) %collective-permute-start.4) | collective-permute-done | bytes 131104 | tf_op jit(solution)/shard_map/ppermute | solution.py:435
  12.7 1.6 %collective-permute-start.5 = (f32[256,128]{1,0:T(8,128)S(1)}, f32[256,128]{1,0:T(8,128)S(1)}, u32[]{:S(2)}, u32[]{:S(2)}) collective-permute-start(f32[256,128]{1,0:T(8,128)S(1)} %add.35), channel_id=1, source_target_pairs={{0,8},{4,12},{8,0},{12,4},{16,24},{20,28},{24,16},{28,20},{1,9},{5... | collective-permute-start | bytes 393224 | tf_op jit(solution)/shard_map/ppermute | solution.py:435
  14.3 0.7 collective-permute-start.1
  15.0 3.7 %collective-permute-done.1.refs_1_ = f32[136,128]{1,0:T(8,128)S(1)} collective-permute-done((f32[136,128]{1,0:T(8,128)S(1)}, f32[136,128]{1,0:T(8,128)S(1)}, u32[]{:S(2)}, u32[]{:S(2)}) %collective-permute-start.1) | collective-permute-done | bytes 69664 | tf_op jit(solution)/shard_map/ppermute | solution.py:435
  18.7 2.7 %collective-permute-start.2 = (f32[136,128]{1,0:T(8,128)S(1)}, f32[136,128]{1,0:T(8,128)S(1)}, u32[]{:S(2)}, u32[]{:S(2)}) collective-permute-start(f32[136,128]{1,0:T(8,128)S(1)} %add.34), channel_id=1, source_target_pairs={{0,16},{4,20},{8,24},{12,28},{16,0},{20,4},{24,8},{28,12},{1,17},{... | collective-permute-start | bytes 208904 | tf_op jit(solution)/shard_map/ppermute | solution.py:435
  21.4 0.4 collective-permute-start.6
  21.8 0.8 shard_map.93.refs_0_
  22.6 0.0 copy-start.5
  22.6 3.9 %collective-permute-done.2.refs_2_ = f32[136,128]{1,0:T(8,128)S(1)} collective-permute-done((f32[136,128]{1,0:T(8,128)S(1)}, f32[136,128]{1,0:T(8,128)S(1)}, u32[]{:S(2)}, u32[]{:S(2)}) %collective-permute-start.2) | collective-permute-done | bytes 69664 | tf_op jit(solution)/shard_map/ppermute | solution.py:435
  26.5 4.2 %shard_map.94 = (bf16[8,8,128,128]{3,2,1,0:T(8,128)(2,1)S(1)}, bf16[8,8,128,128]{3,2,1,0:T(8,128)(2,1)S(1)}, f32[8,128,128]{2,1,0:T(8,128)S(1)}, f32[8,128,128]{2,1,0:T(8,128)S(1)}) custom-call(bf16[1024,256]{1,0:T(8,128)(2,1)S(1)} %copy-done.3, f32[136,128]{1,0:T(8,128)S(1)} %collective-permute-done.refs_0_, f32[136,128]{1,0:T(8,128)S(1)} %collective-permute-done.1.refs_1_, ...), custom_call_target="tpu_custom_call" | custom-call | flops 2000000000 | bytes 8000000 | tf_op jit(solution)/shard_map/pallas_call | solution.py:180
  30.7 0.1 collective-permute-start.8
  30.8 2.4 %shard_map.95 = (bf16[1024,256]{1,0:T(8,128)(2,1)S(1)}, bf16[8,128,256]{2,1,0:T(8,128)(2,1)S(1)}, bf16[8,256,256]{2,1,0:T(8,128)(2,1)S(1)}, bf16[8,256,256]{2,1,0:T(8,128)(2,1)S(1)}) custom-call(bf16[1024,256]{1,0:T(8,128)(2,1)S(1)} %copy-done.6, bf16[1024,256]{1,0:T(8,128)(2,1)S(1)} %copy-done.3, bf16[1024,256]{1,0:T(8,128)(2,1)S(1)} %copy-done.5, ...), custom_call_target="tpu_custom_call" | custom-call | flops 2000000000 | bytes 8000000 | tf_op jit(solution)/shard_map/pallas_call | solution.py:217
  33.2 0.2 collective-permute-done.8.refs_2_.refs_3_
  33.5 0.7 shard_map.96.do_ref
  34.2 1.4 %shard_map.97 = (bf16[2,256,256]{2,1,0:T(8,128)(2,1)S(1)}, bf16[2,256,256]{2,1,0:T(8,128)(2,1)S(1)}, bf16[2,256,256]{2,1,0:T(8,128)(2,1)S(1)}, bf16[2,256,256]{2,1,0:T(8,128)(2,1)S(1)}) custom-call(bf16[1024,256]{1,0:T(8,128)(2,1)S(1)} %get-tuple-element.62.h_ref.refs_0_, bf16[1024,512]{1,0:T(8,128)(2,1)S(1)} %copy-done.1, ...), custom_call_target="tpu_custom_call" | custom-call | flops 1073741824 | bytes 6000000 | tf_op jit(solution)/shard_map/pallas_call | solution.py:401
  35.6 8.1 %shard_map.98 = (bf16[1024,256]{1,0:T(8,128)(2,1)}, f32[1024,256]{1,0:T(8,128)S(1)}, f32[1024,256]{1,0:T(8,128)S(1)}, f32[8,128,128]{2,1,0:T(8,128)S(1)}, f32[8,...) custom-call(bf16[1024,256]{1,0:T(8,128)(2,1)S(1)} %copy-done.6, ...), custom_call_target="tpu_custom_call" | custom-call | flops 4000000000 | bytes 8000000 | tf_op jit(solution)/shard_map/pallas_call | solution.py:296
  43.7 1.5 %collective-permute-start.15 = (bf16[392,128]{1,0:T(8,128)(2,1)S(1)}, bf16[392,128]{1,0:T(8,128)(2,1)S(1)}, u32[]{:S(2)}, u32[]{:S(2)}) collective-permute-start(bf16[392,128]{1,0:T(8,128)(2,1)S(1)} %get-tuple-element.85), channel_id=1, source_target_pairs={{0,4},{4,0},{8,12},{12,8},{16,20},{20,16},{24,28},{28,24},{1,5},{5... | collective-permute-start | bytes 301064 | tf_op jit(solution)/shard_map/ppermute | solution.py:435
  45.2 3.5 %collective-permute-done.15.refs_0_ = bf16[392,128]{1,0:T(8,128)(2,1)S(1)} collective-permute-done((bf16[392,128]{1,0:T(8,128)(2,1)S(1)}, bf16[392,128]{1,0:T(8,128)(2,1)S(1)}, u32[]{:S(2)}, u32[]{:S(2)}) %collective-permute-start.15) | collective-permute-done | bytes 100384 | tf_op jit(solution)/shard_map/ppermute | solution.py:435
  48.8 1.4 %collective-permute-start.16 = (bf16[392,128]{1,0:T(8,128)(2,1)S(1)}, bf16[392,128]{1,0:T(8,128)(2,1)S(1)}, u32[]{:S(2)}, u32[]{:S(2)}) collective-permute-start(bf16[392,128]{1,0:T(8,128)(2,1)S(1)} %fusion.3), channel_id=1, source_target_pairs={{0,8},{4,12},{8,0},{12,4},{16,24},{20,28},{24,16},{28,20},{1,9},{5... | collective-permute-start | bytes 301064 | tf_op jit(solution)/shard_map/ppermute | solution.py:435
  50.2 1.5 %collective-permute-start.19 = (bf16[2,256,256]{2,1,0:T(8,128)(2,1)S(1)}, bf16[2,256,256]{2,1,0:T(8,128)(2,1)S(1)}, u32[]{:S(2)}, u32[]{:S(2)}) collective-permute-start(bf16[2,256,256]{2,1,0:T(8,128)(2,1)S(1)} %get-tuple-element.92), channel_id=1, source_target_pairs={{0,4},{4,0},{8,12},{12,8},{16,20},{20,16},{24,28},{28,24},{1,5},{5... | collective-permute-start | bytes 786440 | tf_op jit(solution)/shard_map/ppermute | solution.py:435
  51.7 0.5 collective-permute-start.18
  52.2 0.1 shard_map.99
  52.3 0.1 collective-permute-start.12
  52.4 1.6 %collective-permute-start.13 = (bf16[256,512]{1,0:T(8,128)(2,1)S(1)}, bf16[256,512]{1,0:T(8,128)(2,1)S(1)}, u32[]{:S(2)}, u32[]{:S(2)}) collective-permute-start(bf16[256,512]{1,0:T(8,128)(2,1)S(1)} %get-tuple-element.78), channel_id=1, source_target_pairs={{0,2},{1,3},{2,0},{3,1},{4,6},{5,7},{6,4},{7,5},{8,10},{9,11},{10,... | collective-permute-start | bytes 786440 | tf_op jit(solution)/shard_map/ppermute | solution.py:435
  53.9 0.8 collective-permute-start.10
  54.8 4.6 %collective-permute-done.19 = bf16[2,256,256]{2,1,0:T(8,128)(2,1)S(1)} collective-permute-done((bf16[2,256,256]{2,1,0:T(8,128)(2,1)S(1)}, bf16[2,256,256]{2,1,0:T(8,128)(2,1)S(1)}, u32[]{:S(2)}, u32[]{:S(2)}) %collective-permute-start.19) | collective-permute-done | bytes 262176 | tf_op jit(solution)/shard_map/ppermute | solution.py:435
  59.3 3.8 %collective-permute-done.18 = bf16[2,256,256]{2,1,0:T(8,128)(2,1)S(1)} collective-permute-done((bf16[2,256,256]{2,1,0:T(8,128)(2,1)S(1)}, bf16[2,256,256]{2,1,0:T(8,128)(2,1)S(1)}, u32[]{:S(2)}, u32[]{:S(2)}) %collective-permute-start.18) | collective-permute-done | bytes 262176 | tf_op jit(solution)/shard_map/ppermute | solution.py:435
  63.1 0.1 convert_add_fusion
  63.2 0.1 add_convert_fusion
  63.3 9.5 %collective-permute-done.10.refs_2_ = bf16[1024,256]{1,0:T(8,128)(2,1)S(1)} collective-permute-done((bf16[1024,256]{1,0:T(8,128)(2,1)S(1)}, bf16[1024,256]{1,0:T(8,128)(2,1)S(1)}, u32[]{:S(2)}, u32[]{:S(2)}) %collective-permute-start.10) | collective-permute-done | bytes 524320 | tf_op jit(solution)/shard_map/ppermute | solution.py:435
  72.9 3.0 %collective-permute-start.17 = (bf16[392,128]{1,0:T(8,128)(2,1)S(1)}, bf16[392,128]{1,0:T(8,128)(2,1)S(1)}, u32[]{:S(2)}, u32[]{:S(2)}) collective-permute-start(bf16[392,128]{1,0:T(8,128)(2,1)S(1)} %add_convert_fusion.1), channel_id=1, source_target_pairs={{0,16},{4,20},{8,24},{12,28},{16,0},{20,4},{24,8},{28,12},{1,17},{... | collective-permute-start | bytes 301064 | tf_op jit(solution)/shard_map/ppermute | solution.py:435
  75.9 0.1 collective-permute-start.20
  76.0 1.4 %collective-permute-done.14.refs_7_ = bf16[256,512]{1,0:T(8,128)(2,1)S(1)} collective-permute-done((bf16[256,512]{1,0:T(8,128)(2,1)S(1)}, bf16[256,512]{1,0:T(8,128)(2,1)S(1)}, u32[]{:S(2)}, u32[]{:S(2)}) %collective-permute-start.14) | collective-permute-done | bytes 262176 | tf_op jit(solution)/shard_map/ppermute | solution.py:435
  77.4 2.5 %collective-permute-start.21 = (bf16[256,256]{1,0:T(8,128)(2,1)S(1)}, bf16[256,256]{1,0:T(8,128)(2,1)S(1)}, u32[]{:S(2)}, u32[]{:S(2)}) collective-permute-start(bf16[256,256]{1,0:T(8,128)(2,1)S(1)} %get-tuple-element.98), channel_id=1, source_target_pairs={{0,24},{4,28},{8,16},{12,20},{16,8},{20,12},{24,0},{28,4},{1,25},{... | collective-permute-start | bytes 393224 | tf_op jit(solution)/shard_map/ppermute | solution.py:435
  79.8 7.1 %collective-permute-done.17.refs_2_ = bf16[392,128]{1,0:T(8,128)(2,1)S(1)} collective-permute-done((bf16[392,128]{1,0:T(8,128)(2,1)S(1)}, bf16[392,128]{1,0:T(8,128)(2,1)S(1)}, u32[]{:S(2)}, u32[]{:S(2)}) %collective-permute-start.17) | collective-permute-done | bytes 100384 | tf_op jit(solution)/shard_map/ppermute | solution.py:435
  87.0 1.9 %shard_map.101 = (bf16[1024,256]{1,0:T(8,128)(2,1)}, bf16[1024,256]{1,0:T(8,128)(2,1)}) custom-call(bf16[1024,256]{1,0:T(8,128)(2,1)S(1)} %copy-done.3, bf16[1024,256]{1,0:T(8,128)(2,1)S(1)} %copy-done.5, f32[1024,256]{1,0:T(8,128)S(1)} %get-tuple-element.81.dk_ref, f32[1024,256]{1,0:T(8,128)S(1)} %get-tuple-element.82.dv_ref, ...), custom_call_target="tpu_custom_call" | custom-call | flops 1000000000 | bytes 6000000 | tf_op jit(solution)/shard_map/pallas_call | solution.py:329
  88.9 2.2 %shard_map.100 = bf16[1024,512]{1,0:T(8,128)(2,1)} custom-call(bf16[1024,256]{1,0:T(8,128)(2,1)S(1)} %get-tuple-element.62.h_ref.refs_0_, bf16[1024,256]{1,0:T(8,128)(2,1)S(1)} %collective-permute-done.9.refs_1_, bf16[1024,256]{1,0:T(8,128)(2,1)S(1)} %collective-permute-done.10.refs_2_, bf16[1024,256]{1,0:T(8,128)(2,1)S(1)} %collective-permute-done.11.refs_3_, ...), custom_call_target="tpu_custom_call" | custom-call | flops 1073741824 | bytes 6000000 | tf_op jit(solution)/shard_map/pallas_call | solution.py:423
  91.2 1.4 %collective-permute-done.22 = bf16[256,256]{1,0:T(8,128)(2,1)S(1)} collective-permute-done((bf16[256,256]{1,0:T(8,128)(2,1)S(1)}, bf16[256,256]{1,0:T(8,128)(2,1)S(1)}, u32[]{:S(2)}, u32[]{:S(2)}) %collective-permute-start.22) | collective-permute-done | bytes 131104 | tf_op jit(solution)/shard_map/ppermute | solution.py:435
  92.6 0.8 fusion.2
  (33 shorter events, 0.2 us)
Async XLA Ops:
  0.6 21.2 %copy-start.1 = (bf16[1024,512]{1,0:T(8,128)(2,1)S(1)}, bf16[1024,512]{1,0:T(8,128)(2,1)}, u32[]{:S(2)}) copy-start(bf16[1024,512]{1,0:T(8,128)(2,1)} %refs_0_.3) | copy-start | bytes 3145732
  0.6 21.2 %copy-start = (bf16[256,2048]{1,0:T(8,128)(2,1)S(1)}, bf16[256,2048]{1,0:T(8,128)(2,1)}, u32[]{:S(2)}) copy-start(bf16[256,2048]{1,0:T(8,128)(2,1)} %w_ref.4) | copy-start | bytes 3145732
  0.7 1.2 %copy-start.2 = (bf16[1024,256]{1,0:T(8,128)(2,1)S(1)}, bf16[1024,256]{1,0:T(8,128)(2,1)}, u32[]{:S(2)}) copy-start(bf16[1024,256]{1,0:T(8,128)(2,1)} %k_ref.9) | copy-start | bytes 1572868
  1.8 1.0 %copy-start.4 = (bf16[1024,256]{1,0:T(8,128)(2,1)S(1)}, bf16[1024,256]{1,0:T(8,128)(2,1)}, u32[]{:S(2)}) copy-start(bf16[1024,256]{1,0:T(8,128)(2,1)} %v_ref.7) | copy-start | bytes 1572868
  3.2 18.6 %collective-permute-start.3 = (bf16[1024,512]{1,0:T(8,128)(2,1)}, bf16[1024,512]{1,0:T(8,128)(2,1)S(1)}, u32[]{:S(2)}, u32[]{:S(2)}) collective-permute-start(bf16[1024,512]{1,0:T(8,128)(2,1)} %refs_0_.3), channel_id=1, source_target_pairs={{0,1},{1,0},{2,3},{3,2},{4,5},{5,4},{6,7},{7,6},{8,9},{9,8},{10,11... | collective-permute-start | bytes 3145736 | tf_op jit(solution)/shard_map/ppermute | solution.py:435
  3.8 26.9 %collective-permute-start.7 = (bf16[1024,512]{1,0:T(8,128)(2,1)}, bf16[1024,512]{1,0:T(8,128)(2,1)S(1)}, u32[]{:S(2)}, u32[]{:S(2)}) collective-permute-start(bf16[1024,512]{1,0:T(8,128)(2,1)} %refs_0_.3), channel_id=1, source_target_pairs={{0,2},{1,3},{2,0},{3,1},{4,6},{5,7},{6,4},{7,5},{8,10},{9,11},{10,... | collective-permute-start | bytes 3145736 | tf_op jit(solution)/shard_map/ppermute | solution.py:435
  6.3 6.3 %collective-permute-start.4 = (f32[256,128]{1,0:T(8,128)S(1)}, f32[256,128]{1,0:T(8,128)S(1)}, u32[]{:S(2)}, u32[]{:S(2)}) collective-permute-start(f32[256,128]{1,0:T(8,128)S(1)} %get-tuple-element.52), channel_id=1, source_target_pairs={{0,4},{4,0},{8,12},{12,8},{16,20},{20,16},{24,28},{28,24},{1,5},{5... | collective-permute-start | bytes 393224 | tf_op jit(solution)/shard_map/ppermute | solution.py:435
  7.9 6.4 %collective-permute-start = (f32[136,128]{1,0:T(8,128)S(1)}, f32[136,128]{1,0:T(8,128)S(1)}, u32[]{:S(2)}, u32[]{:S(2)}) collective-permute-start(f32[136,128]{1,0:T(8,128)S(1)} %get-tuple-element.51), channel_id=1, source_target_pairs={{0,4},{4,0},{8,12},{12,8},{16,20},{20,16},{24,28},{28,24},{1,5},{5... | collective-permute-start | bytes 208904 | tf_op jit(solution)/shard_map/ppermute | solution.py:435
  12.7 8.7 %collective-permute-start.5 = (f32[256,128]{1,0:T(8,128)S(1)}, f32[256,128]{1,0:T(8,128)S(1)}, u32[]{:S(2)}, u32[]{:S(2)}) collective-permute-start(f32[256,128]{1,0:T(8,128)S(1)} %add.35), channel_id=1, source_target_pairs={{0,8},{4,12},{8,0},{12,4},{16,24},{20,28},{24,16},{28,20},{1,9},{5... | collective-permute-start | bytes 393224 | tf_op jit(solution)/shard_map/ppermute | solution.py:435
  14.3 4.4 %collective-permute-start.1 = (f32[136,128]{1,0:T(8,128)S(1)}, f32[136,128]{1,0:T(8,128)S(1)}, u32[]{:S(2)}, u32[]{:S(2)}) collective-permute-start(f32[136,128]{1,0:T(8,128)S(1)} %add.33), channel_id=1, source_target_pairs={{0,8},{4,12},{8,0},{12,4},{16,24},{20,28},{24,16},{28,20},{1,9},{5... | collective-permute-start | bytes 208904 | tf_op jit(solution)/shard_map/ppermute | solution.py:435
  18.7 7.8 %collective-permute-start.2 = (f32[136,128]{1,0:T(8,128)S(1)}, f32[136,128]{1,0:T(8,128)S(1)}, u32[]{:S(2)}, u32[]{:S(2)}) collective-permute-start(f32[136,128]{1,0:T(8,128)S(1)} %add.34), channel_id=1, source_target_pairs={{0,16},{4,20},{8,24},{12,28},{16,0},{20,4},{24,8},{28,12},{1,17},{... | collective-permute-start | bytes 208904 | tf_op jit(solution)/shard_map/ppermute | solution.py:435
  21.4 5.1 %copy-start.3 = (bf16[1024,256]{1,0:T(8,128)(2,1)S(1)}, bf16[1024,256]{1,0:T(8,128)(2,1)}, u32[]{:S(2)}) copy-start(bf16[1024,256]{1,0:T(8,128)(2,1)} %k_ref.9) | copy-start | bytes 1572868
  21.4 9.3 %collective-permute-start.6 = (f32[256,128]{1,0:T(8,128)S(1)}, f32[256,128]{1,0:T(8,128)S(1)}, u32[]{:S(2)}, u32[]{:S(2)}) collective-permute-start(f32[256,128]{1,0:T(8,128)S(1)} %add.36), channel_id=1, source_target_pairs={{0,16},{4,20},{8,24},{12,28},{16,0},{20,4},{24,8},{28,12},{1,17},{... | collective-permute-start | bytes 393224 | tf_op jit(solution)/shard_map/ppermute | solution.py:435
  22.6 8.2 %copy-start.5 = (bf16[1024,256]{1,0:T(8,128)(2,1)S(1)}, bf16[1024,256]{1,0:T(8,128)(2,1)}, u32[]{:S(2)}) copy-start(bf16[1024,256]{1,0:T(8,128)(2,1)} %v_ref.7) | copy-start | bytes 1572868
  22.6 8.2 %copy-start.6 = (bf16[1024,256]{1,0:T(8,128)(2,1)S(1)}, bf16[1024,256]{1,0:T(8,128)(2,1)}, u32[]{:S(2)}) copy-start(bf16[1024,256]{1,0:T(8,128)(2,1)} %q_ref.3) | copy-start | bytes 1572868
  30.7 2.7 %collective-permute-start.8 = (bf16[1024,512]{1,0:T(8,128)(2,1)S(1)}, bf16[1024,512]{1,0:T(8,128)(2,1)S(1)}, u32[]{:S(2)}, u32[]{:S(2)}) collective-permute-start(bf16[1024,512]{1,0:T(8,128)(2,1)S(1)} %collective-permute-done.7.refs_1_.refs_2_), channel_id=1, source_target_pairs={{0,1},{1,0},{2,3},{3,2},{4,5},{5,4},{6,7},{7,6},{8,9},{9,8},{10,11... | collective-permute-start | bytes 3145736 | tf_op jit(solution)/shard_map/ppermute | solution.py:435
  43.7 5.0 %collective-permute-start.15 = (bf16[392,128]{1,0:T(8,128)(2,1)S(1)}, bf16[392,128]{1,0:T(8,128)(2,1)S(1)}, u32[]{:S(2)}, u32[]{:S(2)}) collective-permute-start(bf16[392,128]{1,0:T(8,128)(2,1)S(1)} %get-tuple-element.85), channel_id=1, source_target_pairs={{0,4},{4,0},{8,12},{12,8},{16,20},{20,16},{24,28},{28,24},{1,5},{5... | collective-permute-start | bytes 301064 | tf_op jit(solution)/shard_map/ppermute | solution.py:435
  48.8 5.1 %collective-permute-start.16 = (bf16[392,128]{1,0:T(8,128)(2,1)S(1)}, bf16[392,128]{1,0:T(8,128)(2,1)S(1)}, u32[]{:S(2)}, u32[]{:S(2)}) collective-permute-start(bf16[392,128]{1,0:T(8,128)(2,1)S(1)} %fusion.3), channel_id=1, source_target_pairs={{0,8},{4,12},{8,0},{12,4},{16,24},{20,28},{24,16},{28,20},{1,9},{5... | collective-permute-start | bytes 301064 | tf_op jit(solution)/shard_map/ppermute | solution.py:435
  50.2 9.2 %collective-permute-start.19 = (bf16[2,256,256]{2,1,0:T(8,128)(2,1)S(1)}, bf16[2,256,256]{2,1,0:T(8,128)(2,1)S(1)}, u32[]{:S(2)}, u32[]{:S(2)}) collective-permute-start(bf16[2,256,256]{2,1,0:T(8,128)(2,1)S(1)} %get-tuple-element.92), channel_id=1, source_target_pairs={{0,4},{4,0},{8,12},{12,8},{16,20},{20,16},{24,28},{28,24},{1,5},{5... | collective-permute-start | bytes 786440 | tf_op jit(solution)/shard_map/ppermute | solution.py:435
  51.7 11.5 %collective-permute-start.18 = (bf16[2,256,256]{2,1,0:T(8,128)(2,1)S(1)}, bf16[2,256,256]{2,1,0:T(8,128)(2,1)S(1)}, u32[]{:S(2)}, u32[]{:S(2)}) collective-permute-start(bf16[2,256,256]{2,1,0:T(8,128)(2,1)S(1)} %get-tuple-element.61), channel_id=1, source_target_pairs={{0,4},{4,0},{8,12},{12,8},{16,20},{20,16},{24,28},{28,24},{1,5},{5... | collective-permute-start | bytes 786440 | tf_op jit(solution)/shard_map/ppermute | solution.py:435
  52.3 20.6 %collective-permute-start.12 = (bf16[256,512]{1,0:T(8,128)(2,1)S(1)}, bf16[256,512]{1,0:T(8,128)(2,1)S(1)}, u32[]{:S(2)}, u32[]{:S(2)}) collective-permute-start(bf16[256,512]{1,0:T(8,128)(2,1)S(1)} %get-tuple-element.76), channel_id=1, source_target_pairs={{0,1},{1,0},{2,3},{3,2},{4,5},{5,4},{6,7},{7,6},{8,9},{9,8},{10,11... | collective-permute-start | bytes 786440 | tf_op jit(solution)/shard_map/ppermute | solution.py:435
  52.4 23.6 %collective-permute-start.13 = (bf16[256,512]{1,0:T(8,128)(2,1)S(1)}, bf16[256,512]{1,0:T(8,128)(2,1)S(1)}, u32[]{:S(2)}, u32[]{:S(2)}) collective-permute-start(bf16[256,512]{1,0:T(8,128)(2,1)S(1)} %get-tuple-element.78), channel_id=1, source_target_pairs={{0,2},{1,3},{2,0},{3,1},{4,6},{5,7},{6,4},{7,5},{8,10},{9,11},{10,... | collective-permute-start | bytes 786440 | tf_op jit(solution)/shard_map/ppermute | solution.py:435
  53.9 18.9 %collective-permute-start.10 = (bf16[1024,256]{1,0:T(8,128)(2,1)S(1)}, bf16[1024,256]{1,0:T(8,128)(2,1)S(1)}, u32[]{:S(2)}, u32[]{:S(2)}) collective-permute-start(bf16[1024,256]{1,0:T(8,128)(2,1)S(1)} %get-tuple-element.62.h_ref.refs_0_), channel_id=1, source_target_pairs={{0,2},{1,3},{2,0},{3,1},{4,6},{5,7},{6,4},{7,5},{8,10},{9,11},{10,... | collective-permute-start | bytes 1572872 | tf_op jit(solution)/shard_map/ppermute | solution.py:435
  59.3 18.0 %collective-permute-start.14 = (bf16[256,512]{1,0:T(8,128)(2,1)S(1)}, bf16[256,512]{1,0:T(8,128)(2,1)S(1)}, u32[]{:S(2)}, u32[]{:S(2)}) collective-permute-start(bf16[256,512]{1,0:T(8,128)(2,1)S(1)} %get-tuple-element.80), channel_id=1, source_target_pairs={{0,3},{1,2},{2,1},{3,0},{4,7},{5,6},{6,5},{7,4},{8,11},{9,10},{10,... | collective-permute-start | bytes 786440 | tf_op jit(solution)/shard_map/ppermute | solution.py:435
  63.1 25.8 %collective-permute-start.9 = (bf16[1024,256]{1,0:T(8,128)(2,1)S(1)}, bf16[1024,256]{1,0:T(8,128)(2,1)S(1)}, u32[]{:S(2)}, u32[]{:S(2)}) collective-permute-start(bf16[1024,256]{1,0:T(8,128)(2,1)S(1)} %get-tuple-element.62.h_ref.refs_0_), channel_id=1, source_target_pairs={{0,1},{1,0},{2,3},{3,2},{4,5},{5,4},{6,7},{7,6},{8,9},{9,8},{10,11... | collective-permute-start | bytes 1572872 | tf_op jit(solution)/shard_map/ppermute | solution.py:435
  72.8 16.1 %collective-permute-start.11 = (bf16[1024,256]{1,0:T(8,128)(2,1)S(1)}, bf16[1024,256]{1,0:T(8,128)(2,1)S(1)}, u32[]{:S(2)}, u32[]{:S(2)}) collective-permute-start(bf16[1024,256]{1,0:T(8,128)(2,1)S(1)} %collective-permute-done.10.refs_2_), channel_id=1, source_target_pairs={{0,1},{1,0},{2,3},{3,2},{4,5},{5,4},{6,7},{7,6},{8,9},{9,8},{10,11... | collective-permute-start | bytes 1572872 | tf_op jit(solution)/shard_map/ppermute | solution.py:435
  72.9 14.1 %collective-permute-start.17 = (bf16[392,128]{1,0:T(8,128)(2,1)S(1)}, bf16[392,128]{1,0:T(8,128)(2,1)S(1)}, u32[]{:S(2)}, u32[]{:S(2)}) collective-permute-start(bf16[392,128]{1,0:T(8,128)(2,1)S(1)} %add_convert_fusion.1), channel_id=1, source_target_pairs={{0,16},{4,20},{8,24},{12,28},{16,0},{20,4},{24,8},{28,12},{1,17},{... | collective-permute-start | bytes 301064 | tf_op jit(solution)/shard_map/ppermute | solution.py:435
  75.9 16.7 %collective-permute-start.20 = (bf16[256,256]{1,0:T(8,128)(2,1)S(1)}, bf16[256,256]{1,0:T(8,128)(2,1)S(1)}, u32[]{:S(2)}, u32[]{:S(2)}) collective-permute-start(bf16[256,256]{1,0:T(8,128)(2,1)S(1)} %get-tuple-element.97), channel_id=1, source_target_pairs={{0,16},{4,20},{8,24},{12,28},{16,0},{20,4},{24,8},{28,12},{1,17},{... | collective-permute-start | bytes 393224 | tf_op jit(solution)/shard_map/ppermute | solution.py:435
  77.4 15.2 %collective-permute-start.21 = (bf16[256,256]{1,0:T(8,128)(2,1)S(1)}, bf16[256,256]{1,0:T(8,128)(2,1)S(1)}, u32[]{:S(2)}, u32[]{:S(2)}) collective-permute-start(bf16[256,256]{1,0:T(8,128)(2,1)S(1)} %get-tuple-element.98), channel_id=1, source_target_pairs={{0,24},{4,28},{8,16},{12,20},{16,8},{20,12},{24,0},{28,4},{1,25},{... | collective-permute-start | bytes 393224 | tf_op jit(solution)/shard_map/ppermute | solution.py:435
  87.0 5.6 %collective-permute-start.22 = (bf16[256,256]{1,0:T(8,128)(2,1)S(1)}, bf16[256,256]{1,0:T(8,128)(2,1)S(1)}, u32[]{:S(2)}, u32[]{:S(2)}) collective-permute-start(bf16[256,256]{1,0:T(8,128)(2,1)S(1)} %fusion.4), channel_id=1, source_target_pairs={{0,8},{4,12},{8,0},{12,4},{16,24},{20,28},{24,16},{28,20},{1,9},{5... | collective-permute-start | bytes 393224 | tf_op jit(solution)/shard_map/ppermute | solution.py:435

commit v5 on v4

--- a/solution.py
+++ b/solution.py
@@ -362,19 +362,22 @@
 
 
 def columns_kernel(w_ref, *refs):
+    me = lax.axis_index("head")
     for s, out_ref in enumerate(refs):
-        width = out_ref.shape[1]
-        cols = pl.ds(pl.multiple_of((lax.axis_index("head") ^ s) * width, width), width)
-        out_ref[...] = w_ref[:, cols]
+        width = out_ref.shape[2]
+        for f in range(2):
+            target = me ^ (2 * s + f)
+            cols = pl.ds(pl.multiple_of(target * width, width), width)
+            out_ref[f] = w_ref[:, cols]
 
 
 def column_pieces(w_out, count):
-    piece = shape((w_out.shape[0], w_out.shape[1] // count), BF16)
+    piece = shape((2, w_out.shape[0], w_out.shape[1] // count), BF16)
     return pl.pallas_call(
         columns_kernel,
-        out_shape=(piece,) * count,
+        out_shape=(piece,) * (count // 2),
         in_specs=[VMEM_SPEC],
-        out_specs=(VMEM_SPEC,) * count,
+        out_specs=(VMEM_SPEC,) * (count // 2),
         compiler_params=params(),
         cost_estimate=cost(0, 4 * w_out.size),
     )(w_out)
@@ -450,9 +453,8 @@
     evens = range(2, head_count, 2)
 
     gram, pair = totals(keys, values, heads)
-    cot = after(cotangent, gram, pair)
-    far = {s: swap(cot, "head", s) for s in evens}
-    near = swap(cot, "head", 1)
+    far = {s: swap(cotangent, "head", s) for s in evens}
+    near = swap(after(cotangent, gram, pair), "head", 1)
 
     grams, pairs = [], []
     begun = None
@@ -470,7 +472,7 @@
         parts += [far[s], swap(after(far[s], pairs[-1]), "head", 1)]
     columns = column_pieces(after(w_out, begun), head_count)
     columns = [after(c, pairs[-1], *far.values()) for c in columns]
-    columns = [swap(c, "head", s) if s else c for s, c in enumerate(columns)]
+    columns = [swap(c, "head", 2 * s) if s else c for s, c in enumerate(columns)]
     heads_out, states, solved, scores = outputs(queries, keys, values, last, pairs)
 
     grads = head_grads(w_out, parts, 2, after(begun, heads_out))
@@ -481,29 +483,35 @@
     high = swap(odd_high, "ctx", 1)
     low = swap(odd_low, "ctx", 1)
 
-    outs_out = after(heads_out, odd_low)
-    outs_far = [swap(outs_out, "head", s) for s in evens]
-    outs_near = swap(outs_out, "head", 1)
-
     grad_queries, dk, dv, da, dn, sums, send = tangent(
         queries, keys, values, after(grads, odd_low), [*stash, last, ridged, states, solved, scores]
     )
 
+    outs_out = after(heads_out, grad_queries)
+    outs_far = [swap(outs_out, "head", s) for s in evens]
     high = even_high.astype(F32) + after(high, grad_queries).astype(F32)
     half = ctx_count // 4
-    moved = [swap(high[u].astype(BF16), "ctx", 2 * (half + u)) for u in range(half)]
+    high = [high[u].astype(BF16) for u in range(half)]
+    moved = [swap(part, "ctx", 2 * (half + u)) for u, part in enumerate(high)]
 
     later = []
     for distance in doublings("ctx"):
+        sent = send
         later.append(swap(send, "ctx", distance))
+        if distance == 1:
+            later[0] = after(later[0], *high)
         sums = sums + later[-1].astype(F32)
         send = sums.astype(BF16)
 
     low = even_low.astype(F32) + after(low, *later[:2]).astype(F32)
     moved += [swap(low[u].astype(BF16), "ctx", 2 * u) for u in range(1, half)]
-    outs = [heads_out, outs_near]
+
+    outs = [heads_out, swap(outs_out, "head", 1)]
     for part in outs_far:
-        outs += [part, swap(after(part, grad_queries), "head", 1)]
+        outs += [part, swap(after(part, sent), "head", 1)]
+    columns = [after(c, grad_queries, later[0]) for c in columns]
+    crossing = swap(jnp.stack([c[1] for c in columns]), "head", 1)
+    columns = [c for s in range(head_count // 2) for c in (columns[s][0], crossing[s])]
     layer_out = layer(outs, columns)
     grad_weight = low[0]
     for part in moved:

time: 93.5 us -> 82.9 us (0.89)
  waiting for transfers between devices: 43.4 us -> 33.9 us
  starting transfers between devices: 23.6 us -> 22.3 us
    ppermute x23 -> x22, waiting for transfers between devices: 43.4 us -> 33.9 us  [swap(): return lax.ppermute(value, axis, [(i, i ^ distance) for i in range(count)])]
    ppermute x23 -> x22, starting transfers between devices: 23.6 us -> 22.3 us  [swap(): return lax.ppermute(value, axis, [(i, i ^ distance) for i in range(count)])]
  transfers between devices with their start and end apart: 23 -> 22, of which waited for: 11 -> 8; matrix products, arithmetic and copies ran while one was open for 0% -> 1% of each run, Pallas kernels for 12% -> 26%
where the time goes in v5:
time: 82.9 us; the launch traced here: 82.8 us
  waiting for transfers between devices  33.9 us (41%)
  starting transfers between devices  22.3 us (27%)
  Pallas kernels  22.2 us (27%)
  local copies, waits for them, and re-layouts  2.39 us (3%)
  other arithmetic  1.08 us (1%)
  between operations  0.88 us (1%)
    ppermute x22, waiting for transfers between devices, swap(): return lax.ppermute(value, axis, [(i, i ^ distance) for i in range(count)])  33.9 us
    ppermute x22, starting transfers between devices, swap(): return lax.ppermute(value, axis, [(i, i ^ distance) for i in range(count)])  22.3 us
    pallas_call x1, Pallas kernels, tangent(): pl.pallas_call(tangent_kernel, out_shape=(shape(queries.shape, BF16), wid...  8.14 us
    pallas_call x1, Pallas kernels, inverses(): pl.pallas_call(functools.partial(inverse_kernel, len(grams)), out_shape=(...  4.21 us
    pallas_call x1, Pallas kernels, outputs(): pl.pallas_call(functools.partial(outputs_kernel, len(pairs)), out_shape=(...  2.4 us
    unnamed x14, local copies, waits for them, and re-layouts  2.25 us
    pallas_call x1, Pallas kernels, layer(): pl.pallas_call(layer_kernel, out_shape=shape((rows, cols), BF16), in_spec...  2.22 us
    pallas_call x1, Pallas kernels, finish(): pl.pallas_call(functools.partial(finish_kernel, len(sums)), out_shape=(sh...  1.94 us
  transfers between devices with their start and end apart: 22, of which 8 were waited for; matrix products, arithmetic and copies ran while one was open for 1% of the time, Pallas kernels for 26%

profile of v5, /device:TPU:0, one launch (start us, length us, event | category | flops | bytes accessed | tf_op | source)
XLA Modules:
  0.0 82.8 jit_solution(13626715463962167912)
XLA Ops:
  0.6 0.0 copy-start.1
  0.7 0.0 copy-start.2
  0.7 1.2 %copy-done.2 = bf16[1024,256]{1,0:T(8,128)(2,1)S(1)} copy-done((bf16[1024,256]{1,0:T(8,128)(2,1)S(1)}, bf16[1024,256]{1,0:T(8,128)(2,1)}, u32[]{:S(2)}) %copy-start.2) | copy-done | bytes 524312
  1.8 1.0 %copy-done.4 = bf16[1024,256]{1,0:T(8,128)(2,1)S(1)} copy-done((bf16[1024,256]{1,0:T(8,128)(2,1)S(1)}, bf16[1024,256]{1,0:T(8,128)(2,1)}, u32[]{:S(2)}) %copy-start.4) | copy-done | bytes 524312
  2.9 0.3 shard_map.92
  3.2 0.6 collective-permute-start.3
  3.8 2.6 %collective-permute-start.7 = (bf16[1024,512]{1,0:T(8,128)(2,1)}, bf16[1024,512]{1,0:T(8,128)(2,1)S(1)}, u32[]{:S(2)}, u32[]{:S(2)}) collective-permute-start(bf16[1024,512]{1,0:T(8,128)(2,1)} %refs_0_.3), channel_id=1, source_target_pairs={{0,2},{1,3},{2,0},{3,1},{4,6},{5,7},{6,4},{7,5},{8,10},{9,11},{10,... | collective-permute-start | bytes 3145736 | tf_op jit(solution)/shard_map/ppermute | solution.py:438
  6.3 1.5 %collective-permute-start.4 = (f32[256,128]{1,0:T(8,128)S(1)}, f32[256,128]{1,0:T(8,128)S(1)}, u32[]{:S(2)}, u32[]{:S(2)}) collective-permute-start(f32[256,128]{1,0:T(8,128)S(1)} %get-tuple-element.51), channel_id=1, source_target_pairs={{0,4},{4,0},{8,12},{12,8},{16,20},{20,16},{24,28},{28,24},{1,5},{5... | collective-permute-start | bytes 393224 | tf_op jit(solution)/shard_map/ppermute | solution.py:438
  7.9 0.5 collective-permute-start
  8.4 4.3 %collective-permute-done.4.refs_0_ = f32[256,128]{1,0:T(8,128)S(1)} collective-permute-done((f32[256,128]{1,0:T(8,128)S(1)}, f32[256,128]{1,0:T(8,128)S(1)}, u32[]{:S(2)}, u32[]{:S(2)}) %collective-permute-start.4) | collective-permute-done | bytes 131104 | tf_op jit(solution)/shard_map/ppermute | solution.py:438
  12.7 1.6 %collective-permute-start.5 = (f32[256,128]{1,0:T(8,128)S(1)}, f32[256,128]{1,0:T(8,128)S(1)}, u32[]{:S(2)}, u32[]{:S(2)}) collective-permute-start(f32[256,128]{1,0:T(8,128)S(1)} %add.35), channel_id=1, source_target_pairs={{0,8},{4,12},{8,0},{12,4},{16,24},{20,28},{24,16},{28,20},{1,9},{5... | collective-permute-start | bytes 393224 | tf_op jit(solution)/shard_map/ppermute | solution.py:438
  14.3 0.7 collective-permute-start.1
  15.0 3.7 %collective-permute-done.1.refs_1_ = f32[136,128]{1,0:T(8,128)S(1)} collective-permute-done((f32[136,128]{1,0:T(8,128)S(1)}, f32[136,128]{1,0:T(8,128)S(1)}, u32[]{:S(2)}, u32[]{:S(2)}) %collective-permute-start.1) | collective-permute-done | bytes 69664 | tf_op jit(solution)/shard_map/ppermute | solution.py:438
  18.7 2.7 %collective-permute-start.2 = (f32[136,128]{1,0:T(8,128)S(1)}, f32[136,128]{1,0:T(8,128)S(1)}, u32[]{:S(2)}, u32[]{:S(2)}) collective-permute-start(f32[136,128]{1,0:T(8,128)S(1)} %add.34), channel_id=1, source_target_pairs={{0,16},{4,20},{8,24},{12,28},{16,0},{20,4},{24,8},{28,12},{1,17},{... | collective-permute-start | bytes 208904 | tf_op jit(solution)/shard_map/ppermute | solution.py:438
  21.4 0.0 copy-start.3
  21.4 0.4 collective-permute-start.6
  21.8 0.8 shard_map.93.refs_0_
  22.6 0.0 copy-start.5
  22.6 3.9 %collective-permute-done.2.refs_2_ = f32[136,128]{1,0:T(8,128)S(1)} collective-permute-done((f32[136,128]{1,0:T(8,128)S(1)}, f32[136,128]{1,0:T(8,128)S(1)}, u32[]{:S(2)}, u32[]{:S(2)}) %collective-permute-start.2) | collective-permute-done | bytes 69664 | tf_op jit(solution)/shard_map/ppermute | solution.py:438
  26.5 4.2 %shard_map.94 = (bf16[8,8,128,128]{3,2,1,0:T(8,128)(2,1)S(1)}, bf16[8,8,128,128]{3,2,1,0:T(8,128)(2,1)S(1)}, f32[8,128,128]{2,1,0:T(8,128)S(1)}, f32[8,128,128]{2,1,0:T(8,128)S(1)}) custom-call(bf16[1024,256]{1,0:T(8,128)(2,1)S(1)} %copy-done.3, f32[136,128]{1,0:T(8,128)S(1)} %collective-permute-done.refs_0_, f32[136,128]{1,0:T(8,128)S(1)} %collective-permute-done.1.refs_1_, ...), custom_call_target="tpu_custom_call" | custom-call | flops 2000000000 | bytes 8000000 | tf_op jit(solution)/shard_map/pallas_call | solution.py:180
  30.7 0.1 collective-permute-start.8
  30.8 0.1 shard_map.99
  30.9 1.3 %collective-permute-start.15 = (bf16[2,256,512]{2,1,0:T(8,128)(2,1)S(1)}, bf16[2,256,512]{2,1,0:T(8,128)(2,1)S(1)}, u32[]{:S(2)}, u32[]{:S(2)}) collective-permute-start(bf16[2,256,512]{2,1,0:T(8,128)(2,1)S(1)} %get-tuple-element.82), channel_id=1, source_target_pairs={{0,2},{1,3},{2,0},{3,1},{4,6},{5,7},{6,4},{7,5},{8,10},{9,11},{10,... | collective-permute-start | bytes 1572872 | tf_op jit(solution)/shard_map/ppermute | solution.py:438
  32.2 2.4 %shard_map.95 = (bf16[1024,256]{1,0:T(8,128)(2,1)S(1)}, bf16[8,128,256]{2,1,0:T(8,128)(2,1)S(1)}, bf16[8,256,256]{2,1,0:T(8,128)(2,1)S(1)}, bf16[8,256,256]{2,1,0:T(8,128)(2,1)S(1)}) custom-call(bf16[1024,256]{1,0:T(8,128)(2,1)S(1)} %copy-done.6, bf16[1024,256]{1,0:T(8,128)(2,1)S(1)} %copy-done.3, bf16[1024,256]{1,0:T(8,128)(2,1)S(1)} %copy-done.5, ...), custom_call_target="tpu_custom_call" | custom-call | flops 2000000000 | bytes 8000000 | tf_op jit(solution)/shard_map/pallas_call | solution.py:217
  34.6 0.8 shard_map.96.do_ref
  35.4 1.4 %shard_map.97 = (bf16[2,256,256]{2,1,0:T(8,128)(2,1)S(1)}, bf16[2,256,256]{2,1,0:T(8,128)(2,1)S(1)}, bf16[2,256,256]{2,1,0:T(8,128)(2,1)S(1)}, bf16[2,256,256]{2,1,0:T(8,128)(2,1)S(1)}) custom-call(bf16[1024,256]{1,0:T(8,128)(2,1)S(1)} %get-tuple-element.69.h_ref.refs_0_, bf16[1024,512]{1,0:T(8,128)(2,1)S(1)} %copy-done.1, ...), custom_call_target="tpu_custom_call" | custom-call | flops 1073741824 | bytes 6000000 | tf_op jit(solution)/shard_map/pallas_call | solution.py:404
  36.7 1.6 %collective-permute-start.18 = (bf16[2,256,256]{2,1,0:T(8,128)(2,1)S(1)}, bf16[2,256,256]{2,1,0:T(8,128)(2,1)S(1)}, u32[]{:S(2)}, u32[]{:S(2)}) collective-permute-start(bf16[2,256,256]{2,1,0:T(8,128)(2,1)S(1)} %get-tuple-element.60), channel_id=1, source_target_pairs={{0,4},{4,0},{8,12},{12,8},{16,20},{20,16},{24,28},{28,24},{1,5},{5... | collective-permute-start | bytes 786440 | tf_op jit(solution)/shard_map/ppermute | solution.py:438
  38.3 0.5 collective-permute-start.12
  38.8 8.1 %shard_map.98 = (bf16[1024,256]{1,0:T(8,128)(2,1)}, f32[1024,256]{1,0:T(8,128)S(1)}, f32[1024,256]{1,0:T(8,128)S(1)}, f32[8,128,128]{2,1,0:T(8,128)S(1)}, f32[8,...) custom-call(bf16[1024,256]{1,0:T(8,128)(2,1)S(1)} %copy-done.6, ...), custom_call_target="tpu_custom_call" | custom-call | flops 4000000000 | bytes 8000000 | tf_op jit(solution)/shard_map/pallas_call | solution.py:296
  47.0 0.8 collective-permute-start.10
  47.8 3.1 %collective-permute-done.12 = bf16[2,256,256]{2,1,0:T(8,128)(2,1)S(1)} collective-permute-done((bf16[2,256,256]{2,1,0:T(8,128)(2,1)S(1)}, bf16[2,256,256]{2,1,0:T(8,128)(2,1)S(1)}, u32[]{:S(2)}, u32[]{:S(2)}) %collective-permute-start.12) | collective-permute-done | bytes 262176 | tf_op jit(solution)/shard_map/ppermute | solution.py:438
  50.9 1.5 %collective-permute-start.11 = (bf16[392,128]{1,0:T(8,128)(2,1)S(1)}, bf16[392,128]{1,0:T(8,128)(2,1)S(1)}, u32[]{:S(2)}, u32[]{:S(2)}) collective-permute-start(bf16[392,128]{1,0:T(8,128)(2,1)S(1)} %get-tuple-element.71), channel_id=1, source_target_pairs={{0,4},{4,0},{8,12},{12,8},{16,20},{20,16},{24,28},{28,24},{1,5},{5... | collective-permute-start | bytes 301064 | tf_op jit(solution)/shard_map/ppermute | solution.py:438
  52.4 0.1 add_convert_fusion
  52.5 3.0 %collective-permute-done.11.refs_0_ = bf16[392,128]{1,0:T(8,128)(2,1)S(1)} collective-permute-done((bf16[392,128]{1,0:T(8,128)(2,1)S(1)}, bf16[392,128]{1,0:T(8,128)(2,1)S(1)}, u32[]{:S(2)}, u32[]{:S(2)}) %collective-permute-start.11) | collective-permute-done | bytes 100384 | tf_op jit(solution)/shard_map/ppermute | solution.py:438
  55.5 3.6 %collective-permute-start.20 = (bf16[256,256]{1,0:T(8,128)(2,1)S(1)}, bf16[256,256]{1,0:T(8,128)(2,1)S(1)}, u32[]{:S(2)}, u32[]{:S(2)}) collective-permute-start(bf16[256,256]{1,0:T(8,128)(2,1)S(1)} %get-tuple-element.101), channel_id=1, source_target_pairs={{0,24},{4,28},{8,16},{12,20},{16,8},{20,12},{24,0},{28,4},{1,25},{... | collective-permute-start | bytes 393224 | tf_op jit(solution)/shard_map/ppermute | solution.py:438
  59.1 0.1 collective-permute-start.13
  59.2 0.1 slice_bitcast_fusion.3
  59.3 0.1 pad_maximum_fusion
  59.4 4.5 %collective-permute-done.13.refs_1_ = bf16[392,128]{1,0:T(8,128)(2,1)S(1)} collective-permute-done((bf16[392,128]{1,0:T(8,128)(2,1)S(1)}, bf16[392,128]{1,0:T(8,128)(2,1)S(1)}, u32[]{:S(2)}, u32[]{:S(2)}) %collective-permute-start.13) | collective-permute-done | bytes 100384 | tf_op jit(solution)/shard_map/ppermute | solution.py:438
  63.9 0.3 collective-permute-start.17
  64.2 0.1 convert_add_fusion
  64.3 0.3 collective-permute-start.14
  64.6 7.6 %collective-permute-done.17.refs_2_ = bf16[392,128]{1,0:T(8,128)(2,1)S(1)} collective-permute-done((bf16[392,128]{1,0:T(8,128)(2,1)S(1)}, bf16[392,128]{1,0:T(8,128)(2,1)S(1)}, u32[]{:S(2)}, u32[]{:S(2)}) %collective-permute-start.17) | collective-permute-done | bytes 100384 | tf_op jit(solution)/shard_map/ppermute | solution.py:438
  72.3 1.9 %shard_map.101 = (bf16[1024,256]{1,0:T(8,128)(2,1)}, bf16[1024,256]{1,0:T(8,128)(2,1)}) custom-call(bf16[1024,256]{1,0:T(8,128)(2,1)S(1)} %copy-done.3, bf16[1024,256]{1,0:T(8,128)(2,1)S(1)} %copy-done.5, f32[1024,256]{1,0:T(8,128)S(1)} %get-tuple-element.84.dk_ref, f32[1024,256]{1,0:T(8,128)S(1)} %get-tuple-element.85.dv_ref, ...), custom_call_target="tpu_custom_call" | custom-call | flops 1000000000 | bytes 6000000 | tf_op jit(solution)/shard_map/pallas_call | solution.py:329
  74.2 1.7 %collective-permute-start.21 = (bf16[256,256]{1,0:T(8,128)(2,1)S(1)}, bf16[256,256]{1,0:T(8,128)(2,1)S(1)}, u32[]{:S(2)}, u32[]{:S(2)}) collective-permute-start(bf16[256,256]{1,0:T(8,128)(2,1)S(1)} %fusion.4), channel_id=1, source_target_pairs={{0,8},{4,12},{8,0},{12,4},{16,24},{20,28},{24,16},{28,20},{1,9},{5... | collective-permute-start | bytes 393224 | tf_op jit(solution)/shard_map/ppermute | solution.py:438
  75.9 2.2 %shard_map.100 = bf16[1024,512]{1,0:T(8,128)(2,1)} custom-call(bf16[1024,256]{1,0:T(8,128)(2,1)S(1)} %get-tuple-element.69.h_ref.refs_0_, bf16[1024,256]{1,0:T(8,128)(2,1)S(1)} %collective-permute-done.9.refs_1_, bf16[1024,256]{1,0:T(8,128)(2,1)S(1)} %collective-permute-done.10.refs_2_, bf16[1024,256]{1,0:T(8,128)(2,1)S(1)} %collective-permute-done.14.refs_3_, ...), custom_call_target="tpu_custom_call" | custom-call | flops 1073741824 | bytes 6000000 | tf_op jit(solution)/shard_map/pallas_call | solution.py:426
  78.2 3.8 %collective-permute-done.21 = bf16[256,256]{1,0:T(8,128)(2,1)S(1)} collective-permute-done((bf16[256,256]{1,0:T(8,128)(2,1)S(1)}, bf16[256,256]{1,0:T(8,128)(2,1)S(1)}, u32[]{:S(2)}, u32[]{:S(2)}) %collective-permute-start.21) | collective-permute-done | bytes 131104 | tf_op jit(solution)/shard_map/ppermute | solution.py:438
  82.0 0.8 fusion.2
  (34 shorter events, 0.3 us)
Async XLA Ops:
  0.6 21.2 %copy-start.1 = (bf16[1024,512]{1,0:T(8,128)(2,1)S(1)}, bf16[1024,512]{1,0:T(8,128)(2,1)}, u32[]{:S(2)}) copy-start(bf16[1024,512]{1,0:T(8,128)(2,1)} %refs_0_.3) | copy-start | bytes 3145732
  0.6 21.2 %copy-start = (bf16[256,2048]{1,0:T(8,128)(2,1)S(1)}, bf16[256,2048]{1,0:T(8,128)(2,1)}, u32[]{:S(2)}) copy-start(bf16[256,2048]{1,0:T(8,128)(2,1)} %w_ref.4) | copy-start | bytes 3145732
  0.7 1.2 %copy-start.2 = (bf16[1024,256]{1,0:T(8,128)(2,1)S(1)}, bf16[1024,256]{1,0:T(8,128)(2,1)}, u32[]{:S(2)}) copy-start(bf16[1024,256]{1,0:T(8,128)(2,1)} %k_ref.9) | copy-start | bytes 1572868
  1.8 1.0 %copy-start.4 = (bf16[1024,256]{1,0:T(8,128)(2,1)S(1)}, bf16[1024,256]{1,0:T(8,128)(2,1)}, u32[]{:S(2)}) copy-start(bf16[1024,256]{1,0:T(8,128)(2,1)} %v_ref.7) | copy-start | bytes 1572868
  3.2 18.6 %collective-permute-start.3 = (bf16[1024,512]{1,0:T(8,128)(2,1)}, bf16[1024,512]{1,0:T(8,128)(2,1)S(1)}, u32[]{:S(2)}, u32[]{:S(2)}) collective-permute-start(bf16[1024,512]{1,0:T(8,128)(2,1)} %refs_0_.3), channel_id=1, source_target_pairs={{0,1},{1,0},{2,3},{3,2},{4,5},{5,4},{6,7},{7,6},{8,9},{9,8},{10,11... | collective-permute-start | bytes 3145736 | tf_op jit(solution)/shard_map/ppermute | solution.py:438
  3.8 26.9 %collective-permute-start.7 = (bf16[1024,512]{1,0:T(8,128)(2,1)}, bf16[1024,512]{1,0:T(8,128)(2,1)S(1)}, u32[]{:S(2)}, u32[]{:S(2)}) collective-permute-start(bf16[1024,512]{1,0:T(8,128)(2,1)} %refs_0_.3), channel_id=1, source_target_pairs={{0,2},{1,3},{2,0},{3,1},{4,6},{5,7},{6,4},{7,5},{8,10},{9,11},{10,... | collective-permute-start | bytes 3145736 | tf_op jit(solution)/shard_map/ppermute | solution.py:438
  6.3 6.3 %collective-permute-start.4 = (f32[256,128]{1,0:T(8,128)S(1)}, f32[256,128]{1,0:T(8,128)S(1)}, u32[]{:S(2)}, u32[]{:S(2)}) collective-permute-start(f32[256,128]{1,0:T(8,128)S(1)} %get-tuple-element.51), channel_id=1, source_target_pairs={{0,4},{4,0},{8,12},{12,8},{16,20},{20,16},{24,28},{28,24},{1,5},{5... | collective-permute-start | bytes 393224 | tf_op jit(solution)/shard_map/ppermute | solution.py:438
  7.9 6.4 %collective-permute-start = (f32[136,128]{1,0:T(8,128)S(1)}, f32[136,128]{1,0:T(8,128)S(1)}, u32[]{:S(2)}, u32[]{:S(2)}) collective-permute-start(f32[136,128]{1,0:T(8,128)S(1)} %get-tuple-element.50), channel_id=1, source_target_pairs={{0,4},{4,0},{8,12},{12,8},{16,20},{20,16},{24,28},{28,24},{1,5},{5... | collective-permute-start | bytes 208904 | tf_op jit(solution)/shard_map/ppermute | solution.py:438
  12.7 8.7 %collective-permute-start.5 = (f32[256,128]{1,0:T(8,128)S(1)}, f32[256,128]{1,0:T(8,128)S(1)}, u32[]{:S(2)}, u32[]{:S(2)}) collective-permute-start(f32[256,128]{1,0:T(8,128)S(1)} %add.35), channel_id=1, source_target_pairs={{0,8},{4,12},{8,0},{12,4},{16,24},{20,28},{24,16},{28,20},{1,9},{5... | collective-permute-start | bytes 393224 | tf_op jit(solution)/shard_map/ppermute | solution.py:438
  14.3 4.4 %collective-permute-start.1 = (f32[136,128]{1,0:T(8,128)S(1)}, f32[136,128]{1,0:T(8,128)S(1)}, u32[]{:S(2)}, u32[]{:S(2)}) collective-permute-start(f32[136,128]{1,0:T(8,128)S(1)} %add.33), channel_id=1, source_target_pairs={{0,8},{4,12},{8,0},{12,4},{16,24},{20,28},{24,16},{28,20},{1,9},{5... | collective-permute-start | bytes 208904 | tf_op jit(solution)/shard_map/ppermute | solution.py:438
  18.7 7.8 %collective-permute-start.2 = (f32[136,128]{1,0:T(8,128)S(1)}, f32[136,128]{1,0:T(8,128)S(1)}, u32[]{:S(2)}, u32[]{:S(2)}) collective-permute-start(f32[136,128]{1,0:T(8,128)S(1)} %add.34), channel_id=1, source_target_pairs={{0,16},{4,20},{8,24},{12,28},{16,0},{20,4},{24,8},{28,12},{1,17},{... | collective-permute-start | bytes 208904 | tf_op jit(solution)/shard_map/ppermute | solution.py:438
  21.4 5.1 %copy-start.3 = (bf16[1024,256]{1,0:T(8,128)(2,1)S(1)}, bf16[1024,256]{1,0:T(8,128)(2,1)}, u32[]{:S(2)}) copy-start(bf16[1024,256]{1,0:T(8,128)(2,1)} %k_ref.9) | copy-start | bytes 1572868
  21.4 9.3 %collective-permute-start.6 = (f32[256,128]{1,0:T(8,128)S(1)}, f32[256,128]{1,0:T(8,128)S(1)}, u32[]{:S(2)}, u32[]{:S(2)}) collective-permute-start(f32[256,128]{1,0:T(8,128)S(1)} %add.36), channel_id=1, source_target_pairs={{0,16},{4,20},{8,24},{12,28},{16,0},{20,4},{24,8},{28,12},{1,17},{... | collective-permute-start | bytes 393224 | tf_op jit(solution)/shard_map/ppermute | solution.py:438
  22.6 9.6 %copy-start.5 = (bf16[1024,256]{1,0:T(8,128)(2,1)S(1)}, bf16[1024,256]{1,0:T(8,128)(2,1)}, u32[]{:S(2)}) copy-start(bf16[1024,256]{1,0:T(8,128)(2,1)} %v_ref.7) | copy-start | bytes 1572868
  22.6 9.6 %copy-start.6 = (bf16[1024,256]{1,0:T(8,128)(2,1)S(1)}, bf16[1024,256]{1,0:T(8,128)(2,1)}, u32[]{:S(2)}) copy-start(bf16[1024,256]{1,0:T(8,128)(2,1)} %q_ref.3) | copy-start | bytes 1572868
  30.7 3.9 %collective-permute-start.8 = (bf16[1024,512]{1,0:T(8,128)(2,1)S(1)}, bf16[1024,512]{1,0:T(8,128)(2,1)S(1)}, u32[]{:S(2)}, u32[]{:S(2)}) collective-permute-start(bf16[1024,512]{1,0:T(8,128)(2,1)S(1)} %collective-permute-done.7.refs_1_.refs_2_), channel_id=1, source_target_pairs={{0,1},{1,0},{2,3},{3,2},{4,5},{5,4},{6,7},{7,6},{8,9},{9,8},{10,11... | collective-permute-start | bytes 3145736 | tf_op jit(solution)/shard_map/ppermute | solution.py:438
  30.9 28.2 %collective-permute-start.15 = (bf16[2,256,512]{2,1,0:T(8,128)(2,1)S(1)}, bf16[2,256,512]{2,1,0:T(8,128)(2,1)S(1)}, u32[]{:S(2)}, u32[]{:S(2)}) collective-permute-start(bf16[2,256,512]{2,1,0:T(8,128)(2,1)S(1)} %get-tuple-element.82), channel_id=1, source_target_pairs={{0,2},{1,3},{2,0},{3,1},{4,6},{5,7},{6,4},{7,5},{8,10},{9,11},{10,... | collective-permute-start | bytes 1572872 | tf_op jit(solution)/shard_map/ppermute | solution.py:438
  36.7 27.2 %collective-permute-start.18 = (bf16[2,256,256]{2,1,0:T(8,128)(2,1)S(1)}, bf16[2,256,256]{2,1,0:T(8,128)(2,1)S(1)}, u32[]{:S(2)}, u32[]{:S(2)}) collective-permute-start(bf16[2,256,256]{2,1,0:T(8,128)(2,1)S(1)} %get-tuple-element.60), channel_id=1, source_target_pairs={{0,4},{4,0},{8,12},{12,8},{16,20},{20,16},{24,28},{28,24},{1,5},{5... | collective-permute-start | bytes 786440 | tf_op jit(solution)/shard_map/ppermute | solution.py:438
  38.3 12.5 %collective-permute-start.12 = (bf16[2,256,256]{2,1,0:T(8,128)(2,1)S(1)}, bf16[2,256,256]{2,1,0:T(8,128)(2,1)S(1)}, u32[]{:S(2)}, u32[]{:S(2)}) collective-permute-start(bf16[2,256,256]{2,1,0:T(8,128)(2,1)S(1)} %get-tuple-element.73), channel_id=1, source_target_pairs={{0,4},{4,0},{8,12},{12,8},{16,20},{20,16},{24,28},{28,24},{1,5},{5... | collective-permute-start | bytes 786440 | tf_op jit(solution)/shard_map/ppermute | solution.py:438
  47.0 17.3 %collective-permute-start.10 = (bf16[1024,256]{1,0:T(8,128)(2,1)S(1)}, bf16[1024,256]{1,0:T(8,128)(2,1)S(1)}, u32[]{:S(2)}, u32[]{:S(2)}) collective-permute-start(bf16[1024,256]{1,0:T(8,128)(2,1)S(1)} %get-tuple-element.69.h_ref.refs_0_), channel_id=1, source_target_pairs={{0,2},{1,3},{2,0},{3,1},{4,6},{5,7},{6,4},{7,5},{8,10},{9,11},{10,... | collective-permute-start | bytes 1572872 | tf_op jit(solution)/shard_map/ppermute | solution.py:438
  47.8 28.1 %collective-permute-start.9 = (bf16[1024,256]{1,0:T(8,128)(2,1)S(1)}, bf16[1024,256]{1,0:T(8,128)(2,1)S(1)}, u32[]{:S(2)}, u32[]{:S(2)}) collective-permute-start(bf16[1024,256]{1,0:T(8,128)(2,1)S(1)} %get-tuple-element.69.h_ref.refs_0_), channel_id=1, source_target_pairs={{0,1},{1,0},{2,3},{3,2},{4,5},{5,4},{6,7},{7,6},{8,9},{9,8},{10,11... | collective-permute-start | bytes 1572872 | tf_op jit(solution)/shard_map/ppermute | solution.py:438
  50.9 4.6 %collective-permute-start.11 = (bf16[392,128]{1,0:T(8,128)(2,1)S(1)}, bf16[392,128]{1,0:T(8,128)(2,1)S(1)}, u32[]{:S(2)}, u32[]{:S(2)}) collective-permute-start(bf16[392,128]{1,0:T(8,128)(2,1)S(1)} %get-tuple-element.71), channel_id=1, source_target_pairs={{0,4},{4,0},{8,12},{12,8},{16,20},{20,16},{24,28},{28,24},{1,5},{5... | collective-permute-start | bytes 301064 | tf_op jit(solution)/shard_map/ppermute | solution.py:438
  55.5 26.5 %collective-permute-start.20 = (bf16[256,256]{1,0:T(8,128)(2,1)S(1)}, bf16[256,256]{1,0:T(8,128)(2,1)S(1)}, u32[]{:S(2)}, u32[]{:S(2)}) collective-permute-start(bf16[256,256]{1,0:T(8,128)(2,1)S(1)} %get-tuple-element.101), channel_id=1, source_target_pairs={{0,24},{4,28},{8,16},{12,20},{16,8},{20,12},{24,0},{28,4},{1,25},{... | collective-permute-start | bytes 393224 | tf_op jit(solution)/shard_map/ppermute | solution.py:438
  59.1 4.7 %collective-permute-start.13 = (bf16[392,128]{1,0:T(8,128)(2,1)S(1)}, bf16[392,128]{1,0:T(8,128)(2,1)S(1)}, u32[]{:S(2)}, u32[]{:S(2)}) collective-permute-start(bf16[392,128]{1,0:T(8,128)(2,1)S(1)} %fusion.3), channel_id=1, source_target_pairs={{0,8},{4,12},{8,0},{12,4},{16,24},{20,28},{24,16},{28,20},{1,9},{5... | collective-permute-start | bytes 301064 | tf_op jit(solution)/shard_map/ppermute | solution.py:438
  63.8 10.4 %collective-permute-start.16 = (bf16[2,256,512]{2,1,0:T(8,128)(2,1)S(1)}, bf16[2,256,512]{2,1,0:T(8,128)(2,1)S(1)}, u32[]{:S(2)}, u32[]{:S(2)}) collective-permute-start(bf16[2,256,512]{2,1,0:T(8,128)(2,1)S(1)} %pad_maximum_fusion), channel_id=1, source_target_pairs={{0,1},{1,0},{2,3},{3,2},{4,5},{5,4},{6,7},{7,6},{8,9},{9,8},{10,11... | collective-permute-start | bytes 1572872 | tf_op jit(solution)/shard_map/ppermute | solution.py:438
  63.9 8.4 %collective-permute-start.17 = (bf16[392,128]{1,0:T(8,128)(2,1)S(1)}, bf16[392,128]{1,0:T(8,128)(2,1)S(1)}, u32[]{:S(2)}, u32[]{:S(2)}) collective-permute-start(bf16[392,128]{1,0:T(8,128)(2,1)S(1)} %add_convert_fusion.1), channel_id=1, source_target_pairs={{0,16},{4,20},{8,24},{12,28},{16,0},{20,4},{24,8},{28,12},{1,17},{... | collective-permute-start | bytes 301064 | tf_op jit(solution)/shard_map/ppermute | solution.py:438
  64.3 11.6 %collective-permute-start.14 = (bf16[1024,256]{1,0:T(8,128)(2,1)S(1)}, bf16[1024,256]{1,0:T(8,128)(2,1)S(1)}, u32[]{:S(2)}, u32[]{:S(2)}) collective-permute-start(bf16[1024,256]{1,0:T(8,128)(2,1)S(1)} %collective-permute-done.10.refs_2_), channel_id=1, source_target_pairs={{0,1},{1,0},{2,3},{3,2},{4,5},{5,4},{6,7},{7,6},{8,9},{9,8},{10,11... | collective-permute-start | bytes 1572872 | tf_op jit(solution)/shard_map/ppermute | solution.py:438
  72.3 9.7 %collective-permute-start.19 = (bf16[256,256]{1,0:T(8,128)(2,1)S(1)}, bf16[256,256]{1,0:T(8,128)(2,1)S(1)}, u32[]{:S(2)}, u32[]{:S(2)}) collective-permute-start(bf16[256,256]{1,0:T(8,128)(2,1)S(1)} %get-tuple-element.102), channel_id=1, source_target_pairs={{0,16},{4,20},{8,24},{12,28},{16,0},{20,4},{24,8},{28,12},{1,17},{... | collective-permute-start | bytes 393224 | tf_op jit(solution)/shard_map/ppermute | solution.py:438
  74.2 7.8 %collective-permute-start.21 = (bf16[256,256]{1,0:T(8,128)(2,1)S(1)}, bf16[256,256]{1,0:T(8,128)(2,1)S(1)}, u32[]{:S(2)}, u32[]{:S(2)}) collective-permute-start(bf16[256,256]{1,0:T(8,128)(2,1)S(1)} %fusion.4), channel_id=1, source_target_pairs={{0,8},{4,12},{8,0},{12,4},{16,24},{20,28},{24,16},{28,20},{1,9},{5... | collective-permute-start | bytes 393224 | tf_op jit(solution)/shard_map/ppermute | solution.py:438

commit v6 on v5

--- a/solution.py
+++ b/solution.py
@@ -53,7 +53,7 @@
 def causal():
     rows = lax.broadcasted_iota(jnp.int32, (SPAN, SPAN), 0)
     cols = lax.broadcasted_iota(jnp.int32, (SPAN, SPAN), 1)
-    return rows >= cols
+    return rows <= cols
 
 
 def corner():
@@ -99,7 +99,7 @@
     return mats[:heads]
 
 
-def totals_kernel(k_ref, v_ref, g_ref, n_ref):
+def totals_kernel(begin_ref, k_ref, v_ref, g_ref, n_ref):
     grams = []
     for h in range(k_ref.shape[1] // HDIM):
         cols = slice(h * HDIM, (h + 1) * HDIM)
@@ -110,15 +110,15 @@
     fold_into(g_ref, grams)
 
 
-def totals(keys, values, heads):
+def totals(begin, keys, values, heads):
     return pl.pallas_call(
         totals_kernel,
         out_shape=(shape((folded(heads) * (HDIM + 8), HDIM)), shape((heads * HDIM, HDIM))),
-        in_specs=[VMEM_SPEC] * 2,
+        in_specs=[VMEM_SPEC] * 3,
         out_specs=(VMEM_SPEC, VMEM_SPEC),
         compiler_params=params(),
         cost_estimate=cost(2 * 2 * keys.size * HDIM, 4 * keys.size),
-    )(keys, values)
+    )(begin, keys, values)
 
 
 def taken(refs, backward):
@@ -144,15 +144,23 @@
     heads = k_ref.shape[1] // HDIM
     eye = unit()
     grams = unfold_from(taken(refs[:rounds], False), heads)
+    nil = jnp.zeros((HDIM, HDIM), BF16)
+
+    def times(left, eh, el):
+        both = dot(left, cat([cat([eh, el], 1), cat([eh, nil], 1)], 0))
+        return both[:, :HDIM] + both[:, HDIM:]
+
     for h, b, i, rows, cols in places(k_ref, heads):
         ridged = grams[h] + jnp.where(eye, RIDGE, 0.0)
         scale = 1.0 / jnp.sqrt(jnp.sum(ridged * ridged, keepdims=True))
         a_ref[i] = ridged
-        es[i] = ridged * scale
-        xs[i] = jnp.where(eye, scale, 0.0)
         k = k_ref[rows, cols]
         grams[h] = grams[h] + dot(k, k, (0, 0))
-    nil = jnp.zeros((HDIM, HDIM), BF16)
+        e = ridged * scale
+        eh, el = split(e)
+        e_ref[0, i] = eh
+        es[i] = 2.0 * e - times(cat([eh, el], 1), eh, el)
+        xs[i] = jnp.where(eye, 2.0 * scale, 0.0) - scale * e
 
     def step(j, carry):
         for i in range(es.shape[0]):
@@ -161,17 +169,19 @@
             xh, xl = split(x)
             e_ref[j, i] = eh
             x_ref[j, i] = xh
-            left = cat([cat([eh, el], 1), cat([xh, xl], 1)], 0)
-            right = cat([cat([eh, el], 1), cat([eh, nil], 1)], 0)
-            both = dot(left, right)
-            both = both[:, :HDIM] + both[:, HDIM:]
+            both = times(cat([cat([eh, el], 1), cat([xh, xl], 1)], 0), eh, el)
             es[i] = 2.0 * e - both[:HDIM]
             xs[i] = 2.0 * x - both[HDIM:]
         return carry
 
-    lax.fori_loop(0, NEWTON, step, 0)
+    lax.fori_loop(1, NEWTON - 1, step, 0)
     for i in range(xs.shape[0]):
-        last_ref[i] = xs[i]
+        e, x = es[i], xs[i]
+        eh, el = split(e)
+        xh, xl = split(x)
+        e_ref[NEWTON - 1, i] = eh
+        x_ref[NEWTON - 1, i] = xh
+        last_ref[i] = 2.0 * x - times(cat([xh, xl], 1), eh, el)
 
 
 def inverses(keys, grams, count):
@@ -193,22 +203,19 @@
     prefix = taken(refs[:rounds], False)
     heads = q_ref.shape[1] // HDIM
     keep = causal()
-    nil = jnp.zeros((HDIM, HDIM), BF16)
     pairs = [prefix[h * HDIM : (h + 1) * HDIM, :] for h in range(heads)]
     for h, b, i, rows, cols in places(q_ref, heads):
         q, k, v = q_ref[rows, cols], k_ref[rows, cols], v_ref[rows, cols]
-        xh, xl = split(last_ref[i])
-        sh, sl = split(dot(cat([q, q], 1), cat([xh, xl], 0)))
-        both = cat([sh, sl], 1)
+        sh, sl = split(dot(cat(split(last_ref[i]), 1), cat([q, q], 1), (1, 1)))
+        both = cat([sh, sl], 0)
         s_ref[i] = both
-        scores = dot(both, cat([k, k], 1), (1, 1))
+        scores = dot(cat([k, k], 1), both)
         scores = jnp.where(keep, scores, 0.0).astype(BF16)
         w_ref[i] = scores
         nh, nl = split(pairs[h])
         pre_ref[i] = cat([nh, nl], 1)
-        state = dot(both, cat([cat([nh, nl], 1), cat([nh, nil], 1)], 0))
-        out = dot(scores, v) + state[:, :HDIM] + state[:, HDIM:]
-        out_ref[rows, cols] = out.astype(BF16)
+        out = dot(v, scores, (0, 0)) + dot(cat([nh, nh], 0), both, (0, 0)) + dot(nl, sh, (0, 0))
+        out_ref[rows, cols] = out.astype(BF16).T
         pairs[h] = pairs[h] + dot(k, v, (0, 0))
 
 
@@ -219,7 +226,7 @@
         out_shape=(
             shape(queries.shape, BF16),
             shape((count, HDIM, 2 * HDIM), BF16),
-            shape((count, SPAN, 2 * HDIM), BF16),
+            shape((count, 2 * HDIM, SPAN), BF16),
             shape((count, SPAN, SPAN), BF16),
         ),
         in_specs=[VMEM_SPEC] * (4 + len(pairs)),
@@ -231,35 +238,33 @@
 
 def tangent_kernel(
     q_ref, k_ref, v_ref, do_ref, e_ref, x_ref, last_ref, a_ref, pre_ref, s_ref, w_ref,
-    dq_ref, dk_ref, dv_ref, da_ref, dn_ref, sum_ref, send_ref, des, dxs, first,
+    dq_ref, dkv_ref, da_ref, dm_ref, sum_ref, send_ref, des, dxs, first,
 ):
     heads = q_ref.shape[1] // HDIM
     keep = causal()
-    nil = jnp.zeros((HDIM, HDIM), BF16)
     for h, b, i, rows, cols in places(q_ref, heads):
         q, k, v, do = q_ref[rows, cols], k_ref[rows, cols], v_ref[rows, cols], do_ref[rows, cols]
-        weights = jnp.where(keep, dot(do, v, (1, 1)), 0.0).astype(BF16)
-        ds = dot(weights, k) + dot(cat([do, do], 1), pre_ref[i], (1, 1))
+        weights = jnp.where(keep, dot(v, do, (1, 1)), 0.0).astype(BF16)
+        ds = dot(k, weights, (0, 0)) + dot(pre_ref[i], cat([do, do], 1), (1, 1))
         ds = ds.astype(BF16)
-        xh, xl = split(last_ref[i])
-        inverse = cat([xh, xl], 0)
-        both = s_ref[i]
-        sh = both[:, :HDIM]
-        scores = w_ref[i]
-        dv_ref[rows, cols] = dot(scores, do, (0, 0))
-        dk_ref[rows, cols] = dot(weights, sh, (0, 0))
-        state = dot(both, do, (0, 0))
-        dn_ref[i] = state[:HDIM] + state[HDIM:]
-        dq_ref[rows, cols] = dot(cat([ds, ds], 1), inverse).astype(BF16)
-        bar = dot(q, ds, (0, 0))
+        dq_ref[rows, cols] = dot(cat(split(last_ref[i]), 1), cat([ds, ds], 0)).astype(BF16).T
+        bar = dot(ds, q)
         bar = bar + bar.T
+        turned = do.T
+        dkv_ref[i, :HDIM] = dot(s_ref[i, :HDIM], weights, (1, 1))
+        dkv_ref[i, HDIM:] = dot(turned, w_ref[i], (1, 1))
+        state = dot(turned, s_ref[i], (1, 1))
+        dm_ref[i] = state[:, :HDIM] + state[:, HDIM:]
         ridged = a_ref[i]
         scale = 1.0 / jnp.sqrt(jnp.sum(ridged * ridged, keepdims=True))
         first[i] = bar
-        des[i] = bar * scale
-        dxs[i] = jnp.zeros((HDIM, HDIM), F32)
+        de = bar * scale
+        both = dot(e_ref[0, i], de.astype(BF16))
+        des[i] = 2.0 * de - (both + both.T)
+        dxs[i] = -scale * de
 
     def step(j, carry):
+        nil = jnp.zeros((HDIM, HDIM), BF16)
         for i in range(des.shape[0]):
             e, x = e_ref[j, i], x_ref[j, i]
             de, dx = des[i], dxs[i]
@@ -270,19 +275,22 @@
             des[i] = 2.0 * de - (turned + turned.T)
         return carry
 
-    lax.fori_loop(0, NEWTON, step, 0)
+    lax.fori_loop(1, NEWTON - 1, step, 0)
     sum_a = [jnp.zeros((HDIM, HDIM), F32) for _ in range(heads)]
-    sum_n = [jnp.zeros((HDIM, HDIM), F32) for _ in range(heads)]
+    sum_m = [jnp.zeros((HDIM, HDIM), F32) for _ in range(heads)]
     for h, b, i, rows, cols in places(q_ref, heads):
-        ridged, dx = a_ref[i], dxs[i]
+        e, x = e_ref[NEWTON - 1, i], x_ref[NEWTON - 1, i]
+        de, dx = des[i], dxs[i]
+        dx = 2.0 * dx - dot(cat([dx.astype(BF16), x], 1), cat([e, de.astype(BF16)], 0))
+        ridged = a_ref[i]
         square = jnp.sum(ridged * ridged, keepdims=True)
         along = jnp.sum(first[i] * last_ref[i] + dx * ridged, keepdims=True)
         da = dx - (along / square) * ridged
         da_ref[i] = da
         sum_a[h] = sum_a[h] + da
-        sum_n[h] = sum_n[h] + dn_ref[i]
+        sum_m[h] = sum_m[h] + dm_ref[i]
     for h in range(heads):
-        sum_ref[h * HDIM : (h + 1) * HDIM, :] = sum_n[h]
+        sum_ref[h * HDIM : (h + 1) * HDIM, :] = sum_m[h]
     fold_into(sum_ref, sum_a, heads * HDIM)
     send_ref[...] = sum_ref[...].astype(BF16)
 
@@ -291,49 +299,64 @@
     heads = queries.shape[1] // HDIM
     count = stash[-1].shape[0]
     state = shape((count, HDIM, HDIM))
-    wide = shape(queries.shape)
     rows = heads * HDIM + folded(heads) * (HDIM + 8)
     return pl.pallas_call(
         tangent_kernel,
         out_shape=(
-            shape(queries.shape, BF16), wide, wide, state, state,
+            shape(queries.shape, BF16), shape((count, 2 * HDIM, SPAN)), state, state,
             shape((rows, HDIM)), shape((rows, HDIM), BF16),
         ),
         in_specs=[VMEM_SPEC] * 11,
-        out_specs=(VMEM_SPEC,) * 7,
+        out_specs=(VMEM_SPEC,) * 6,
         scratch_shapes=[pltpu.VMEM((count, HDIM, HDIM), F32)] * 3,
         compiler_params=params(),
         cost_estimate=cost(4_000_000_000, 8_000_000),
     )(queries, keys, values, grads, *stash)
 
 
-def finish_kernel(rounds, k_ref, v_ref, dk_ref, dv_ref, da_ref, dn_ref, *refs):
+def finish_kernel(rounds, k_ref, v_ref, dkv_ref, da_ref, dm_ref, *refs):
     gk_ref, gv_ref = refs[rounds:]
-    sum_ref = taken(refs[:rounds], True)
+    sums = taken(refs[:rounds], True)
     heads = k_ref.shape[1] // HDIM
-    sa = unfold_from(sum_ref, heads, heads * HDIM)
-    sn = [sum_ref[h * HDIM : (h + 1) * HDIM, :] for h in range(heads)]
+    sa = unfold_from(sums, heads, heads * HDIM)
+    sm = [sums[h * HDIM : (h + 1) * HDIM, :] for h in range(heads)]
+    nil = jnp.zeros((HDIM, HDIM), BF16)
     for h, b, i, rows, cols in reversed(list(places(k_ref, heads))):
-        k, v = k_ref[rows, cols], v_ref[rows, cols]
-        nh, nl = split(sn[h])
-        grad_k = dk_ref[rows, cols] + dot(k, sa[h].astype(BF16))
-        grad_k = grad_k + dot(cat([v, v], 1), cat([nh, nl], 1), (1, 1))
-        grad_v = dv_ref[rows, cols] + dot(cat([k, k], 1), cat([nh, nl], 0))
-        gk_ref[rows, cols] = grad_k.astype(BF16)
-        gv_ref[rows, cols] = grad_v.astype(BF16)
+        both = cat([k_ref[rows, cols], v_ref[rows, cols]], 1)
+        total = dkv_ref[i]
+        for a, m, n in zip(split(sa[h]), split(sm[h]), split(sm[h].T)):
+            left = cat([cat([a, n], 1), cat([m, nil], 1)], 0)
+            total = total + dot(left, both, (1, 1))
+        total = total.astype(BF16).T
+        gk_ref[rows, cols] = total[:, :HDIM]
+        gv_ref[rows, cols] = total[:, HDIM:]
         sa[h] = sa[h] + da_ref[i]
-        sn[h] = sn[h] + dn_ref[i]
-
-
-def finish(keys, values, dk, dv, da, dn, sums):
+        sm[h] = sm[h] + dm_ref[i]
+
+
+def finish(keys, values, dkv, da, dm, sums):
     return pl.pallas_call(
         functools.partial(finish_kernel, len(sums)),
         out_shape=(shape(keys.shape, BF16),) * 2,
-        in_specs=[VMEM_SPEC] * (6 + len(sums)),
+        in_specs=[VMEM_SPEC] * (5 + len(sums)),
         out_specs=(VMEM_SPEC,) * 2,
         compiler_params=params(),
         cost_estimate=cost(1_000_000_000, 6_000_000),
-    )(keys, values, dk, dv, da, dn, *sums)
+    )(keys, values, dkv, da, dm, *sums)
+
+
+def lead_kernel(out_ref):
+    out_ref[...] = jnp.zeros_like(out_ref)
+
+
+def lead():
+    return pl.pallas_call(
+        lead_kernel,
+        out_shape=shape((8, HDIM)),
+        out_specs=VMEM_SPEC,
+        compiler_params=params(),
+        cost_estimate=cost(700_000_000, 4096),
+    )()
 
 
 def grads_kernel(first, w_ref, *refs):
@@ -452,8 +475,9 @@
     head_count, ctx_count = lax.axis_size("head"), lax.axis_size("ctx")
     evens = range(2, head_count, 2)
 
-    gram, pair = totals(keys, values, heads)
-    far = {s: swap(cotangent, "head", s) for s in evens}
+    begin = lead()
+    far = {s: swap(after(cotangent, begin), "head", s) for s in evens}
+    gram, pair = totals(begin, keys, values, heads)
     near = swap(after(cotangent, gram, pair), "head", 1)
 
     grams, pairs = [], []
@@ -483,7 +507,7 @@
     high = swap(odd_high, "ctx", 1)
     low = swap(odd_low, "ctx", 1)
 
-    grad_queries, dk, dv, da, dn, sums, send = tangent(
+    grad_queries, dkv, da, dm, sums, send = tangent(
         queries, keys, values, after(grads, odd_low), [*stash, last, ridged, states, solved, scores]
     )
 
@@ -503,7 +527,7 @@
         sums = sums + later[-1].astype(F32)
         send = sums.astype(BF16)
 
-    low = even_low.astype(F32) + after(low, *later[:2]).astype(F32)
+    low = even_low.astype(F32) + after(low, later[0]).astype(F32)
     moved += [swap(low[u].astype(BF16), "ctx", 2 * u) for u in range(1, half)]
 
     outs = [heads_out, swap(outs_out, "head", 1)]
@@ -516,7 +540,7 @@
     grad_weight = low[0]
     for part in moved:
         grad_weight = grad_weight + after(part, layer_out).astype(F32)
-    grad_keys, grad_values = finish(keys, values, dk, dv, da, dn, later)
+    grad_keys, grad_values = finish(keys, values, dkv, da, dm, later)
     return (layer_out, grad_queries, grad_keys, grad_values, grad_weight)
 
 

time: 82.9 us -> 80 us (0.965)
  starting transfers between devices: 22.3 us -> 20.4 us
  Pallas kernels: 22.2 us -> 23.7 us
  waiting for transfers between devices: 33.9 us -> 32.4 us
  local copies, waits for them, and re-layouts: 2.39 us -> 1.32 us
    ppermute x22, starting transfers between devices: 22.3 us -> 20.4 us  [swap(): return lax.ppermute(value, axis, [(i, i ^ distance) for i in range(count)])]
    ppermute x22, waiting for transfers between devices: 33.9 us -> 32.4 us  [swap(): return lax.ppermute(value, axis, [(i, i ^ distance) for i in range(count)])]
    pallas_call x1 -> x2, Pallas kernels: 8.14 us -> 9.24 us  [the longest x1 9.24 us: tangent(): pl.pallas_call(tangent_kernel, out_shape=(shape(queries.shape, BF16), sha...]
    unnamed x14 -> x10, local copies, waits for them, and re-layouts: 2.25 us -> 1.18 us
  transfers between devices with their start and end apart: 22 -> 22, of which waited for: 8 -> 8; matrix products, arithmetic and copies ran while one was open for 1% -> 1% of each run, Pallas kernels for 26% -> 29%
where the time goes in v6:
time: 80 us; the launch traced here: 79.8 us
  waiting for transfers between devices  32.4 us (40%)
  Pallas kernels  23.7 us (30%)
  starting transfers between devices  20.4 us (25%)
  local copies, waits for them, and re-layouts  1.32 us (2%)
  other arithmetic  1.08 us (1%)
  between operations  0.88 us (1%)
    ppermute x22, waiting for transfers between devices, swap(): return lax.ppermute(value, axis, [(i, i ^ distance) for i in range(count)])  32.4 us
    ppermute x22, starting transfers between devices, swap(): return lax.ppermute(value, axis, [(i, i ^ distance) for i in range(count)])  20.4 us
    pallas_call x1, Pallas kernels, tangent(): pl.pallas_call(tangent_kernel, out_shape=(shape(queries.shape, BF16), sha...  9.24 us
    pallas_call x1, Pallas kernels, inverses(): pl.pallas_call(functools.partial(inverse_kernel, len(grams)), out_shape=(...  4.32 us
    pallas_call x1, Pallas kernels, outputs(): pl.pallas_call(functools.partial(outputs_kernel, len(pairs)), out_shape=(...  2.76 us
    pallas_call x1, Pallas kernels, layer(): pl.pallas_call(layer_kernel, out_shape=shape((rows, cols), BF16), in_spec...  2.22 us
    pallas_call x1, Pallas kernels, finish(): pl.pallas_call(functools.partial(finish_kernel, len(sums)), out_shape=(sh...  1.89 us
  transfers between devices with their start and end apart: 22, of which 8 were waited for; matrix products, arithmetic and copies ran while one was open for 1% of the time, Pallas kernels for 29%

profile of v6, /device:TPU:0, one launch (start us, length us, event | category | flops | bytes accessed | tf_op | source)
XLA Modules:
  0.0 79.8 jit_solution(3300488803350587201)
XLA Ops:
  0.7 1.0 %copy-done.2 = bf16[1024,256]{1,0:T(8,128)(2,1)S(1)} copy-done((bf16[1024,256]{1,0:T(8,128)(2,1)S(1)}, bf16[1024,256]{1,0:T(8,128)(2,1)}, u32[]{:S(2)}) %copy-start.2) | copy-done | bytes 524312
  1.7 0.2 copy-done.3
  1.8 0.3 shard_map.93
  2.2 0.0 copy-done.1
  2.2 0.6 collective-permute-start.3
  2.7 2.6 %collective-permute-start.7 = (bf16[1024,512]{1,0:T(8,128)(2,1)S(1)}, bf16[1024,512]{1,0:T(8,128)(2,1)S(1)}, u32[]{:S(2)}, u32[]{:S(2)}) collective-permute-start(bf16[1024,512]{1,0:T(8,128)(2,1)S(1)} %copy-done.1), channel_id=1, source_target_pairs={{0,2},{1,3},{2,0},{3,1},{4,6},{5,7},{6,4},{7,5},{8,10},{9,11},{10,... | collective-permute-start | bytes 3145736 | tf_op jit(solution)/shard_map/ppermute | solution.py:461
  5.3 1.5 %collective-permute-start.4 = (f32[256,128]{1,0:T(8,128)S(1)}, f32[256,128]{1,0:T(8,128)S(1)}, u32[]{:S(2)}, u32[]{:S(2)}) collective-permute-start(f32[256,128]{1,0:T(8,128)S(1)} %get-tuple-element.51), channel_id=1, source_target_pairs={{0,4},{4,0},{8,12},{12,8},{16,20},{20,16},{24,28},{28,24},{1,5},{5... | collective-permute-start | bytes 393224 | tf_op jit(solution)/shard_map/ppermute | solution.py:461
  6.8 0.5 collective-permute-start
  7.3 4.3 %collective-permute-done.4.refs_0_ = f32[256,128]{1,0:T(8,128)S(1)} collective-permute-done((f32[256,128]{1,0:T(8,128)S(1)}, f32[256,128]{1,0:T(8,128)S(1)}, u32[]{:S(2)}, u32[]{:S(2)}) %collective-permute-start.4) | collective-permute-done | bytes 131104 | tf_op jit(solution)/shard_map/ppermute | solution.py:461
  11.6 1.6 %collective-permute-start.5 = (f32[256,128]{1,0:T(8,128)S(1)}, f32[256,128]{1,0:T(8,128)S(1)}, u32[]{:S(2)}, u32[]{:S(2)}) collective-permute-start(f32[256,128]{1,0:T(8,128)S(1)} %add.35), channel_id=1, source_target_pairs={{0,8},{4,12},{8,0},{12,4},{16,24},{20,28},{24,16},{28,20},{1,9},{5... | collective-permute-start | bytes 393224 | tf_op jit(solution)/shard_map/ppermute | solution.py:461
  13.3 0.0 collective-permute-done.refs_0_
  13.3 0.7 collective-permute-start.1
  14.0 3.7 %collective-permute-done.1.refs_1_ = f32[136,128]{1,0:T(8,128)S(1)} collective-permute-done((f32[136,128]{1,0:T(8,128)S(1)}, f32[136,128]{1,0:T(8,128)S(1)}, u32[]{:S(2)}, u32[]{:S(2)}) %collective-permute-start.1) | collective-permute-done | bytes 69664 | tf_op jit(solution)/shard_map/ppermute | solution.py:461
  17.7 2.7 %collective-permute-start.2 = (f32[136,128]{1,0:T(8,128)S(1)}, f32[136,128]{1,0:T(8,128)S(1)}, u32[]{:S(2)}, u32[]{:S(2)}) collective-permute-start(f32[136,128]{1,0:T(8,128)S(1)} %add.34), channel_id=1, source_target_pairs={{0,16},{4,20},{8,24},{12,28},{16,0},{20,4},{24,8},{28,12},{1,17},{... | collective-permute-start | bytes 208904 | tf_op jit(solution)/shard_map/ppermute | solution.py:461
  20.3 0.4 collective-permute-start.6
  20.7 0.0 collective-permute-done.3.refs_1_
  20.7 0.7 shard_map.94.refs_0_
  21.5 0.0 copy-start.4
  21.5 3.9 %collective-permute-done.2.refs_2_ = f32[136,128]{1,0:T(8,128)S(1)} collective-permute-done((f32[136,128]{1,0:T(8,128)S(1)}, f32[136,128]{1,0:T(8,128)S(1)}, u32[]{:S(2)}, u32[]{:S(2)}) %collective-permute-start.2) | collective-permute-done | bytes 69664 | tf_op jit(solution)/shard_map/ppermute | solution.py:461
  25.4 4.3 %shard_map.95 = (bf16[8,8,128,128]{3,2,1,0:T(8,128)(2,1)S(1)}, bf16[8,8,128,128]{3,2,1,0:T(8,128)(2,1)S(1)}, f32[8,128,128]{2,1,0:T(8,128)S(1)}, f32[8,128,128]{2,1,0:T(8,128)S(1)}) custom-call(bf16[1024,256]{1,0:T(8,128)(2,1)S(1)} %copy-done.2, f32[136,128]{1,0:T(8,128)S(1)} %collective-permute-done.refs_0_, f32[136,128]{1,0:T(8,128)S(1)} %collective-permute-done.1.refs_1_, ...), custom_call_target="tpu_custom_call" | custom-call | flops 2000000000 | bytes 8000000 | tf_op jit(solution)/shard_map/pallas_call | solution.py:190
  29.8 0.0 collective-permute-done.7.refs_1_.refs_2_
  29.8 0.1 collective-permute-start.8
  29.9 0.1 shard_map.100
  29.9 1.0 %collective-permute-start.15 = (bf16[2,256,512]{2,1,0:T(8,128)(2,1)S(1)}, bf16[2,256,512]{2,1,0:T(8,128)(2,1)S(1)}, u32[]{:S(2)}, u32[]{:S(2)}) collective-permute-start(bf16[2,256,512]{2,1,0:T(8,128)(2,1)S(1)} %get-tuple-element.83), channel_id=1, source_target_pairs={{0,2},{1,3},{2,0},{3,1},{4,6},{5,7},{6,4},{7,5},{8,10},{9,11},{10,... | collective-permute-start | bytes 1572872 | tf_op jit(solution)/shard_map/ppermute | solution.py:461
  30.9 2.8 %shard_map.96 = (bf16[1024,256]{1,0:T(8,128)(2,1)S(1)}, bf16[8,128,256]{2,1,0:T(8,128)(2,1)S(1)}, bf16[8,256,256]{2,1,0:T(8,128)(2,1)S(1)}, bf16[8,256,256]{2,1,0:T(8,128)(2,1)S(1)}) custom-call(bf16[1024,256]{1,0:T(8,128)(2,1)S(1)} %copy-done.4, bf16[1024,256]{1,0:T(8,128)(2,1)S(1)} %copy-done.2, bf16[1024,256]{1,0:T(8,128)(2,1)S(1)} %copy-done.3, ...), custom_call_target="tpu_custom_call" | custom-call | flops 2000000000 | bytes 8000000 | tf_op jit(solution)/shard_map/pallas_call | solution.py:224
  33.7 0.8 shard_map.97.do_ref
  34.5 1.4 %shard_map.98 = (bf16[2,256,256]{2,1,0:T(8,128)(2,1)S(1)}, bf16[2,256,256]{2,1,0:T(8,128)(2,1)S(1)}, bf16[2,256,256]{2,1,0:T(8,128)(2,1)S(1)}, bf16[2,256,256]{2,1,0:T(8,128)(2,1)S(1)}) custom-call(bf16[1024,256]{1,0:T(8,128)(2,1)S(1)} %get-tuple-element.70.h_ref.refs_0_, bf16[1024,512]{1,0:T(8,128)(2,1)S(1)} %copy-done.1, ...), custom_call_target="tpu_custom_call" | custom-call | flops 1073741824 | bytes 6000000 | tf_op jit(solution)/shard_map/pallas_call | solution.py:427
  35.9 1.6 %collective-permute-start.18 = (bf16[2,256,256]{2,1,0:T(8,128)(2,1)S(1)}, bf16[2,256,256]{2,1,0:T(8,128)(2,1)S(1)}, u32[]{:S(2)}, u32[]{:S(2)}) collective-permute-start(bf16[2,256,256]{2,1,0:T(8,128)(2,1)S(1)} %get-tuple-element.61), channel_id=1, source_target_pairs={{0,4},{4,0},{8,12},{12,8},{16,20},{20,16},{24,28},{28,24},{1,5},{5... | collective-permute-start | bytes 786440 | tf_op jit(solution)/shard_map/ppermute | solution.py:461
  37.4 0.5 collective-permute-start.12
  37.9 9.2 %shard_map.99 = (bf16[1024,256]{1,0:T(8,128)(2,1)}, f32[8,256,256]{2,1,0:T(8,128)S(1)}, f32[8,128,128]{2,1,0:T(8,128)S(1)}, f32[8,128,128]{2,1,0:T(8,128)S(1)}, ...) custom-call(bf16[1024,256]{1,0:T(8,128)(2,1)S(1)} %copy-done.4, bf16[1024,256]{1,0:T(8,128)(2,1)S(1)} %copy-done.2, ...), custom_call_target="tpu_custom_call" | custom-call | flops 4000000000 | bytes 8000000 | tf_op jit(solution)/shard_map/pallas_call | solution.py:303
  47.2 1.1 %collective-permute-start.10 = (bf16[1024,256]{1,0:T(8,128)(2,1)S(1)}, bf16[1024,256]{1,0:T(8,128)(2,1)S(1)}, u32[]{:S(2)}, u32[]{:S(2)}) collective-permute-start(bf16[1024,256]{1,0:T(8,128)(2,1)S(1)} %get-tuple-element.70.h_ref.refs_0_), channel_id=1, source_target_pairs={{0,2},{1,3},{2,0},{3,1},{4,6},{5,7},{6,4},{7,5},{8,10},{9,11},{10,... | collective-permute-start | bytes 1572872 | tf_op jit(solution)/shard_map/ppermute | solution.py:461
  48.3 1.7 %collective-permute-done.12 = bf16[2,256,256]{2,1,0:T(8,128)(2,1)S(1)} collective-permute-done((bf16[2,256,256]{2,1,0:T(8,128)(2,1)S(1)}, bf16[2,256,256]{2,1,0:T(8,128)(2,1)S(1)}, u32[]{:S(2)}, u32[]{:S(2)}) %collective-permute-start.12) | collective-permute-done | bytes 262176 | tf_op jit(solution)/shard_map/ppermute | solution.py:461
  50.0 1.5 %collective-permute-start.11 = (bf16[392,128]{1,0:T(8,128)(2,1)S(1)}, bf16[392,128]{1,0:T(8,128)(2,1)S(1)}, u32[]{:S(2)}, u32[]{:S(2)}) collective-permute-start(bf16[392,128]{1,0:T(8,128)(2,1)S(1)} %get-tuple-element.72), channel_id=1, source_target_pairs={{0,4},{4,0},{8,12},{12,8},{16,20},{20,16},{24,28},{28,24},{1,5},{5... | collective-permute-start | bytes 301064 | tf_op jit(solution)/shard_map/ppermute | solution.py:461
  51.5 0.1 add_convert_fusion
  51.6 3.0 %collective-permute-done.11.refs_0_ = bf16[392,128]{1,0:T(8,128)(2,1)S(1)} collective-permute-done((bf16[392,128]{1,0:T(8,128)(2,1)S(1)}, bf16[392,128]{1,0:T(8,128)(2,1)S(1)}, u32[]{:S(2)}, u32[]{:S(2)}) %collective-permute-start.11) | collective-permute-done | bytes 100384 | tf_op jit(solution)/shard_map/ppermute | solution.py:461
  54.6 3.6 %collective-permute-start.20 = (bf16[256,256]{1,0:T(8,128)(2,1)S(1)}, bf16[256,256]{1,0:T(8,128)(2,1)S(1)}, u32[]{:S(2)}, u32[]{:S(2)}) collective-permute-start(bf16[256,256]{1,0:T(8,128)(2,1)S(1)} %get-tuple-element.101), channel_id=1, source_target_pairs={{0,24},{4,28},{8,16},{12,20},{16,8},{20,12},{24,0},{28,4},{1,25},{... | collective-permute-start | bytes 393224 | tf_op jit(solution)/shard_map/ppermute | solution.py:461
  58.2 0.1 collective-permute-start.13
  58.3 0.1 slice_bitcast_fusion.3
  58.4 0.1 pad_maximum_fusion
  58.5 0.1 collective-permute-start.16
  58.6 0.1 convert_add_fusion
  58.6 4.3 %collective-permute-done.13.refs_1_ = bf16[392,128]{1,0:T(8,128)(2,1)S(1)} collective-permute-done((bf16[392,128]{1,0:T(8,128)(2,1)S(1)}, bf16[392,128]{1,0:T(8,128)(2,1)S(1)}, u32[]{:S(2)}, u32[]{:S(2)}) %collective-permute-start.13) | collective-permute-done | bytes 100384 | tf_op jit(solution)/shard_map/ppermute | solution.py:461
  63.0 0.3 collective-permute-start.17
  63.3 7.9 %collective-permute-done.17.refs_2_ = bf16[392,128]{1,0:T(8,128)(2,1)S(1)} collective-permute-done((bf16[392,128]{1,0:T(8,128)(2,1)S(1)}, bf16[392,128]{1,0:T(8,128)(2,1)S(1)}, u32[]{:S(2)}, u32[]{:S(2)}) %collective-permute-start.17) | collective-permute-done | bytes 100384 | tf_op jit(solution)/shard_map/ppermute | solution.py:461
  71.3 1.9 %shard_map.102 = (bf16[1024,256]{1,0:T(8,128)(2,1)}, bf16[1024,256]{1,0:T(8,128)(2,1)}) custom-call(bf16[1024,256]{1,0:T(8,128)(2,1)S(1)} %copy-done.2, bf16[1024,256]{1,0:T(8,128)(2,1)S(1)} %copy-done.3, f32[8,256,256]{2,1,0:T(8,128)S(1)} %get-tuple-element.85.dkv_ref, f32[8,128,128]{2,1,0:T(8,128)S(1)} %get-tuple-element.86.da_ref, ...), custom_call_target="tpu_custom_call" | custom-call | flops 1000000000 | bytes 6000000 | tf_op jit(solution)/shard_map/pallas_call | solution.py:338
  73.2 2.2 %shard_map.101 = bf16[1024,512]{1,0:T(8,128)(2,1)} custom-call(bf16[1024,256]{1,0:T(8,128)(2,1)S(1)} %get-tuple-element.70.h_ref.refs_0_, bf16[1024,256]{1,0:T(8,128)(2,1)S(1)} %collective-permute-done.9.refs_1_, bf16[1024,256]{1,0:T(8,128)(2,1)S(1)} %collective-permute-done.10.refs_2_, bf16[1024,256]{1,0:T(8,128)(2,1)S(1)} %collective-permute-done.14.refs_3_, ...), custom_call_target="tpu_custom_call" | custom-call | flops 1073741824 | bytes 6000000 | tf_op jit(solution)/shard_map/pallas_call | solution.py:449
  75.4 3.6 %collective-permute-done.21 = bf16[256,256]{1,0:T(8,128)(2,1)S(1)} collective-permute-done((bf16[256,256]{1,0:T(8,128)(2,1)S(1)}, bf16[256,256]{1,0:T(8,128)(2,1)S(1)}, u32[]{:S(2)}, u32[]{:S(2)}) %collective-permute-start.21) | collective-permute-done | bytes 131104 | tf_op jit(solution)/shard_map/ppermute | solution.py:461
  79.1 0.8 fusion.2
  (31 shorter events, 0.2 us)
Async XLA Ops:
  0.6 1.0 %copy-start.2 = (bf16[1024,256]{1,0:T(8,128)(2,1)S(1)}, bf16[1024,256]{1,0:T(8,128)(2,1)}, u32[]{:S(2)}) copy-start(bf16[1024,256]{1,0:T(8,128)(2,1)} %k_ref.9) | copy-start | bytes 1572868
  0.6 1.2 %copy-start.3 = (bf16[1024,256]{1,0:T(8,128)(2,1)S(1)}, bf16[1024,256]{1,0:T(8,128)(2,1)}, u32[]{:S(2)}) copy-start(bf16[1024,256]{1,0:T(8,128)(2,1)} %v_ref.7) | copy-start | bytes 1572868
  0.7 1.5 %copy-start.1 = (bf16[1024,512]{1,0:T(8,128)(2,1)S(1)}, bf16[1024,512]{1,0:T(8,128)(2,1)}, u32[]{:S(2)}) copy-start(bf16[1024,512]{1,0:T(8,128)(2,1)} %refs_0_.3) | copy-start | bytes 3145732
  0.7 20.1 %copy-start = (bf16[256,2048]{1,0:T(8,128)(2,1)S(1)}, bf16[256,2048]{1,0:T(8,128)(2,1)}, u32[]{:S(2)}) copy-start(bf16[256,2048]{1,0:T(8,128)(2,1)} %w_ref.4) | copy-start | bytes 3145732
  2.2 18.6 %collective-permute-start.3 = (bf16[1024,512]{1,0:T(8,128)(2,1)S(1)}, bf16[1024,512]{1,0:T(8,128)(2,1)S(1)}, u32[]{:S(2)}, u32[]{:S(2)}) collective-permute-start(bf16[1024,512]{1,0:T(8,128)(2,1)S(1)} %copy-done.1), channel_id=1, source_target_pairs={{0,1},{1,0},{2,3},{3,2},{4,5},{5,4},{6,7},{7,6},{8,9},{9,8},{10,11... | collective-permute-start | bytes 3145736 | tf_op jit(solution)/shard_map/ppermute | solution.py:461
  2.7 27.0 %collective-permute-start.7 = (bf16[1024,512]{1,0:T(8,128)(2,1)S(1)}, bf16[1024,512]{1,0:T(8,128)(2,1)S(1)}, u32[]{:S(2)}, u32[]{:S(2)}) collective-permute-start(bf16[1024,512]{1,0:T(8,128)(2,1)S(1)} %copy-done.1), channel_id=1, source_target_pairs={{0,2},{1,3},{2,0},{3,1},{4,6},{5,7},{6,4},{7,5},{8,10},{9,11},{10,... | collective-permute-start | bytes 3145736 | tf_op jit(solution)/shard_map/ppermute | solution.py:461
  5.3 6.3 %collective-permute-start.4 = (f32[256,128]{1,0:T(8,128)S(1)}, f32[256,128]{1,0:T(8,128)S(1)}, u32[]{:S(2)}, u32[]{:S(2)}) collective-permute-start(f32[256,128]{1,0:T(8,128)S(1)} %get-tuple-element.51), channel_id=1, source_target_pairs={{0,4},{4,0},{8,12},{12,8},{16,20},{20,16},{24,28},{28,24},{1,5},{5... | collective-permute-start | bytes 393224 | tf_op jit(solution)/shard_map/ppermute | solution.py:461
  6.8 6.4 %collective-permute-start = (f32[136,128]{1,0:T(8,128)S(1)}, f32[136,128]{1,0:T(8,128)S(1)}, u32[]{:S(2)}, u32[]{:S(2)}) collective-permute-start(f32[136,128]{1,0:T(8,128)S(1)} %get-tuple-element.50), channel_id=1, source_target_pairs={{0,4},{4,0},{8,12},{12,8},{16,20},{20,16},{24,28},{28,24},{1,5},{5... | collective-permute-start | bytes 208904 | tf_op jit(solution)/shard_map/ppermute | solution.py:461
  11.6 8.7 %collective-permute-start.5 = (f32[256,128]{1,0:T(8,128)S(1)}, f32[256,128]{1,0:T(8,128)S(1)}, u32[]{:S(2)}, u32[]{:S(2)}) collective-permute-start(f32[256,128]{1,0:T(8,128)S(1)} %add.35), channel_id=1, source_target_pairs={{0,8},{4,12},{8,0},{12,4},{16,24},{20,28},{24,16},{28,20},{1,9},{5... | collective-permute-start | bytes 393224 | tf_op jit(solution)/shard_map/ppermute | solution.py:461
  13.3 4.4 %collective-permute-start.1 = (f32[136,128]{1,0:T(8,128)S(1)}, f32[136,128]{1,0:T(8,128)S(1)}, u32[]{:S(2)}, u32[]{:S(2)}) collective-permute-start(f32[136,128]{1,0:T(8,128)S(1)} %add.33), channel_id=1, source_target_pairs={{0,8},{4,12},{8,0},{12,4},{16,24},{20,28},{24,16},{28,20},{1,9},{5... | collective-permute-start | bytes 208904 | tf_op jit(solution)/shard_map/ppermute | solution.py:461
  17.7 7.8 %collective-permute-start.2 = (f32[136,128]{1,0:T(8,128)S(1)}, f32[136,128]{1,0:T(8,128)S(1)}, u32[]{:S(2)}, u32[]{:S(2)}) collective-permute-start(f32[136,128]{1,0:T(8,128)S(1)} %add.34), channel_id=1, source_target_pairs={{0,16},{4,20},{8,24},{12,28},{16,0},{20,4},{24,8},{28,12},{1,17},{... | collective-permute-start | bytes 208904 | tf_op jit(solution)/shard_map/ppermute | solution.py:461
  20.3 9.4 %collective-permute-start.6 = (f32[256,128]{1,0:T(8,128)S(1)}, f32[256,128]{1,0:T(8,128)S(1)}, u32[]{:S(2)}, u32[]{:S(2)}) collective-permute-start(f32[256,128]{1,0:T(8,128)S(1)} %add.36), channel_id=1, source_target_pairs={{0,16},{4,20},{8,24},{12,28},{16,0},{20,4},{24,8},{28,12},{1,17},{... | collective-permute-start | bytes 393224 | tf_op jit(solution)/shard_map/ppermute | solution.py:461
  21.5 9.4 %copy-start.4 = (bf16[1024,256]{1,0:T(8,128)(2,1)S(1)}, bf16[1024,256]{1,0:T(8,128)(2,1)}, u32[]{:S(2)}) copy-start(bf16[1024,256]{1,0:T(8,128)(2,1)} %q_ref.3) | copy-start | bytes 1572868
  29.8 3.9 %collective-permute-start.8 = (bf16[1024,512]{1,0:T(8,128)(2,1)S(1)}, bf16[1024,512]{1,0:T(8,128)(2,1)S(1)}, u32[]{:S(2)}, u32[]{:S(2)}) collective-permute-start(bf16[1024,512]{1,0:T(8,128)(2,1)S(1)} %collective-permute-done.7.refs_1_.refs_2_), channel_id=1, source_target_pairs={{0,1},{1,0},{2,3},{3,2},{4,5},{5,4},{6,7},{7,6},{8,9},{9,8},{10,11... | collective-permute-start | bytes 3145736 | tf_op jit(solution)/shard_map/ppermute | solution.py:461
  29.9 28.3 %collective-permute-start.15 = (bf16[2,256,512]{2,1,0:T(8,128)(2,1)S(1)}, bf16[2,256,512]{2,1,0:T(8,128)(2,1)S(1)}, u32[]{:S(2)}, u32[]{:S(2)}) collective-permute-start(bf16[2,256,512]{2,1,0:T(8,128)(2,1)S(1)} %get-tuple-element.83), channel_id=1, source_target_pairs={{0,2},{1,3},{2,0},{3,1},{4,6},{5,7},{6,4},{7,5},{8,10},{9,11},{10,... | collective-permute-start | bytes 1572872 | tf_op jit(solution)/shard_map/ppermute | solution.py:461
  35.9 22.6 %collective-permute-start.18 = (bf16[2,256,256]{2,1,0:T(8,128)(2,1)S(1)}, bf16[2,256,256]{2,1,0:T(8,128)(2,1)S(1)}, u32[]{:S(2)}, u32[]{:S(2)}) collective-permute-start(bf16[2,256,256]{2,1,0:T(8,128)(2,1)S(1)} %get-tuple-element.61), channel_id=1, source_target_pairs={{0,4},{4,0},{8,12},{12,8},{16,20},{20,16},{24,28},{28,24},{1,5},{5... | collective-permute-start | bytes 786440 | tf_op jit(solution)/shard_map/ppermute | solution.py:461
  37.4 12.5 %collective-permute-start.12 = (bf16[2,256,256]{2,1,0:T(8,128)(2,1)S(1)}, bf16[2,256,256]{2,1,0:T(8,128)(2,1)S(1)}, u32[]{:S(2)}, u32[]{:S(2)}) collective-permute-start(bf16[2,256,256]{2,1,0:T(8,128)(2,1)S(1)} %get-tuple-element.74), channel_id=1, source_target_pairs={{0,4},{4,0},{8,12},{12,8},{16,20},{20,16},{24,28},{28,24},{1,5},{5... | collective-permute-start | bytes 786440 | tf_op jit(solution)/shard_map/ppermute | solution.py:461
  47.2 16.1 %collective-permute-start.10 = (bf16[1024,256]{1,0:T(8,128)(2,1)S(1)}, bf16[1024,256]{1,0:T(8,128)(2,1)S(1)}, u32[]{:S(2)}, u32[]{:S(2)}) collective-permute-start(bf16[1024,256]{1,0:T(8,128)(2,1)S(1)} %get-tuple-element.70.h_ref.refs_0_), channel_id=1, source_target_pairs={{0,2},{1,3},{2,0},{3,1},{4,6},{5,7},{6,4},{7,5},{8,10},{9,11},{10,... | collective-permute-start | bytes 1572872 | tf_op jit(solution)/shard_map/ppermute | solution.py:461
  48.3 24.9 %collective-permute-start.9 = (bf16[1024,256]{1,0:T(8,128)(2,1)S(1)}, bf16[1024,256]{1,0:T(8,128)(2,1)S(1)}, u32[]{:S(2)}, u32[]{:S(2)}) collective-permute-start(bf16[1024,256]{1,0:T(8,128)(2,1)S(1)} %get-tuple-element.70.h_ref.refs_0_), channel_id=1, source_target_pairs={{0,1},{1,0},{2,3},{3,2},{4,5},{5,4},{6,7},{7,6},{8,9},{9,8},{10,11... | collective-permute-start | bytes 1572872 | tf_op jit(solution)/shard_map/ppermute | solution.py:461
  50.0 4.6 %collective-permute-start.11 = (bf16[392,128]{1,0:T(8,128)(2,1)S(1)}, bf16[392,128]{1,0:T(8,128)(2,1)S(1)}, u32[]{:S(2)}, u32[]{:S(2)}) collective-permute-start(bf16[392,128]{1,0:T(8,128)(2,1)S(1)} %get-tuple-element.72), channel_id=1, source_target_pairs={{0,4},{4,0},{8,12},{12,8},{16,20},{20,16},{24,28},{28,24},{1,5},{5... | collective-permute-start | bytes 301064 | tf_op jit(solution)/shard_map/ppermute | solution.py:461
  54.6 24.4 %collective-permute-start.20 = (bf16[256,256]{1,0:T(8,128)(2,1)S(1)}, bf16[256,256]{1,0:T(8,128)(2,1)S(1)}, u32[]{:S(2)}, u32[]{:S(2)}) collective-permute-start(bf16[256,256]{1,0:T(8,128)(2,1)S(1)} %get-tuple-element.101), channel_id=1, source_target_pairs={{0,24},{4,28},{8,16},{12,20},{16,8},{20,12},{24,0},{28,4},{1,25},{... | collective-permute-start | bytes 393224 | tf_op jit(solution)/shard_map/ppermute | solution.py:461
  58.2 4.7 %collective-permute-start.13 = (bf16[392,128]{1,0:T(8,128)(2,1)S(1)}, bf16[392,128]{1,0:T(8,128)(2,1)S(1)}, u32[]{:S(2)}, u32[]{:S(2)}) collective-permute-start(bf16[392,128]{1,0:T(8,128)(2,1)S(1)} %fusion.3), channel_id=1, source_target_pairs={{0,8},{4,12},{8,0},{12,4},{16,24},{20,28},{24,16},{28,20},{1,9},{5... | collective-permute-start | bytes 301064 | tf_op jit(solution)/shard_map/ppermute | solution.py:461
  58.5 14.7 %collective-permute-start.16 = (bf16[2,256,512]{2,1,0:T(8,128)(2,1)S(1)}, bf16[2,256,512]{2,1,0:T(8,128)(2,1)S(1)}, u32[]{:S(2)}, u32[]{:S(2)}) collective-permute-start(bf16[2,256,512]{2,1,0:T(8,128)(2,1)S(1)} %pad_maximum_fusion), channel_id=1, source_target_pairs={{0,1},{1,0},{2,3},{3,2},{4,5},{5,4},{6,7},{7,6},{8,9},{9,8},{10,11... | collective-permute-start | bytes 1572872 | tf_op jit(solution)/shard_map/ppermute | solution.py:461
  63.0 8.3 %collective-permute-start.17 = (bf16[392,128]{1,0:T(8,128)(2,1)S(1)}, bf16[392,128]{1,0:T(8,128)(2,1)S(1)}, u32[]{:S(2)}, u32[]{:S(2)}) collective-permute-start(bf16[392,128]{1,0:T(8,128)(2,1)S(1)} %add_convert_fusion.1), channel_id=1, source_target_pairs={{0,16},{4,20},{8,24},{12,28},{16,0},{20,4},{24,8},{28,12},{1,17},{... | collective-permute-start | bytes 301064 | tf_op jit(solution)/shard_map/ppermute | solution.py:461
  63.3 9.9 %collective-permute-start.14 = (bf16[1024,256]{1,0:T(8,128)(2,1)S(1)}, bf16[1024,256]{1,0:T(8,128)(2,1)S(1)}, u32[]{:S(2)}, u32[]{:S(2)}) collective-permute-start(bf16[1024,256]{1,0:T(8,128)(2,1)S(1)} %collective-permute-done.10.refs_2_), channel_id=1, source_target_pairs={{0,1},{1,0},{2,3},{3,2},{4,5},{5,4},{6,7},{7,6},{8,9},{9,8},{10,11... | collective-permute-start | bytes 1572872 | tf_op jit(solution)/shard_map/ppermute | solution.py:461
  71.2 7.8 %collective-permute-start.19 = (bf16[256,256]{1,0:T(8,128)(2,1)S(1)}, bf16[256,256]{1,0:T(8,128)(2,1)S(1)}, u32[]{:S(2)}, u32[]{:S(2)}) collective-permute-start(bf16[256,256]{1,0:T(8,128)(2,1)S(1)} %get-tuple-element.102), channel_id=1, source_target_pairs={{0,16},{4,20},{8,24},{12,28},{16,0},{20,4},{24,8},{28,12},{1,17},{... | collective-permute-start | bytes 393224 | tf_op jit(solution)/shard_map/ppermute | solution.py:461
  73.1 5.9 %collective-permute-start.21 = (bf16[256,256]{1,0:T(8,128)(2,1)S(1)}, bf16[256,256]{1,0:T(8,128)(2,1)S(1)}, u32[]{:S(2)}, u32[]{:S(2)}) collective-permute-start(bf16[256,256]{1,0:T(8,128)(2,1)S(1)} %fusion.4), channel_id=1, source_target_pairs={{0,8},{4,12},{8,0},{12,4},{16,24},{20,28},{24,16},{28,20},{1,9},{5... | collective-permute-start | bytes 393224 | tf_op jit(solution)/shard_map/ppermute | solution.py:461

commit v7 on v5

--- a/solution.py
+++ b/solution.py
@@ -99,7 +99,7 @@
     return mats[:heads]
 
 
-def totals_kernel(k_ref, v_ref, g_ref, n_ref):
+def totals_kernel(begin_ref, k_ref, v_ref, g_ref, n_ref):
     grams = []
     for h in range(k_ref.shape[1] // HDIM):
         cols = slice(h * HDIM, (h + 1) * HDIM)
@@ -110,15 +110,15 @@
     fold_into(g_ref, grams)
 
 
-def totals(keys, values, heads):
+def totals(begin, keys, values, heads):
     return pl.pallas_call(
         totals_kernel,
         out_shape=(shape((folded(heads) * (HDIM + 8), HDIM)), shape((heads * HDIM, HDIM))),
-        in_specs=[VMEM_SPEC] * 2,
+        in_specs=[VMEM_SPEC] * 3,
         out_specs=(VMEM_SPEC, VMEM_SPEC),
         compiler_params=params(),
         cost_estimate=cost(2 * 2 * keys.size * HDIM, 4 * keys.size),
-    )(keys, values)
+    )(begin, keys, values)
 
 
 def taken(refs, backward):
@@ -336,6 +336,20 @@
     )(keys, values, dk, dv, da, dn, *sums)
 
 
+def lead_kernel(out_ref):
+    out_ref[...] = jnp.zeros_like(out_ref)
+
+
+def lead():
+    return pl.pallas_call(
+        lead_kernel,
+        out_shape=shape((8, HDIM)),
+        out_specs=VMEM_SPEC,
+        compiler_params=params(),
+        cost_estimate=cost(700_000_000, 4096),
+    )()
+
+
 def grads_kernel(first, w_ref, *refs):
     out_ref = refs[-1]
     me = lax.axis_index("head")
@@ -452,18 +466,19 @@
     head_count, ctx_count = lax.axis_size("head"), lax.axis_size("ctx")
     evens = range(2, head_count, 2)
 
-    gram, pair = totals(keys, values, heads)
-    far = {s: swap(cotangent, "head", s) for s in evens}
+    begin = lead()
+    far = {s: swap(after(cotangent, begin), "head", s) for s in evens}
+    gram, pair = totals(begin, keys, values, heads)
     near = swap(after(cotangent, gram, pair), "head", 1)
 
     grams, pairs = [], []
     begun = None
     for distance in doublings("ctx"):
         grams.append(swap(gram, "ctx", distance))
-        pairs.append(swap(pair, "ctx", distance))
+        pairs.append(swap(pair.astype(BF16), "ctx", distance))
         if begun is None:
             begun = head_grads(w_out, [cotangent, near], 0)
-        gram, pair = gram + grams[-1], pair + pairs[-1]
+        gram, pair = gram + grams[-1], pair + pairs[-1].astype(F32)
     grams[-1] = after(grams[-1], begun)
     *stash, last, ridged = inverses(keys, grams, count)
     pairs[-1] = after(pairs[-1], last)
@@ -503,7 +518,7 @@
         sums = sums + later[-1].astype(F32)
         send = sums.astype(BF16)
 
-    low = even_low.astype(F32) + after(low, *later[:2]).astype(F32)
+    low = even_low.astype(F32) + after(low, later[0]).astype(F32)
     moved += [swap(low[u].astype(BF16), "ctx", 2 * u) for u in range(1, half)]
 
     outs = [heads_out, swap(outs_out, "head", 1)]

time: 82.9 us -> 79.6 us (0.960)
  waiting for transfers between devices: 33.9 us -> 31.6 us
  local copies, waits for them, and re-layouts: 2.39 us -> 1.32 us
    ppermute x22, waiting for transfers between devices: 33.9 us -> 31.6 us  [swap(): return lax.ppermute(value, axis, [(i, i ^ distance) for i in range(count)])]
    unnamed x14 -> x10, local copies, waits for them, and re-layouts: 2.25 us -> 1.18 us
  transfers between devices with their start and end apart: 22 -> 22, of which waited for: 8 -> 9; matrix products, arithmetic and copies ran while one was open for 1% -> 1% of each run, Pallas kernels for 26% -> 27%
where the time goes in v7:
time: 79.6 us; the launch traced here: 79.5 us
  waiting for transfers between devices  31.6 us (40%)
  starting transfers between devices  22.4 us (28%)
  Pallas kernels  22.2 us (28%)
  local copies, waits for them, and re-layouts  1.32 us (2%)
  other arithmetic  1.11 us (1%)
  between operations  0.87 us (1%)
    ppermute x22, waiting for transfers between devices, swap(): return lax.ppermute(value, axis, [(i, i ^ distance) for i in range(count)])  31.6 us
    ppermute x22, starting transfers between devices, swap(): return lax.ppermute(value, axis, [(i, i ^ distance) for i in range(count)])  22.4 us
    pallas_call x1, Pallas kernels, tangent(): pl.pallas_call(tangent_kernel, out_shape=(shape(queries.shape, BF16), wid...  8.14 us
    pallas_call x1, Pallas kernels, inverses(): pl.pallas_call(functools.partial(inverse_kernel, len(grams)), out_shape=(...  4.2 us
    pallas_call x1, Pallas kernels, outputs(): pl.pallas_call(functools.partial(outputs_kernel, len(pairs)), out_shape=(...  2.4 us
    pallas_call x1, Pallas kernels, layer(): pl.pallas_call(layer_kernel, out_shape=shape((rows, cols), BF16), in_spec...  2.22 us
    pallas_call x1, Pallas kernels, finish(): pl.pallas_call(functools.partial(finish_kernel, len(sums)), out_shape=(sh...  1.94 us
  transfers between devices with their start and end apart: 22, of which 9 were waited for; matrix products, arithmetic and copies ran while one was open for 1% of the time, Pallas kernels for 27%

profile of v7, /device:TPU:0, one launch (start us, length us, event | category | flops | bytes accessed | tf_op | source)
XLA Modules:
  0.0 79.5 jit_solution(4899401750782061971)
XLA Ops:
  0.7 1.0 %copy-done.2 = bf16[1024,256]{1,0:T(8,128)(2,1)S(1)} copy-done((bf16[1024,256]{1,0:T(8,128)(2,1)S(1)}, bf16[1024,256]{1,0:T(8,128)(2,1)}, u32[]{:S(2)}) %copy-start.2) | copy-done | bytes 524312
  1.7 0.2 copy-done.3
  1.8 0.3 shard_map.93
  2.2 0.0 copy-done.1
  2.2 0.6 collective-permute-start.3
  2.7 2.6 %collective-permute-start.7 = (bf16[1024,512]{1,0:T(8,128)(2,1)S(1)}, bf16[1024,512]{1,0:T(8,128)(2,1)S(1)}, u32[]{:S(2)}, u32[]{:S(2)}) collective-permute-start(bf16[1024,512]{1,0:T(8,128)(2,1)S(1)} %copy-done.1), channel_id=1, source_target_pairs={{0,2},{1,3},{2,0},{3,1},{4,6},{5,7},{6,4},{7,5},{8,10},{9,11},{10,... | collective-permute-start | bytes 3145736 | tf_op jit(solution)/shard_map/ppermute | solution.py:452
  5.3 1.5 %collective-permute-start = (f32[136,128]{1,0:T(8,128)S(1)}, f32[136,128]{1,0:T(8,128)S(1)}, u32[]{:S(2)}, u32[]{:S(2)}) collective-permute-start(f32[136,128]{1,0:T(8,128)S(1)} %get-tuple-element.51), channel_id=1, source_target_pairs={{0,4},{4,0},{8,12},{12,8},{16,20},{20,16},{24,28},{28,24},{1,5},{5... | collective-permute-start | bytes 208904 | tf_op jit(solution)/shard_map/ppermute | solution.py:452
  6.8 0.6 collective-permute-start.4
  7.4 2.4 %collective-permute-done.refs_0_ = f32[136,128]{1,0:T(8,128)S(1)} collective-permute-done((f32[136,128]{1,0:T(8,128)S(1)}, f32[136,128]{1,0:T(8,128)S(1)}, u32[]{:S(2)}, u32[]{:S(2)}) %collective-permute-start) | collective-permute-done | bytes 69664 | tf_op jit(solution)/shard_map/ppermute | solution.py:452
  9.9 1.6 %collective-permute-start.1 = (f32[136,128]{1,0:T(8,128)S(1)}, f32[136,128]{1,0:T(8,128)S(1)}, u32[]{:S(2)}, u32[]{:S(2)}) collective-permute-start(f32[136,128]{1,0:T(8,128)S(1)} %add.33), channel_id=1, source_target_pairs={{0,8},{4,12},{8,0},{12,4},{16,24},{20,28},{24,16},{28,20},{1,9},{5... | collective-permute-start | bytes 208904 | tf_op jit(solution)/shard_map/ppermute | solution.py:452
  11.5 1.3 %collective-permute-start.5 = (bf16[256,128]{1,0:T(8,128)(2,1)S(1)}, bf16[256,128]{1,0:T(8,128)(2,1)S(1)}, u32[]{:S(2)}, u32[]{:S(2)}) collective-permute-start(bf16[256,128]{1,0:T(8,128)(2,1)S(1)} %fusion.5), channel_id=1, source_target_pairs={{0,8},{4,12},{8,0},{12,4},{16,24},{20,28},{24,16},{28,20},{1,9},{5... | collective-permute-start | bytes 196616 | tf_op jit(solution)/shard_map/ppermute | solution.py:452
  12.8 1.7 %collective-permute-done.1.refs_1_ = f32[136,128]{1,0:T(8,128)S(1)} collective-permute-done((f32[136,128]{1,0:T(8,128)S(1)}, f32[136,128]{1,0:T(8,128)S(1)}, u32[]{:S(2)}, u32[]{:S(2)}) %collective-permute-start.1) | collective-permute-done | bytes 69664 | tf_op jit(solution)/shard_map/ppermute | solution.py:452
  14.6 2.7 %collective-permute-start.2 = (f32[136,128]{1,0:T(8,128)S(1)}, f32[136,128]{1,0:T(8,128)S(1)}, u32[]{:S(2)}, u32[]{:S(2)}) collective-permute-start(f32[136,128]{1,0:T(8,128)S(1)} %add.34), channel_id=1, source_target_pairs={{0,16},{4,20},{8,24},{12,28},{16,0},{20,4},{24,8},{28,12},{1,17},{... | collective-permute-start | bytes 208904 | tf_op jit(solution)/shard_map/ppermute | solution.py:452
  17.3 1.9 %collective-permute-start.6 = (bf16[256,128]{1,0:T(8,128)(2,1)S(1)}, bf16[256,128]{1,0:T(8,128)(2,1)S(1)}, u32[]{:S(2)}, u32[]{:S(2)}) collective-permute-start(bf16[256,128]{1,0:T(8,128)(2,1)S(1)} %add_convert_fusion.2), channel_id=1, source_target_pairs={{0,16},{4,20},{8,24},{12,28},{16,0},{20,4},{24,8},{28,12},{1,17},{... | collective-permute-start | bytes 196616 | tf_op jit(solution)/shard_map/ppermute | solution.py:452
  19.1 0.7 shard_map.94.refs_0_
  19.9 0.0 copy-start.4
  19.9 1.4 %collective-permute-done.2.refs_2_ = f32[136,128]{1,0:T(8,128)S(1)} collective-permute-done((f32[136,128]{1,0:T(8,128)S(1)}, f32[136,128]{1,0:T(8,128)S(1)}, u32[]{:S(2)}, u32[]{:S(2)}) %collective-permute-start.2) | collective-permute-done | bytes 69664 | tf_op jit(solution)/shard_map/ppermute | solution.py:452
  21.3 4.2 %shard_map.95 = (bf16[8,8,128,128]{3,2,1,0:T(8,128)(2,1)S(1)}, bf16[8,8,128,128]{3,2,1,0:T(8,128)(2,1)S(1)}, f32[8,128,128]{2,1,0:T(8,128)S(1)}, f32[8,128,128]{2,1,0:T(8,128)S(1)}) custom-call(bf16[1024,256]{1,0:T(8,128)(2,1)S(1)} %copy-done.2, f32[136,128]{1,0:T(8,128)S(1)} %collective-permute-done.refs_0_, f32[136,128]{1,0:T(8,128)S(1)} %collective-permute-done.1.refs_1_, ...), custom_call_target="tpu_custom_call" | custom-call | flops 2000000000 | bytes 8000000 | tf_op jit(solution)/shard_map/pallas_call | solution.py:180
  25.5 0.0 collective-permute-done.6.refs_2_
  25.5 3.5 %collective-permute-done.7.refs_1_.refs_2_ = bf16[1024,512]{1,0:T(8,128)(2,1)S(1)} collective-permute-done((bf16[1024,512]{1,0:T(8,128)(2,1)S(1)}, bf16[1024,512]{1,0:T(8,128)(2,1)S(1)}, u32[]{:S(2)}, u32[]{:S(2)}) %collective-permute-start.7) | collective-permute-done | bytes 1048608 | tf_op jit(solution)/shard_map/ppermute | solution.py:452
  29.0 0.0 collective-permute-start.8
  29.0 0.1 shard_map.100
  29.1 1.8 %collective-permute-start.15 = (bf16[2,256,512]{2,1,0:T(8,128)(2,1)S(1)}, bf16[2,256,512]{2,1,0:T(8,128)(2,1)S(1)}, u32[]{:S(2)}, u32[]{:S(2)}) collective-permute-start(bf16[2,256,512]{2,1,0:T(8,128)(2,1)S(1)} %get-tuple-element.84), channel_id=1, source_target_pairs={{0,2},{1,3},{2,0},{3,1},{4,6},{5,7},{6,4},{7,5},{8,10},{9,11},{10,... | collective-permute-start | bytes 1572872 | tf_op jit(solution)/shard_map/ppermute | solution.py:452
  30.9 2.4 %shard_map.96 = (bf16[1024,256]{1,0:T(8,128)(2,1)S(1)}, bf16[8,128,256]{2,1,0:T(8,128)(2,1)S(1)}, bf16[8,256,256]{2,1,0:T(8,128)(2,1)S(1)}, bf16[8,256,256]{2,1,0:T(8,128)(2,1)S(1)}) custom-call(bf16[1024,256]{1,0:T(8,128)(2,1)S(1)} %copy-done.4, bf16[1024,256]{1,0:T(8,128)(2,1)S(1)} %copy-done.2, bf16[1024,256]{1,0:T(8,128)(2,1)S(1)} %copy-done.3, ...), custom_call_target="tpu_custom_call" | custom-call | flops 2000000000 | bytes 8000000 | tf_op jit(solution)/shard_map/pallas_call | solution.py:217
  33.4 0.8 shard_map.97.do_ref
  34.1 1.4 %shard_map.98 = (bf16[2,256,256]{2,1,0:T(8,128)(2,1)S(1)}, bf16[2,256,256]{2,1,0:T(8,128)(2,1)S(1)}, bf16[2,256,256]{2,1,0:T(8,128)(2,1)S(1)}, bf16[2,256,256]{2,1,0:T(8,128)(2,1)S(1)}) custom-call(bf16[1024,256]{1,0:T(8,128)(2,1)S(1)} %get-tuple-element.71.h_ref.refs_0_, bf16[1024,512]{1,0:T(8,128)(2,1)S(1)} %copy-done.1, ...), custom_call_target="tpu_custom_call" | custom-call | flops 1073741824 | bytes 6000000 | tf_op jit(solution)/shard_map/pallas_call | solution.py:418
  35.5 1.6 %collective-permute-start.18 = (bf16[2,256,256]{2,1,0:T(8,128)(2,1)S(1)}, bf16[2,256,256]{2,1,0:T(8,128)(2,1)S(1)}, u32[]{:S(2)}, u32[]{:S(2)}) collective-permute-start(bf16[2,256,256]{2,1,0:T(8,128)(2,1)S(1)} %get-tuple-element.62), channel_id=1, source_target_pairs={{0,4},{4,0},{8,12},{12,8},{16,20},{20,16},{24,28},{28,24},{1,5},{5... | collective-permute-start | bytes 786440 | tf_op jit(solution)/shard_map/ppermute | solution.py:452
  37.1 0.5 collective-permute-start.12
  37.6 8.1 %shard_map.99 = (bf16[1024,256]{1,0:T(8,128)(2,1)}, f32[1024,256]{1,0:T(8,128)S(1)}, f32[1024,256]{1,0:T(8,128)S(1)}, f32[8,128,128]{2,1,0:T(8,128)S(1)}, f32[8,...) custom-call(bf16[1024,256]{1,0:T(8,128)(2,1)S(1)} %copy-done.4, ...), custom_call_target="tpu_custom_call" | custom-call | flops 4000000000 | bytes 8000000 | tf_op jit(solution)/shard_map/pallas_call | solution.py:296
  45.7 0.3 collective-permute-start.10
  46.0 3.6 %collective-permute-done.12 = bf16[2,256,256]{2,1,0:T(8,128)(2,1)S(1)} collective-permute-done((bf16[2,256,256]{2,1,0:T(8,128)(2,1)S(1)}, bf16[2,256,256]{2,1,0:T(8,128)(2,1)S(1)}, u32[]{:S(2)}, u32[]{:S(2)}) %collective-permute-start.12) | collective-permute-done | bytes 262176 | tf_op jit(solution)/shard_map/ppermute | solution.py:452
  49.6 1.5 %collective-permute-start.11 = (bf16[392,128]{1,0:T(8,128)(2,1)S(1)}, bf16[392,128]{1,0:T(8,128)(2,1)S(1)}, u32[]{:S(2)}, u32[]{:S(2)}) collective-permute-start(bf16[392,128]{1,0:T(8,128)(2,1)S(1)} %get-tuple-element.73), channel_id=1, source_target_pairs={{0,4},{4,0},{8,12},{12,8},{16,20},{20,16},{24,28},{28,24},{1,5},{5... | collective-permute-start | bytes 301064 | tf_op jit(solution)/shard_map/ppermute | solution.py:452
  51.1 0.1 add_convert_fusion
  51.2 3.0 %collective-permute-done.11.refs_0_ = bf16[392,128]{1,0:T(8,128)(2,1)S(1)} collective-permute-done((bf16[392,128]{1,0:T(8,128)(2,1)S(1)}, bf16[392,128]{1,0:T(8,128)(2,1)S(1)}, u32[]{:S(2)}, u32[]{:S(2)}) %collective-permute-start.11) | collective-permute-done | bytes 100384 | tf_op jit(solution)/shard_map/ppermute | solution.py:452
  54.2 3.6 %collective-permute-start.20 = (bf16[256,256]{1,0:T(8,128)(2,1)S(1)}, bf16[256,256]{1,0:T(8,128)(2,1)S(1)}, u32[]{:S(2)}, u32[]{:S(2)}) collective-permute-start(bf16[256,256]{1,0:T(8,128)(2,1)S(1)} %get-tuple-element.103), channel_id=1, source_target_pairs={{0,24},{4,28},{8,16},{12,20},{16,8},{20,12},{24,0},{28,4},{1,25},{... | collective-permute-start | bytes 393224 | tf_op jit(solution)/shard_map/ppermute | solution.py:452
  57.9 0.1 collective-permute-start.13
  58.0 0.1 slice_bitcast_fusion.3
  58.0 0.1 pad_maximum_fusion
  58.1 0.0 collective-permute-done.18
  58.1 0.1 collective-permute-start.16
  58.2 0.1 convert_add_fusion
  58.3 4.3 %collective-permute-done.13.refs_1_ = bf16[392,128]{1,0:T(8,128)(2,1)S(1)} collective-permute-done((bf16[392,128]{1,0:T(8,128)(2,1)S(1)}, bf16[392,128]{1,0:T(8,128)(2,1)S(1)}, u32[]{:S(2)}, u32[]{:S(2)}) %collective-permute-start.13) | collective-permute-done | bytes 100384 | tf_op jit(solution)/shard_map/ppermute | solution.py:452
  62.6 0.3 collective-permute-start.17
  63.0 7.9 %collective-permute-done.17.refs_2_ = bf16[392,128]{1,0:T(8,128)(2,1)S(1)} collective-permute-done((bf16[392,128]{1,0:T(8,128)(2,1)S(1)}, bf16[392,128]{1,0:T(8,128)(2,1)S(1)}, u32[]{:S(2)}, u32[]{:S(2)}) %collective-permute-start.17) | collective-permute-done | bytes 100384 | tf_op jit(solution)/shard_map/ppermute | solution.py:452
  70.9 1.9 %shard_map.102 = (bf16[1024,256]{1,0:T(8,128)(2,1)}, bf16[1024,256]{1,0:T(8,128)(2,1)}) custom-call(bf16[1024,256]{1,0:T(8,128)(2,1)S(1)} %copy-done.2, bf16[1024,256]{1,0:T(8,128)(2,1)S(1)} %copy-done.3, f32[1024,256]{1,0:T(8,128)S(1)} %get-tuple-element.86.dk_ref, f32[1024,256]{1,0:T(8,128)S(1)} %get-tuple-element.87.dv_ref, ...), custom_call_target="tpu_custom_call" | custom-call | flops 1000000000 | bytes 6000000 | tf_op jit(solution)/shard_map/pallas_call | solution.py:329
  72.9 2.2 %shard_map.101 = bf16[1024,512]{1,0:T(8,128)(2,1)} custom-call(bf16[1024,256]{1,0:T(8,128)(2,1)S(1)} %get-tuple-element.71.h_ref.refs_0_, bf16[1024,256]{1,0:T(8,128)(2,1)S(1)} %collective-permute-done.9.refs_1_, bf16[1024,256]{1,0:T(8,128)(2,1)S(1)} %collective-permute-done.10.refs_2_, bf16[1024,256]{1,0:T(8,128)(2,1)S(1)} %collective-permute-done.14.refs_3_, ...), custom_call_target="tpu_custom_call" | custom-call | flops 1073741824 | bytes 6000000 | tf_op jit(solution)/shard_map/pallas_call | solution.py:440
  75.1 3.6 %collective-permute-done.21 = bf16[256,256]{1,0:T(8,128)(2,1)S(1)} collective-permute-done((bf16[256,256]{1,0:T(8,128)(2,1)S(1)}, bf16[256,256]{1,0:T(8,128)(2,1)S(1)}, u32[]{:S(2)}, u32[]{:S(2)}) %collective-permute-start.21) | collective-permute-done | bytes 131104 | tf_op jit(solution)/shard_map/ppermute | solution.py:452
  78.7 0.8 fusion.2
  (32 shorter events, 0.3 us)
Async XLA Ops:
  0.6 1.0 %copy-start.2 = (bf16[1024,256]{1,0:T(8,128)(2,1)S(1)}, bf16[1024,256]{1,0:T(8,128)(2,1)}, u32[]{:S(2)}) copy-start(bf16[1024,256]{1,0:T(8,128)(2,1)} %k_ref.9) | copy-start | bytes 1572868
  0.6 1.2 %copy-start.3 = (bf16[1024,256]{1,0:T(8,128)(2,1)S(1)}, bf16[1024,256]{1,0:T(8,128)(2,1)}, u32[]{:S(2)}) copy-start(bf16[1024,256]{1,0:T(8,128)(2,1)} %v_ref.7) | copy-start | bytes 1572868
  0.7 1.5 %copy-start.1 = (bf16[1024,512]{1,0:T(8,128)(2,1)S(1)}, bf16[1024,512]{1,0:T(8,128)(2,1)}, u32[]{:S(2)}) copy-start(bf16[1024,512]{1,0:T(8,128)(2,1)} %refs_0_.3) | copy-start | bytes 3145732
  0.7 18.5 %copy-start = (bf16[256,2048]{1,0:T(8,128)(2,1)S(1)}, bf16[256,2048]{1,0:T(8,128)(2,1)}, u32[]{:S(2)}) copy-start(bf16[256,2048]{1,0:T(8,128)(2,1)} %w_ref.4) | copy-start | bytes 3145732
  2.2 16.9 %collective-permute-start.3 = (bf16[1024,512]{1,0:T(8,128)(2,1)S(1)}, bf16[1024,512]{1,0:T(8,128)(2,1)S(1)}, u32[]{:S(2)}, u32[]{:S(2)}) collective-permute-start(bf16[1024,512]{1,0:T(8,128)(2,1)S(1)} %copy-done.1), channel_id=1, source_target_pairs={{0,1},{1,0},{2,3},{3,2},{4,5},{5,4},{6,7},{7,6},{8,9},{9,8},{10,11... | collective-permute-start | bytes 3145736 | tf_op jit(solution)/shard_map/ppermute | solution.py:452
  2.7 26.3 %collective-permute-start.7 = (bf16[1024,512]{1,0:T(8,128)(2,1)S(1)}, bf16[1024,512]{1,0:T(8,128)(2,1)S(1)}, u32[]{:S(2)}, u32[]{:S(2)}) collective-permute-start(bf16[1024,512]{1,0:T(8,128)(2,1)S(1)} %copy-done.1), channel_id=1, source_target_pairs={{0,2},{1,3},{2,0},{3,1},{4,6},{5,7},{6,4},{7,5},{8,10},{9,11},{10,... | collective-permute-start | bytes 3145736 | tf_op jit(solution)/shard_map/ppermute | solution.py:452
  5.3 4.6 %collective-permute-start = (f32[136,128]{1,0:T(8,128)S(1)}, f32[136,128]{1,0:T(8,128)S(1)}, u32[]{:S(2)}, u32[]{:S(2)}) collective-permute-start(f32[136,128]{1,0:T(8,128)S(1)} %get-tuple-element.51), channel_id=1, source_target_pairs={{0,4},{4,0},{8,12},{12,8},{16,20},{20,16},{24,28},{28,24},{1,5},{5... | collective-permute-start | bytes 208904 | tf_op jit(solution)/shard_map/ppermute | solution.py:452
  6.8 4.7 %collective-permute-start.4 = (bf16[256,128]{1,0:T(8,128)(2,1)S(1)}, bf16[256,128]{1,0:T(8,128)(2,1)S(1)}, u32[]{:S(2)}, u32[]{:S(2)}) collective-permute-start(bf16[256,128]{1,0:T(8,128)(2,1)S(1)} %convert_element_type.60), channel_id=1, source_target_pairs={{0,4},{4,0},{8,12},{12,8},{16,20},{20,16},{24,28},{28,24},{1,5},{5... | collective-permute-start | bytes 196616 | tf_op jit(solution)/shard_map/ppermute | solution.py:452
  9.9 4.7 %collective-permute-start.1 = (f32[136,128]{1,0:T(8,128)S(1)}, f32[136,128]{1,0:T(8,128)S(1)}, u32[]{:S(2)}, u32[]{:S(2)}) collective-permute-start(f32[136,128]{1,0:T(8,128)S(1)} %add.33), channel_id=1, source_target_pairs={{0,8},{4,12},{8,0},{12,4},{16,24},{20,28},{24,16},{28,20},{1,9},{5... | collective-permute-start | bytes 208904 | tf_op jit(solution)/shard_map/ppermute | solution.py:452
  11.5 5.7 %collective-permute-start.5 = (bf16[256,128]{1,0:T(8,128)(2,1)S(1)}, bf16[256,128]{1,0:T(8,128)(2,1)S(1)}, u32[]{:S(2)}, u32[]{:S(2)}) collective-permute-start(bf16[256,128]{1,0:T(8,128)(2,1)S(1)} %fusion.5), channel_id=1, source_target_pairs={{0,8},{4,12},{8,0},{12,4},{16,24},{20,28},{24,16},{28,20},{1,9},{5... | collective-permute-start | bytes 196616 | tf_op jit(solution)/shard_map/ppermute | solution.py:452
  14.6 6.8 %collective-permute-start.2 = (f32[136,128]{1,0:T(8,128)S(1)}, f32[136,128]{1,0:T(8,128)S(1)}, u32[]{:S(2)}, u32[]{:S(2)}) collective-permute-start(f32[136,128]{1,0:T(8,128)S(1)} %add.34), channel_id=1, source_target_pairs={{0,16},{4,20},{8,24},{12,28},{16,0},{20,4},{24,8},{28,12},{1,17},{... | collective-permute-start | bytes 208904 | tf_op jit(solution)/shard_map/ppermute | solution.py:452
  17.3 8.3 %collective-permute-start.6 = (bf16[256,128]{1,0:T(8,128)(2,1)S(1)}, bf16[256,128]{1,0:T(8,128)(2,1)S(1)}, u32[]{:S(2)}, u32[]{:S(2)}) collective-permute-start(bf16[256,128]{1,0:T(8,128)(2,1)S(1)} %add_convert_fusion.2), channel_id=1, source_target_pairs={{0,16},{4,20},{8,24},{12,28},{16,0},{20,4},{24,8},{28,12},{1,17},{... | collective-permute-start | bytes 196616 | tf_op jit(solution)/shard_map/ppermute | solution.py:452
  19.9 11.0 %copy-start.4 = (bf16[1024,256]{1,0:T(8,128)(2,1)S(1)}, bf16[1024,256]{1,0:T(8,128)(2,1)}, u32[]{:S(2)}) copy-start(bf16[1024,256]{1,0:T(8,128)(2,1)} %q_ref.3) | copy-start | bytes 1572868
  29.0 4.3 %collective-permute-start.8 = (bf16[1024,512]{1,0:T(8,128)(2,1)S(1)}, bf16[1024,512]{1,0:T(8,128)(2,1)S(1)}, u32[]{:S(2)}, u32[]{:S(2)}) collective-permute-start(bf16[1024,512]{1,0:T(8,128)(2,1)S(1)} %collective-permute-done.7.refs_1_.refs_2_), channel_id=1, source_target_pairs={{0,1},{1,0},{2,3},{3,2},{4,5},{5,4},{6,7},{7,6},{8,9},{9,8},{10,11... | collective-permute-start | bytes 3145736 | tf_op jit(solution)/shard_map/ppermute | solution.py:452
  29.1 28.7 %collective-permute-start.15 = (bf16[2,256,512]{2,1,0:T(8,128)(2,1)S(1)}, bf16[2,256,512]{2,1,0:T(8,128)(2,1)S(1)}, u32[]{:S(2)}, u32[]{:S(2)}) collective-permute-start(bf16[2,256,512]{2,1,0:T(8,128)(2,1)S(1)} %get-tuple-element.84), channel_id=1, source_target_pairs={{0,2},{1,3},{2,0},{3,1},{4,6},{5,7},{6,4},{7,5},{8,10},{9,11},{10,... | collective-permute-start | bytes 1572872 | tf_op jit(solution)/shard_map/ppermute | solution.py:452
  35.5 22.6 %collective-permute-start.18 = (bf16[2,256,256]{2,1,0:T(8,128)(2,1)S(1)}, bf16[2,256,256]{2,1,0:T(8,128)(2,1)S(1)}, u32[]{:S(2)}, u32[]{:S(2)}) collective-permute-start(bf16[2,256,256]{2,1,0:T(8,128)(2,1)S(1)} %get-tuple-element.62), channel_id=1, source_target_pairs={{0,4},{4,0},{8,12},{12,8},{16,20},{20,16},{24,28},{28,24},{1,5},{5... | collective-permute-start | bytes 786440 | tf_op jit(solution)/shard_map/ppermute | solution.py:452
  37.1 12.5 %collective-permute-start.12 = (bf16[2,256,256]{2,1,0:T(8,128)(2,1)S(1)}, bf16[2,256,256]{2,1,0:T(8,128)(2,1)S(1)}, u32[]{:S(2)}, u32[]{:S(2)}) collective-permute-start(bf16[2,256,256]{2,1,0:T(8,128)(2,1)S(1)} %get-tuple-element.75), channel_id=1, source_target_pairs={{0,4},{4,0},{8,12},{12,8},{16,20},{20,16},{24,28},{28,24},{1,5},{5... | collective-permute-start | bytes 786440 | tf_op jit(solution)/shard_map/ppermute | solution.py:452
  45.7 17.2 %collective-permute-start.10 = (bf16[1024,256]{1,0:T(8,128)(2,1)S(1)}, bf16[1024,256]{1,0:T(8,128)(2,1)S(1)}, u32[]{:S(2)}, u32[]{:S(2)}) collective-permute-start(bf16[1024,256]{1,0:T(8,128)(2,1)S(1)} %get-tuple-element.71.h_ref.refs_0_), channel_id=1, source_target_pairs={{0,2},{1,3},{2,0},{3,1},{4,6},{5,7},{6,4},{7,5},{8,10},{9,11},{10,... | collective-permute-start | bytes 1572872 | tf_op jit(solution)/shard_map/ppermute | solution.py:452
  46.0 26.9 %collective-permute-start.9 = (bf16[1024,256]{1,0:T(8,128)(2,1)S(1)}, bf16[1024,256]{1,0:T(8,128)(2,1)S(1)}, u32[]{:S(2)}, u32[]{:S(2)}) collective-permute-start(bf16[1024,256]{1,0:T(8,128)(2,1)S(1)} %get-tuple-element.71.h_ref.refs_0_), channel_id=1, source_target_pairs={{0,1},{1,0},{2,3},{3,2},{4,5},{5,4},{6,7},{7,6},{8,9},{9,8},{10,11... | collective-permute-start | bytes 1572872 | tf_op jit(solution)/shard_map/ppermute | solution.py:452
  49.6 4.6 %collective-permute-start.11 = (bf16[392,128]{1,0:T(8,128)(2,1)S(1)}, bf16[392,128]{1,0:T(8,128)(2,1)S(1)}, u32[]{:S(2)}, u32[]{:S(2)}) collective-permute-start(bf16[392,128]{1,0:T(8,128)(2,1)S(1)} %get-tuple-element.73), channel_id=1, source_target_pairs={{0,4},{4,0},{8,12},{12,8},{16,20},{20,16},{24,28},{28,24},{1,5},{5... | collective-permute-start | bytes 301064 | tf_op jit(solution)/shard_map/ppermute | solution.py:452
  54.2 24.4 %collective-permute-start.20 = (bf16[256,256]{1,0:T(8,128)(2,1)S(1)}, bf16[256,256]{1,0:T(8,128)(2,1)S(1)}, u32[]{:S(2)}, u32[]{:S(2)}) collective-permute-start(bf16[256,256]{1,0:T(8,128)(2,1)S(1)} %get-tuple-element.103), channel_id=1, source_target_pairs={{0,24},{4,28},{8,16},{12,20},{16,8},{20,12},{24,0},{28,4},{1,25},{... | collective-permute-start | bytes 393224 | tf_op jit(solution)/shard_map/ppermute | solution.py:452
  57.9 4.7 %collective-permute-start.13 = (bf16[392,128]{1,0:T(8,128)(2,1)S(1)}, bf16[392,128]{1,0:T(8,128)(2,1)S(1)}, u32[]{:S(2)}, u32[]{:S(2)}) collective-permute-start(bf16[392,128]{1,0:T(8,128)(2,1)S(1)} %fusion.3), channel_id=1, source_target_pairs={{0,8},{4,12},{8,0},{12,4},{16,24},{20,28},{24,16},{28,20},{1,9},{5... | collective-permute-start | bytes 301064 | tf_op jit(solution)/shard_map/ppermute | solution.py:452
  58.1 14.7 %collective-permute-start.16 = (bf16[2,256,512]{2,1,0:T(8,128)(2,1)S(1)}, bf16[2,256,512]{2,1,0:T(8,128)(2,1)S(1)}, u32[]{:S(2)}, u32[]{:S(2)}) collective-permute-start(bf16[2,256,512]{2,1,0:T(8,128)(2,1)S(1)} %pad_maximum_fusion), channel_id=1, source_target_pairs={{0,1},{1,0},{2,3},{3,2},{4,5},{5,4},{6,7},{7,6},{8,9},{9,8},{10,11... | collective-permute-start | bytes 1572872 | tf_op jit(solution)/shard_map/ppermute | solution.py:452
  62.6 8.3 %collective-permute-start.17 = (bf16[392,128]{1,0:T(8,128)(2,1)S(1)}, bf16[392,128]{1,0:T(8,128)(2,1)S(1)}, u32[]{:S(2)}, u32[]{:S(2)}) collective-permute-start(bf16[392,128]{1,0:T(8,128)(2,1)S(1)} %add_convert_fusion.1), channel_id=1, source_target_pairs={{0,16},{4,20},{8,24},{12,28},{16,0},{20,4},{24,8},{28,12},{1,17},{... | collective-permute-start | bytes 301064 | tf_op jit(solution)/shard_map/ppermute | solution.py:452
  62.9 10.0 %collective-permute-start.14 = (bf16[1024,256]{1,0:T(8,128)(2,1)S(1)}, bf16[1024,256]{1,0:T(8,128)(2,1)S(1)}, u32[]{:S(2)}, u32[]{:S(2)}) collective-permute-start(bf16[1024,256]{1,0:T(8,128)(2,1)S(1)} %collective-permute-done.10.refs_2_), channel_id=1, source_target_pairs={{0,1},{1,0},{2,3},{3,2},{4,5},{5,4},{6,7},{7,6},{8,9},{9,8},{10,11... | collective-permute-start | bytes 1572872 | tf_op jit(solution)/shard_map/ppermute | solution.py:452
  70.9 7.8 %collective-permute-start.19 = (bf16[256,256]{1,0:T(8,128)(2,1)S(1)}, bf16[256,256]{1,0:T(8,128)(2,1)S(1)}, u32[]{:S(2)}, u32[]{:S(2)}) collective-permute-start(bf16[256,256]{1,0:T(8,128)(2,1)S(1)} %get-tuple-element.104), channel_id=1, source_target_pairs={{0,16},{4,20},{8,24},{12,28},{16,0},{20,4},{24,8},{28,12},{1,17},{... | collective-permute-start | bytes 393224 | tf_op jit(solution)/shard_map/ppermute | solution.py:452
  72.8 5.9 %collective-permute-start.21 = (bf16[256,256]{1,0:T(8,128)(2,1)S(1)}, bf16[256,256]{1,0:T(8,128)(2,1)S(1)}, u32[]{:S(2)}, u32[]{:S(2)}) collective-permute-start(bf16[256,256]{1,0:T(8,128)(2,1)S(1)} %fusion.4), channel_id=1, source_target_pairs={{0,8},{4,12},{8,0},{12,4},{16,24},{20,28},{24,16},{28,20},{1,9},{5... | collective-permute-start | bytes 393224 | tf_op jit(solution)/shard_map/ppermute | solution.py:452

commit v8 on v7

--- a/solution.py
+++ b/solution.py
@@ -15,6 +15,7 @@
 F32 = jnp.float32
 BF16 = jnp.bfloat16
 VMEM_SPEC = pl.BlockSpec(memory_space=pltpu.VMEM)
+ANY_SPEC = pl.BlockSpec(memory_space=pl.ANY)
 
 
 def dot(left, right, axes=(1, 0)):
@@ -230,8 +231,8 @@
 
 
 def tangent_kernel(
-    q_ref, k_ref, v_ref, do_ref, e_ref, x_ref, last_ref, a_ref, pre_ref, s_ref, w_ref,
-    dq_ref, dk_ref, dv_ref, da_ref, dn_ref, sum_ref, send_ref, des, dxs, first,
+    q_ref, k_ref, v_ref, do_ref, e_ref, x_ref, last_ref, a_ref, pre_ref, s_ref,
+    p_ref, ds_ref, da_ref, dn_ref, sum_ref, send_ref, des, dxs, first,
 ):
     heads = q_ref.shape[1] // HDIM
     keep = causal()
@@ -239,18 +240,12 @@
     for h, b, i, rows, cols in places(q_ref, heads):
         q, k, v, do = q_ref[rows, cols], k_ref[rows, cols], v_ref[rows, cols], do_ref[rows, cols]
         weights = jnp.where(keep, dot(do, v, (1, 1)), 0.0).astype(BF16)
+        p_ref[i] = weights
         ds = dot(weights, k) + dot(cat([do, do], 1), pre_ref[i], (1, 1))
         ds = ds.astype(BF16)
-        xh, xl = split(last_ref[i])
-        inverse = cat([xh, xl], 0)
-        both = s_ref[i]
-        sh = both[:, :HDIM]
-        scores = w_ref[i]
-        dv_ref[rows, cols] = dot(scores, do, (0, 0))
-        dk_ref[rows, cols] = dot(weights, sh, (0, 0))
-        state = dot(both, do, (0, 0))
+        ds_ref[rows, cols] = ds
+        state = dot(s_ref[i], do, (0, 0))
         dn_ref[i] = state[:HDIM] + state[HDIM:]
-        dq_ref[rows, cols] = dot(cat([ds, ds], 1), inverse).astype(BF16)
         bar = dot(q, ds, (0, 0))
         bar = bar + bar.T
         ridged = a_ref[i]
@@ -291,49 +286,92 @@
     heads = queries.shape[1] // HDIM
     count = stash[-1].shape[0]
     state = shape((count, HDIM, HDIM))
-    wide = shape(queries.shape)
     rows = heads * HDIM + folded(heads) * (HDIM + 8)
     return pl.pallas_call(
         tangent_kernel,
         out_shape=(
-            shape(queries.shape, BF16), wide, wide, state, state,
+            shape((count, SPAN, SPAN), BF16), shape(queries.shape, BF16), state, state,
             shape((rows, HDIM)), shape((rows, HDIM), BF16),
         ),
-        in_specs=[VMEM_SPEC] * 11,
-        out_specs=(VMEM_SPEC,) * 7,
+        in_specs=[VMEM_SPEC] * 10,
+        out_specs=(VMEM_SPEC,) * 6,
         scratch_shapes=[pltpu.VMEM((count, HDIM, HDIM), F32)] * 3,
         compiler_params=params(),
         cost_estimate=cost(4_000_000_000, 8_000_000),
     )(queries, keys, values, grads, *stash)
 
 
-def finish_kernel(rounds, k_ref, v_ref, dk_ref, dv_ref, da_ref, dn_ref, *refs):
-    gk_ref, gv_ref = refs[rounds:]
-    sum_ref = taken(refs[:rounds], True)
+def rest_kernel(
+    k_ref, v_ref, do_ref, last_ref, s_ref, w_ref, p_ref, ds_ref, da_ref, dn_ref,
+    dq_ref, dk_ref, dv_ref,
+):
     heads = k_ref.shape[1] // HDIM
-    sa = unfold_from(sum_ref, heads, heads * HDIM)
-    sn = [sum_ref[h * HDIM : (h + 1) * HDIM, :] for h in range(heads)]
+    sa, sn = [None] * heads, [None] * heads
     for h, b, i, rows, cols in reversed(list(places(k_ref, heads))):
-        k, v = k_ref[rows, cols], v_ref[rows, cols]
-        nh, nl = split(sn[h])
-        grad_k = dk_ref[rows, cols] + dot(k, sa[h].astype(BF16))
-        grad_k = grad_k + dot(cat([v, v], 1), cat([nh, nl], 1), (1, 1))
-        grad_v = dv_ref[rows, cols] + dot(cat([k, k], 1), cat([nh, nl], 0))
-        gk_ref[rows, cols] = grad_k.astype(BF16)
-        gv_ref[rows, cols] = grad_v.astype(BF16)
-        sa[h] = sa[h] + da_ref[i]
-        sn[h] = sn[h] + dn_ref[i]
-
-
-def finish(keys, values, dk, dv, da, dn, sums):
+        k, v, do, ds = k_ref[rows, cols], v_ref[rows, cols], do_ref[rows, cols], ds_ref[rows, cols]
+        dq_ref[rows, cols] = dot(cat([ds, ds], 1), cat(split(last_ref[i]), 0)).astype(BF16)
+        dk = dot(p_ref[i], s_ref[i, :, :HDIM], (0, 0))
+        dv = dot(w_ref[i], do, (0, 0))
+        if sa[h] is None:
+            sa[h], sn[h] = da_ref[i], dn_ref[i]
+        else:
+            nh, nl = split(sn[h])
+            dk = dk + dot(k, sa[h].astype(BF16)) + dot(cat([v, v], 1), cat([nh, nl], 1), (1, 1))
+            dv = dv + dot(cat([k, k], 1), cat([nh, nl], 0))
+            sa[h], sn[h] = sa[h] + da_ref[i], sn[h] + dn_ref[i]
+        dk_ref[rows, cols] = dk
+        dv_ref[rows, cols] = dv
+
+
+def rest(keys, values, grads, *stash):
+    wide = shape(keys.shape)
+    return pl.pallas_call(
+        rest_kernel,
+        out_shape=(shape(keys.shape, BF16), wide, wide),
+        in_specs=[VMEM_SPEC] * 10,
+        out_specs=(VMEM_SPEC,) * 3,
+        compiler_params=params(),
+        cost_estimate=cost(2_000_000_000, 6_000_000),
+    )(keys, values, grads, *stash)
+
+
+def finish_kernel(rounds, k_ref, v_ref, dk_ref, dv_ref, *refs):
+    gk_hbm, gv_hbm, gk_ref, gv_ref, sems = refs[rounds:]
+    sums = taken(refs[:rounds], True)
+    heads = k_ref.shape[1] // HDIM
+    nil = jnp.zeros((HDIM, HDIM), BF16)
+    right = []
+    for h, sa in enumerate(unfold_from(sums, heads, heads * HDIM)):
+        sn = sums[h * HDIM : (h + 1) * HDIM, :]
+        top = cat([sa.astype(BF16), sn.astype(BF16)], 1)
+        right.append(cat([top, cat([sn.T.astype(BF16), nil], 1)], 0))
+    copies = []
+    for b in range(k_ref.shape[0] // SPAN):
+        rows = slice(b * SPAN, (b + 1) * SPAN)
+        for h in range(heads):
+            cols = slice(h * HDIM, (h + 1) * HDIM)
+            total = dot(cat([k_ref[rows, cols], v_ref[rows, cols]], 1), right[h])
+            gk_ref[rows, cols] = (dk_ref[rows, cols] + total[:, :HDIM]).astype(BF16)
+            gv_ref[rows, cols] = (dv_ref[rows, cols] + total[:, HDIM:]).astype(BF16)
+        for i, (ref, hbm) in enumerate(((gk_ref, gk_hbm), (gv_ref, gv_hbm))):
+            copies.append(pltpu.make_async_copy(ref.at[rows], hbm.at[rows], sems.at[b, i]))
+            copies[-1].start()
+    for copy in copies:
+        copy.wait()
+
+
+def finish(keys, values, dk, dv, sums):
+    blocks = keys.shape[0] // SPAN
     return pl.pallas_call(
         functools.partial(finish_kernel, len(sums)),
         out_shape=(shape(keys.shape, BF16),) * 2,
-        in_specs=[VMEM_SPEC] * (6 + len(sums)),
-        out_specs=(VMEM_SPEC,) * 2,
+        in_specs=[VMEM_SPEC] * (4 + len(sums)),
+        out_specs=(ANY_SPEC,) * 2,
+        scratch_shapes=[pltpu.VMEM(keys.shape, BF16)] * 2
+        + [pltpu.SemaphoreType.DMA((blocks, 2))],
         compiler_params=params(),
         cost_estimate=cost(1_000_000_000, 6_000_000),
-    )(keys, values, dk, dv, da, dn, *sums)
+    )(keys, values, dk, dv, *sums)
 
 
 def lead_kernel(out_ref):
@@ -473,12 +511,17 @@
 
     grams, pairs = [], []
     begun = None
-    for distance in doublings("ctx"):
+    rounds = doublings("ctx")
+    for r, distance in enumerate(rounds):
         grams.append(swap(gram, "ctx", distance))
-        pairs.append(swap(pair.astype(BF16), "ctx", distance))
         if begun is None:
             begun = head_grads(w_out, [cotangent, near], 0)
-        gram, pair = gram + grams[-1], pair + pairs[-1].astype(F32)
+        if distance != rounds[-1]:
+            gram = gram + grams[-1]
+        if r:
+            pairs[-1] = after(pairs[-1], gram)
+            pair = pair + pairs[-1].astype(F32)
+        pairs.append(swap(pair.astype(BF16), "ctx", distance))
     grams[-1] = after(grams[-1], begun)
     *stash, last, ridged = inverses(keys, grams, count)
     pairs[-1] = after(pairs[-1], last)
@@ -498,13 +541,13 @@
     high = swap(odd_high, "ctx", 1)
     low = swap(odd_low, "ctx", 1)
 
-    grad_queries, dk, dv, da, dn, sums, send = tangent(
-        queries, keys, values, after(grads, odd_low), [*stash, last, ridged, states, solved, scores]
+    weights, ds, da, dn, sums, send = tangent(
+        queries, keys, values, after(grads, odd_low), [*stash, last, ridged, states, solved]
     )
 
-    outs_out = after(heads_out, grad_queries)
+    outs_out = after(heads_out, send)
     outs_far = [swap(outs_out, "head", s) for s in evens]
-    high = even_high.astype(F32) + after(high, grad_queries).astype(F32)
+    high = even_high.astype(F32) + after(high, send).astype(F32)
     half = ctx_count // 4
     high = [high[u].astype(BF16) for u in range(half)]
     moved = [swap(part, "ctx", 2 * (half + u)) for u, part in enumerate(high)]
@@ -524,14 +567,17 @@
     outs = [heads_out, swap(outs_out, "head", 1)]
     for part in outs_far:
         outs += [part, swap(after(part, sent), "head", 1)]
-    columns = [after(c, grad_queries, later[0]) for c in columns]
+    columns = [after(c, later[0]) for c in columns]
     crossing = swap(jnp.stack([c[1] for c in columns]), "head", 1)
     columns = [c for s in range(head_count // 2) for c in (columns[s][0], crossing[s])]
+    grad_queries, dk, dv = rest(
+        keys, values, grads, last, solved, scores, weights, after(ds, sent), da, dn
+    )
     layer_out = layer(outs, columns)
     grad_weight = low[0]
     for part in moved:
         grad_weight = grad_weight + after(part, layer_out).astype(F32)
-    grad_keys, grad_values = finish(keys, values, dk, dv, da, dn, later)
+    grad_keys, grad_values = finish(keys, values, dk, dv, later)
     return (layer_out, grad_queries, grad_keys, grad_values, grad_weight)
 
 

time: 79.6 us -> 74 us (0.930)
  waiting for transfers between devices: 31.6 us -> 22.1 us
  starting transfers between devices: 22.4 us -> 26.3 us
    ppermute x22, waiting for transfers between devices: 31.6 us -> 22.1 us  [swap(): return lax.ppermute(value, axis, [(i, i ^ distance) for i in range(count)])]
    ppermute x22, starting transfers between devices: 22.4 us -> 26.3 us  [swap(): return lax.ppermute(value, axis, [(i, i ^ distance) for i in range(count)])]
    pallas_call x1 -> x2, Pallas kernels: 8.14 us -> 8.82 us  [the longest x1 6.64 us: tangent(): pl.pallas_call(tangent_kernel, out_shape=(shape((count, SPAN, SPAN), BF16...]
  transfers between devices with their start and end apart: 22 -> 22, of which waited for: 9 -> 11; matrix products, arithmetic and copies ran while one was open for 1% -> 1% of each run, Pallas kernels for 27% -> 30%
where the time goes in v8:
time: 74 us; the launch traced here: 73.9 us
  starting transfers between devices  26.3 us (36%)
  Pallas kernels  22.2 us (30%)
  waiting for transfers between devices  22.1 us (30%)
  local copies, waits for them, and re-layouts  1.32 us (2%)
  other arithmetic  1.09 us (1%)
  between operations  0.88 us (1%)
    ppermute x22, starting transfers between devices, swap(): return lax.ppermute(value, axis, [(i, i ^ distance) for i in range(count)])  26.3 us
    ppermute x22, waiting for transfers between devices, swap(): return lax.ppermute(value, axis, [(i, i ^ distance) for i in range(count)])  22.1 us
    pallas_call x1, Pallas kernels, tangent(): pl.pallas_call(tangent_kernel, out_shape=(shape((count, SPAN, SPAN), BF16...  6.64 us
    pallas_call x1, Pallas kernels, inverses(): pl.pallas_call(functools.partial(inverse_kernel, len(grams)), out_shape=(...  4.12 us
    pallas_call x1, Pallas kernels, outputs(): pl.pallas_call(functools.partial(outputs_kernel, len(pairs)), out_shape=(...  2.39 us
    pallas_call x1, Pallas kernels, layer(): pl.pallas_call(layer_kernel, out_shape=shape((rows, cols), BF16), in_spec...  2.22 us
    pallas_call x1, Pallas kernels, rest(): pl.pallas_call(rest_kernel, out_shape=(shape(keys.shape, BF16), wide, wid...  2.18 us
    pallas_call x2, Pallas kernels, head_grads(): pl.pallas_call(functools.partial(grads_kernel, first), out_shape=shape((r...  1.5 us
  transfers between devices with their start and end apart: 22, of which 11 were waited for; matrix products, arithmetic and copies ran while one was open for 1% of the time, Pallas kernels for 30%

profile of v8, /device:TPU:0, one launch (start us, length us, event | category | flops | bytes accessed | tf_op | source)
XLA Modules:
  0.0 73.9 jit_solution(14169643443132837714)
XLA Ops:
  0.7 1.0 %copy-done.2 = bf16[1024,256]{1,0:T(8,128)(2,1)S(1)} copy-done((bf16[1024,256]{1,0:T(8,128)(2,1)S(1)}, bf16[1024,256]{1,0:T(8,128)(2,1)}, u32[]{:S(2)}) %copy-start.2) | copy-done | bytes 524312
  1.7 0.2 copy-done.3
  1.8 0.3 shard_map.93
  2.2 0.0 copy-done.1
  2.2 0.6 collective-permute-start.3
  2.7 2.6 %collective-permute-start.7 = (bf16[1024,512]{1,0:T(8,128)(2,1)S(1)}, bf16[1024,512]{1,0:T(8,128)(2,1)S(1)}, u32[]{:S(2)}, u32[]{:S(2)}) collective-permute-start(bf16[1024,512]{1,0:T(8,128)(2,1)S(1)} %copy-done.1), channel_id=1, source_target_pairs={{0,2},{1,3},{2,0},{3,1},{4,6},{5,7},{6,4},{7,5},{8,10},{9,11},{10,... | collective-permute-start | bytes 3145736 | tf_op jit(solution)/shard_map/ppermute | solution.py:490
  5.3 1.5 %collective-permute-start = (f32[136,128]{1,0:T(8,128)S(1)}, f32[136,128]{1,0:T(8,128)S(1)}, u32[]{:S(2)}, u32[]{:S(2)}) collective-permute-start(f32[136,128]{1,0:T(8,128)S(1)} %get-tuple-element.56), channel_id=1, source_target_pairs={{0,4},{4,0},{8,12},{12,8},{16,20},{20,16},{24,28},{28,24},{1,5},{5... | collective-permute-start | bytes 208904 | tf_op jit(solution)/shard_map/ppermute | solution.py:490
  6.8 2.8 %collective-permute-done.refs_0_ = f32[136,128]{1,0:T(8,128)S(1)} collective-permute-done((f32[136,128]{1,0:T(8,128)S(1)}, f32[136,128]{1,0:T(8,128)S(1)}, u32[]{:S(2)}, u32[]{:S(2)}) %collective-permute-start) | collective-permute-done | bytes 69664 | tf_op jit(solution)/shard_map/ppermute | solution.py:490
  9.6 1.6 %collective-permute-start.1 = (f32[136,128]{1,0:T(8,128)S(1)}, f32[136,128]{1,0:T(8,128)S(1)}, u32[]{:S(2)}, u32[]{:S(2)}) collective-permute-start(f32[136,128]{1,0:T(8,128)S(1)} %add.33), channel_id=1, source_target_pairs={{0,8},{4,12},{8,0},{12,4},{16,24},{20,28},{24,16},{28,20},{1,9},{5... | collective-permute-start | bytes 208904 | tf_op jit(solution)/shard_map/ppermute | solution.py:490
  11.3 1.6 %collective-permute-start.4 = (bf16[256,128]{1,0:T(8,128)(2,1)S(1)}, bf16[256,128]{1,0:T(8,128)(2,1)S(1)}, u32[]{:S(2)}, u32[]{:S(2)}) collective-permute-start(bf16[256,128]{1,0:T(8,128)(2,1)S(1)} %convert_element_type.60), channel_id=1, source_target_pairs={{0,4},{4,0},{8,12},{12,8},{16,20},{20,16},{24,28},{28,24},{1,5},{5... | collective-permute-start | bytes 196616 | tf_op jit(solution)/shard_map/ppermute | solution.py:490
  12.9 1.1 %collective-permute-done.1.refs_1_ = f32[136,128]{1,0:T(8,128)S(1)} collective-permute-done((f32[136,128]{1,0:T(8,128)S(1)}, f32[136,128]{1,0:T(8,128)S(1)}, u32[]{:S(2)}, u32[]{:S(2)}) %collective-permute-start.1) | collective-permute-done | bytes 69664 | tf_op jit(solution)/shard_map/ppermute | solution.py:490
  14.0 1.6 %collective-permute-done.4.refs_0_ = bf16[256,128]{1,0:T(8,128)(2,1)S(1)} collective-permute-done((bf16[256,128]{1,0:T(8,128)(2,1)S(1)}, bf16[256,128]{1,0:T(8,128)(2,1)S(1)}, u32[]{:S(2)}, u32[]{:S(2)}) %collective-permute-start.4) | collective-permute-done | bytes 65568 | tf_op jit(solution)/shard_map/ppermute | solution.py:490
  15.6 0.5 collective-permute-start.5
  16.1 2.6 %collective-permute-start.2 = (f32[136,128]{1,0:T(8,128)S(1)}, f32[136,128]{1,0:T(8,128)S(1)}, u32[]{:S(2)}, u32[]{:S(2)}) collective-permute-start(f32[136,128]{1,0:T(8,128)S(1)} %add.34), channel_id=1, source_target_pairs={{0,16},{4,20},{8,24},{12,28},{16,0},{20,4},{24,8},{28,12},{1,17},{... | collective-permute-start | bytes 208904 | tf_op jit(solution)/shard_map/ppermute | solution.py:490
  18.7 1.2 %collective-permute-done.5.refs_1_ = bf16[256,128]{1,0:T(8,128)(2,1)S(1)} collective-permute-done((bf16[256,128]{1,0:T(8,128)(2,1)S(1)}, bf16[256,128]{1,0:T(8,128)(2,1)S(1)}, u32[]{:S(2)}, u32[]{:S(2)}) %collective-permute-start.5) | collective-permute-done | bytes 65568 | tf_op jit(solution)/shard_map/ppermute | solution.py:490
  20.0 3.0 %collective-permute-start.6 = (bf16[256,128]{1,0:T(8,128)(2,1)S(1)}, bf16[256,128]{1,0:T(8,128)(2,1)S(1)}, u32[]{:S(2)}, u32[]{:S(2)}) collective-permute-start(bf16[256,128]{1,0:T(8,128)(2,1)S(1)} %add_convert_fusion.2), channel_id=1, source_target_pairs={{0,16},{4,20},{8,24},{12,28},{16,0},{20,4},{24,8},{28,12},{1,17},{... | collective-permute-start | bytes 196616 | tf_op jit(solution)/shard_map/ppermute | solution.py:490
  23.0 0.7 %shard_map.94.refs_0_ = f32[1024,256]{1,0:T(8,128)S(1)} custom-call(bf16[256,2048]{1,0:T(8,128)(2,1)S(1)} %copy-done, bf16[1024,512]{1,0:T(8,128)(2,1)S(1)} %copy-done.1, bf16[1024,512]{1,0:T(8,128)(2,1)S(1)} %collective-permute-done.3.refs_1_), custom_call_target="tpu_custom_call" | custom-call | flops 536870912 | bytes 4000000 | tf_op jit(solution)/shard_map/pallas_call | solution.py:406
  23.8 4.1 %shard_map.95 = (bf16[8,8,128,128]{3,2,1,0:T(8,128)(2,1)S(1)}, bf16[8,8,128,128]{3,2,1,0:T(8,128)(2,1)S(1)}, f32[8,128,128]{2,1,0:T(8,128)S(1)}, f32[8,128,128]{2,1,0:T(8,128)S(1)}) custom-call(bf16[1024,256]{1,0:T(8,128)(2,1)S(1)} %copy-done.2, f32[136,128]{1,0:T(8,128)S(1)} %collective-permute-done.refs_0_, f32[136,128]{1,0:T(8,128)S(1)} %collective-permute-done.1.refs_1_, ...), custom_call_target="tpu_custom_call" | custom-call | flops 2000000000 | bytes 8000000 | tf_op jit(solution)/shard_map/pallas_call | solution.py:181
  27.9 1.1 %collective-permute-done.7.refs_1_.refs_2_ = bf16[1024,512]{1,0:T(8,128)(2,1)S(1)} collective-permute-done((bf16[1024,512]{1,0:T(8,128)(2,1)S(1)}, bf16[1024,512]{1,0:T(8,128)(2,1)S(1)}, u32[]{:S(2)}, u32[]{:S(2)}) %collective-permute-start.7) | collective-permute-done | bytes 1048608 | tf_op jit(solution)/shard_map/ppermute | solution.py:490
  29.0 0.1 shard_map.100
  29.1 1.8 %collective-permute-start.15 = (bf16[2,256,512]{2,1,0:T(8,128)(2,1)S(1)}, bf16[2,256,512]{2,1,0:T(8,128)(2,1)S(1)}, u32[]{:S(2)}, u32[]{:S(2)}) collective-permute-start(bf16[2,256,512]{2,1,0:T(8,128)(2,1)S(1)} %get-tuple-element.89), channel_id=1, source_target_pairs={{0,2},{1,3},{2,0},{3,1},{4,6},{5,7},{6,4},{7,5},{8,10},{9,11},{10,... | collective-permute-start | bytes 1572872 | tf_op jit(solution)/shard_map/ppermute | solution.py:490
  30.9 2.4 %shard_map.96 = (bf16[1024,256]{1,0:T(8,128)(2,1)S(1)}, bf16[8,128,256]{2,1,0:T(8,128)(2,1)S(1)}, bf16[8,256,256]{2,1,0:T(8,128)(2,1)S(1)}, bf16[8,256,256]{2,1,0:T(8,128)(2,1)S(1)}) custom-call(bf16[1024,256]{1,0:T(8,128)(2,1)S(1)} %copy-done.4, bf16[1024,256]{1,0:T(8,128)(2,1)S(1)} %copy-done.2, bf16[1024,256]{1,0:T(8,128)(2,1)S(1)} %copy-done.3, ...), custom_call_target="tpu_custom_call" | custom-call | flops 2000000000 | bytes 8000000 | tf_op jit(solution)/shard_map/pallas_call | solution.py:218
  33.3 0.8 %shard_map.97.do_ref = bf16[1024,256]{1,0:T(8,128)(2,1)S(1)} custom-call(bf16[256,2048]{1,0:T(8,128)(2,1)S(1)} %copy-done, f32[1024,256]{1,0:T(8,128)S(1)} %shard_map.94.refs_0_, bf16[1024,512]{1,0:T(8,128)(2,1)S(1)} %collective-permute-done.7.refs_1_.refs_2_, bf16[1024,512]{1,0:T(8,128)(2,1)S(1)} %collective-permute-done.8.refs_2_.refs_3_), custom_call_target="tpu_custom_call" | custom-call | flops 536870912 | bytes 4000000 | tf_op jit(solution)/shard_map/pallas_call | solution.py:406
  34.1 1.4 %shard_map.98 = (bf16[2,256,256]{2,1,0:T(8,128)(2,1)S(1)}, bf16[2,256,256]{2,1,0:T(8,128)(2,1)S(1)}, bf16[2,256,256]{2,1,0:T(8,128)(2,1)S(1)}, bf16[2,256,256]{2,1,0:T(8,128)(2,1)S(1)}) custom-call(bf16[1024,256]{1,0:T(8,128)(2,1)S(1)} %get-tuple-element.77.h_ref.refs_0_, bf16[1024,512]{1,0:T(8,128)(2,1)S(1)} %copy-done.1, ...), custom_call_target="tpu_custom_call" | custom-call | flops 1073741824 | bytes 6000000 | tf_op jit(solution)/shard_map/pallas_call | solution.py:456
  35.5 1.6 %collective-permute-start.12 = (bf16[2,256,256]{2,1,0:T(8,128)(2,1)S(1)}, bf16[2,256,256]{2,1,0:T(8,128)(2,1)S(1)}, u32[]{:S(2)}, u32[]{:S(2)}) collective-permute-start(bf16[2,256,256]{2,1,0:T(8,128)(2,1)S(1)} %get-tuple-element.80), channel_id=1, source_target_pairs={{0,4},{4,0},{8,12},{12,8},{16,20},{20,16},{24,28},{28,24},{1,5},{5... | collective-permute-start | bytes 786440 | tf_op jit(solution)/shard_map/ppermute | solution.py:490
  37.1 6.6 %shard_map.99 = (bf16[8,256,256]{2,1,0:T(8,128)(2,1)S(1)}, bf16[1024,256]{1,0:T(8,128)(2,1)S(1)}, f32[8,128,128]{2,1,0:T(8,128)S(1)}, f32[8,128,128]{2,1,0:T(8,1...) custom-call(bf16[1024,256]{1,0:T(8,128)(2,1)S(1)} %copy-done.4, bf16[1024,256]{1,0:T(8,128)(2,1)S(1)} %copy-done.2, ...), custom_call_target="tpu_custom_call" | custom-call | flops 4000000000 | bytes 8000000 | tf_op jit(solution)/shard_map/pallas_call | solution.py:290
  43.7 0.5 collective-permute-start.11
  44.2 1.6 %collective-permute-start.18 = (bf16[2,256,256]{2,1,0:T(8,128)(2,1)S(1)}, bf16[2,256,256]{2,1,0:T(8,128)(2,1)S(1)}, u32[]{:S(2)}, u32[]{:S(2)}) collective-permute-start(bf16[2,256,256]{2,1,0:T(8,128)(2,1)S(1)} %get-tuple-element.69), channel_id=1, source_target_pairs={{0,4},{4,0},{8,12},{12,8},{16,20},{20,16},{24,28},{28,24},{1,5},{5... | collective-permute-start | bytes 786440 | tf_op jit(solution)/shard_map/ppermute | solution.py:490
  45.8 0.5 collective-permute-start.10
  46.3 0.1 add_convert_fusion
  46.4 3.1 %collective-permute-done.11.refs_0_ = bf16[392,128]{1,0:T(8,128)(2,1)S(1)} collective-permute-done((bf16[392,128]{1,0:T(8,128)(2,1)S(1)}, bf16[392,128]{1,0:T(8,128)(2,1)S(1)}, u32[]{:S(2)}, u32[]{:S(2)}) %collective-permute-start.11) | collective-permute-done | bytes 100384 | tf_op jit(solution)/shard_map/ppermute | solution.py:490
  49.5 3.6 %collective-permute-start.20 = (bf16[256,256]{1,0:T(8,128)(2,1)S(1)}, bf16[256,256]{1,0:T(8,128)(2,1)S(1)}, u32[]{:S(2)}, u32[]{:S(2)}) collective-permute-start(bf16[256,256]{1,0:T(8,128)(2,1)S(1)} %get-tuple-element.113), channel_id=1, source_target_pairs={{0,24},{4,28},{8,16},{12,20},{16,8},{20,12},{24,0},{28,4},{1,25},{... | collective-permute-start | bytes 393224 | tf_op jit(solution)/shard_map/ppermute | solution.py:490
  53.1 0.1 collective-permute-start.13
  53.2 0.9 %collective-permute-done.18 = bf16[2,256,256]{2,1,0:T(8,128)(2,1)S(1)} collective-permute-done((bf16[2,256,256]{2,1,0:T(8,128)(2,1)S(1)}, bf16[2,256,256]{2,1,0:T(8,128)(2,1)S(1)}, u32[]{:S(2)}, u32[]{:S(2)}) %collective-permute-start.18) | collective-permute-done | bytes 262176 | tf_op jit(solution)/shard_map/ppermute | solution.py:490
  54.1 0.1 slice_bitcast_fusion.3
  54.1 0.1 pad_maximum_fusion
  54.2 0.1 collective-permute-start.16
  54.3 0.1 convert_add_fusion
  54.4 3.4 %collective-permute-done.13.refs_1_ = bf16[392,128]{1,0:T(8,128)(2,1)S(1)} collective-permute-done((bf16[392,128]{1,0:T(8,128)(2,1)S(1)}, bf16[392,128]{1,0:T(8,128)(2,1)S(1)}, u32[]{:S(2)}, u32[]{:S(2)}) %collective-permute-start.13) | collective-permute-done | bytes 100384 | tf_op jit(solution)/shard_map/ppermute | solution.py:490
  57.8 0.2 collective-permute-start.17
  58.0 0.9 %collective-permute-done.10.refs_2_ = bf16[1024,256]{1,0:T(8,128)(2,1)S(1)} collective-permute-done((bf16[1024,256]{1,0:T(8,128)(2,1)S(1)}, bf16[1024,256]{1,0:T(8,128)(2,1)S(1)}, u32[]{:S(2)}, u32[]{:S(2)}) %collective-permute-start.10) | collective-permute-done | bytes 524320 | tf_op jit(solution)/shard_map/ppermute | solution.py:490
  59.0 2.2 %shard_map.102 = (bf16[1024,256]{1,0:T(8,128)(2,1)}, f32[1024,256]{1,0:T(8,128)S(1)}, f32[1024,256]{1,0:T(8,128)S(1)}) custom-call(bf16[1024,256]{1,0:T(8,128)(2,1)S(1)} %copy-done.2, bf16[1024,256]{1,0:T(8,128)(2,1)S(1)} %copy-done.3, bf16[1024,256]{1,0:T(8,128)(2,1)S(1)} %shard_map.97.do_ref, f32[8,128,128]{2,1,0:T(8,128)S(1)} %get-tuple-element.60.last_ref, ...), custom_call_target="tpu_custom_call" | custom-call | flops 2000000000 | bytes 6000000 | tf_op jit(solution)/shard_map/pallas_call | solution.py:328
  61.2 3.3 %collective-permute-done.17.refs_2_ = bf16[392,128]{1,0:T(8,128)(2,1)S(1)} collective-permute-done((bf16[392,128]{1,0:T(8,128)(2,1)S(1)}, bf16[392,128]{1,0:T(8,128)(2,1)S(1)}, u32[]{:S(2)}, u32[]{:S(2)}) %collective-permute-start.17) | collective-permute-done | bytes 100384 | tf_op jit(solution)/shard_map/ppermute | solution.py:490
  64.5 1.4 %shard_map.103 = (bf16[1024,256]{1,0:T(8,128)(2,1)}, bf16[1024,256]{1,0:T(8,128)(2,1)}) custom-call(bf16[1024,256]{1,0:T(8,128)(2,1)S(1)} %copy-done.2, bf16[1024,256]{1,0:T(8,128)(2,1)S(1)} %copy-done.3, f32[1024,256]{1,0:T(8,128)S(1)} %get-tuple-element.98.dk_ref, f32[1024,256]{1,0:T(8,128)S(1)} %get-tuple-element.99.dv_ref, ...), custom_call_target="tpu_custom_call" | custom-call | flops 1000000000 | bytes 6000000 | tf_op jit(solution)/shard_map/pallas_call | solution.py:365
  65.9 2.4 %collective-permute-start.21 = (bf16[256,256]{1,0:T(8,128)(2,1)S(1)}, bf16[256,256]{1,0:T(8,128)(2,1)S(1)}, u32[]{:S(2)}, u32[]{:S(2)}) collective-permute-start(bf16[256,256]{1,0:T(8,128)(2,1)S(1)} %fusion.4), channel_id=1, source_target_pairs={{0,8},{4,12},{8,0},{12,4},{16,24},{20,28},{24,16},{28,20},{1,9},{5... | collective-permute-start | bytes 393224 | tf_op jit(solution)/shard_map/ppermute | solution.py:490
  68.4 2.2 %shard_map.101 = bf16[1024,512]{1,0:T(8,128)(2,1)} custom-call(bf16[1024,256]{1,0:T(8,128)(2,1)S(1)} %get-tuple-element.77.h_ref.refs_0_, bf16[1024,256]{1,0:T(8,128)(2,1)S(1)} %collective-permute-done.9.refs_1_, bf16[1024,256]{1,0:T(8,128)(2,1)S(1)} %collective-permute-done.10.refs_2_, bf16[1024,256]{1,0:T(8,128)(2,1)S(1)} %collective-permute-done.14.refs_3_, ...), custom_call_target="tpu_custom_call" | custom-call | flops 1073741824 | bytes 6000000 | tf_op jit(solution)/shard_map/pallas_call | solution.py:478
  70.6 2.5 %collective-permute-done.21 = bf16[256,256]{1,0:T(8,128)(2,1)S(1)} collective-permute-done((bf16[256,256]{1,0:T(8,128)(2,1)S(1)}, bf16[256,256]{1,0:T(8,128)(2,1)S(1)}, u32[]{:S(2)}, u32[]{:S(2)}) %collective-permute-start.21) | collective-permute-done | bytes 131104 | tf_op jit(solution)/shard_map/ppermute | solution.py:490
  73.1 0.8 %fusion.2 = f32[256,256]{1,0:T(8,128)} fusion(f32[2,256,256]{2,1,0:T(8,128)S(1)} %convert_add_fusion, bf16[256,256]{1,0:T(8,128)(2,1)S(1)} %collective-permute-done.21, bf16[256,256]{1,0:T(8,128)(2,1)S(1)} %collective-permute-done.20, bf16[256,256]{1,0:T(8,128)(2,1)S(1)} %collective-permute-done.19), kind=kLoop, calls=%fused_computation.7 | loop fusion | flops 393216 | bytes 917504 | tf_op jit(solution)/shard_map/add | solution.py:579
  (33 shorter events, 0.3 us)
Async XLA Ops:
  0.6 1.0 %copy-start.2 = (bf16[1024,256]{1,0:T(8,128)(2,1)S(1)}, bf16[1024,256]{1,0:T(8,128)(2,1)}, u32[]{:S(2)}) copy-start(bf16[1024,256]{1,0:T(8,128)(2,1)} %k_ref.11) | copy-start | bytes 1572868
  0.6 1.2 %copy-start.3 = (bf16[1024,256]{1,0:T(8,128)(2,1)S(1)}, bf16[1024,256]{1,0:T(8,128)(2,1)}, u32[]{:S(2)}) copy-start(bf16[1024,256]{1,0:T(8,128)(2,1)} %v_ref.9) | copy-start | bytes 1572868
  0.7 1.5 %copy-start.1 = (bf16[1024,512]{1,0:T(8,128)(2,1)S(1)}, bf16[1024,512]{1,0:T(8,128)(2,1)}, u32[]{:S(2)}) copy-start(bf16[1024,512]{1,0:T(8,128)(2,1)} %refs_0_.3) | copy-start | bytes 3145732
  0.7 22.3 %copy-start = (bf16[256,2048]{1,0:T(8,128)(2,1)S(1)}, bf16[256,2048]{1,0:T(8,128)(2,1)}, u32[]{:S(2)}) copy-start(bf16[256,2048]{1,0:T(8,128)(2,1)} %w_ref.4) | copy-start | bytes 3145732
  2.2 20.8 %collective-permute-start.3 = (bf16[1024,512]{1,0:T(8,128)(2,1)S(1)}, bf16[1024,512]{1,0:T(8,128)(2,1)S(1)}, u32[]{:S(2)}, u32[]{:S(2)}) collective-permute-start(bf16[1024,512]{1,0:T(8,128)(2,1)S(1)} %copy-done.1), channel_id=1, source_target_pairs={{0,1},{1,0},{2,3},{3,2},{4,5},{5,4},{6,7},{7,6},{8,9},{9,8},{10,11... | collective-permute-start | bytes 3145736 | tf_op jit(solution)/shard_map/ppermute | solution.py:490
  2.7 26.3 %collective-permute-start.7 = (bf16[1024,512]{1,0:T(8,128)(2,1)S(1)}, bf16[1024,512]{1,0:T(8,128)(2,1)S(1)}, u32[]{:S(2)}, u32[]{:S(2)}) collective-permute-start(bf16[1024,512]{1,0:T(8,128)(2,1)S(1)} %copy-done.1), channel_id=1, source_target_pairs={{0,2},{1,3},{2,0},{3,1},{4,6},{5,7},{6,4},{7,5},{8,10},{9,11},{10,... | collective-permute-start | bytes 3145736 | tf_op jit(solution)/shard_map/ppermute | solution.py:490
  5.3 4.3 %collective-permute-start = (f32[136,128]{1,0:T(8,128)S(1)}, f32[136,128]{1,0:T(8,128)S(1)}, u32[]{:S(2)}, u32[]{:S(2)}) collective-permute-start(f32[136,128]{1,0:T(8,128)S(1)} %get-tuple-element.56), channel_id=1, source_target_pairs={{0,4},{4,0},{8,12},{12,8},{16,20},{20,16},{24,28},{28,24},{1,5},{5... | collective-permute-start | bytes 208904 | tf_op jit(solution)/shard_map/ppermute | solution.py:490
  9.6 4.4 %collective-permute-start.1 = (f32[136,128]{1,0:T(8,128)S(1)}, f32[136,128]{1,0:T(8,128)S(1)}, u32[]{:S(2)}, u32[]{:S(2)}) collective-permute-start(f32[136,128]{1,0:T(8,128)S(1)} %add.33), channel_id=1, source_target_pairs={{0,8},{4,12},{8,0},{12,4},{16,24},{20,28},{24,16},{28,20},{1,9},{5... | collective-permute-start | bytes 208904 | tf_op jit(solution)/shard_map/ppermute | solution.py:490
  11.3 4.3 %collective-permute-start.4 = (bf16[256,128]{1,0:T(8,128)(2,1)S(1)}, bf16[256,128]{1,0:T(8,128)(2,1)S(1)}, u32[]{:S(2)}, u32[]{:S(2)}) collective-permute-start(bf16[256,128]{1,0:T(8,128)(2,1)S(1)} %convert_element_type.60), channel_id=1, source_target_pairs={{0,4},{4,0},{8,12},{12,8},{16,20},{20,16},{24,28},{28,24},{1,5},{5... | collective-permute-start | bytes 196616 | tf_op jit(solution)/shard_map/ppermute | solution.py:490
  15.6 4.3 %collective-permute-start.5 = (bf16[256,128]{1,0:T(8,128)(2,1)S(1)}, bf16[256,128]{1,0:T(8,128)(2,1)S(1)}, u32[]{:S(2)}, u32[]{:S(2)}) collective-permute-start(bf16[256,128]{1,0:T(8,128)(2,1)S(1)} %fusion.5), channel_id=1, source_target_pairs={{0,8},{4,12},{8,0},{12,4},{16,24},{20,28},{24,16},{28,20},{1,9},{5... | collective-permute-start | bytes 196616 | tf_op jit(solution)/shard_map/ppermute | solution.py:490
  16.1 7.6 %collective-permute-start.2 = (f32[136,128]{1,0:T(8,128)S(1)}, f32[136,128]{1,0:T(8,128)S(1)}, u32[]{:S(2)}, u32[]{:S(2)}) collective-permute-start(f32[136,128]{1,0:T(8,128)S(1)} %add.34), channel_id=1, source_target_pairs={{0,16},{4,20},{8,24},{12,28},{16,0},{20,4},{24,8},{28,12},{1,17},{... | collective-permute-start | bytes 208904 | tf_op jit(solution)/shard_map/ppermute | solution.py:490
  20.0 7.9 %collective-permute-start.6 = (bf16[256,128]{1,0:T(8,128)(2,1)S(1)}, bf16[256,128]{1,0:T(8,128)(2,1)S(1)}, u32[]{:S(2)}, u32[]{:S(2)}) collective-permute-start(bf16[256,128]{1,0:T(8,128)(2,1)S(1)} %add_convert_fusion.2), channel_id=1, source_target_pairs={{0,16},{4,20},{8,24},{12,28},{16,0},{20,4},{24,8},{28,12},{1,17},{... | collective-permute-start | bytes 196616 | tf_op jit(solution)/shard_map/ppermute | solution.py:490
  23.8 7.2 %copy-start.4 = (bf16[1024,256]{1,0:T(8,128)(2,1)S(1)}, bf16[1024,256]{1,0:T(8,128)(2,1)}, u32[]{:S(2)}) copy-start(bf16[1024,256]{1,0:T(8,128)(2,1)} %q_ref.3) | copy-start | bytes 1572868
  29.0 4.3 %collective-permute-start.8 = (bf16[1024,512]{1,0:T(8,128)(2,1)S(1)}, bf16[1024,512]{1,0:T(8,128)(2,1)S(1)}, u32[]{:S(2)}, u32[]{:S(2)}) collective-permute-start(bf16[1024,512]{1,0:T(8,128)(2,1)S(1)} %collective-permute-done.7.refs_1_.refs_2_), channel_id=1, source_target_pairs={{0,1},{1,0},{2,3},{3,2},{4,5},{5,4},{6,7},{7,6},{8,9},{9,8},{10,11... | collective-permute-start | bytes 3145736 | tf_op jit(solution)/shard_map/ppermute | solution.py:490
  29.1 23.9 %collective-permute-start.15 = (bf16[2,256,512]{2,1,0:T(8,128)(2,1)S(1)}, bf16[2,256,512]{2,1,0:T(8,128)(2,1)S(1)}, u32[]{:S(2)}, u32[]{:S(2)}) collective-permute-start(bf16[2,256,512]{2,1,0:T(8,128)(2,1)S(1)} %get-tuple-element.89), channel_id=1, source_target_pairs={{0,2},{1,3},{2,0},{3,1},{4,6},{5,7},{6,4},{7,5},{8,10},{9,11},{10,... | collective-permute-start | bytes 1572872 | tf_op jit(solution)/shard_map/ppermute | solution.py:490
  35.5 10.8 %collective-permute-start.12 = (bf16[2,256,256]{2,1,0:T(8,128)(2,1)S(1)}, bf16[2,256,256]{2,1,0:T(8,128)(2,1)S(1)}, u32[]{:S(2)}, u32[]{:S(2)}) collective-permute-start(bf16[2,256,256]{2,1,0:T(8,128)(2,1)S(1)} %get-tuple-element.80), channel_id=1, source_target_pairs={{0,4},{4,0},{8,12},{12,8},{16,20},{20,16},{24,28},{28,24},{1,5},{5... | collective-permute-start | bytes 786440 | tf_op jit(solution)/shard_map/ppermute | solution.py:490
  43.7 5.8 %collective-permute-start.11 = (bf16[392,128]{1,0:T(8,128)(2,1)S(1)}, bf16[392,128]{1,0:T(8,128)(2,1)S(1)}, u32[]{:S(2)}, u32[]{:S(2)}) collective-permute-start(bf16[392,128]{1,0:T(8,128)(2,1)S(1)} %get-tuple-element.76), channel_id=1, source_target_pairs={{0,4},{4,0},{8,12},{12,8},{16,20},{20,16},{24,28},{28,24},{1,5},{5... | collective-permute-start | bytes 301064 | tf_op jit(solution)/shard_map/ppermute | solution.py:490
  44.2 9.8 %collective-permute-start.18 = (bf16[2,256,256]{2,1,0:T(8,128)(2,1)S(1)}, bf16[2,256,256]{2,1,0:T(8,128)(2,1)S(1)}, u32[]{:S(2)}, u32[]{:S(2)}) collective-permute-start(bf16[2,256,256]{2,1,0:T(8,128)(2,1)S(1)} %get-tuple-element.69), channel_id=1, source_target_pairs={{0,4},{4,0},{8,12},{12,8},{16,20},{20,16},{24,28},{28,24},{1,5},{5... | collective-permute-start | bytes 786440 | tf_op jit(solution)/shard_map/ppermute | solution.py:490
  45.8 13.2 %collective-permute-start.10 = (bf16[1024,256]{1,0:T(8,128)(2,1)S(1)}, bf16[1024,256]{1,0:T(8,128)(2,1)S(1)}, u32[]{:S(2)}, u32[]{:S(2)}) collective-permute-start(bf16[1024,256]{1,0:T(8,128)(2,1)S(1)} %get-tuple-element.77.h_ref.refs_0_), channel_id=1, source_target_pairs={{0,2},{1,3},{2,0},{3,1},{4,6},{5,7},{6,4},{7,5},{8,10},{9,11},{10,... | collective-permute-start | bytes 1572872 | tf_op jit(solution)/shard_map/ppermute | solution.py:490
  46.3 22.0 %collective-permute-start.9 = (bf16[1024,256]{1,0:T(8,128)(2,1)S(1)}, bf16[1024,256]{1,0:T(8,128)(2,1)S(1)}, u32[]{:S(2)}, u32[]{:S(2)}) collective-permute-start(bf16[1024,256]{1,0:T(8,128)(2,1)S(1)} %get-tuple-element.77.h_ref.refs_0_), channel_id=1, source_target_pairs={{0,1},{1,0},{2,3},{3,2},{4,5},{5,4},{6,7},{7,6},{8,9},{9,8},{10,11... | collective-permute-start | bytes 1572872 | tf_op jit(solution)/shard_map/ppermute | solution.py:490
  49.5 23.6 %collective-permute-start.20 = (bf16[256,256]{1,0:T(8,128)(2,1)S(1)}, bf16[256,256]{1,0:T(8,128)(2,1)S(1)}, u32[]{:S(2)}, u32[]{:S(2)}) collective-permute-start(bf16[256,256]{1,0:T(8,128)(2,1)S(1)} %get-tuple-element.113), channel_id=1, source_target_pairs={{0,24},{4,28},{8,16},{12,20},{16,8},{20,12},{24,0},{28,4},{1,25},{... | collective-permute-start | bytes 393224 | tf_op jit(solution)/shard_map/ppermute | solution.py:490
  53.1 4.7 %collective-permute-start.13 = (bf16[392,128]{1,0:T(8,128)(2,1)S(1)}, bf16[392,128]{1,0:T(8,128)(2,1)S(1)}, u32[]{:S(2)}, u32[]{:S(2)}) collective-permute-start(bf16[392,128]{1,0:T(8,128)(2,1)S(1)} %fusion.3), channel_id=1, source_target_pairs={{0,8},{4,12},{8,0},{12,4},{16,24},{20,28},{24,16},{28,20},{1,9},{5... | collective-permute-start | bytes 301064 | tf_op jit(solution)/shard_map/ppermute | solution.py:490
  54.2 11.7 %collective-permute-start.16 = (bf16[2,256,512]{2,1,0:T(8,128)(2,1)S(1)}, bf16[2,256,512]{2,1,0:T(8,128)(2,1)S(1)}, u32[]{:S(2)}, u32[]{:S(2)}) collective-permute-start(bf16[2,256,512]{2,1,0:T(8,128)(2,1)S(1)} %pad_maximum_fusion), channel_id=1, source_target_pairs={{0,1},{1,0},{2,3},{3,2},{4,5},{5,4},{6,7},{7,6},{8,9},{9,8},{10,11... | collective-permute-start | bytes 1572872 | tf_op jit(solution)/shard_map/ppermute | solution.py:490
  57.8 6.7 %collective-permute-start.17 = (bf16[392,128]{1,0:T(8,128)(2,1)S(1)}, bf16[392,128]{1,0:T(8,128)(2,1)S(1)}, u32[]{:S(2)}, u32[]{:S(2)}) collective-permute-start(bf16[392,128]{1,0:T(8,128)(2,1)S(1)} %add_convert_fusion.1), channel_id=1, source_target_pairs={{0,16},{4,20},{8,24},{12,28},{16,0},{20,4},{24,8},{28,12},{1,17},{... | collective-permute-start | bytes 301064 | tf_op jit(solution)/shard_map/ppermute | solution.py:490
  59.0 9.4 %collective-permute-start.14 = (bf16[1024,256]{1,0:T(8,128)(2,1)S(1)}, bf16[1024,256]{1,0:T(8,128)(2,1)S(1)}, u32[]{:S(2)}, u32[]{:S(2)}) collective-permute-start(bf16[1024,256]{1,0:T(8,128)(2,1)S(1)} %collective-permute-done.10.refs_2_), channel_id=1, source_target_pairs={{0,1},{1,0},{2,3},{3,2},{4,5},{5,4},{6,7},{7,6},{8,9},{9,8},{10,11... | collective-permute-start | bytes 1572872 | tf_op jit(solution)/shard_map/ppermute | solution.py:490
  64.5 8.6 %collective-permute-start.19 = (bf16[256,256]{1,0:T(8,128)(2,1)S(1)}, bf16[256,256]{1,0:T(8,128)(2,1)S(1)}, u32[]{:S(2)}, u32[]{:S(2)}) collective-permute-start(bf16[256,256]{1,0:T(8,128)(2,1)S(1)} %get-tuple-element.114), channel_id=1, source_target_pairs={{0,16},{4,20},{8,24},{12,28},{16,0},{20,4},{24,8},{28,12},{1,17},{... | collective-permute-start | bytes 393224 | tf_op jit(solution)/shard_map/ppermute | solution.py:490
  65.9 7.2 %collective-permute-start.21 = (bf16[256,256]{1,0:T(8,128)(2,1)S(1)}, bf16[256,256]{1,0:T(8,128)(2,1)S(1)}, u32[]{:S(2)}, u32[]{:S(2)}) collective-permute-start(bf16[256,256]{1,0:T(8,128)(2,1)S(1)} %fusion.4), channel_id=1, source_target_pairs={{0,8},{4,12},{8,0},{12,4},{16,24},{20,28},{24,16},{28,20},{1,9},{5... | collective-permute-start | bytes 393224 | tf_op jit(solution)/shard_map/ppermute | solution.py:490

commit v9 on v8

--- a/solution.py
+++ b/solution.py
@@ -504,8 +504,8 @@
     head_count, ctx_count = lax.axis_size("head"), lax.axis_size("ctx")
     evens = range(2, head_count, 2)
 
+    far = {s: swap(cotangent, "head", s) for s in evens}
     begin = lead()
-    far = {s: swap(after(cotangent, begin), "head", s) for s in evens}
     gram, pair = totals(begin, keys, values, heads)
     near = swap(after(cotangent, gram, pair), "head", 1)
 
@@ -539,12 +539,12 @@
         after(heads_out, grads), parts, ctx_count
     )
     high = swap(odd_high, "ctx", 1)
-    low = swap(odd_low, "ctx", 1)
 
     weights, ds, da, dn, sums, send = tangent(
         queries, keys, values, after(grads, odd_low), [*stash, last, ridged, states, solved]
     )
 
+    low = swap(after(odd_low, send), "ctx", 1)
     outs_out = after(heads_out, send)
     outs_far = [swap(outs_out, "head", s) for s in evens]
     high = even_high.astype(F32) + after(high, send).astype(F32)
@@ -552,26 +552,27 @@
     high = [high[u].astype(BF16) for u in range(half)]
     moved = [swap(part, "ctx", 2 * (half + u)) for u, part in enumerate(high)]
 
-    later = []
+    later, sends = [], []
     for distance in doublings("ctx"):
-        sent = send
+        sends.append(send)
         later.append(swap(send, "ctx", distance))
         if distance == 1:
             later[0] = after(later[0], *high)
         sums = sums + later[-1].astype(F32)
         send = sums.astype(BF16)
 
-    low = even_low.astype(F32) + after(low, later[0]).astype(F32)
+    low = even_low.astype(F32) + after(low, sends[1]).astype(F32)
     moved += [swap(low[u].astype(BF16), "ctx", 2 * u) for u in range(1, half)]
 
     outs = [heads_out, swap(outs_out, "head", 1)]
     for part in outs_far:
-        outs += [part, swap(after(part, sent), "head", 1)]
-    columns = [after(c, later[0]) for c in columns]
-    crossing = swap(jnp.stack([c[1] for c in columns]), "head", 1)
+        outs += [part, swap(after(part, sends[-1]), "head", 1)]
+    columns = [after(c, sends[1]) for c in columns]
+    crossing = jnp.stack([c[1] for c in columns])
+    crossing = swap(crossing, "head", 1)
     columns = [c for s in range(head_count // 2) for c in (columns[s][0], crossing[s])]
     grad_queries, dk, dv = rest(
-        keys, values, grads, last, solved, scores, weights, after(ds, sent), da, dn
+        keys, values, grads, last, solved, scores, weights, after(ds, sends[-1]), da, dn
     )
     layer_out = layer(outs, columns)
     grad_weight = low[0]

time: 74 us -> 75.1 us (1.015)
  starting transfers between devices: 26.3 us -> 32.8 us
  waiting for transfers between devices: 22.1 us -> 16.7 us
    ppermute x22, starting transfers between devices: 26.3 us -> 32.8 us  [swap(): return lax.ppermute(value, axis, [(i, i ^ distance) for i in range(count)])]
    ppermute x22, waiting for transfers between devices: 22.1 us -> 16.7 us  [swap(): return lax.ppermute(value, axis, [(i, i ^ distance) for i in range(count)])]
  transfers between devices with their start and end apart: 22 -> 22, of which waited for: 11 -> 10; matrix products, arithmetic and copies ran while one was open for 1% -> 1% of each run, Pallas kernels for 30% -> 29%
where the time goes in v9:
time: 75.1 us; the launch traced here: 75 us
  starting transfers between devices  32.8 us (44%)
  Pallas kernels  22.2 us (30%)
  waiting for transfers between devices  16.7 us (22%)
  local copies, waits for them, and re-layouts  1.32 us (2%)
  other arithmetic  1.09 us (1%)
  between operations  0.87 us (1%)
    ppermute x22, starting transfers between devices, swap(): return lax.ppermute(value, axis, [(i, i ^ distance) for i in range(count)])  32.8 us
    ppermute x22, waiting for transfers between devices, swap(): return lax.ppermute(value, axis, [(i, i ^ distance) for i in range(count)])  16.7 us
    pallas_call x1, Pallas kernels, tangent(): pl.pallas_call(tangent_kernel, out_shape=(shape((count, SPAN, SPAN), BF16...  6.64 us
    pallas_call x1, Pallas kernels, inverses(): pl.pallas_call(functools.partial(inverse_kernel, len(grams)), out_shape=(...  4.12 us
    pallas_call x1, Pallas kernels, outputs(): pl.pallas_call(functools.partial(outputs_kernel, len(pairs)), out_shape=(...  2.39 us
    pallas_call x1, Pallas kernels, layer(): pl.pallas_call(layer_kernel, out_shape=shape((rows, cols), BF16), in_spec...  2.22 us
    pallas_call x1, Pallas kernels, rest(): pl.pallas_call(rest_kernel, out_shape=(shape(keys.shape, BF16), wide, wid...  2.18 us
  transfers between devices with their start and end apart: 22, of which 10 were waited for; matrix products, arithmetic and copies ran while one was open for 1% of the time, Pallas kernels for 29%

profile of v9, /device:TPU:0, one launch (start us, length us, event | category | flops | bytes accessed | tf_op | source)
XLA Modules:
  0.0 75.0 jit_solution(5373083840120858981)
XLA Ops:
  0.7 1.0 %copy-done.2 = bf16[1024,256]{1,0:T(8,128)(2,1)S(1)} copy-done((bf16[1024,256]{1,0:T(8,128)(2,1)S(1)}, bf16[1024,256]{1,0:T(8,128)(2,1)}, u32[]{:S(2)}) %copy-start.2) | copy-done | bytes 524312
  1.7 0.2 copy-done.3
  1.8 0.3 shard_map.93
  2.2 0.0 copy-done.1
  2.2 0.6 collective-permute-start.3
  2.7 2.6 %collective-permute-start.7 = (bf16[1024,512]{1,0:T(8,128)(2,1)S(1)}, bf16[1024,512]{1,0:T(8,128)(2,1)S(1)}, u32[]{:S(2)}, u32[]{:S(2)}) collective-permute-start(bf16[1024,512]{1,0:T(8,128)(2,1)S(1)} %copy-done.1), channel_id=1, source_target_pairs={{0,2},{1,3},{2,0},{3,1},{4,6},{5,7},{6,4},{7,5},{8,10},{9,11},{10,... | collective-permute-start | bytes 3145736 | tf_op jit(solution)/shard_map/ppermute | solution.py:490
  5.3 1.5 %collective-permute-start = (f32[136,128]{1,0:T(8,128)S(1)}, f32[136,128]{1,0:T(8,128)S(1)}, u32[]{:S(2)}, u32[]{:S(2)}) collective-permute-start(f32[136,128]{1,0:T(8,128)S(1)} %get-tuple-element.56), channel_id=1, source_target_pairs={{0,4},{4,0},{8,12},{12,8},{16,20},{20,16},{24,28},{28,24},{1,5},{5... | collective-permute-start | bytes 208904 | tf_op jit(solution)/shard_map/ppermute | solution.py:490
  6.8 2.8 %collective-permute-done.refs_0_ = f32[136,128]{1,0:T(8,128)S(1)} collective-permute-done((f32[136,128]{1,0:T(8,128)S(1)}, f32[136,128]{1,0:T(8,128)S(1)}, u32[]{:S(2)}, u32[]{:S(2)}) %collective-permute-start) | collective-permute-done | bytes 69664 | tf_op jit(solution)/shard_map/ppermute | solution.py:490
  9.6 1.6 %collective-permute-start.1 = (f32[136,128]{1,0:T(8,128)S(1)}, f32[136,128]{1,0:T(8,128)S(1)}, u32[]{:S(2)}, u32[]{:S(2)}) collective-permute-start(f32[136,128]{1,0:T(8,128)S(1)} %add.33), channel_id=1, source_target_pairs={{0,8},{4,12},{8,0},{12,4},{16,24},{20,28},{24,16},{28,20},{1,9},{5... | collective-permute-start | bytes 208904 | tf_op jit(solution)/shard_map/ppermute | solution.py:490
  11.3 1.6 %collective-permute-start.4 = (bf16[256,128]{1,0:T(8,128)(2,1)S(1)}, bf16[256,128]{1,0:T(8,128)(2,1)S(1)}, u32[]{:S(2)}, u32[]{:S(2)}) collective-permute-start(bf16[256,128]{1,0:T(8,128)(2,1)S(1)} %convert_element_type.60), channel_id=1, source_target_pairs={{0,4},{4,0},{8,12},{12,8},{16,20},{20,16},{24,28},{28,24},{1,5},{5... | collective-permute-start | bytes 196616 | tf_op jit(solution)/shard_map/ppermute | solution.py:490
  12.9 1.1 %collective-permute-done.1.refs_1_ = f32[136,128]{1,0:T(8,128)S(1)} collective-permute-done((f32[136,128]{1,0:T(8,128)S(1)}, f32[136,128]{1,0:T(8,128)S(1)}, u32[]{:S(2)}, u32[]{:S(2)}) %collective-permute-start.1) | collective-permute-done | bytes 69664 | tf_op jit(solution)/shard_map/ppermute | solution.py:490
  14.0 1.6 %collective-permute-done.4.refs_0_ = bf16[256,128]{1,0:T(8,128)(2,1)S(1)} collective-permute-done((bf16[256,128]{1,0:T(8,128)(2,1)S(1)}, bf16[256,128]{1,0:T(8,128)(2,1)S(1)}, u32[]{:S(2)}, u32[]{:S(2)}) %collective-permute-start.4) | collective-permute-done | bytes 65568 | tf_op jit(solution)/shard_map/ppermute | solution.py:490
  15.6 0.5 collective-permute-start.5
  16.1 2.6 %collective-permute-start.2 = (f32[136,128]{1,0:T(8,128)S(1)}, f32[136,128]{1,0:T(8,128)S(1)}, u32[]{:S(2)}, u32[]{:S(2)}) collective-permute-start(f32[136,128]{1,0:T(8,128)S(1)} %add.34), channel_id=1, source_target_pairs={{0,16},{4,20},{8,24},{12,28},{16,0},{20,4},{24,8},{28,12},{1,17},{... | collective-permute-start | bytes 208904 | tf_op jit(solution)/shard_map/ppermute | solution.py:490
  18.7 1.2 %collective-permute-done.5.refs_1_ = bf16[256,128]{1,0:T(8,128)(2,1)S(1)} collective-permute-done((bf16[256,128]{1,0:T(8,128)(2,1)S(1)}, bf16[256,128]{1,0:T(8,128)(2,1)S(1)}, u32[]{:S(2)}, u32[]{:S(2)}) %collective-permute-start.5) | collective-permute-done | bytes 65568 | tf_op jit(solution)/shard_map/ppermute | solution.py:490
  20.0 3.0 %collective-permute-start.6 = (bf16[256,128]{1,0:T(8,128)(2,1)S(1)}, bf16[256,128]{1,0:T(8,128)(2,1)S(1)}, u32[]{:S(2)}, u32[]{:S(2)}) collective-permute-start(bf16[256,128]{1,0:T(8,128)(2,1)S(1)} %add_convert_fusion.2), channel_id=1, source_target_pairs={{0,16},{4,20},{8,24},{12,28},{16,0},{20,4},{24,8},{28,12},{1,17},{... | collective-permute-start | bytes 196616 | tf_op jit(solution)/shard_map/ppermute | solution.py:490
  23.0 0.7 shard_map.94.refs_0_
  23.8 4.1 %shard_map.95 = (bf16[8,8,128,128]{3,2,1,0:T(8,128)(2,1)S(1)}, bf16[8,8,128,128]{3,2,1,0:T(8,128)(2,1)S(1)}, f32[8,128,128]{2,1,0:T(8,128)S(1)}, f32[8,128,128]{2,1,0:T(8,128)S(1)}) custom-call(bf16[1024,256]{1,0:T(8,128)(2,1)S(1)} %copy-done.2, f32[136,128]{1,0:T(8,128)S(1)} %collective-permute-done.refs_0_, f32[136,128]{1,0:T(8,128)S(1)} %collective-permute-done.1.refs_1_, ...), custom_call_target="tpu_custom_call" | custom-call | flops 2000000000 | bytes 8000000 | tf_op jit(solution)/shard_map/pallas_call | solution.py:181
  27.9 1.1 %collective-permute-done.7.refs_1_.refs_2_ = bf16[1024,512]{1,0:T(8,128)(2,1)S(1)} collective-permute-done((bf16[1024,512]{1,0:T(8,128)(2,1)S(1)}, bf16[1024,512]{1,0:T(8,128)(2,1)S(1)}, u32[]{:S(2)}, u32[]{:S(2)}) %collective-permute-start.7) | collective-permute-done | bytes 1048608 | tf_op jit(solution)/shard_map/ppermute | solution.py:490
  29.0 0.1 shard_map.100
  29.1 1.8 %collective-permute-start.15 = (bf16[2,256,512]{2,1,0:T(8,128)(2,1)S(1)}, bf16[2,256,512]{2,1,0:T(8,128)(2,1)S(1)}, u32[]{:S(2)}, u32[]{:S(2)}) collective-permute-start(bf16[2,256,512]{2,1,0:T(8,128)(2,1)S(1)} %get-tuple-element.88), channel_id=1, source_target_pairs={{0,2},{1,3},{2,0},{3,1},{4,6},{5,7},{6,4},{7,5},{8,10},{9,11},{10,... | collective-permute-start | bytes 1572872 | tf_op jit(solution)/shard_map/ppermute | solution.py:490
  30.9 2.4 %shard_map.96 = (bf16[1024,256]{1,0:T(8,128)(2,1)S(1)}, bf16[8,128,256]{2,1,0:T(8,128)(2,1)S(1)}, bf16[8,256,256]{2,1,0:T(8,128)(2,1)S(1)}, bf16[8,256,256]{2,1,0:T(8,128)(2,1)S(1)}) custom-call(bf16[1024,256]{1,0:T(8,128)(2,1)S(1)} %copy-done.4, bf16[1024,256]{1,0:T(8,128)(2,1)S(1)} %copy-done.2, bf16[1024,256]{1,0:T(8,128)(2,1)S(1)} %copy-done.3, ...), custom_call_target="tpu_custom_call" | custom-call | flops 2000000000 | bytes 8000000 | tf_op jit(solution)/shard_map/pallas_call | solution.py:218
  33.3 0.8 %shard_map.97.do_ref = bf16[1024,256]{1,0:T(8,128)(2,1)S(1)} custom-call(bf16[256,2048]{1,0:T(8,128)(2,1)S(1)} %copy-done, f32[1024,256]{1,0:T(8,128)S(1)} %shard_map.94.refs_0_, bf16[1024,512]{1,0:T(8,128)(2,1)S(1)} %collective-permute-done.7.refs_1_.refs_2_, bf16[1024,512]{1,0:T(8,128)(2,1)S(1)} %collective-permute-done.8.refs_2_.refs_3_), custom_call_target="tpu_custom_call" | custom-call | flops 536870912 | bytes 4000000 | tf_op jit(solution)/shard_map/pallas_call | solution.py:406
  34.1 1.4 %shard_map.98 = (bf16[2,256,256]{2,1,0:T(8,128)(2,1)S(1)}, bf16[2,256,256]{2,1,0:T(8,128)(2,1)S(1)}, bf16[2,256,256]{2,1,0:T(8,128)(2,1)S(1)}, bf16[2,256,256]{2,1,0:T(8,128)(2,1)S(1)}) custom-call(bf16[1024,256]{1,0:T(8,128)(2,1)S(1)} %get-tuple-element.76.h_ref.refs_0_, bf16[1024,512]{1,0:T(8,128)(2,1)S(1)} %copy-done.1, ...), custom_call_target="tpu_custom_call" | custom-call | flops 1073741824 | bytes 6000000 | tf_op jit(solution)/shard_map/pallas_call | solution.py:456
  35.5 1.6 %collective-permute-start.12 = (bf16[2,256,256]{2,1,0:T(8,128)(2,1)S(1)}, bf16[2,256,256]{2,1,0:T(8,128)(2,1)S(1)}, u32[]{:S(2)}, u32[]{:S(2)}) collective-permute-start(bf16[2,256,256]{2,1,0:T(8,128)(2,1)S(1)} %get-tuple-element.79), channel_id=1, source_target_pairs={{0,4},{4,0},{8,12},{12,8},{16,20},{20,16},{24,28},{28,24},{1,5},{5... | collective-permute-start | bytes 786440 | tf_op jit(solution)/shard_map/ppermute | solution.py:490
  37.1 6.6 %shard_map.99 = (bf16[8,256,256]{2,1,0:T(8,128)(2,1)S(1)}, bf16[1024,256]{1,0:T(8,128)(2,1)S(1)}, f32[8,128,128]{2,1,0:T(8,128)S(1)}, f32[8,128,128]{2,1,0:T(8,1...) custom-call(bf16[1024,256]{1,0:T(8,128)(2,1)S(1)} %copy-done.4, bf16[1024,256]{1,0:T(8,128)(2,1)S(1)} %copy-done.2, ...), custom_call_target="tpu_custom_call" | custom-call | flops 4000000000 | bytes 8000000 | tf_op jit(solution)/shard_map/pallas_call | solution.py:290
  43.7 0.5 collective-permute-start.11
  44.2 0.3 collective-permute-start.10
  44.5 1.8 %collective-permute-start.18 = (bf16[2,256,256]{2,1,0:T(8,128)(2,1)S(1)}, bf16[2,256,256]{2,1,0:T(8,128)(2,1)S(1)}, u32[]{:S(2)}, u32[]{:S(2)}) collective-permute-start(bf16[2,256,256]{2,1,0:T(8,128)(2,1)S(1)} %get-tuple-element.102), channel_id=1, source_target_pairs={{0,4},{4,0},{8,12},{12,8},{16,20},{20,16},{24,28},{28,24},{1,5},{5... | collective-permute-start | bytes 786440 | tf_op jit(solution)/shard_map/ppermute | solution.py:490
  46.3 0.1 add_convert_fusion
  46.4 2.8 %collective-permute-done.11.refs_0_ = bf16[392,128]{1,0:T(8,128)(2,1)S(1)} collective-permute-done((bf16[392,128]{1,0:T(8,128)(2,1)S(1)}, bf16[392,128]{1,0:T(8,128)(2,1)S(1)}, u32[]{:S(2)}, u32[]{:S(2)}) %collective-permute-start.11) | collective-permute-done | bytes 100384 | tf_op jit(solution)/shard_map/ppermute | solution.py:490
  49.2 3.4 %collective-permute-start.20 = (bf16[256,256]{1,0:T(8,128)(2,1)S(1)}, bf16[256,256]{1,0:T(8,128)(2,1)S(1)}, u32[]{:S(2)}, u32[]{:S(2)}) collective-permute-start(bf16[256,256]{1,0:T(8,128)(2,1)S(1)} %get-tuple-element.113), channel_id=1, source_target_pairs={{0,24},{4,28},{8,16},{12,20},{16,8},{20,12},{24,0},{28,4},{1,25},{... | collective-permute-start | bytes 393224 | tf_op jit(solution)/shard_map/ppermute | solution.py:490
  52.6 1.4 %collective-permute-done.18 = bf16[2,256,256]{2,1,0:T(8,128)(2,1)S(1)} collective-permute-done((bf16[2,256,256]{2,1,0:T(8,128)(2,1)S(1)}, bf16[2,256,256]{2,1,0:T(8,128)(2,1)S(1)}, u32[]{:S(2)}, u32[]{:S(2)}) %collective-permute-start.18) | collective-permute-done | bytes 262176 | tf_op jit(solution)/shard_map/ppermute | solution.py:490
  54.1 1.6 %collective-permute-start.13 = (bf16[392,128]{1,0:T(8,128)(2,1)S(1)}, bf16[392,128]{1,0:T(8,128)(2,1)S(1)}, u32[]{:S(2)}, u32[]{:S(2)}) collective-permute-start(bf16[392,128]{1,0:T(8,128)(2,1)S(1)} %fusion.3), channel_id=1, source_target_pairs={{0,8},{4,12},{8,0},{12,4},{16,24},{20,28},{24,16},{28,20},{1,9},{5... | collective-permute-start | bytes 301064 | tf_op jit(solution)/shard_map/ppermute | solution.py:490
  55.6 0.1 slice_bitcast_fusion.3
  55.7 0.1 pad_maximum_fusion
  55.8 0.1 collective-permute-start.16
  55.8 0.1 convert_add_fusion
  55.9 2.8 %collective-permute-done.13.refs_1_ = bf16[392,128]{1,0:T(8,128)(2,1)S(1)} collective-permute-done((bf16[392,128]{1,0:T(8,128)(2,1)S(1)}, bf16[392,128]{1,0:T(8,128)(2,1)S(1)}, u32[]{:S(2)}, u32[]{:S(2)}) %collective-permute-start.13) | collective-permute-done | bytes 100384 | tf_op jit(solution)/shard_map/ppermute | solution.py:490
  58.7 2.6 %collective-permute-start.17 = (bf16[392,128]{1,0:T(8,128)(2,1)S(1)}, bf16[392,128]{1,0:T(8,128)(2,1)S(1)}, u32[]{:S(2)}, u32[]{:S(2)}) collective-permute-start(bf16[392,128]{1,0:T(8,128)(2,1)S(1)} %add_convert_fusion.1), channel_id=1, source_target_pairs={{0,16},{4,20},{8,24},{12,28},{16,0},{20,4},{24,8},{28,12},{1,17},{... | collective-permute-start | bytes 301064 | tf_op jit(solution)/shard_map/ppermute | solution.py:490
  61.4 2.2 %shard_map.102 = (bf16[1024,256]{1,0:T(8,128)(2,1)}, f32[1024,256]{1,0:T(8,128)S(1)}, f32[1024,256]{1,0:T(8,128)S(1)}) custom-call(bf16[1024,256]{1,0:T(8,128)(2,1)S(1)} %copy-done.2, bf16[1024,256]{1,0:T(8,128)(2,1)S(1)} %copy-done.3, bf16[1024,256]{1,0:T(8,128)(2,1)S(1)} %shard_map.97.do_ref, f32[8,128,128]{2,1,0:T(8,128)S(1)} %get-tuple-element.60.last_ref, ...), custom_call_target="tpu_custom_call" | custom-call | flops 2000000000 | bytes 6000000 | tf_op jit(solution)/shard_map/pallas_call | solution.py:328
  63.6 0.8 %collective-permute-done.17.refs_2_ = bf16[392,128]{1,0:T(8,128)(2,1)S(1)} collective-permute-done((bf16[392,128]{1,0:T(8,128)(2,1)S(1)}, bf16[392,128]{1,0:T(8,128)(2,1)S(1)}, u32[]{:S(2)}, u32[]{:S(2)}) %collective-permute-start.17) | collective-permute-done | bytes 100384 | tf_op jit(solution)/shard_map/ppermute | solution.py:490
  64.4 2.7 %collective-permute-start.19 = (bf16[256,256]{1,0:T(8,128)(2,1)S(1)}, bf16[256,256]{1,0:T(8,128)(2,1)S(1)}, u32[]{:S(2)}, u32[]{:S(2)}) collective-permute-start(bf16[256,256]{1,0:T(8,128)(2,1)S(1)} %get-tuple-element.114), channel_id=1, source_target_pairs={{0,16},{4,20},{8,24},{12,28},{16,0},{20,4},{24,8},{28,12},{1,17},{... | collective-permute-start | bytes 393224 | tf_op jit(solution)/shard_map/ppermute | solution.py:490
  67.0 1.4 %shard_map.103 = (bf16[1024,256]{1,0:T(8,128)(2,1)}, bf16[1024,256]{1,0:T(8,128)(2,1)}) custom-call(bf16[1024,256]{1,0:T(8,128)(2,1)S(1)} %copy-done.2, bf16[1024,256]{1,0:T(8,128)(2,1)S(1)} %copy-done.3, f32[1024,256]{1,0:T(8,128)S(1)} %get-tuple-element.97.dk_ref, f32[1024,256]{1,0:T(8,128)S(1)} %get-tuple-element.98.dv_ref, ...), custom_call_target="tpu_custom_call" | custom-call | flops 1000000000 | bytes 6000000 | tf_op jit(solution)/shard_map/pallas_call | solution.py:365
  68.4 2.5 %collective-permute-start.21 = (bf16[256,256]{1,0:T(8,128)(2,1)S(1)}, bf16[256,256]{1,0:T(8,128)(2,1)S(1)}, u32[]{:S(2)}, u32[]{:S(2)}) collective-permute-start(bf16[256,256]{1,0:T(8,128)(2,1)S(1)} %fusion.4), channel_id=1, source_target_pairs={{0,8},{4,12},{8,0},{12,4},{16,24},{20,28},{24,16},{28,20},{1,9},{5... | collective-permute-start | bytes 393224 | tf_op jit(solution)/shard_map/ppermute | solution.py:490
  71.0 2.2 %shard_map.101 = bf16[1024,512]{1,0:T(8,128)(2,1)} custom-call(bf16[1024,256]{1,0:T(8,128)(2,1)S(1)} %get-tuple-element.76.h_ref.refs_0_, bf16[1024,256]{1,0:T(8,128)(2,1)S(1)} %collective-permute-done.9.refs_1_, bf16[1024,256]{1,0:T(8,128)(2,1)S(1)} %collective-permute-done.10.refs_2_, bf16[1024,256]{1,0:T(8,128)(2,1)S(1)} %collective-permute-done.14.refs_3_, ...), custom_call_target="tpu_custom_call" | custom-call | flops 1073741824 | bytes 6000000 | tf_op jit(solution)/shard_map/pallas_call | solution.py:478
  73.2 1.0 %collective-permute-done.21 = bf16[256,256]{1,0:T(8,128)(2,1)S(1)} collective-permute-done((bf16[256,256]{1,0:T(8,128)(2,1)S(1)}, bf16[256,256]{1,0:T(8,128)(2,1)S(1)}, u32[]{:S(2)}, u32[]{:S(2)}) %collective-permute-start.21) | collective-permute-done | bytes 131104 | tf_op jit(solution)/shard_map/ppermute | solution.py:490
  74.2 0.8 %fusion.2 = f32[256,256]{1,0:T(8,128)} fusion(f32[2,256,256]{2,1,0:T(8,128)S(1)} %convert_add_fusion, bf16[256,256]{1,0:T(8,128)(2,1)S(1)} %collective-permute-done.21, bf16[256,256]{1,0:T(8,128)(2,1)S(1)} %collective-permute-done.20, bf16[256,256]{1,0:T(8,128)(2,1)S(1)} %collective-permute-done.19), kind=kLoop, calls=%fused_computation.7 | loop fusion | flops 393216 | bytes 917504 | tf_op jit(solution)/shard_map/add | solution.py:580
  (33 shorter events, 0.3 us)
Async XLA Ops:
  0.6 1.0 %copy-start.2 = (bf16[1024,256]{1,0:T(8,128)(2,1)S(1)}, bf16[1024,256]{1,0:T(8,128)(2,1)}, u32[]{:S(2)}) copy-start(bf16[1024,256]{1,0:T(8,128)(2,1)} %k_ref.11) | copy-start | bytes 1572868
  0.6 1.2 %copy-start.3 = (bf16[1024,256]{1,0:T(8,128)(2,1)S(1)}, bf16[1024,256]{1,0:T(8,128)(2,1)}, u32[]{:S(2)}) copy-start(bf16[1024,256]{1,0:T(8,128)(2,1)} %v_ref.9) | copy-start | bytes 1572868
  0.7 1.5 %copy-start.1 = (bf16[1024,512]{1,0:T(8,128)(2,1)S(1)}, bf16[1024,512]{1,0:T(8,128)(2,1)}, u32[]{:S(2)}) copy-start(bf16[1024,512]{1,0:T(8,128)(2,1)} %refs_0_.3) | copy-start | bytes 3145732
  0.7 22.3 %copy-start = (bf16[256,2048]{1,0:T(8,128)(2,1)S(1)}, bf16[256,2048]{1,0:T(8,128)(2,1)}, u32[]{:S(2)}) copy-start(bf16[256,2048]{1,0:T(8,128)(2,1)} %w_ref.4) | copy-start | bytes 3145732
  2.2 20.8 %collective-permute-start.3 = (bf16[1024,512]{1,0:T(8,128)(2,1)S(1)}, bf16[1024,512]{1,0:T(8,128)(2,1)S(1)}, u32[]{:S(2)}, u32[]{:S(2)}) collective-permute-start(bf16[1024,512]{1,0:T(8,128)(2,1)S(1)} %copy-done.1), channel_id=1, source_target_pairs={{0,1},{1,0},{2,3},{3,2},{4,5},{5,4},{6,7},{7,6},{8,9},{9,8},{10,11... | collective-permute-start | bytes 3145736 | tf_op jit(solution)/shard_map/ppermute | solution.py:490
  2.7 26.3 %collective-permute-start.7 = (bf16[1024,512]{1,0:T(8,128)(2,1)S(1)}, bf16[1024,512]{1,0:T(8,128)(2,1)S(1)}, u32[]{:S(2)}, u32[]{:S(2)}) collective-permute-start(bf16[1024,512]{1,0:T(8,128)(2,1)S(1)} %copy-done.1), channel_id=1, source_target_pairs={{0,2},{1,3},{2,0},{3,1},{4,6},{5,7},{6,4},{7,5},{8,10},{9,11},{10,... | collective-permute-start | bytes 3145736 | tf_op jit(solution)/shard_map/ppermute | solution.py:490
  5.3 4.3 %collective-permute-start = (f32[136,128]{1,0:T(8,128)S(1)}, f32[136,128]{1,0:T(8,128)S(1)}, u32[]{:S(2)}, u32[]{:S(2)}) collective-permute-start(f32[136,128]{1,0:T(8,128)S(1)} %get-tuple-element.56), channel_id=1, source_target_pairs={{0,4},{4,0},{8,12},{12,8},{16,20},{20,16},{24,28},{28,24},{1,5},{5... | collective-permute-start | bytes 208904 | tf_op jit(solution)/shard_map/ppermute | solution.py:490
  9.6 4.4 %collective-permute-start.1 = (f32[136,128]{1,0:T(8,128)S(1)}, f32[136,128]{1,0:T(8,128)S(1)}, u32[]{:S(2)}, u32[]{:S(2)}) collective-permute-start(f32[136,128]{1,0:T(8,128)S(1)} %add.33), channel_id=1, source_target_pairs={{0,8},{4,12},{8,0},{12,4},{16,24},{20,28},{24,16},{28,20},{1,9},{5... | collective-permute-start | bytes 208904 | tf_op jit(solution)/shard_map/ppermute | solution.py:490
  11.3 4.3 %collective-permute-start.4 = (bf16[256,128]{1,0:T(8,128)(2,1)S(1)}, bf16[256,128]{1,0:T(8,128)(2,1)S(1)}, u32[]{:S(2)}, u32[]{:S(2)}) collective-permute-start(bf16[256,128]{1,0:T(8,128)(2,1)S(1)} %convert_element_type.60), channel_id=1, source_target_pairs={{0,4},{4,0},{8,12},{12,8},{16,20},{20,16},{24,28},{28,24},{1,5},{5... | collective-permute-start | bytes 196616 | tf_op jit(solution)/shard_map/ppermute | solution.py:490
  15.6 4.3 %collective-permute-start.5 = (bf16[256,128]{1,0:T(8,128)(2,1)S(1)}, bf16[256,128]{1,0:T(8,128)(2,1)S(1)}, u32[]{:S(2)}, u32[]{:S(2)}) collective-permute-start(bf16[256,128]{1,0:T(8,128)(2,1)S(1)} %fusion.5), channel_id=1, source_target_pairs={{0,8},{4,12},{8,0},{12,4},{16,24},{20,28},{24,16},{28,20},{1,9},{5... | collective-permute-start | bytes 196616 | tf_op jit(solution)/shard_map/ppermute | solution.py:490
  16.1 7.6 %collective-permute-start.2 = (f32[136,128]{1,0:T(8,128)S(1)}, f32[136,128]{1,0:T(8,128)S(1)}, u32[]{:S(2)}, u32[]{:S(2)}) collective-permute-start(f32[136,128]{1,0:T(8,128)S(1)} %add.34), channel_id=1, source_target_pairs={{0,16},{4,20},{8,24},{12,28},{16,0},{20,4},{24,8},{28,12},{1,17},{... | collective-permute-start | bytes 208904 | tf_op jit(solution)/shard_map/ppermute | solution.py:490
  20.0 7.9 %collective-permute-start.6 = (bf16[256,128]{1,0:T(8,128)(2,1)S(1)}, bf16[256,128]{1,0:T(8,128)(2,1)S(1)}, u32[]{:S(2)}, u32[]{:S(2)}) collective-permute-start(bf16[256,128]{1,0:T(8,128)(2,1)S(1)} %add_convert_fusion.2), channel_id=1, source_target_pairs={{0,16},{4,20},{8,24},{12,28},{16,0},{20,4},{24,8},{28,12},{1,17},{... | collective-permute-start | bytes 196616 | tf_op jit(solution)/shard_map/ppermute | solution.py:490
  23.8 7.2 %copy-start.4 = (bf16[1024,256]{1,0:T(8,128)(2,1)S(1)}, bf16[1024,256]{1,0:T(8,128)(2,1)}, u32[]{:S(2)}) copy-start(bf16[1024,256]{1,0:T(8,128)(2,1)} %q_ref.3) | copy-start | bytes 1572868
  29.0 4.3 %collective-permute-start.8 = (bf16[1024,512]{1,0:T(8,128)(2,1)S(1)}, bf16[1024,512]{1,0:T(8,128)(2,1)S(1)}, u32[]{:S(2)}, u32[]{:S(2)}) collective-permute-start(bf16[1024,512]{1,0:T(8,128)(2,1)S(1)} %collective-permute-done.7.refs_1_.refs_2_), channel_id=1, source_target_pairs={{0,1},{1,0},{2,3},{3,2},{4,5},{5,4},{6,7},{7,6},{8,9},{9,8},{10,11... | collective-permute-start | bytes 3145736 | tf_op jit(solution)/shard_map/ppermute | solution.py:490
  29.1 26.5 %collective-permute-start.15 = (bf16[2,256,512]{2,1,0:T(8,128)(2,1)S(1)}, bf16[2,256,512]{2,1,0:T(8,128)(2,1)S(1)}, u32[]{:S(2)}, u32[]{:S(2)}) collective-permute-start(bf16[2,256,512]{2,1,0:T(8,128)(2,1)S(1)} %get-tuple-element.88), channel_id=1, source_target_pairs={{0,2},{1,3},{2,0},{3,1},{4,6},{5,7},{6,4},{7,5},{8,10},{9,11},{10,... | collective-permute-start | bytes 1572872 | tf_op jit(solution)/shard_map/ppermute | solution.py:490
  35.5 9.1 %collective-permute-start.12 = (bf16[2,256,256]{2,1,0:T(8,128)(2,1)S(1)}, bf16[2,256,256]{2,1,0:T(8,128)(2,1)S(1)}, u32[]{:S(2)}, u32[]{:S(2)}) collective-permute-start(bf16[2,256,256]{2,1,0:T(8,128)(2,1)S(1)} %get-tuple-element.79), channel_id=1, source_target_pairs={{0,4},{4,0},{8,12},{12,8},{16,20},{20,16},{24,28},{28,24},{1,5},{5... | collective-permute-start | bytes 786440 | tf_op jit(solution)/shard_map/ppermute | solution.py:490
  43.7 5.5 %collective-permute-start.11 = (bf16[392,128]{1,0:T(8,128)(2,1)S(1)}, bf16[392,128]{1,0:T(8,128)(2,1)S(1)}, u32[]{:S(2)}, u32[]{:S(2)}) collective-permute-start(bf16[392,128]{1,0:T(8,128)(2,1)S(1)} %get-tuple-element.75), channel_id=1, source_target_pairs={{0,4},{4,0},{8,12},{12,8},{16,20},{20,16},{24,28},{28,24},{1,5},{5... | collective-permute-start | bytes 301064 | tf_op jit(solution)/shard_map/ppermute | solution.py:490
  44.2 17.1 %collective-permute-start.10 = (bf16[1024,256]{1,0:T(8,128)(2,1)S(1)}, bf16[1024,256]{1,0:T(8,128)(2,1)S(1)}, u32[]{:S(2)}, u32[]{:S(2)}) collective-permute-start(bf16[1024,256]{1,0:T(8,128)(2,1)S(1)} %get-tuple-element.76.h_ref.refs_0_), channel_id=1, source_target_pairs={{0,2},{1,3},{2,0},{3,1},{4,6},{5,7},{6,4},{7,5},{8,10},{9,11},{10,... | collective-permute-start | bytes 1572872 | tf_op jit(solution)/shard_map/ppermute | solution.py:490
  44.5 26.5 %collective-permute-start.9 = (bf16[1024,256]{1,0:T(8,128)(2,1)S(1)}, bf16[1024,256]{1,0:T(8,128)(2,1)S(1)}, u32[]{:S(2)}, u32[]{:S(2)}) collective-permute-start(bf16[1024,256]{1,0:T(8,128)(2,1)S(1)} %get-tuple-element.76.h_ref.refs_0_), channel_id=1, source_target_pairs={{0,1},{1,0},{2,3},{3,2},{4,5},{5,4},{6,7},{7,6},{8,9},{9,8},{10,11... | collective-permute-start | bytes 1572872 | tf_op jit(solution)/shard_map/ppermute | solution.py:490
  44.5 9.5 %collective-permute-start.18 = (bf16[2,256,256]{2,1,0:T(8,128)(2,1)S(1)}, bf16[2,256,256]{2,1,0:T(8,128)(2,1)S(1)}, u32[]{:S(2)}, u32[]{:S(2)}) collective-permute-start(bf16[2,256,256]{2,1,0:T(8,128)(2,1)S(1)} %get-tuple-element.102), channel_id=1, source_target_pairs={{0,4},{4,0},{8,12},{12,8},{16,20},{20,16},{24,28},{28,24},{1,5},{5... | collective-permute-start | bytes 786440 | tf_op jit(solution)/shard_map/ppermute | solution.py:490
  49.2 25.0 %collective-permute-start.20 = (bf16[256,256]{1,0:T(8,128)(2,1)S(1)}, bf16[256,256]{1,0:T(8,128)(2,1)S(1)}, u32[]{:S(2)}, u32[]{:S(2)}) collective-permute-start(bf16[256,256]{1,0:T(8,128)(2,1)S(1)} %get-tuple-element.113), channel_id=1, source_target_pairs={{0,24},{4,28},{8,16},{12,20},{16,8},{20,12},{24,0},{28,4},{1,25},{... | collective-permute-start | bytes 393224 | tf_op jit(solution)/shard_map/ppermute | solution.py:490
  54.1 4.6 %collective-permute-start.13 = (bf16[392,128]{1,0:T(8,128)(2,1)S(1)}, bf16[392,128]{1,0:T(8,128)(2,1)S(1)}, u32[]{:S(2)}, u32[]{:S(2)}) collective-permute-start(bf16[392,128]{1,0:T(8,128)(2,1)S(1)} %fusion.3), channel_id=1, source_target_pairs={{0,8},{4,12},{8,0},{12,4},{16,24},{20,28},{24,16},{28,20},{1,9},{5... | collective-permute-start | bytes 301064 | tf_op jit(solution)/shard_map/ppermute | solution.py:490
  55.8 12.7 %collective-permute-start.16 = (bf16[2,256,512]{2,1,0:T(8,128)(2,1)S(1)}, bf16[2,256,512]{2,1,0:T(8,128)(2,1)S(1)}, u32[]{:S(2)}, u32[]{:S(2)}) collective-permute-start(bf16[2,256,512]{2,1,0:T(8,128)(2,1)S(1)} %pad_maximum_fusion), channel_id=1, source_target_pairs={{0,1},{1,0},{2,3},{3,2},{4,5},{5,4},{6,7},{7,6},{8,9},{9,8},{10,11... | collective-permute-start | bytes 1572872 | tf_op jit(solution)/shard_map/ppermute | solution.py:490
  58.7 5.6 %collective-permute-start.17 = (bf16[392,128]{1,0:T(8,128)(2,1)S(1)}, bf16[392,128]{1,0:T(8,128)(2,1)S(1)}, u32[]{:S(2)}, u32[]{:S(2)}) collective-permute-start(bf16[392,128]{1,0:T(8,128)(2,1)S(1)} %add_convert_fusion.1), channel_id=1, source_target_pairs={{0,16},{4,20},{8,24},{12,28},{16,0},{20,4},{24,8},{28,12},{1,17},{... | collective-permute-start | bytes 301064 | tf_op jit(solution)/shard_map/ppermute | solution.py:490
  61.4 9.6 %collective-permute-start.14 = (bf16[1024,256]{1,0:T(8,128)(2,1)S(1)}, bf16[1024,256]{1,0:T(8,128)(2,1)S(1)}, u32[]{:S(2)}, u32[]{:S(2)}) collective-permute-start(bf16[1024,256]{1,0:T(8,128)(2,1)S(1)} %collective-permute-done.10.refs_2_), channel_id=1, source_target_pairs={{0,1},{1,0},{2,3},{3,2},{4,5},{5,4},{6,7},{7,6},{8,9},{9,8},{10,11... | collective-permute-start | bytes 1572872 | tf_op jit(solution)/shard_map/ppermute | solution.py:490
  64.4 9.9 %collective-permute-start.19 = (bf16[256,256]{1,0:T(8,128)(2,1)S(1)}, bf16[256,256]{1,0:T(8,128)(2,1)S(1)}, u32[]{:S(2)}, u32[]{:S(2)}) collective-permute-start(bf16[256,256]{1,0:T(8,128)(2,1)S(1)} %get-tuple-element.114), channel_id=1, source_target_pairs={{0,16},{4,20},{8,24},{12,28},{16,0},{20,4},{24,8},{28,12},{1,17},{... | collective-permute-start | bytes 393224 | tf_op jit(solution)/shard_map/ppermute | solution.py:490
  68.4 5.8 %collective-permute-start.21 = (bf16[256,256]{1,0:T(8,128)(2,1)S(1)}, bf16[256,256]{1,0:T(8,128)(2,1)S(1)}, u32[]{:S(2)}, u32[]{:S(2)}) collective-permute-start(bf16[256,256]{1,0:T(8,128)(2,1)S(1)} %fusion.4), channel_id=1, source_target_pairs={{0,8},{4,12},{8,0},{12,4},{16,24},{20,28},{24,16},{28,20},{1,9},{5... | collective-permute-start | bytes 393224 | tf_op jit(solution)/shard_map/ppermute | solution.py:490

commit v10 on v9

--- a/solution.py
+++ b/solution.py
@@ -189,7 +189,7 @@
     )(keys, *grams)
 
 
-def outputs_kernel(rounds, q_ref, k_ref, v_ref, last_ref, *refs):
+def outputs_kernel(rounds, mark_ref, q_ref, k_ref, v_ref, last_ref, *refs):
     out_ref, pre_ref, s_ref, w_ref = refs[rounds:]
     prefix = taken(refs[:rounds], False)
     heads = q_ref.shape[1] // HDIM
@@ -213,7 +213,7 @@
         pairs[h] = pairs[h] + dot(k, v, (0, 0))
 
 
-def outputs(queries, keys, values, last, pairs):
+def outputs(mark, queries, keys, values, last, pairs):
     count = last.shape[0]
     return pl.pallas_call(
         functools.partial(outputs_kernel, len(pairs)),
@@ -223,11 +223,11 @@
             shape((count, SPAN, 2 * HDIM), BF16),
             shape((count, SPAN, SPAN), BF16),
         ),
-        in_specs=[VMEM_SPEC] * (4 + len(pairs)),
+        in_specs=[VMEM_SPEC] * (5 + len(pairs)),
         out_specs=(VMEM_SPEC,) * 4,
         compiler_params=params(),
         cost_estimate=cost(2_000_000_000, 8_000_000),
-    )(queries, keys, values, last, *pairs)
+    )(mark, queries, keys, values, last, *pairs)
 
 
 def tangent_kernel(
@@ -303,10 +303,11 @@
 
 def rest_kernel(
     k_ref, v_ref, do_ref, last_ref, s_ref, w_ref, p_ref, ds_ref, da_ref, dn_ref,
-    dq_ref, dk_ref, dv_ref,
+    dq_hbm, dk_ref, dv_ref, dq_ref, sems,
 ):
     heads = k_ref.shape[1] // HDIM
     sa, sn = [None] * heads, [None] * heads
+    copies = []
     for h, b, i, rows, cols in reversed(list(places(k_ref, heads))):
         k, v, do, ds = k_ref[rows, cols], v_ref[rows, cols], do_ref[rows, cols], ds_ref[rows, cols]
         dq_ref[rows, cols] = dot(cat([ds, ds], 1), cat(split(last_ref[i]), 0)).astype(BF16)
@@ -321,6 +322,12 @@
             sa[h], sn[h] = sa[h] + da_ref[i], sn[h] + dn_ref[i]
         dk_ref[rows, cols] = dk
         dv_ref[rows, cols] = dv
+        copies.append(
+            pltpu.make_async_copy(dq_ref.at[rows, cols], dq_hbm.at[rows, cols], sems.at[i])
+        )
+        copies[-1].start()
+    for copy in copies:
+        copy.wait()
 
 
 def rest(keys, values, grads, *stash):
@@ -329,14 +336,24 @@
         rest_kernel,
         out_shape=(shape(keys.shape, BF16), wide, wide),
         in_specs=[VMEM_SPEC] * 10,
-        out_specs=(VMEM_SPEC,) * 3,
+        out_specs=(ANY_SPEC, VMEM_SPEC, VMEM_SPEC),
+        scratch_shapes=[
+            pltpu.VMEM(keys.shape, BF16),
+            pltpu.SemaphoreType.DMA((stash[0].shape[0],)),
+        ],
         compiler_params=params(),
         cost_estimate=cost(2_000_000_000, 6_000_000),
     )(keys, values, grads, *stash)
 
 
 def finish_kernel(rounds, k_ref, v_ref, dk_ref, dv_ref, *refs):
-    gk_hbm, gv_hbm, gk_ref, gv_ref, sems = refs[rounds:]
+    low_ref, pieces = refs[rounds], refs[rounds + 1 : -8]
+    gk_hbm, gv_hbm, gw_hbm, gk_ref, gv_ref, gw_ref, sems, gw_sem = refs[-8:]
+    gw_ref[...] = low_ref[...]
+    for piece in pieces:
+        gw_ref[...] += piece[...].astype(F32)
+    gw_copy = pltpu.make_async_copy(gw_ref, gw_hbm, gw_sem)
+    gw_copy.start()
     sums = taken(refs[:rounds], True)
     heads = k_ref.shape[1] // HDIM
     nil = jnp.zeros((HDIM, HDIM), BF16)
@@ -358,34 +375,37 @@
             copies[-1].start()
     for copy in copies:
         copy.wait()
-
-
-def finish(keys, values, dk, dv, sums):
+    gw_copy.wait()
+
+
+def finish(keys, values, dk, dv, sums, low, pieces):
     blocks = keys.shape[0] // SPAN
     return pl.pallas_call(
         functools.partial(finish_kernel, len(sums)),
-        out_shape=(shape(keys.shape, BF16),) * 2,
-        in_specs=[VMEM_SPEC] * (4 + len(sums)),
-        out_specs=(ANY_SPEC,) * 2,
+        out_shape=(shape(keys.shape, BF16),) * 2 + (shape(low.shape),),
+        in_specs=[VMEM_SPEC] * (5 + len(sums) + len(pieces)),
+        out_specs=(ANY_SPEC,) * 3,
         scratch_shapes=[pltpu.VMEM(keys.shape, BF16)] * 2
-        + [pltpu.SemaphoreType.DMA((blocks, 2))],
+        + [pltpu.VMEM(low.shape, F32)]
+        + [pltpu.SemaphoreType.DMA((blocks, 2)), pltpu.SemaphoreType.DMA(())],
         compiler_params=params(),
         cost_estimate=cost(1_000_000_000, 6_000_000),
-    )(keys, values, dk, dv, *sums)
-
-
-def lead_kernel(out_ref):
-    out_ref[...] = jnp.zeros_like(out_ref)
-
-
-def lead():
+    )(keys, values, dk, dv, *sums, low, *pieces)
+
+
+def lead_kernel(*refs):
+    refs[-1][...] = jnp.zeros_like(refs[-1])
+
+
+def lead(flops, *behind):
     return pl.pallas_call(
         lead_kernel,
         out_shape=shape((8, HDIM)),
+        in_specs=[VMEM_SPEC] * len(behind),
         out_specs=VMEM_SPEC,
         compiler_params=params(),
-        cost_estimate=cost(700_000_000, 4096),
-    )()
+        cost_estimate=cost(flops, 4096),
+    )(*behind)
 
 
 def grads_kernel(first, w_ref, *refs):
@@ -465,24 +485,34 @@
 
 
 def layer_kernel(*refs):
-    count = (len(refs) - 1) // 2
-    total = None
-    for s in range(count):
-        term = dot(refs[s][...], refs[count + s][...])
-        total = term if total is None else total + term
-    refs[-1][...] = total.astype(BF16)
-
-
-def layer(parts, blocks):
-    rows, cols = parts[0].shape[0], blocks[0].shape[1]
+    hbm, ref, sems = refs[-3:]
+    count = (len(refs) - 3) // 2
+    step = ref.shape[0] // sems.shape[0]
+    copies = []
+    for b in range(sems.shape[0]):
+        rows = slice(b * step, (b + 1) * step)
+        total = None
+        for s in range(count):
+            term = dot(refs[s][rows, :], refs[count + s][...])
+            total = term if total is None else total + term
+        ref[rows, :] = total.astype(BF16)
+        copies.append(pltpu.make_async_copy(ref.at[rows], hbm.at[rows], sems.at[b]))
+        copies[-1].start()
+    for copy in copies:
+        copy.wait()
+
+
+def layer(parts, columns):
+    rows, cols = parts[0].shape[0], columns[0].shape[1]
     return pl.pallas_call(
         layer_kernel,
         out_shape=shape((rows, cols), BF16),
-        in_specs=[VMEM_SPEC] * (len(parts) + len(blocks)),
-        out_specs=VMEM_SPEC,
+        in_specs=[VMEM_SPEC] * (len(parts) + len(columns)),
+        out_specs=ANY_SPEC,
+        scratch_shapes=[pltpu.VMEM((rows, cols), BF16), pltpu.SemaphoreType.DMA((4,))],
         compiler_params=params(),
         cost_estimate=cost(2 * rows * cols * sum(p.shape[1] for p in parts), 6_000_000),
-    )(*parts, *blocks)
+    )(*parts, *columns)
 
 
 def swap(value, axis, distance):
@@ -505,7 +535,7 @@
     evens = range(2, head_count, 2)
 
     far = {s: swap(cotangent, "head", s) for s in evens}
-    begin = lead()
+    begin = lead(700_000_000)
     gram, pair = totals(begin, keys, values, heads)
     near = swap(after(cotangent, gram, pair), "head", 1)
 
@@ -529,9 +559,10 @@
     for s in evens:
         parts += [far[s], swap(after(far[s], pairs[-1]), "head", 1)]
     columns = column_pieces(after(w_out, begun), head_count)
-    columns = [after(c, pairs[-1], *far.values()) for c in columns]
+    columns = [after(c, pairs[-1]) for c in columns]
     columns = [swap(c, "head", 2 * s) if s else c for s, c in enumerate(columns)]
-    heads_out, states, solved, scores = outputs(queries, keys, values, last, pairs)
+    mark = lead(1000, last)
+    heads_out, states, solved, scores = outputs(mark, queries, keys, values, last, pairs)
 
     grads = head_grads(w_out, parts, 2, after(begun, heads_out))
     parts = [cotangent, near] + parts
@@ -563,6 +594,9 @@
 
     low = even_low.astype(F32) + after(low, sends[1]).astype(F32)
     moved += [swap(low[u].astype(BF16), "ctx", 2 * u) for u in range(1, half)]
+    grad_queries, dk, dv = rest(
+        keys, values, grads, last, solved, scores, weights, after(ds, low), da, dn
+    )
 
     outs = [heads_out, swap(outs_out, "head", 1)]
     for part in outs_far:
@@ -571,14 +605,9 @@
     crossing = jnp.stack([c[1] for c in columns])
     crossing = swap(crossing, "head", 1)
     columns = [c for s in range(head_count // 2) for c in (columns[s][0], crossing[s])]
-    grad_queries, dk, dv = rest(
-        keys, values, grads, last, solved, scores, weights, after(ds, sends[-1]), da, dn
-    )
     layer_out = layer(outs, columns)
-    grad_weight = low[0]
-    for part in moved:
-        grad_weight = grad_weight + after(part, layer_out).astype(F32)
-    grad_keys, grad_values = finish(keys, values, dk, dv, later)
+    moved = [after(part, layer_out) for part in moved]
+    grad_keys, grad_values, grad_weight = finish(keys, values, dk, dv, later, low[0], moved)
     return (layer_out, grad_queries, grad_keys, grad_values, grad_weight)
 
 

time: 75.1 us -> 71.7 us (0.955)
  waiting for transfers between devices: 16.7 us -> 14.3 us
  other arithmetic: 1.09 us -> 0.32 us
    ppermute x22, waiting for transfers between devices: 16.7 us -> 14.3 us  [swap(): return lax.ppermute(value, axis, [(i, i ^ distance) for i in range(count)])]
    add x1 -> x0, other arithmetic: 0.76 us -> none  [shards(): grad_weight = grad_weight + after(part, layer_out).astype(F32)]
  transfers between devices with their start and end apart: 22 -> 22, of which waited for: 10 -> 9; matrix products, arithmetic and copies ran while one was open for 1% -> 1% of each run, Pallas kernels for 29% -> 28%
where the time goes in v10:
time: 71.7 us; the launch traced here: 71.6 us
  starting transfers between devices  32.6 us (45%)
  Pallas kernels  22.2 us (31%)
  waiting for transfers between devices  14.3 us (20%)
  local copies, waits for them, and re-layouts  1.34 us (2%)
  between operations  0.89 us (1%)
    ppermute x22, starting transfers between devices, swap(): return lax.ppermute(value, axis, [(i, i ^ distance) for i in range(count)])  32.6 us
    ppermute x22, waiting for transfers between devices, swap(): return lax.ppermute(value, axis, [(i, i ^ distance) for i in range(count)])  14.3 us
    pallas_call x1, Pallas kernels, tangent(): pl.pallas_call(tangent_kernel, out_shape=(shape((count, SPAN, SPAN), BF16...  6.75 us
    pallas_call x1, Pallas kernels, inverses(): pl.pallas_call(functools.partial(inverse_kernel, len(grams)), out_shape=(...  4.21 us
    pallas_call x1, Pallas kernels, outputs(): pl.pallas_call(functools.partial(outputs_kernel, len(pairs)), out_shape=(...  2.4 us
    pallas_call x1, Pallas kernels, rest(): pl.pallas_call(rest_kernel, out_shape=(shape(keys.shape, BF16), wide, wid...  2.08 us
    pallas_call x1, Pallas kernels, layer(): pl.pallas_call(layer_kernel, out_shape=shape((rows, cols), BF16), in_spec...  1.99 us
    pallas_call x2, Pallas kernels, head_grads(): pl.pallas_call(functools.partial(grads_kernel, first), out_shape=shape((r...  1.5 us
  transfers between devices with their start and end apart: 22, of which 9 were waited for; matrix products, arithmetic and copies ran while one was open for 1% of the time, Pallas kernels for 28%

profile of v10, /device:TPU:0, one launch (start us, length us, event | category | flops | bytes accessed | tf_op | source)
XLA Modules:
  0.0 71.6 jit_solution(1896797520530411378)
XLA Ops:
  0.7 1.0 %copy-done.2 = bf16[1024,256]{1,0:T(8,128)(2,1)S(1)} copy-done((bf16[1024,256]{1,0:T(8,128)(2,1)S(1)}, bf16[1024,256]{1,0:T(8,128)(2,1)}, u32[]{:S(2)}) %copy-start.2) | copy-done | bytes 524312
  1.7 0.2 copy-done.3
  1.8 0.3 shard_map.93
  2.2 0.0 copy-done.1
  2.2 0.6 collective-permute-start.3
  2.7 2.6 %collective-permute-start.7 = (bf16[1024,512]{1,0:T(8,128)(2,1)S(1)}, bf16[1024,512]{1,0:T(8,128)(2,1)S(1)}, u32[]{:S(2)}, u32[]{:S(2)}) collective-permute-start(bf16[1024,512]{1,0:T(8,128)(2,1)S(1)} %copy-done.1), channel_id=1, source_target_pairs={{0,2},{1,3},{2,0},{3,1},{4,6},{5,7},{6,4},{7,5},{8,10},{9,11},{10,... | collective-permute-start | bytes 3145736 | tf_op jit(solution)/shard_map/ppermute | solution.py:520
  5.3 1.5 %collective-permute-start = (f32[136,128]{1,0:T(8,128)S(1)}, f32[136,128]{1,0:T(8,128)S(1)}, u32[]{:S(2)}, u32[]{:S(2)}) collective-permute-start(f32[136,128]{1,0:T(8,128)S(1)} %get-tuple-element.57), channel_id=1, source_target_pairs={{0,4},{4,0},{8,12},{12,8},{16,20},{20,16},{24,28},{28,24},{1,5},{5... | collective-permute-start | bytes 208904 | tf_op jit(solution)/shard_map/ppermute | solution.py:520
  6.8 2.8 %collective-permute-done.refs_0_ = f32[136,128]{1,0:T(8,128)S(1)} collective-permute-done((f32[136,128]{1,0:T(8,128)S(1)}, f32[136,128]{1,0:T(8,128)S(1)}, u32[]{:S(2)}, u32[]{:S(2)}) %collective-permute-start) | collective-permute-done | bytes 69664 | tf_op jit(solution)/shard_map/ppermute | solution.py:520
  9.6 1.6 %collective-permute-start.1 = (f32[136,128]{1,0:T(8,128)S(1)}, f32[136,128]{1,0:T(8,128)S(1)}, u32[]{:S(2)}, u32[]{:S(2)}) collective-permute-start(f32[136,128]{1,0:T(8,128)S(1)} %add.24), channel_id=1, source_target_pairs={{0,8},{4,12},{8,0},{12,4},{16,24},{20,28},{24,16},{28,20},{1,9},{5... | collective-permute-start | bytes 208904 | tf_op jit(solution)/shard_map/ppermute | solution.py:520
  11.3 1.6 %collective-permute-start.4 = (bf16[256,128]{1,0:T(8,128)(2,1)S(1)}, bf16[256,128]{1,0:T(8,128)(2,1)S(1)}, u32[]{:S(2)}, u32[]{:S(2)}) collective-permute-start(bf16[256,128]{1,0:T(8,128)(2,1)S(1)} %convert_element_type.51), channel_id=1, source_target_pairs={{0,4},{4,0},{8,12},{12,8},{16,20},{20,16},{24,28},{28,24},{1,5},{5... | collective-permute-start | bytes 196616 | tf_op jit(solution)/shard_map/ppermute | solution.py:520
  12.9 1.1 %collective-permute-done.1.refs_1_ = f32[136,128]{1,0:T(8,128)S(1)} collective-permute-done((f32[136,128]{1,0:T(8,128)S(1)}, f32[136,128]{1,0:T(8,128)S(1)}, u32[]{:S(2)}, u32[]{:S(2)}) %collective-permute-start.1) | collective-permute-done | bytes 69664 | tf_op jit(solution)/shard_map/ppermute | solution.py:520
  14.0 1.6 %collective-permute-done.4.refs_0_ = bf16[256,128]{1,0:T(8,128)(2,1)S(1)} collective-permute-done((bf16[256,128]{1,0:T(8,128)(2,1)S(1)}, bf16[256,128]{1,0:T(8,128)(2,1)S(1)}, u32[]{:S(2)}, u32[]{:S(2)}) %collective-permute-start.4) | collective-permute-done | bytes 65568 | tf_op jit(solution)/shard_map/ppermute | solution.py:520
  15.6 0.5 collective-permute-start.5
  16.1 2.6 %collective-permute-start.2 = (f32[136,128]{1,0:T(8,128)S(1)}, f32[136,128]{1,0:T(8,128)S(1)}, u32[]{:S(2)}, u32[]{:S(2)}) collective-permute-start(f32[136,128]{1,0:T(8,128)S(1)} %add.25), channel_id=1, source_target_pairs={{0,16},{4,20},{8,24},{12,28},{16,0},{20,4},{24,8},{28,12},{1,17},{... | collective-permute-start | bytes 208904 | tf_op jit(solution)/shard_map/ppermute | solution.py:520
  18.7 1.2 %collective-permute-done.5.refs_1_ = bf16[256,128]{1,0:T(8,128)(2,1)S(1)} collective-permute-done((bf16[256,128]{1,0:T(8,128)(2,1)S(1)}, bf16[256,128]{1,0:T(8,128)(2,1)S(1)}, u32[]{:S(2)}, u32[]{:S(2)}) %collective-permute-start.5) | collective-permute-done | bytes 65568 | tf_op jit(solution)/shard_map/ppermute | solution.py:520
  20.0 3.0 %collective-permute-start.6 = (bf16[256,128]{1,0:T(8,128)(2,1)S(1)}, bf16[256,128]{1,0:T(8,128)(2,1)S(1)}, u32[]{:S(2)}, u32[]{:S(2)}) collective-permute-start(bf16[256,128]{1,0:T(8,128)(2,1)S(1)} %add_convert_fusion.2), channel_id=1, source_target_pairs={{0,16},{4,20},{8,24},{12,28},{16,0},{20,4},{24,8},{28,12},{1,17},{... | collective-permute-start | bytes 196616 | tf_op jit(solution)/shard_map/ppermute | solution.py:520
  23.0 0.7 %shard_map.94.refs_0_ = f32[1024,256]{1,0:T(8,128)S(1)} custom-call(bf16[256,2048]{1,0:T(8,128)(2,1)S(1)} %copy-done, bf16[1024,512]{1,0:T(8,128)(2,1)S(1)} %copy-done.1, bf16[1024,512]{1,0:T(8,128)(2,1)S(1)} %collective-permute-done.3.refs_1_), custom_call_target="tpu_custom_call" | custom-call | flops 536870912 | bytes 4000000 | tf_op jit(solution)/shard_map/pallas_call | solution.py:426
  23.8 0.0 copy-start.4
  23.8 4.2 %shard_map.95 = (bf16[8,8,128,128]{3,2,1,0:T(8,128)(2,1)S(1)}, bf16[8,8,128,128]{3,2,1,0:T(8,128)(2,1)S(1)}, f32[8,128,128]{2,1,0:T(8,128)S(1)}, f32[8,128,128]{2,1,0:T(8,128)S(1)}) custom-call(bf16[1024,256]{1,0:T(8,128)(2,1)S(1)} %copy-done.2, f32[136,128]{1,0:T(8,128)S(1)} %collective-permute-done.refs_0_, f32[136,128]{1,0:T(8,128)S(1)} %collective-permute-done.1.refs_1_, ...), custom_call_target="tpu_custom_call" | custom-call | flops 2000000000 | bytes 8000000 | tf_op jit(solution)/shard_map/pallas_call | solution.py:181
  28.0 1.0 %collective-permute-done.7.refs_1_.refs_2_ = bf16[1024,512]{1,0:T(8,128)(2,1)S(1)} collective-permute-done((bf16[1024,512]{1,0:T(8,128)(2,1)S(1)}, bf16[1024,512]{1,0:T(8,128)(2,1)S(1)}, u32[]{:S(2)}, u32[]{:S(2)}) %collective-permute-start.7) | collective-permute-done | bytes 1048608 | tf_op jit(solution)/shard_map/ppermute | solution.py:520
  29.0 0.1 shard_map.101
  29.1 1.8 %collective-permute-start.15 = (bf16[2,256,512]{2,1,0:T(8,128)(2,1)S(1)}, bf16[2,256,512]{2,1,0:T(8,128)(2,1)S(1)}, u32[]{:S(2)}, u32[]{:S(2)}) collective-permute-start(bf16[2,256,512]{2,1,0:T(8,128)(2,1)S(1)} %get-tuple-element.89), channel_id=1, source_target_pairs={{0,2},{1,3},{2,0},{3,1},{4,6},{5,7},{6,4},{7,5},{8,10},{9,11},{10,... | collective-permute-start | bytes 1572872 | tf_op jit(solution)/shard_map/ppermute | solution.py:520
  30.9 2.4 %shard_map.97 = (bf16[1024,256]{1,0:T(8,128)(2,1)S(1)}, bf16[8,128,256]{2,1,0:T(8,128)(2,1)S(1)}, bf16[8,256,256]{2,1,0:T(8,128)(2,1)S(1)}, bf16[8,256,256]{2,1,0:T(8,128)(2,1)S(1)}) custom-call(f32[8,128]{1,0:T(8,128)S(1)} %shard_map.96.mark_ref, bf16[1024,256]{1,0:T(8,128)(2,1)S(1)} %copy-done.4, bf16[1024,256]{1,0:T(8,128)(2,1)S(1)} %copy-done.2, ...), custom_call_target="tpu_custom_call" | custom-call | flops 2000000000 | bytes 8000000 | tf_op jit(solution)/shard_map/pallas_call | solution.py:218
  33.4 0.7 %shard_map.98.do_ref = bf16[1024,256]{1,0:T(8,128)(2,1)S(1)} custom-call(bf16[256,2048]{1,0:T(8,128)(2,1)S(1)} %copy-done, f32[1024,256]{1,0:T(8,128)S(1)} %shard_map.94.refs_0_, bf16[1024,512]{1,0:T(8,128)(2,1)S(1)} %collective-permute-done.7.refs_1_.refs_2_, bf16[1024,512]{1,0:T(8,128)(2,1)S(1)} %collective-permute-done.8.refs_2_.refs_3_), custom_call_target="tpu_custom_call" | custom-call | flops 536870912 | bytes 4000000 | tf_op jit(solution)/shard_map/pallas_call | solution.py:426
  34.1 1.4 %shard_map.99 = (bf16[2,256,256]{2,1,0:T(8,128)(2,1)S(1)}, bf16[2,256,256]{2,1,0:T(8,128)(2,1)S(1)}, bf16[2,256,256]{2,1,0:T(8,128)(2,1)S(1)}, bf16[2,256,256]{2,1,0:T(8,128)(2,1)S(1)}) custom-call(bf16[1024,256]{1,0:T(8,128)(2,1)S(1)} %get-tuple-element.77.h_ref.refs_0_, bf16[1024,512]{1,0:T(8,128)(2,1)S(1)} %copy-done.1, ...), custom_call_target="tpu_custom_call" | custom-call | flops 1073741824 | bytes 6000000 | tf_op jit(solution)/shard_map/pallas_call | solution.py:476
  35.5 1.6 %collective-permute-start.12 = (bf16[2,256,256]{2,1,0:T(8,128)(2,1)S(1)}, bf16[2,256,256]{2,1,0:T(8,128)(2,1)S(1)}, u32[]{:S(2)}, u32[]{:S(2)}) collective-permute-start(bf16[2,256,256]{2,1,0:T(8,128)(2,1)S(1)} %get-tuple-element.80), channel_id=1, source_target_pairs={{0,4},{4,0},{8,12},{12,8},{16,20},{20,16},{24,28},{28,24},{1,5},{5... | collective-permute-start | bytes 786440 | tf_op jit(solution)/shard_map/ppermute | solution.py:520
  37.1 6.7 %shard_map.100 = (bf16[8,256,256]{2,1,0:T(8,128)(2,1)S(1)}, bf16[1024,256]{1,0:T(8,128)(2,1)S(1)}, f32[8,128,128]{2,1,0:T(8,128)S(1)}, f32[8,128,128]{2,1,0:T(8,...) custom-call(bf16[1024,256]{1,0:T(8,128)(2,1)S(1)} %copy-done.4, bf16[1024,256]{1,0:T(8,128)(2,1)S(1)} %copy-done.2, ...), custom_call_target="tpu_custom_call" | custom-call | flops 4000000000 | bytes 8000000 | tf_op jit(solution)/shard_map/pallas_call | solution.py:290
  43.8 0.6 collective-permute-start.11
  44.4 0.3 collective-permute-start.10
  44.7 1.8 %collective-permute-start.17 = (bf16[2,256,256]{2,1,0:T(8,128)(2,1)S(1)}, bf16[2,256,256]{2,1,0:T(8,128)(2,1)S(1)}, u32[]{:S(2)}, u32[]{:S(2)}) collective-permute-start(bf16[2,256,256]{2,1,0:T(8,128)(2,1)S(1)} %get-tuple-element.95), channel_id=1, source_target_pairs={{0,4},{4,0},{8,12},{12,8},{16,20},{20,16},{24,28},{28,24},{1,5},{5... | collective-permute-start | bytes 786440 | tf_op jit(solution)/shard_map/ppermute | solution.py:520
  46.4 0.1 add_convert_fusion
  46.5 2.8 %collective-permute-done.11.refs_0_ = bf16[392,128]{1,0:T(8,128)(2,1)S(1)} collective-permute-done((bf16[392,128]{1,0:T(8,128)(2,1)S(1)}, bf16[392,128]{1,0:T(8,128)(2,1)S(1)}, u32[]{:S(2)}, u32[]{:S(2)}) %collective-permute-start.11) | collective-permute-done | bytes 100384 | tf_op jit(solution)/shard_map/ppermute | solution.py:520
  49.3 3.4 %collective-permute-start.20 = (bf16[256,256]{1,0:T(8,128)(2,1)S(1)}, bf16[256,256]{1,0:T(8,128)(2,1)S(1)}, u32[]{:S(2)}, u32[]{:S(2)}) collective-permute-start(bf16[256,256]{1,0:T(8,128)(2,1)S(1)} %get-tuple-element.115), channel_id=1, source_target_pairs={{0,24},{4,28},{8,16},{12,20},{16,8},{20,12},{24,0},{28,4},{1,25},{... | collective-permute-start | bytes 393224 | tf_op jit(solution)/shard_map/ppermute | solution.py:520
  52.7 1.4 %collective-permute-done.17 = bf16[2,256,256]{2,1,0:T(8,128)(2,1)S(1)} collective-permute-done((bf16[2,256,256]{2,1,0:T(8,128)(2,1)S(1)}, bf16[2,256,256]{2,1,0:T(8,128)(2,1)S(1)}, u32[]{:S(2)}, u32[]{:S(2)}) %collective-permute-start.17) | collective-permute-done | bytes 262176 | tf_op jit(solution)/shard_map/ppermute | solution.py:520
  54.2 1.6 %collective-permute-start.13 = (bf16[392,128]{1,0:T(8,128)(2,1)S(1)}, bf16[392,128]{1,0:T(8,128)(2,1)S(1)}, u32[]{:S(2)}, u32[]{:S(2)}) collective-permute-start(bf16[392,128]{1,0:T(8,128)(2,1)S(1)} %fusion), channel_id=1, source_target_pairs={{0,8},{4,12},{8,0},{12,4},{16,24},{20,28},{24,16},{28,20},{1,9},{5... | collective-permute-start | bytes 301064 | tf_op jit(solution)/shard_map/ppermute | solution.py:520
  55.8 0.1 convert_add_fusion
  55.8 2.7 %collective-permute-start.19 = (bf16[256,256]{1,0:T(8,128)(2,1)S(1)}, bf16[256,256]{1,0:T(8,128)(2,1)S(1)}, u32[]{:S(2)}, u32[]{:S(2)}) collective-permute-start(bf16[256,256]{1,0:T(8,128)(2,1)S(1)} %get-tuple-element.116), channel_id=1, source_target_pairs={{0,16},{4,20},{8,24},{12,28},{16,0},{20,4},{24,8},{28,12},{1,17},{... | collective-permute-start | bytes 393224 | tf_op jit(solution)/shard_map/ppermute | solution.py:520
  58.5 0.1 slice_bitcast_fusion.3
  58.6 0.1 pad_maximum_fusion
  58.6 1.0 %collective-permute-done.13.refs_1_ = bf16[392,128]{1,0:T(8,128)(2,1)S(1)} collective-permute-done((bf16[392,128]{1,0:T(8,128)(2,1)S(1)}, bf16[392,128]{1,0:T(8,128)(2,1)S(1)}, u32[]{:S(2)}, u32[]{:S(2)}) %collective-permute-start.13) | collective-permute-done | bytes 100384 | tf_op jit(solution)/shard_map/ppermute | solution.py:520
  59.8 0.6 collective-permute-start.14
  60.3 2.1 %shard_map.103 = (bf16[1024,256]{1,0:T(8,128)(2,1)}, f32[1024,256]{1,0:T(8,128)S(1)}, f32[1024,256]{1,0:T(8,128)S(1)}) custom-call(bf16[1024,256]{1,0:T(8,128)(2,1)S(1)} %copy-done.2, bf16[1024,256]{1,0:T(8,128)(2,1)S(1)} %copy-done.3, bf16[1024,256]{1,0:T(8,128)(2,1)S(1)} %shard_map.98.do_ref, f32[8,128,128]{2,1,0:T(8,128)S(1)} %get-tuple-element.61.refs_0_.last_ref, ...), custom_call_target="tpu_custom_call" | custom-call | flops 2000000000 | bytes 6000000 | tf_op jit(solution)/shard_map/pallas_call | solution.py:335
  62.5 0.8 %collective-permute-start.21 = (bf16[256,256]{1,0:T(8,128)(2,1)S(1)}, bf16[256,256]{1,0:T(8,128)(2,1)S(1)}, u32[]{:S(2)}, u32[]{:S(2)}) collective-permute-start(bf16[256,256]{1,0:T(8,128)(2,1)S(1)} %fusion.1), channel_id=1, source_target_pairs={{0,8},{4,12},{8,0},{12,4},{16,24},{20,28},{24,16},{28,20},{1,9},{5... | collective-permute-start | bytes 393224 | tf_op jit(solution)/shard_map/ppermute | solution.py:520
  63.3 3.6 %collective-permute-start.18 = (bf16[392,128]{1,0:T(8,128)(2,1)S(1)}, bf16[392,128]{1,0:T(8,128)(2,1)S(1)}, u32[]{:S(2)}, u32[]{:S(2)}) collective-permute-start(bf16[392,128]{1,0:T(8,128)(2,1)S(1)} %add_convert_fusion.1), channel_id=1, source_target_pairs={{0,16},{4,20},{8,24},{12,28},{16,0},{20,4},{24,8},{28,12},{1,17},{... | collective-permute-start | bytes 301064 | tf_op jit(solution)/shard_map/ppermute | solution.py:520
  66.9 2.0 %shard_map.102 = bf16[1024,512]{1,0:T(8,128)(2,1)} custom-call(bf16[1024,256]{1,0:T(8,128)(2,1)S(1)} %get-tuple-element.77.h_ref.refs_0_, bf16[1024,256]{1,0:T(8,128)(2,1)S(1)} %collective-permute-done.9.refs_1_, bf16[1024,256]{1,0:T(8,128)(2,1)S(1)} %collective-permute-done.10.refs_2_, bf16[1024,256]{1,0:T(8,128)(2,1)S(1)} %collective-permute-done.14.refs_3_, ...), custom_call_target="tpu_custom_call" | custom-call | flops 1073741824 | bytes 6000000 | tf_op jit(solution)/shard_map/pallas_call | solution.py:507
  68.9 1.2 %collective-permute-done.21.refs_6_ = bf16[256,256]{1,0:T(8,128)(2,1)S(1)} collective-permute-done((bf16[256,256]{1,0:T(8,128)(2,1)S(1)}, bf16[256,256]{1,0:T(8,128)(2,1)S(1)}, u32[]{:S(2)}, u32[]{:S(2)}) %collective-permute-start.21) | collective-permute-done | bytes 131104 | tf_op jit(solution)/shard_map/ppermute | solution.py:520
  70.1 0.0 collective-permute-done.18.refs_2_
  70.1 1.5 %shard_map.104 = (bf16[1024,256]{1,0:T(8,128)(2,1)}, bf16[1024,256]{1,0:T(8,128)(2,1)}, f32[256,256]{1,0:T(8,128)}) custom-call(bf16[1024,256]{1,0:T(8,128)(2,1)S(1)} %copy-done.2, bf16[1024,256]{1,0:T(8,128)(2,1)S(1)} %copy-done.3, f32[1024,256]{1,0:T(8,128)S(1)} %get-tuple-element.101.dk_ref, f32[1024,256]{1,0:T(8,128)S(1)} %get-tuple-element.102.dv_ref, ...), custom_call_target="tpu_custom_call" | custom-call | flops 1000000000 | bytes 6000000 | tf_op jit(solution)/shard_map/pallas_call | solution.py:383
  (34 shorter events, 0.3 us)
Async XLA Ops:
  0.6 1.0 %copy-start.2 = (bf16[1024,256]{1,0:T(8,128)(2,1)S(1)}, bf16[1024,256]{1,0:T(8,128)(2,1)}, u32[]{:S(2)}) copy-start(bf16[1024,256]{1,0:T(8,128)(2,1)} %k_ref.11) | copy-start | bytes 1572868
  0.6 1.2 %copy-start.3 = (bf16[1024,256]{1,0:T(8,128)(2,1)S(1)}, bf16[1024,256]{1,0:T(8,128)(2,1)}, u32[]{:S(2)}) copy-start(bf16[1024,256]{1,0:T(8,128)(2,1)} %v_ref.9) | copy-start | bytes 1572868
  0.7 1.5 %copy-start.1 = (bf16[1024,512]{1,0:T(8,128)(2,1)S(1)}, bf16[1024,512]{1,0:T(8,128)(2,1)}, u32[]{:S(2)}) copy-start(bf16[1024,512]{1,0:T(8,128)(2,1)} %refs_0_.3) | copy-start | bytes 3145732
  0.7 22.3 %copy-start = (bf16[256,2048]{1,0:T(8,128)(2,1)S(1)}, bf16[256,2048]{1,0:T(8,128)(2,1)}, u32[]{:S(2)}) copy-start(bf16[256,2048]{1,0:T(8,128)(2,1)} %w_ref.4) | copy-start | bytes 3145732
  2.2 20.8 %collective-permute-start.3 = (bf16[1024,512]{1,0:T(8,128)(2,1)S(1)}, bf16[1024,512]{1,0:T(8,128)(2,1)S(1)}, u32[]{:S(2)}, u32[]{:S(2)}) collective-permute-start(bf16[1024,512]{1,0:T(8,128)(2,1)S(1)} %copy-done.1), channel_id=1, source_target_pairs={{0,1},{1,0},{2,3},{3,2},{4,5},{5,4},{6,7},{7,6},{8,9},{9,8},{10,11... | collective-permute-start | bytes 3145736 | tf_op jit(solution)/shard_map/ppermute | solution.py:520
  2.7 26.3 %collective-permute-start.7 = (bf16[1024,512]{1,0:T(8,128)(2,1)S(1)}, bf16[1024,512]{1,0:T(8,128)(2,1)S(1)}, u32[]{:S(2)}, u32[]{:S(2)}) collective-permute-start(bf16[1024,512]{1,0:T(8,128)(2,1)S(1)} %copy-done.1), channel_id=1, source_target_pairs={{0,2},{1,3},{2,0},{3,1},{4,6},{5,7},{6,4},{7,5},{8,10},{9,11},{10,... | collective-permute-start | bytes 3145736 | tf_op jit(solution)/shard_map/ppermute | solution.py:520
  5.3 4.3 %collective-permute-start = (f32[136,128]{1,0:T(8,128)S(1)}, f32[136,128]{1,0:T(8,128)S(1)}, u32[]{:S(2)}, u32[]{:S(2)}) collective-permute-start(f32[136,128]{1,0:T(8,128)S(1)} %get-tuple-element.57), channel_id=1, source_target_pairs={{0,4},{4,0},{8,12},{12,8},{16,20},{20,16},{24,28},{28,24},{1,5},{5... | collective-permute-start | bytes 208904 | tf_op jit(solution)/shard_map/ppermute | solution.py:520
  9.6 4.4 %collective-permute-start.1 = (f32[136,128]{1,0:T(8,128)S(1)}, f32[136,128]{1,0:T(8,128)S(1)}, u32[]{:S(2)}, u32[]{:S(2)}) collective-permute-start(f32[136,128]{1,0:T(8,128)S(1)} %add.24), channel_id=1, source_target_pairs={{0,8},{4,12},{8,0},{12,4},{16,24},{20,28},{24,16},{28,20},{1,9},{5... | collective-permute-start | bytes 208904 | tf_op jit(solution)/shard_map/ppermute | solution.py:520
  11.3 4.3 %collective-permute-start.4 = (bf16[256,128]{1,0:T(8,128)(2,1)S(1)}, bf16[256,128]{1,0:T(8,128)(2,1)S(1)}, u32[]{:S(2)}, u32[]{:S(2)}) collective-permute-start(bf16[256,128]{1,0:T(8,128)(2,1)S(1)} %convert_element_type.51), channel_id=1, source_target_pairs={{0,4},{4,0},{8,12},{12,8},{16,20},{20,16},{24,28},{28,24},{1,5},{5... | collective-permute-start | bytes 196616 | tf_op jit(solution)/shard_map/ppermute | solution.py:520
  15.6 4.3 %collective-permute-start.5 = (bf16[256,128]{1,0:T(8,128)(2,1)S(1)}, bf16[256,128]{1,0:T(8,128)(2,1)S(1)}, u32[]{:S(2)}, u32[]{:S(2)}) collective-permute-start(bf16[256,128]{1,0:T(8,128)(2,1)S(1)} %fusion.2), channel_id=1, source_target_pairs={{0,8},{4,12},{8,0},{12,4},{16,24},{20,28},{24,16},{28,20},{1,9},{5... | collective-permute-start | bytes 196616 | tf_op jit(solution)/shard_map/ppermute | solution.py:520
  16.1 7.6 %collective-permute-start.2 = (f32[136,128]{1,0:T(8,128)S(1)}, f32[136,128]{1,0:T(8,128)S(1)}, u32[]{:S(2)}, u32[]{:S(2)}) collective-permute-start(f32[136,128]{1,0:T(8,128)S(1)} %add.25), channel_id=1, source_target_pairs={{0,16},{4,20},{8,24},{12,28},{16,0},{20,4},{24,8},{28,12},{1,17},{... | collective-permute-start | bytes 208904 | tf_op jit(solution)/shard_map/ppermute | solution.py:520
  20.0 8.0 %collective-permute-start.6 = (bf16[256,128]{1,0:T(8,128)(2,1)S(1)}, bf16[256,128]{1,0:T(8,128)(2,1)S(1)}, u32[]{:S(2)}, u32[]{:S(2)}) collective-permute-start(bf16[256,128]{1,0:T(8,128)(2,1)S(1)} %add_convert_fusion.2), channel_id=1, source_target_pairs={{0,16},{4,20},{8,24},{12,28},{16,0},{20,4},{24,8},{28,12},{1,17},{... | collective-permute-start | bytes 196616 | tf_op jit(solution)/shard_map/ppermute | solution.py:520
  23.8 7.2 %copy-start.4 = (bf16[1024,256]{1,0:T(8,128)(2,1)S(1)}, bf16[1024,256]{1,0:T(8,128)(2,1)}, u32[]{:S(2)}) copy-start(bf16[1024,256]{1,0:T(8,128)(2,1)} %q_ref.3) | copy-start | bytes 1572868
  29.0 4.3 %collective-permute-start.8 = (bf16[1024,512]{1,0:T(8,128)(2,1)S(1)}, bf16[1024,512]{1,0:T(8,128)(2,1)S(1)}, u32[]{:S(2)}, u32[]{:S(2)}) collective-permute-start(bf16[1024,512]{1,0:T(8,128)(2,1)S(1)} %collective-permute-done.7.refs_1_.refs_2_), channel_id=1, source_target_pairs={{0,1},{1,0},{2,3},{3,2},{4,5},{5,4},{6,7},{7,6},{8,9},{9,8},{10,11... | collective-permute-start | bytes 3145736 | tf_op jit(solution)/shard_map/ppermute | solution.py:520
  29.1 26.7 %collective-permute-start.15 = (bf16[2,256,512]{2,1,0:T(8,128)(2,1)S(1)}, bf16[2,256,512]{2,1,0:T(8,128)(2,1)S(1)}, u32[]{:S(2)}, u32[]{:S(2)}) collective-permute-start(bf16[2,256,512]{2,1,0:T(8,128)(2,1)S(1)} %get-tuple-element.89), channel_id=1, source_target_pairs={{0,2},{1,3},{2,0},{3,1},{4,6},{5,7},{6,4},{7,5},{8,10},{9,11},{10,... | collective-permute-start | bytes 1572872 | tf_op jit(solution)/shard_map/ppermute | solution.py:520
  35.5 9.2 %collective-permute-start.12 = (bf16[2,256,256]{2,1,0:T(8,128)(2,1)S(1)}, bf16[2,256,256]{2,1,0:T(8,128)(2,1)S(1)}, u32[]{:S(2)}, u32[]{:S(2)}) collective-permute-start(bf16[2,256,256]{2,1,0:T(8,128)(2,1)S(1)} %get-tuple-element.80), channel_id=1, source_target_pairs={{0,4},{4,0},{8,12},{12,8},{16,20},{20,16},{24,28},{28,24},{1,5},{5... | collective-permute-start | bytes 786440 | tf_op jit(solution)/shard_map/ppermute | solution.py:520
  43.8 5.5 %collective-permute-start.11 = (bf16[392,128]{1,0:T(8,128)(2,1)S(1)}, bf16[392,128]{1,0:T(8,128)(2,1)S(1)}, u32[]{:S(2)}, u32[]{:S(2)}) collective-permute-start(bf16[392,128]{1,0:T(8,128)(2,1)S(1)} %get-tuple-element.76), channel_id=1, source_target_pairs={{0,4},{4,0},{8,12},{12,8},{16,20},{20,16},{24,28},{28,24},{1,5},{5... | collective-permute-start | bytes 301064 | tf_op jit(solution)/shard_map/ppermute | solution.py:520
  44.4 15.4 %collective-permute-start.10 = (bf16[1024,256]{1,0:T(8,128)(2,1)S(1)}, bf16[1024,256]{1,0:T(8,128)(2,1)S(1)}, u32[]{:S(2)}, u32[]{:S(2)}) collective-permute-start(bf16[1024,256]{1,0:T(8,128)(2,1)S(1)} %get-tuple-element.77.h_ref.refs_0_), channel_id=1, source_target_pairs={{0,2},{1,3},{2,0},{3,1},{4,6},{5,7},{6,4},{7,5},{8,10},{9,11},{10,... | collective-permute-start | bytes 1572872 | tf_op jit(solution)/shard_map/ppermute | solution.py:520
  44.7 18.6 %collective-permute-start.9 = (bf16[1024,256]{1,0:T(8,128)(2,1)S(1)}, bf16[1024,256]{1,0:T(8,128)(2,1)S(1)}, u32[]{:S(2)}, u32[]{:S(2)}) collective-permute-start(bf16[1024,256]{1,0:T(8,128)(2,1)S(1)} %get-tuple-element.77.h_ref.refs_0_), channel_id=1, source_target_pairs={{0,1},{1,0},{2,3},{3,2},{4,5},{5,4},{6,7},{7,6},{8,9},{9,8},{10,11... | collective-permute-start | bytes 1572872 | tf_op jit(solution)/shard_map/ppermute | solution.py:520
  44.7 9.5 %collective-permute-start.17 = (bf16[2,256,256]{2,1,0:T(8,128)(2,1)S(1)}, bf16[2,256,256]{2,1,0:T(8,128)(2,1)S(1)}, u32[]{:S(2)}, u32[]{:S(2)}) collective-permute-start(bf16[2,256,256]{2,1,0:T(8,128)(2,1)S(1)} %get-tuple-element.95), channel_id=1, source_target_pairs={{0,4},{4,0},{8,12},{12,8},{16,20},{20,16},{24,28},{28,24},{1,5},{5... | collective-permute-start | bytes 786440 | tf_op jit(solution)/shard_map/ppermute | solution.py:520
  49.3 20.7 %collective-permute-start.20 = (bf16[256,256]{1,0:T(8,128)(2,1)S(1)}, bf16[256,256]{1,0:T(8,128)(2,1)S(1)}, u32[]{:S(2)}, u32[]{:S(2)}) collective-permute-start(bf16[256,256]{1,0:T(8,128)(2,1)S(1)} %get-tuple-element.115), channel_id=1, source_target_pairs={{0,24},{4,28},{8,16},{12,20},{16,8},{20,12},{24,0},{28,4},{1,25},{... | collective-permute-start | bytes 393224 | tf_op jit(solution)/shard_map/ppermute | solution.py:520
  54.2 5.5 %collective-permute-start.13 = (bf16[392,128]{1,0:T(8,128)(2,1)S(1)}, bf16[392,128]{1,0:T(8,128)(2,1)S(1)}, u32[]{:S(2)}, u32[]{:S(2)}) collective-permute-start(bf16[392,128]{1,0:T(8,128)(2,1)S(1)} %fusion), channel_id=1, source_target_pairs={{0,8},{4,12},{8,0},{12,4},{16,24},{20,28},{24,16},{28,20},{1,9},{5... | collective-permute-start | bytes 301064 | tf_op jit(solution)/shard_map/ppermute | solution.py:520
  55.8 14.2 %collective-permute-start.19 = (bf16[256,256]{1,0:T(8,128)(2,1)S(1)}, bf16[256,256]{1,0:T(8,128)(2,1)S(1)}, u32[]{:S(2)}, u32[]{:S(2)}) collective-permute-start(bf16[256,256]{1,0:T(8,128)(2,1)S(1)} %get-tuple-element.116), channel_id=1, source_target_pairs={{0,16},{4,20},{8,24},{12,28},{16,0},{20,4},{24,8},{28,12},{1,17},{... | collective-permute-start | bytes 393224 | tf_op jit(solution)/shard_map/ppermute | solution.py:520
  59.7 2.8 %collective-permute-start.16 = (bf16[2,256,512]{2,1,0:T(8,128)(2,1)S(1)}, bf16[2,256,512]{2,1,0:T(8,128)(2,1)S(1)}, u32[]{:S(2)}, u32[]{:S(2)}) collective-permute-start(bf16[2,256,512]{2,1,0:T(8,128)(2,1)S(1)} %pad_maximum_fusion), channel_id=1, source_target_pairs={{0,1},{1,0},{2,3},{3,2},{4,5},{5,4},{6,7},{7,6},{8,9},{9,8},{10,11... | collective-permute-start | bytes 1572872 | tf_op jit(solution)/shard_map/ppermute | solution.py:520
  59.8 7.1 %collective-permute-start.14 = (bf16[1024,256]{1,0:T(8,128)(2,1)S(1)}, bf16[1024,256]{1,0:T(8,128)(2,1)S(1)}, u32[]{:S(2)}, u32[]{:S(2)}) collective-permute-start(bf16[1024,256]{1,0:T(8,128)(2,1)S(1)} %collective-permute-done.10.refs_2_), channel_id=1, source_target_pairs={{0,1},{1,0},{2,3},{3,2},{4,5},{5,4},{6,7},{7,6},{8,9},{9,8},{10,11... | collective-permute-start | bytes 1572872 | tf_op jit(solution)/shard_map/ppermute | solution.py:520
  62.5 7.6 %collective-permute-start.21 = (bf16[256,256]{1,0:T(8,128)(2,1)S(1)}, bf16[256,256]{1,0:T(8,128)(2,1)S(1)}, u32[]{:S(2)}, u32[]{:S(2)}) collective-permute-start(bf16[256,256]{1,0:T(8,128)(2,1)S(1)} %fusion.1), channel_id=1, source_target_pairs={{0,8},{4,12},{8,0},{12,4},{16,24},{20,28},{24,16},{28,20},{1,9},{5... | collective-permute-start | bytes 393224 | tf_op jit(solution)/shard_map/ppermute | solution.py:520
  63.3 6.8 %collective-permute-start.18 = (bf16[392,128]{1,0:T(8,128)(2,1)S(1)}, bf16[392,128]{1,0:T(8,128)(2,1)S(1)}, u32[]{:S(2)}, u32[]{:S(2)}) collective-permute-start(bf16[392,128]{1,0:T(8,128)(2,1)S(1)} %add_convert_fusion.1), channel_id=1, source_target_pairs={{0,16},{4,20},{8,24},{12,28},{16,0},{20,4},{24,8},{28,12},{1,17},{... | collective-permute-start | bytes 301064 | tf_op jit(solution)/shard_map/ppermute | solution.py:520

commit v11 on v10

--- a/solution.py
+++ b/solution.py
@@ -302,7 +302,7 @@
 
 
 def rest_kernel(
-    k_ref, v_ref, do_ref, last_ref, s_ref, w_ref, p_ref, ds_ref, da_ref, dn_ref,
+    early_ref, k_ref, v_ref, do_ref, last_ref, s_ref, w_ref, p_ref, ds_ref, da_ref, dn_ref,
     dq_hbm, dk_ref, dv_ref, dq_ref, sems,
 ):
     heads = k_ref.shape[1] // HDIM
@@ -330,12 +330,12 @@
         copy.wait()
 
 
-def rest(keys, values, grads, *stash):
+def rest(early, keys, values, grads, *stash):
     wide = shape(keys.shape)
     return pl.pallas_call(
         rest_kernel,
         out_shape=(shape(keys.shape, BF16), wide, wide),
-        in_specs=[VMEM_SPEC] * 10,
+        in_specs=[VMEM_SPEC] * 11,
         out_specs=(ANY_SPEC, VMEM_SPEC, VMEM_SPEC),
         scratch_shapes=[
             pltpu.VMEM(keys.shape, BF16),
@@ -343,7 +343,7 @@
         ],
         compiler_params=params(),
         cost_estimate=cost(2_000_000_000, 6_000_000),
-    )(keys, values, grads, *stash)
+    )(early, keys, values, grads, *stash)
 
 
 def finish_kernel(rounds, k_ref, v_ref, dk_ref, dv_ref, *refs):
@@ -484,7 +484,7 @@
     )(heads_out, *parts)
 
 
-def layer_kernel(*refs):
+def layer_kernel(mark_ref, *refs):
     hbm, ref, sems = refs[-3:]
     count = (len(refs) - 3) // 2
     step = ref.shape[0] // sems.shape[0]
@@ -502,17 +502,17 @@
         copy.wait()
 
 
-def layer(parts, columns):
+def layer(mark, parts, columns):
     rows, cols = parts[0].shape[0], columns[0].shape[1]
     return pl.pallas_call(
         layer_kernel,
         out_shape=shape((rows, cols), BF16),
-        in_specs=[VMEM_SPEC] * (len(parts) + len(columns)),
+        in_specs=[VMEM_SPEC] * (1 + len(parts) + len(columns)),
         out_specs=ANY_SPEC,
         scratch_shapes=[pltpu.VMEM((rows, cols), BF16), pltpu.SemaphoreType.DMA((4,))],
         compiler_params=params(),
         cost_estimate=cost(2 * rows * cols * sum(p.shape[1] for p in parts), 6_000_000),
-    )(*parts, *columns)
+    )(mark, *parts, *columns)
 
 
 def swap(value, axis, distance):
@@ -564,15 +564,14 @@
     mark = lead(1000, last)
     heads_out, states, solved, scores = outputs(mark, queries, keys, values, last, pairs)
 
-    grads = head_grads(w_out, parts, 2, after(begun, heads_out))
-    parts = [cotangent, near] + parts
     even_low, even_high, odd_low, odd_high = weight_terms(
-        after(heads_out, grads), parts, ctx_count
+        heads_out, [cotangent, near] + parts, ctx_count
     )
     high = swap(odd_high, "ctx", 1)
+    grads = head_grads(w_out, parts, 2, after(begun, odd_low))
 
     weights, ds, da, dn, sums, send = tangent(
-        queries, keys, values, after(grads, odd_low), [*stash, last, ridged, states, solved]
+        queries, keys, values, grads, [*stash, last, ridged, states, solved]
     )
 
     low = swap(after(odd_low, send), "ctx", 1)
@@ -583,6 +582,7 @@
     high = [high[u].astype(BF16) for u in range(half)]
     moved = [swap(part, "ctx", 2 * (half + u)) for u, part in enumerate(high)]
 
+    early = lead(1000, send)
     later, sends = [], []
     for distance in doublings("ctx"):
         sends.append(send)
@@ -592,20 +592,21 @@
         sums = sums + later[-1].astype(F32)
         send = sums.astype(BF16)
 
-    low = even_low.astype(F32) + after(low, sends[1]).astype(F32)
+    grad_queries, dk, dv = rest(
+        early, keys, values, grads, last, solved, scores, weights, after(ds, sends[1]), da, dn
+    )
+
+    mark = lead(1000, sends[-1])
+    low = even_low.astype(F32) + after(low, sends[-1]).astype(F32)
     moved += [swap(low[u].astype(BF16), "ctx", 2 * u) for u in range(1, half)]
-    grad_queries, dk, dv = rest(
-        keys, values, grads, last, solved, scores, weights, after(ds, low), da, dn
-    )
-
     outs = [heads_out, swap(outs_out, "head", 1)]
     for part in outs_far:
-        outs += [part, swap(after(part, sends[-1]), "head", 1)]
+        outs += [part, swap(after(part, sends[1]), "head", 1)]
     columns = [after(c, sends[1]) for c in columns]
     crossing = jnp.stack([c[1] for c in columns])
     crossing = swap(crossing, "head", 1)
     columns = [c for s in range(head_count // 2) for c in (columns[s][0], crossing[s])]
-    layer_out = layer(outs, columns)
+    layer_out = layer(mark, outs, columns)
     moved = [after(part, layer_out) for part in moved]
     grad_keys, grad_values, grad_weight = finish(keys, values, dk, dv, later, low[0], moved)
     return (layer_out, grad_queries, grad_keys, grad_values, grad_weight)

time: 71.7 us -> 70.6 us (0.985)
  starting transfers between devices: 32.6 us -> 28.7 us
  waiting for transfers between devices: 14.3 us -> 16.9 us
    ppermute x22, starting transfers between devices: 32.6 us -> 28.7 us  [swap(): return lax.ppermute(value, axis, [(i, i ^ distance) for i in range(count)])]
    ppermute x22, waiting for transfers between devices: 14.3 us -> 16.9 us  [swap(): return lax.ppermute(value, axis, [(i, i ^ distance) for i in range(count)])]
  transfers between devices with their start and end apart: 22 -> 22, of which waited for: 9 -> 10; matrix products, arithmetic and copies ran while one was open for 1% -> 1% of each run, Pallas kernels for 28% -> 29%
where the time goes in v11:
time: 70.6 us; the launch traced here: 70.4 us
  starting transfers between devices  28.7 us (41%)
  Pallas kernels  22.3 us (32%)
  waiting for transfers between devices  16.9 us (24%)
  local copies, waits for them, and re-layouts  1.36 us (2%)
  between operations  0.9 us (1%)
    ppermute x22, starting transfers between devices, swap(): return lax.ppermute(value, axis, [(i, i ^ distance) for i in range(count)])  28.7 us
    ppermute x22, waiting for transfers between devices, swap(): return lax.ppermute(value, axis, [(i, i ^ distance) for i in range(count)])  16.9 us
    pallas_call x1, Pallas kernels, tangent(): pl.pallas_call(tangent_kernel, out_shape=(shape((count, SPAN, SPAN), BF16...  6.8 us
    pallas_call x1, Pallas kernels, inverses(): pl.pallas_call(functools.partial(inverse_kernel, len(grams)), out_shape=(...  4.23 us
    pallas_call x1, Pallas kernels, outputs(): pl.pallas_call(functools.partial(outputs_kernel, len(pairs)), out_shape=(...  2.4 us
    pallas_call x1, Pallas kernels, rest(): pl.pallas_call(rest_kernel, out_shape=(shape(keys.shape, BF16), wide, wid...  2.09 us
    pallas_call x1, Pallas kernels, layer(): pl.pallas_call(layer_kernel, out_shape=shape((rows, cols), BF16), in_spec...  1.99 us
    pallas_call x2, Pallas kernels, head_grads(): pl.pallas_call(functools.partial(grads_kernel, first), out_shape=shape((r...  1.49 us
  transfers between devices with their start and end apart: 22, of which 10 were waited for; matrix products, arithmetic and copies ran while one was open for 1% of the time, Pallas kernels for 29%

profile of v11, /device:TPU:0, one launch (start us, length us, event | category | flops | bytes accessed | tf_op | source)
XLA Modules:
  0.0 70.4 jit_solution(1887509213325258238)
XLA Ops:
  0.7 1.0 %copy-done.2 = bf16[1024,256]{1,0:T(8,128)(2,1)S(1)} copy-done((bf16[1024,256]{1,0:T(8,128)(2,1)S(1)}, bf16[1024,256]{1,0:T(8,128)(2,1)}, u32[]{:S(2)}) %copy-start.2) | copy-done | bytes 524312
  1.7 0.2 copy-done.3
  1.8 0.3 shard_map.93
  2.2 0.0 copy-done.1
  2.2 0.6 collective-permute-start
  2.7 2.6 %collective-permute-start.7 = (bf16[1024,512]{1,0:T(8,128)(2,1)S(1)}, bf16[1024,512]{1,0:T(8,128)(2,1)S(1)}, u32[]{:S(2)}, u32[]{:S(2)}) collective-permute-start(bf16[1024,512]{1,0:T(8,128)(2,1)S(1)} %copy-done.1), channel_id=1, source_target_pairs={{0,2},{1,3},{2,0},{3,1},{4,6},{5,7},{6,4},{7,5},{8,10},{9,11},{10,... | collective-permute-start | bytes 3145736 | tf_op jit(solution)/shard_map/ppermute | solution.py:520
  5.3 1.5 %collective-permute-start.1 = (f32[136,128]{1,0:T(8,128)S(1)}, f32[136,128]{1,0:T(8,128)S(1)}, u32[]{:S(2)}, u32[]{:S(2)}) collective-permute-start(f32[136,128]{1,0:T(8,128)S(1)} %get-tuple-element.55), channel_id=1, source_target_pairs={{0,4},{4,0},{8,12},{12,8},{16,20},{20,16},{24,28},{28,24},{1,5},{5... | collective-permute-start | bytes 208904 | tf_op jit(solution)/shard_map/ppermute | solution.py:520
  6.8 2.8 %collective-permute-done.1.refs_0_ = f32[136,128]{1,0:T(8,128)S(1)} collective-permute-done((f32[136,128]{1,0:T(8,128)S(1)}, f32[136,128]{1,0:T(8,128)S(1)}, u32[]{:S(2)}, u32[]{:S(2)}) %collective-permute-start.1) | collective-permute-done | bytes 69664 | tf_op jit(solution)/shard_map/ppermute | solution.py:520
  9.6 1.6 %collective-permute-start.2 = (f32[136,128]{1,0:T(8,128)S(1)}, f32[136,128]{1,0:T(8,128)S(1)}, u32[]{:S(2)}, u32[]{:S(2)}) collective-permute-start(f32[136,128]{1,0:T(8,128)S(1)} %add.24), channel_id=1, source_target_pairs={{0,8},{4,12},{8,0},{12,4},{16,24},{20,28},{24,16},{28,20},{1,9},{5... | collective-permute-start | bytes 208904 | tf_op jit(solution)/shard_map/ppermute | solution.py:520
  11.3 1.6 %collective-permute-start.4 = (bf16[256,128]{1,0:T(8,128)(2,1)S(1)}, bf16[256,128]{1,0:T(8,128)(2,1)S(1)}, u32[]{:S(2)}, u32[]{:S(2)}) collective-permute-start(bf16[256,128]{1,0:T(8,128)(2,1)S(1)} %convert_element_type.51), channel_id=1, source_target_pairs={{0,4},{4,0},{8,12},{12,8},{16,20},{20,16},{24,28},{28,24},{1,5},{5... | collective-permute-start | bytes 196616 | tf_op jit(solution)/shard_map/ppermute | solution.py:520
  12.9 1.1 %collective-permute-done.2.refs_1_ = f32[136,128]{1,0:T(8,128)S(1)} collective-permute-done((f32[136,128]{1,0:T(8,128)S(1)}, f32[136,128]{1,0:T(8,128)S(1)}, u32[]{:S(2)}, u32[]{:S(2)}) %collective-permute-start.2) | collective-permute-done | bytes 69664 | tf_op jit(solution)/shard_map/ppermute | solution.py:520
  14.0 1.6 %collective-permute-done.4.refs_0_ = bf16[256,128]{1,0:T(8,128)(2,1)S(1)} collective-permute-done((bf16[256,128]{1,0:T(8,128)(2,1)S(1)}, bf16[256,128]{1,0:T(8,128)(2,1)S(1)}, u32[]{:S(2)}, u32[]{:S(2)}) %collective-permute-start.4) | collective-permute-done | bytes 65568 | tf_op jit(solution)/shard_map/ppermute | solution.py:520
  15.6 0.5 collective-permute-start.5
  16.1 2.6 %collective-permute-start.3 = (f32[136,128]{1,0:T(8,128)S(1)}, f32[136,128]{1,0:T(8,128)S(1)}, u32[]{:S(2)}, u32[]{:S(2)}) collective-permute-start(f32[136,128]{1,0:T(8,128)S(1)} %add.25), channel_id=1, source_target_pairs={{0,16},{4,20},{8,24},{12,28},{16,0},{20,4},{24,8},{28,12},{1,17},{... | collective-permute-start | bytes 208904 | tf_op jit(solution)/shard_map/ppermute | solution.py:520
  18.7 1.2 %collective-permute-done.5.refs_1_ = bf16[256,128]{1,0:T(8,128)(2,1)S(1)} collective-permute-done((bf16[256,128]{1,0:T(8,128)(2,1)S(1)}, bf16[256,128]{1,0:T(8,128)(2,1)S(1)}, u32[]{:S(2)}, u32[]{:S(2)}) %collective-permute-start.5) | collective-permute-done | bytes 65568 | tf_op jit(solution)/shard_map/ppermute | solution.py:520
  20.0 3.0 %collective-permute-start.6 = (bf16[256,128]{1,0:T(8,128)(2,1)S(1)}, bf16[256,128]{1,0:T(8,128)(2,1)S(1)}, u32[]{:S(2)}, u32[]{:S(2)}) collective-permute-start(bf16[256,128]{1,0:T(8,128)(2,1)S(1)} %add_convert_fusion.2), channel_id=1, source_target_pairs={{0,16},{4,20},{8,24},{12,28},{16,0},{20,4},{24,8},{28,12},{1,17},{... | collective-permute-start | bytes 196616 | tf_op jit(solution)/shard_map/ppermute | solution.py:520
  23.0 0.7 %shard_map.94.refs_0_ = f32[1024,256]{1,0:T(8,128)S(1)} custom-call(bf16[256,2048]{1,0:T(8,128)(2,1)S(1)} %copy-done, bf16[1024,512]{1,0:T(8,128)(2,1)S(1)} %copy-done.1, bf16[1024,512]{1,0:T(8,128)(2,1)S(1)} %collective-permute-done.refs_1_), custom_call_target="tpu_custom_call" | custom-call | flops 536870912 | bytes 4000000 | tf_op jit(solution)/shard_map/pallas_call | solution.py:426
  23.8 0.0 copy-start.4
  23.8 4.2 %shard_map.95 = (bf16[8,8,128,128]{3,2,1,0:T(8,128)(2,1)S(1)}, bf16[8,8,128,128]{3,2,1,0:T(8,128)(2,1)S(1)}, f32[8,128,128]{2,1,0:T(8,128)S(1)}, f32[8,128,128]{2,1,0:T(8,128)S(1)}) custom-call(bf16[1024,256]{1,0:T(8,128)(2,1)S(1)} %copy-done.2, f32[136,128]{1,0:T(8,128)S(1)} %collective-permute-done.1.refs_0_, ...), custom_call_target="tpu_custom_call" | custom-call | flops 2000000000 | bytes 8000000 | tf_op jit(solution)/shard_map/pallas_call | solution.py:181
  28.0 1.0 %collective-permute-done.7.refs_2_.refs_1_ = bf16[1024,512]{1,0:T(8,128)(2,1)S(1)} collective-permute-done((bf16[1024,512]{1,0:T(8,128)(2,1)S(1)}, bf16[1024,512]{1,0:T(8,128)(2,1)S(1)}, u32[]{:S(2)}, u32[]{:S(2)}) %collective-permute-start.7) | collective-permute-done | bytes 1048608 | tf_op jit(solution)/shard_map/ppermute | solution.py:520
  29.0 0.1 shard_map.102
  29.1 1.8 %collective-permute-start.15 = (bf16[2,256,512]{2,1,0:T(8,128)(2,1)S(1)}, bf16[2,256,512]{2,1,0:T(8,128)(2,1)S(1)}, u32[]{:S(2)}, u32[]{:S(2)}) collective-permute-start(bf16[2,256,512]{2,1,0:T(8,128)(2,1)S(1)} %get-tuple-element.85), channel_id=1, source_target_pairs={{0,2},{1,3},{2,0},{3,1},{4,6},{5,7},{6,4},{7,5},{8,10},{9,11},{10,... | collective-permute-start | bytes 1572872 | tf_op jit(solution)/shard_map/ppermute | solution.py:520
  30.9 2.4 %shard_map.97 = (bf16[1024,256]{1,0:T(8,128)(2,1)S(1)}, bf16[8,128,256]{2,1,0:T(8,128)(2,1)S(1)}, bf16[8,256,256]{2,1,0:T(8,128)(2,1)S(1)}, bf16[8,256,256]{2,1,0:T(8,128)(2,1)S(1)}) custom-call(f32[8,128]{1,0:T(8,128)S(1)} %shard_map.96.mark_ref, bf16[1024,256]{1,0:T(8,128)(2,1)S(1)} %copy-done.4, bf16[1024,256]{1,0:T(8,128)(2,1)S(1)} %copy-done.2, ...), custom_call_target="tpu_custom_call" | custom-call | flops 2000000000 | bytes 8000000 | tf_op jit(solution)/shard_map/pallas_call | solution.py:218
  33.4 1.4 %shard_map.98 = (bf16[2,256,256]{2,1,0:T(8,128)(2,1)S(1)}, bf16[2,256,256]{2,1,0:T(8,128)(2,1)S(1)}, bf16[2,256,256]{2,1,0:T(8,128)(2,1)S(1)}, bf16[2,256,256]{2,1,0:T(8,128)(2,1)S(1)}) custom-call(bf16[1024,256]{1,0:T(8,128)(2,1)S(1)} %get-tuple-element.78.h_ref.refs_0_, bf16[1024,512]{1,0:T(8,128)(2,1)S(1)} %copy-done.1, ...), custom_call_target="tpu_custom_call" | custom-call | flops 1073741824 | bytes 6000000 | tf_op jit(solution)/shard_map/pallas_call | solution.py:476
  34.7 1.6 %collective-permute-start.10 = (bf16[2,256,256]{2,1,0:T(8,128)(2,1)S(1)}, bf16[2,256,256]{2,1,0:T(8,128)(2,1)S(1)}, u32[]{:S(2)}, u32[]{:S(2)}) collective-permute-start(bf16[2,256,256]{2,1,0:T(8,128)(2,1)S(1)} %get-tuple-element.75), channel_id=1, source_target_pairs={{0,4},{4,0},{8,12},{12,8},{16,20},{20,16},{24,28},{28,24},{1,5},{5... | collective-permute-start | bytes 786440 | tf_op jit(solution)/shard_map/ppermute | solution.py:520
  36.3 0.7 %shard_map.99.do_ref = bf16[1024,256]{1,0:T(8,128)(2,1)S(1)} custom-call(bf16[256,2048]{1,0:T(8,128)(2,1)S(1)} %copy-done, f32[1024,256]{1,0:T(8,128)S(1)} %shard_map.94.refs_0_, bf16[1024,512]{1,0:T(8,128)(2,1)S(1)} %collective-permute-done.7.refs_2_.refs_1_, bf16[1024,512]{1,0:T(8,128)(2,1)S(1)} %collective-permute-done.8.refs_3_.refs_2_), custom_call_target="tpu_custom_call" | custom-call | flops 536870912 | bytes 4000000 | tf_op jit(solution)/shard_map/pallas_call | solution.py:426
  37.1 6.8 %shard_map.100 = (bf16[8,256,256]{2,1,0:T(8,128)(2,1)S(1)}, bf16[1024,256]{1,0:T(8,128)(2,1)S(1)}, f32[8,128,128]{2,1,0:T(8,128)S(1)}, f32[8,128,128]{2,1,0:T(8,...) custom-call(bf16[1024,256]{1,0:T(8,128)(2,1)S(1)} %copy-done.4, bf16[1024,256]{1,0:T(8,128)(2,1)S(1)} %copy-done.2, ...), custom_call_target="tpu_custom_call" | custom-call | flops 4000000000 | bytes 8000000 | tf_op jit(solution)/shard_map/pallas_call | solution.py:290
  43.9 0.6 collective-permute-start.9
  44.4 0.3 collective-permute-start.13
  44.7 1.8 %collective-permute-start.18 = (bf16[2,256,256]{2,1,0:T(8,128)(2,1)S(1)}, bf16[2,256,256]{2,1,0:T(8,128)(2,1)S(1)}, u32[]{:S(2)}, u32[]{:S(2)}) collective-permute-start(bf16[2,256,256]{2,1,0:T(8,128)(2,1)S(1)} %get-tuple-element.97), channel_id=1, source_target_pairs={{0,4},{4,0},{8,12},{12,8},{16,20},{20,16},{24,28},{28,24},{1,5},{5... | collective-permute-start | bytes 786440 | tf_op jit(solution)/shard_map/ppermute | solution.py:520
  46.6 0.1 add_convert_fusion
  46.6 2.7 %collective-permute-done.9.refs_0_ = bf16[392,128]{1,0:T(8,128)(2,1)S(1)} collective-permute-done((bf16[392,128]{1,0:T(8,128)(2,1)S(1)}, bf16[392,128]{1,0:T(8,128)(2,1)S(1)}, u32[]{:S(2)}, u32[]{:S(2)}) %collective-permute-start.9) | collective-permute-done | bytes 100384 | tf_op jit(solution)/shard_map/ppermute | solution.py:520
  49.4 1.4 %collective-permute-start.11 = (bf16[392,128]{1,0:T(8,128)(2,1)S(1)}, bf16[392,128]{1,0:T(8,128)(2,1)S(1)}, u32[]{:S(2)}, u32[]{:S(2)}) collective-permute-start(bf16[392,128]{1,0:T(8,128)(2,1)S(1)} %fusion), channel_id=1, source_target_pairs={{0,8},{4,12},{8,0},{12,4},{16,24},{20,28},{24,16},{28,20},{1,9},{5... | collective-permute-start | bytes 301064 | tf_op jit(solution)/shard_map/ppermute | solution.py:520
  50.8 2.5 %collective-permute-start.20 = (bf16[256,256]{1,0:T(8,128)(2,1)S(1)}, bf16[256,256]{1,0:T(8,128)(2,1)S(1)}, u32[]{:S(2)}, u32[]{:S(2)}) collective-permute-start(bf16[256,256]{1,0:T(8,128)(2,1)S(1)} %get-tuple-element.111), channel_id=1, source_target_pairs={{0,24},{4,28},{8,16},{12,20},{16,8},{20,12},{24,0},{28,4},{1,25},{... | collective-permute-start | bytes 393224 | tf_op jit(solution)/shard_map/ppermute | solution.py:520
  53.3 0.1 slice_bitcast_fusion.3
  53.4 2.1 %shard_map.105 = (bf16[1024,256]{1,0:T(8,128)(2,1)}, f32[1024,256]{1,0:T(8,128)S(1)}, f32[1024,256]{1,0:T(8,128)S(1)}) custom-call(f32[8,128]{1,0:T(8,128)S(1)} %shard_map.104.early_ref, bf16[1024,256]{1,0:T(8,128)(2,1)S(1)} %copy-done.2, bf16[1024,256]{1,0:T(8,128)(2,1)S(1)} %copy-done.3, bf16[1024,256]{1,0:T(8,128)(2,1)S(1)} %shard_map.99.do_ref, ...), custom_call_target="tpu_custom_call" | custom-call | flops 2000000000 | bytes 6000000 | tf_op jit(solution)/shard_map/pallas_call | solution.py:335
  55.5 0.1 pad_maximum_fusion
  55.6 1.0 %collective-permute-start.19 = (bf16[256,256]{1,0:T(8,128)(2,1)S(1)}, bf16[256,256]{1,0:T(8,128)(2,1)S(1)}, u32[]{:S(2)}, u32[]{:S(2)}) collective-permute-start(bf16[256,256]{1,0:T(8,128)(2,1)S(1)} %get-tuple-element.112), channel_id=1, source_target_pairs={{0,16},{4,20},{8,24},{12,28},{16,0},{20,4},{24,8},{28,12},{1,17},{... | collective-permute-start | bytes 393224 | tf_op jit(solution)/shard_map/ppermute | solution.py:520
  56.7 0.1 collective-permute-start.16
  56.7 0.1 convert_add_fusion
  56.8 1.1 %collective-permute-done.13.refs_2_ = bf16[1024,256]{1,0:T(8,128)(2,1)S(1)} collective-permute-done((bf16[1024,256]{1,0:T(8,128)(2,1)S(1)}, bf16[1024,256]{1,0:T(8,128)(2,1)S(1)}, u32[]{:S(2)}, u32[]{:S(2)}) %collective-permute-start.13) | collective-permute-done | bytes 524320 | tf_op jit(solution)/shard_map/ppermute | solution.py:520
  58.0 0.7 collective-permute-done.16
  58.6 2.5 %collective-permute-start.21 = (bf16[256,256]{1,0:T(8,128)(2,1)S(1)}, bf16[256,256]{1,0:T(8,128)(2,1)S(1)}, u32[]{:S(2)}, u32[]{:S(2)}) collective-permute-start(bf16[256,256]{1,0:T(8,128)(2,1)S(1)} %fusion.1), channel_id=1, source_target_pairs={{0,8},{4,12},{8,0},{12,4},{16,24},{20,28},{24,16},{28,20},{1,9},{5... | collective-permute-start | bytes 393224 | tf_op jit(solution)/shard_map/ppermute | solution.py:520
  61.2 1.1 %collective-permute-start.17 = (bf16[392,128]{1,0:T(8,128)(2,1)S(1)}, bf16[392,128]{1,0:T(8,128)(2,1)S(1)}, u32[]{:S(2)}, u32[]{:S(2)}) collective-permute-start(bf16[392,128]{1,0:T(8,128)(2,1)S(1)} %add_convert_fusion.1.refs_0_), channel_id=1, source_target_pairs={{0,16},{4,20},{8,24},{12,28},{16,0},{20,4},{24,8},{28,12},{1,17},{... | collective-permute-start | bytes 301064 | tf_op jit(solution)/shard_map/ppermute | solution.py:520
  62.4 2.0 %shard_map.103 = bf16[1024,512]{1,0:T(8,128)(2,1)} custom-call(f32[8,128]{1,0:T(8,128)S(1)} %shard_map.101.mark_ref, bf16[1024,256]{1,0:T(8,128)(2,1)S(1)} %get-tuple-element.78.h_ref.refs_0_, bf16[1024,256]{1,0:T(8,128)(2,1)S(1)} %collective-permute-done.12.refs_1_, bf16[1024,256]{1,0:T(8,128)(2,1)S(1)} %collective-permute-done.13.refs_2_, ...), custom_call_target="tpu_custom_call" | custom-call | flops 1073741824 | bytes 6000000 | tf_op jit(solution)/shard_map/pallas_call | solution.py:507
  64.3 3.7 %collective-permute-done.21.refs_6_ = bf16[256,256]{1,0:T(8,128)(2,1)S(1)} collective-permute-done((bf16[256,256]{1,0:T(8,128)(2,1)S(1)}, bf16[256,256]{1,0:T(8,128)(2,1)S(1)}, u32[]{:S(2)}, u32[]{:S(2)}) %collective-permute-start.21) | collective-permute-done | bytes 131104 | tf_op jit(solution)/shard_map/ppermute | solution.py:520
  68.1 0.9 %collective-permute-done.17.refs_2_ = bf16[392,128]{1,0:T(8,128)(2,1)S(1)} collective-permute-done((bf16[392,128]{1,0:T(8,128)(2,1)S(1)}, bf16[392,128]{1,0:T(8,128)(2,1)S(1)}, u32[]{:S(2)}, u32[]{:S(2)}) %collective-permute-start.17) | collective-permute-done | bytes 100384 | tf_op jit(solution)/shard_map/ppermute | solution.py:520
  68.9 1.5 %shard_map.106 = (bf16[1024,256]{1,0:T(8,128)(2,1)}, bf16[1024,256]{1,0:T(8,128)(2,1)}, f32[256,256]{1,0:T(8,128)}) custom-call(bf16[1024,256]{1,0:T(8,128)(2,1)S(1)} %copy-done.2, bf16[1024,256]{1,0:T(8,128)(2,1)S(1)} %copy-done.3, f32[1024,256]{1,0:T(8,128)S(1)} %get-tuple-element.94.dk_ref, f32[1024,256]{1,0:T(8,128)S(1)} %get-tuple-element.95.dv_ref, ...), custom_call_target="tpu_custom_call" | custom-call | flops 1000000000 | bytes 6000000 | tf_op jit(solution)/shard_map/pallas_call | solution.py:383
  (36 shorter events, 0.3 us)
Async XLA Ops:
  0.6 1.0 %copy-start.2 = (bf16[1024,256]{1,0:T(8,128)(2,1)S(1)}, bf16[1024,256]{1,0:T(8,128)(2,1)}, u32[]{:S(2)}) copy-start(bf16[1024,256]{1,0:T(8,128)(2,1)} %k_ref.11) | copy-start | bytes 1572868
  0.6 1.2 %copy-start.3 = (bf16[1024,256]{1,0:T(8,128)(2,1)S(1)}, bf16[1024,256]{1,0:T(8,128)(2,1)}, u32[]{:S(2)}) copy-start(bf16[1024,256]{1,0:T(8,128)(2,1)} %v_ref.9) | copy-start | bytes 1572868
  0.7 1.5 %copy-start.1 = (bf16[1024,512]{1,0:T(8,128)(2,1)S(1)}, bf16[1024,512]{1,0:T(8,128)(2,1)}, u32[]{:S(2)}) copy-start(bf16[1024,512]{1,0:T(8,128)(2,1)} %refs_0_.3) | copy-start | bytes 3145732
  0.7 22.3 %copy-start = (bf16[256,2048]{1,0:T(8,128)(2,1)S(1)}, bf16[256,2048]{1,0:T(8,128)(2,1)}, u32[]{:S(2)}) copy-start(bf16[256,2048]{1,0:T(8,128)(2,1)} %w_ref.4) | copy-start | bytes 3145732
  2.2 20.8 %collective-permute-start = (bf16[1024,512]{1,0:T(8,128)(2,1)S(1)}, bf16[1024,512]{1,0:T(8,128)(2,1)S(1)}, u32[]{:S(2)}, u32[]{:S(2)}) collective-permute-start(bf16[1024,512]{1,0:T(8,128)(2,1)S(1)} %copy-done.1), channel_id=1, source_target_pairs={{0,1},{1,0},{2,3},{3,2},{4,5},{5,4},{6,7},{7,6},{8,9},{9,8},{10,11... | collective-permute-start | bytes 3145736 | tf_op jit(solution)/shard_map/ppermute | solution.py:520
  2.7 26.3 %collective-permute-start.7 = (bf16[1024,512]{1,0:T(8,128)(2,1)S(1)}, bf16[1024,512]{1,0:T(8,128)(2,1)S(1)}, u32[]{:S(2)}, u32[]{:S(2)}) collective-permute-start(bf16[1024,512]{1,0:T(8,128)(2,1)S(1)} %copy-done.1), channel_id=1, source_target_pairs={{0,2},{1,3},{2,0},{3,1},{4,6},{5,7},{6,4},{7,5},{8,10},{9,11},{10,... | collective-permute-start | bytes 3145736 | tf_op jit(solution)/shard_map/ppermute | solution.py:520
  5.3 4.3 %collective-permute-start.1 = (f32[136,128]{1,0:T(8,128)S(1)}, f32[136,128]{1,0:T(8,128)S(1)}, u32[]{:S(2)}, u32[]{:S(2)}) collective-permute-start(f32[136,128]{1,0:T(8,128)S(1)} %get-tuple-element.55), channel_id=1, source_target_pairs={{0,4},{4,0},{8,12},{12,8},{16,20},{20,16},{24,28},{28,24},{1,5},{5... | collective-permute-start | bytes 208904 | tf_op jit(solution)/shard_map/ppermute | solution.py:520
  9.6 4.4 %collective-permute-start.2 = (f32[136,128]{1,0:T(8,128)S(1)}, f32[136,128]{1,0:T(8,128)S(1)}, u32[]{:S(2)}, u32[]{:S(2)}) collective-permute-start(f32[136,128]{1,0:T(8,128)S(1)} %add.24), channel_id=1, source_target_pairs={{0,8},{4,12},{8,0},{12,4},{16,24},{20,28},{24,16},{28,20},{1,9},{5... | collective-permute-start | bytes 208904 | tf_op jit(solution)/shard_map/ppermute | solution.py:520
  11.3 4.3 %collective-permute-start.4 = (bf16[256,128]{1,0:T(8,128)(2,1)S(1)}, bf16[256,128]{1,0:T(8,128)(2,1)S(1)}, u32[]{:S(2)}, u32[]{:S(2)}) collective-permute-start(bf16[256,128]{1,0:T(8,128)(2,1)S(1)} %convert_element_type.51), channel_id=1, source_target_pairs={{0,4},{4,0},{8,12},{12,8},{16,20},{20,16},{24,28},{28,24},{1,5},{5... | collective-permute-start | bytes 196616 | tf_op jit(solution)/shard_map/ppermute | solution.py:520
  15.6 4.3 %collective-permute-start.5 = (bf16[256,128]{1,0:T(8,128)(2,1)S(1)}, bf16[256,128]{1,0:T(8,128)(2,1)S(1)}, u32[]{:S(2)}, u32[]{:S(2)}) collective-permute-start(bf16[256,128]{1,0:T(8,128)(2,1)S(1)} %fusion.2), channel_id=1, source_target_pairs={{0,8},{4,12},{8,0},{12,4},{16,24},{20,28},{24,16},{28,20},{1,9},{5... | collective-permute-start | bytes 196616 | tf_op jit(solution)/shard_map/ppermute | solution.py:520
  16.1 7.6 %collective-permute-start.3 = (f32[136,128]{1,0:T(8,128)S(1)}, f32[136,128]{1,0:T(8,128)S(1)}, u32[]{:S(2)}, u32[]{:S(2)}) collective-permute-start(f32[136,128]{1,0:T(8,128)S(1)} %add.25), channel_id=1, source_target_pairs={{0,16},{4,20},{8,24},{12,28},{16,0},{20,4},{24,8},{28,12},{1,17},{... | collective-permute-start | bytes 208904 | tf_op jit(solution)/shard_map/ppermute | solution.py:520
  20.0 8.0 %collective-permute-start.6 = (bf16[256,128]{1,0:T(8,128)(2,1)S(1)}, bf16[256,128]{1,0:T(8,128)(2,1)S(1)}, u32[]{:S(2)}, u32[]{:S(2)}) collective-permute-start(bf16[256,128]{1,0:T(8,128)(2,1)S(1)} %add_convert_fusion.2), channel_id=1, source_target_pairs={{0,16},{4,20},{8,24},{12,28},{16,0},{20,4},{24,8},{28,12},{1,17},{... | collective-permute-start | bytes 196616 | tf_op jit(solution)/shard_map/ppermute | solution.py:520
  23.8 7.2 %copy-start.4 = (bf16[1024,256]{1,0:T(8,128)(2,1)S(1)}, bf16[1024,256]{1,0:T(8,128)(2,1)}, u32[]{:S(2)}) copy-start(bf16[1024,256]{1,0:T(8,128)(2,1)} %q_ref.3) | copy-start | bytes 1572868
  29.0 4.3 %collective-permute-start.8 = (bf16[1024,512]{1,0:T(8,128)(2,1)S(1)}, bf16[1024,512]{1,0:T(8,128)(2,1)S(1)}, u32[]{:S(2)}, u32[]{:S(2)}) collective-permute-start(bf16[1024,512]{1,0:T(8,128)(2,1)S(1)} %collective-permute-done.7.refs_2_.refs_1_), channel_id=1, source_target_pairs={{0,1},{1,0},{2,3},{3,2},{4,5},{5,4},{6,7},{7,6},{8,9},{9,8},{10,11... | collective-permute-start | bytes 3145736 | tf_op jit(solution)/shard_map/ppermute | solution.py:520
  29.1 21.7 %collective-permute-start.15 = (bf16[2,256,512]{2,1,0:T(8,128)(2,1)S(1)}, bf16[2,256,512]{2,1,0:T(8,128)(2,1)S(1)}, u32[]{:S(2)}, u32[]{:S(2)}) collective-permute-start(bf16[2,256,512]{2,1,0:T(8,128)(2,1)S(1)} %get-tuple-element.85), channel_id=1, source_target_pairs={{0,2},{1,3},{2,0},{3,1},{4,6},{5,7},{6,4},{7,5},{8,10},{9,11},{10,... | collective-permute-start | bytes 1572872 | tf_op jit(solution)/shard_map/ppermute | solution.py:520
  34.7 10.0 %collective-permute-start.10 = (bf16[2,256,256]{2,1,0:T(8,128)(2,1)S(1)}, bf16[2,256,256]{2,1,0:T(8,128)(2,1)S(1)}, u32[]{:S(2)}, u32[]{:S(2)}) collective-permute-start(bf16[2,256,256]{2,1,0:T(8,128)(2,1)S(1)} %get-tuple-element.75), channel_id=1, source_target_pairs={{0,4},{4,0},{8,12},{12,8},{16,20},{20,16},{24,28},{28,24},{1,5},{5... | collective-permute-start | bytes 786440 | tf_op jit(solution)/shard_map/ppermute | solution.py:520
  43.9 5.5 %collective-permute-start.9 = (bf16[392,128]{1,0:T(8,128)(2,1)S(1)}, bf16[392,128]{1,0:T(8,128)(2,1)S(1)}, u32[]{:S(2)}, u32[]{:S(2)}) collective-permute-start(bf16[392,128]{1,0:T(8,128)(2,1)S(1)} %get-tuple-element.73.refs_0_), channel_id=1, source_target_pairs={{0,4},{4,0},{8,12},{12,8},{16,20},{20,16},{24,28},{28,24},{1,5},{5... | collective-permute-start | bytes 301064 | tf_op jit(solution)/shard_map/ppermute | solution.py:520
  44.4 13.5 %collective-permute-start.13 = (bf16[1024,256]{1,0:T(8,128)(2,1)S(1)}, bf16[1024,256]{1,0:T(8,128)(2,1)S(1)}, u32[]{:S(2)}, u32[]{:S(2)}) collective-permute-start(bf16[1024,256]{1,0:T(8,128)(2,1)S(1)} %get-tuple-element.78.h_ref.refs_0_), channel_id=1, source_target_pairs={{0,2},{1,3},{2,0},{3,1},{4,6},{5,7},{6,4},{7,5},{8,10},{9,11},{10,... | collective-permute-start | bytes 1572872 | tf_op jit(solution)/shard_map/ppermute | solution.py:520
  44.7 16.5 %collective-permute-start.12 = (bf16[1024,256]{1,0:T(8,128)(2,1)S(1)}, bf16[1024,256]{1,0:T(8,128)(2,1)S(1)}, u32[]{:S(2)}, u32[]{:S(2)}) collective-permute-start(bf16[1024,256]{1,0:T(8,128)(2,1)S(1)} %get-tuple-element.78.h_ref.refs_0_), channel_id=1, source_target_pairs={{0,1},{1,0},{2,3},{3,2},{4,5},{5,4},{6,7},{7,6},{8,9},{9,8},{10,11... | collective-permute-start | bytes 1572872 | tf_op jit(solution)/shard_map/ppermute | solution.py:520
  44.7 11.9 %collective-permute-start.18 = (bf16[2,256,256]{2,1,0:T(8,128)(2,1)S(1)}, bf16[2,256,256]{2,1,0:T(8,128)(2,1)S(1)}, u32[]{:S(2)}, u32[]{:S(2)}) collective-permute-start(bf16[2,256,256]{2,1,0:T(8,128)(2,1)S(1)} %get-tuple-element.97), channel_id=1, source_target_pairs={{0,4},{4,0},{8,12},{12,8},{16,20},{20,16},{24,28},{28,24},{1,5},{5... | collective-permute-start | bytes 786440 | tf_op jit(solution)/shard_map/ppermute | solution.py:520
  49.4 6.1 %collective-permute-start.11 = (bf16[392,128]{1,0:T(8,128)(2,1)S(1)}, bf16[392,128]{1,0:T(8,128)(2,1)S(1)}, u32[]{:S(2)}, u32[]{:S(2)}) collective-permute-start(bf16[392,128]{1,0:T(8,128)(2,1)S(1)} %fusion), channel_id=1, source_target_pairs={{0,8},{4,12},{8,0},{12,4},{16,24},{20,28},{24,16},{28,20},{1,9},{5... | collective-permute-start | bytes 301064 | tf_op jit(solution)/shard_map/ppermute | solution.py:520
  50.8 17.2 %collective-permute-start.20 = (bf16[256,256]{1,0:T(8,128)(2,1)S(1)}, bf16[256,256]{1,0:T(8,128)(2,1)S(1)}, u32[]{:S(2)}, u32[]{:S(2)}) collective-permute-start(bf16[256,256]{1,0:T(8,128)(2,1)S(1)} %get-tuple-element.111), channel_id=1, source_target_pairs={{0,24},{4,28},{8,16},{12,20},{16,8},{20,12},{24,0},{28,4},{1,25},{... | collective-permute-start | bytes 393224 | tf_op jit(solution)/shard_map/ppermute | solution.py:520
  55.6 12.5 %collective-permute-start.19 = (bf16[256,256]{1,0:T(8,128)(2,1)S(1)}, bf16[256,256]{1,0:T(8,128)(2,1)S(1)}, u32[]{:S(2)}, u32[]{:S(2)}) collective-permute-start(bf16[256,256]{1,0:T(8,128)(2,1)S(1)} %get-tuple-element.112), channel_id=1, source_target_pairs={{0,16},{4,20},{8,24},{12,28},{16,0},{20,4},{24,8},{28,12},{1,17},{... | collective-permute-start | bytes 393224 | tf_op jit(solution)/shard_map/ppermute | solution.py:520
  56.7 2.0 %collective-permute-start.16 = (bf16[2,256,512]{2,1,0:T(8,128)(2,1)S(1)}, bf16[2,256,512]{2,1,0:T(8,128)(2,1)S(1)}, u32[]{:S(2)}, u32[]{:S(2)}) collective-permute-start(bf16[2,256,512]{2,1,0:T(8,128)(2,1)S(1)} %pad_maximum_fusion), channel_id=1, source_target_pairs={{0,1},{1,0},{2,3},{3,2},{4,5},{5,4},{6,7},{7,6},{8,9},{9,8},{10,11... | collective-permute-start | bytes 1572872 | tf_op jit(solution)/shard_map/ppermute | solution.py:520
  57.9 4.4 %collective-permute-start.14 = (bf16[1024,256]{1,0:T(8,128)(2,1)S(1)}, bf16[1024,256]{1,0:T(8,128)(2,1)S(1)}, u32[]{:S(2)}, u32[]{:S(2)}) collective-permute-start(bf16[1024,256]{1,0:T(8,128)(2,1)S(1)} %collective-permute-done.13.refs_2_), channel_id=1, source_target_pairs={{0,1},{1,0},{2,3},{3,2},{4,5},{5,4},{6,7},{7,6},{8,9},{9,8},{10,11... | collective-permute-start | bytes 1572872 | tf_op jit(solution)/shard_map/ppermute | solution.py:520
  58.6 9.4 %collective-permute-start.21 = (bf16[256,256]{1,0:T(8,128)(2,1)S(1)}, bf16[256,256]{1,0:T(8,128)(2,1)S(1)}, u32[]{:S(2)}, u32[]{:S(2)}) collective-permute-start(bf16[256,256]{1,0:T(8,128)(2,1)S(1)} %fusion.1), channel_id=1, source_target_pairs={{0,8},{4,12},{8,0},{12,4},{16,24},{20,28},{24,16},{28,20},{1,9},{5... | collective-permute-start | bytes 393224 | tf_op jit(solution)/shard_map/ppermute | solution.py:520
  61.2 7.7 %collective-permute-start.17 = (bf16[392,128]{1,0:T(8,128)(2,1)S(1)}, bf16[392,128]{1,0:T(8,128)(2,1)S(1)}, u32[]{:S(2)}, u32[]{:S(2)}) collective-permute-start(bf16[392,128]{1,0:T(8,128)(2,1)S(1)} %add_convert_fusion.1.refs_0_), channel_id=1, source_target_pairs={{0,16},{4,20},{8,24},{12,28},{16,0},{20,4},{24,8},{28,12},{1,17},{... | collective-permute-start | bytes 301064 | tf_op jit(solution)/shard_map/ppermute | solution.py:520

commit v12 on v11

--- a/solution.py
+++ b/solution.py
@@ -579,29 +579,30 @@
     outs_far = [swap(outs_out, "head", s) for s in evens]
     high = even_high.astype(F32) + after(high, send).astype(F32)
     half = ctx_count // 4
-    high = [high[u].astype(BF16) for u in range(half)]
-    moved = [swap(part, "ctx", 2 * (half + u)) for u, part in enumerate(high)]
+    aside = [swap(high[u].astype(BF16), "ctx", 2 * u) for u in range(1, half)]
 
     early = lead(1000, send)
     later, sends = [], []
     for distance in doublings("ctx"):
         sends.append(send)
         later.append(swap(send, "ctx", distance))
-        if distance == 1:
-            later[0] = after(later[0], *high)
         sums = sums + later[-1].astype(F32)
         send = sums.astype(BF16)
 
+    far_sum = high[0]
+    for part in aside:
+        far_sum = far_sum + after(part, sends[1]).astype(F32)
+    moved = [swap(far_sum.astype(BF16), "ctx", 2 * half)]
     grad_queries, dk, dv = rest(
         early, keys, values, grads, last, solved, scores, weights, after(ds, sends[1]), da, dn
     )
 
-    mark = lead(1000, sends[-1])
-    low = even_low.astype(F32) + after(low, sends[-1]).astype(F32)
+    mark = lead(1000, dk)
+    low = even_low.astype(F32) + after(low, dk).astype(F32)
     moved += [swap(low[u].astype(BF16), "ctx", 2 * u) for u in range(1, half)]
     outs = [heads_out, swap(outs_out, "head", 1)]
     for part in outs_far:
-        outs += [part, swap(after(part, sends[1]), "head", 1)]
+        outs += [part, swap(after(part, sends[-1]), "head", 1)]
     columns = [after(c, sends[1]) for c in columns]
     crossing = jnp.stack([c[1] for c in columns])
     crossing = swap(crossing, "head", 1)

time: 70.6 us -> 78.5 us (1.11)
  waiting for transfers between devices: 16.9 us -> 23.6 us
  starting transfers between devices: 28.7 us -> 29.8 us
    ppermute x22, waiting for transfers between devices: 16.9 us -> 23.6 us  [swap(): return lax.ppermute(value, axis, [(i, i ^ distance) for i in range(count)])]
    ppermute x22, starting transfers between devices: 28.7 us -> 29.8 us  [swap(): return lax.ppermute(value, axis, [(i, i ^ distance) for i in range(count)])]
  transfers between devices with their start and end apart: 22 -> 22, of which waited for: 10 -> 11; matrix products, arithmetic and copies ran while one was open for 1% -> 1% of each run, Pallas kernels for 29% -> 26%
where the time goes in v12:
time: 78.5 us; the launch traced here: 78.3 us
  starting transfers between devices  29.8 us (38%)
  waiting for transfers between devices  23.6 us (30%)
  Pallas kernels  22.3 us (28%)
  local copies, waits for them, and re-layouts  1.35 us (2%)
  between operations  0.93 us (1%)
    ppermute x22, starting transfers between devices, swap(): return lax.ppermute(value, axis, [(i, i ^ distance) for i in range(count)])  29.8 us
    ppermute x22, waiting for transfers between devices, swap(): return lax.ppermute(value, axis, [(i, i ^ distance) for i in range(count)])  23.6 us
    pallas_call x1, Pallas kernels, tangent(): pl.pallas_call(tangent_kernel, out_shape=(shape((count, SPAN, SPAN), BF16...  6.81 us
    pallas_call x1, Pallas kernels, inverses(): pl.pallas_call(functools.partial(inverse_kernel, len(grams)), out_shape=(...  4.23 us
    pallas_call x1, Pallas kernels, outputs(): pl.pallas_call(functools.partial(outputs_kernel, len(pairs)), out_shape=(...  2.4 us
    pallas_call x1, Pallas kernels, rest(): pl.pallas_call(rest_kernel, out_shape=(shape(keys.shape, BF16), wide, wid...  2.09 us
    pallas_call x1, Pallas kernels, layer(): pl.pallas_call(layer_kernel, out_shape=shape((rows, cols), BF16), in_spec...  1.99 us
  transfers between devices with their start and end apart: 22, of which 11 were waited for; matrix products, arithmetic and copies ran while one was open for 1% of the time, Pallas kernels for 26%

profile of v12, /device:TPU:0, one launch (start us, length us, event | category | flops | bytes accessed | tf_op | source)
XLA Modules:
  0.0 78.3 jit_solution(9797416676593168381)
XLA Ops:
  0.7 1.0 %copy-done.2 = bf16[1024,256]{1,0:T(8,128)(2,1)S(1)} copy-done((bf16[1024,256]{1,0:T(8,128)(2,1)S(1)}, bf16[1024,256]{1,0:T(8,128)(2,1)}, u32[]{:S(2)}) %copy-start.2) | copy-done | bytes 524312
  1.7 0.2 copy-done.3
  1.8 0.3 shard_map.93
  2.2 0.0 copy-done.1
  2.2 0.6 collective-permute-start
  2.7 2.6 %collective-permute-start.7 = (bf16[1024,512]{1,0:T(8,128)(2,1)S(1)}, bf16[1024,512]{1,0:T(8,128)(2,1)S(1)}, u32[]{:S(2)}, u32[]{:S(2)}) collective-permute-start(bf16[1024,512]{1,0:T(8,128)(2,1)S(1)} %copy-done.1), channel_id=1, source_target_pairs={{0,2},{1,3},{2,0},{3,1},{4,6},{5,7},{6,4},{7,5},{8,10},{9,11},{10,... | collective-permute-start | bytes 3145736 | tf_op jit(solution)/shard_map/ppermute | solution.py:520
  5.3 1.5 %collective-permute-start.1 = (f32[136,128]{1,0:T(8,128)S(1)}, f32[136,128]{1,0:T(8,128)S(1)}, u32[]{:S(2)}, u32[]{:S(2)}) collective-permute-start(f32[136,128]{1,0:T(8,128)S(1)} %get-tuple-element.54), channel_id=1, source_target_pairs={{0,4},{4,0},{8,12},{12,8},{16,20},{20,16},{24,28},{28,24},{1,5},{5... | collective-permute-start | bytes 208904 | tf_op jit(solution)/shard_map/ppermute | solution.py:520
  6.8 2.8 %collective-permute-done.1.refs_0_ = f32[136,128]{1,0:T(8,128)S(1)} collective-permute-done((f32[136,128]{1,0:T(8,128)S(1)}, f32[136,128]{1,0:T(8,128)S(1)}, u32[]{:S(2)}, u32[]{:S(2)}) %collective-permute-start.1) | collective-permute-done | bytes 69664 | tf_op jit(solution)/shard_map/ppermute | solution.py:520
  9.6 1.6 %collective-permute-start.2 = (f32[136,128]{1,0:T(8,128)S(1)}, f32[136,128]{1,0:T(8,128)S(1)}, u32[]{:S(2)}, u32[]{:S(2)}) collective-permute-start(f32[136,128]{1,0:T(8,128)S(1)} %add.27), channel_id=1, source_target_pairs={{0,8},{4,12},{8,0},{12,4},{16,24},{20,28},{24,16},{28,20},{1,9},{5... | collective-permute-start | bytes 208904 | tf_op jit(solution)/shard_map/ppermute | solution.py:520
  11.3 1.6 %collective-permute-start.4 = (bf16[256,128]{1,0:T(8,128)(2,1)S(1)}, bf16[256,128]{1,0:T(8,128)(2,1)S(1)}, u32[]{:S(2)}, u32[]{:S(2)}) collective-permute-start(bf16[256,128]{1,0:T(8,128)(2,1)S(1)} %convert_element_type.53), channel_id=1, source_target_pairs={{0,4},{4,0},{8,12},{12,8},{16,20},{20,16},{24,28},{28,24},{1,5},{5... | collective-permute-start | bytes 196616 | tf_op jit(solution)/shard_map/ppermute | solution.py:520
  12.9 1.1 %collective-permute-done.2.refs_1_ = f32[136,128]{1,0:T(8,128)S(1)} collective-permute-done((f32[136,128]{1,0:T(8,128)S(1)}, f32[136,128]{1,0:T(8,128)S(1)}, u32[]{:S(2)}, u32[]{:S(2)}) %collective-permute-start.2) | collective-permute-done | bytes 69664 | tf_op jit(solution)/shard_map/ppermute | solution.py:520
  14.0 1.6 %collective-permute-done.4.refs_0_ = bf16[256,128]{1,0:T(8,128)(2,1)S(1)} collective-permute-done((bf16[256,128]{1,0:T(8,128)(2,1)S(1)}, bf16[256,128]{1,0:T(8,128)(2,1)S(1)}, u32[]{:S(2)}, u32[]{:S(2)}) %collective-permute-start.4) | collective-permute-done | bytes 65568 | tf_op jit(solution)/shard_map/ppermute | solution.py:520
  15.6 0.5 collective-permute-start.5
  16.1 2.6 %collective-permute-start.3 = (f32[136,128]{1,0:T(8,128)S(1)}, f32[136,128]{1,0:T(8,128)S(1)}, u32[]{:S(2)}, u32[]{:S(2)}) collective-permute-start(f32[136,128]{1,0:T(8,128)S(1)} %add.28), channel_id=1, source_target_pairs={{0,16},{4,20},{8,24},{12,28},{16,0},{20,4},{24,8},{28,12},{1,17},{... | collective-permute-start | bytes 208904 | tf_op jit(solution)/shard_map/ppermute | solution.py:520
  18.7 1.2 %collective-permute-done.5.refs_1_ = bf16[256,128]{1,0:T(8,128)(2,1)S(1)} collective-permute-done((bf16[256,128]{1,0:T(8,128)(2,1)S(1)}, bf16[256,128]{1,0:T(8,128)(2,1)S(1)}, u32[]{:S(2)}, u32[]{:S(2)}) %collective-permute-start.5) | collective-permute-done | bytes 65568 | tf_op jit(solution)/shard_map/ppermute | solution.py:520
  20.0 3.0 %collective-permute-start.6 = (bf16[256,128]{1,0:T(8,128)(2,1)S(1)}, bf16[256,128]{1,0:T(8,128)(2,1)S(1)}, u32[]{:S(2)}, u32[]{:S(2)}) collective-permute-start(bf16[256,128]{1,0:T(8,128)(2,1)S(1)} %add_convert_fusion.1), channel_id=1, source_target_pairs={{0,16},{4,20},{8,24},{12,28},{16,0},{20,4},{24,8},{28,12},{1,17},{... | collective-permute-start | bytes 196616 | tf_op jit(solution)/shard_map/ppermute | solution.py:520
  23.0 0.7 shard_map.94.refs_0_
  23.8 4.2 %shard_map.95 = (bf16[8,8,128,128]{3,2,1,0:T(8,128)(2,1)S(1)}, bf16[8,8,128,128]{3,2,1,0:T(8,128)(2,1)S(1)}, f32[8,128,128]{2,1,0:T(8,128)S(1)}, f32[8,128,128]{2,1,0:T(8,128)S(1)}) custom-call(bf16[1024,256]{1,0:T(8,128)(2,1)S(1)} %copy-done.2, f32[136,128]{1,0:T(8,128)S(1)} %collective-permute-done.1.refs_0_, ...), custom_call_target="tpu_custom_call" | custom-call | flops 2000000000 | bytes 8000000 | tf_op jit(solution)/shard_map/pallas_call | solution.py:181
  28.0 1.0 %collective-permute-done.7.refs_2_.refs_1_ = bf16[1024,512]{1,0:T(8,128)(2,1)S(1)} collective-permute-done((bf16[1024,512]{1,0:T(8,128)(2,1)S(1)}, bf16[1024,512]{1,0:T(8,128)(2,1)S(1)}, u32[]{:S(2)}, u32[]{:S(2)}) %collective-permute-start.7) | collective-permute-done | bytes 1048608 | tf_op jit(solution)/shard_map/ppermute | solution.py:520
  29.0 0.1 shard_map.104
  29.1 1.8 %collective-permute-start.14 = (bf16[2,256,512]{2,1,0:T(8,128)(2,1)S(1)}, bf16[2,256,512]{2,1,0:T(8,128)(2,1)S(1)}, u32[]{:S(2)}, u32[]{:S(2)}) collective-permute-start(bf16[2,256,512]{2,1,0:T(8,128)(2,1)S(1)} %get-tuple-element.87), channel_id=1, source_target_pairs={{0,2},{1,3},{2,0},{3,1},{4,6},{5,7},{6,4},{7,5},{8,10},{9,11},{10,... | collective-permute-start | bytes 1572872 | tf_op jit(solution)/shard_map/ppermute | solution.py:520
  30.9 2.4 %shard_map.97 = (bf16[1024,256]{1,0:T(8,128)(2,1)S(1)}, bf16[8,128,256]{2,1,0:T(8,128)(2,1)S(1)}, bf16[8,256,256]{2,1,0:T(8,128)(2,1)S(1)}, bf16[8,256,256]{2,1,0:T(8,128)(2,1)S(1)}) custom-call(f32[8,128]{1,0:T(8,128)S(1)} %shard_map.96.mark_ref, bf16[1024,256]{1,0:T(8,128)(2,1)S(1)} %copy-done.4, bf16[1024,256]{1,0:T(8,128)(2,1)S(1)} %copy-done.2, ...), custom_call_target="tpu_custom_call" | custom-call | flops 2000000000 | bytes 8000000 | tf_op jit(solution)/shard_map/pallas_call | solution.py:218
  33.4 1.4 %shard_map.98 = (bf16[2,256,256]{2,1,0:T(8,128)(2,1)S(1)}, bf16[2,256,256]{2,1,0:T(8,128)(2,1)S(1)}, bf16[2,256,256]{2,1,0:T(8,128)(2,1)S(1)}, bf16[2,256,256]{2,1,0:T(8,128)(2,1)S(1)}) custom-call(bf16[1024,256]{1,0:T(8,128)(2,1)S(1)} %get-tuple-element.80.h_ref.refs_0_, bf16[1024,512]{1,0:T(8,128)(2,1)S(1)} %copy-done.1, ...), custom_call_target="tpu_custom_call" | custom-call | flops 1073741824 | bytes 6000000 | tf_op jit(solution)/shard_map/pallas_call | solution.py:476
  34.7 0.8 shard_map.99.do_ref
  35.5 6.8 %shard_map.100 = (bf16[8,256,256]{2,1,0:T(8,128)(2,1)S(1)}, bf16[1024,256]{1,0:T(8,128)(2,1)S(1)}, f32[8,128,128]{2,1,0:T(8,128)S(1)}, f32[8,128,128]{2,1,0:T(8,...) custom-call(bf16[1024,256]{1,0:T(8,128)(2,1)S(1)} %copy-done.4, bf16[1024,256]{1,0:T(8,128)(2,1)S(1)} %copy-done.2, ...), custom_call_target="tpu_custom_call" | custom-call | flops 4000000000 | bytes 8000000 | tf_op jit(solution)/shard_map/pallas_call | solution.py:290
  42.3 1.6 %collective-permute-start.9 = (bf16[392,128]{1,0:T(8,128)(2,1)S(1)}, bf16[392,128]{1,0:T(8,128)(2,1)S(1)}, u32[]{:S(2)}, u32[]{:S(2)}) collective-permute-start(bf16[392,128]{1,0:T(8,128)(2,1)S(1)} %get-tuple-element.71.refs_0_), channel_id=1, source_target_pairs={{0,4},{4,0},{8,12},{12,8},{16,20},{20,16},{24,28},{28,24},{1,5},{5... | collective-permute-start | bytes 301064 | tf_op jit(solution)/shard_map/ppermute | solution.py:520
  43.9 0.5 collective-permute-start.11
  44.4 0.3 collective-permute-start.17
  44.7 2.7 %collective-permute-done.9.refs_0_ = bf16[392,128]{1,0:T(8,128)(2,1)S(1)} collective-permute-done((bf16[392,128]{1,0:T(8,128)(2,1)S(1)}, bf16[392,128]{1,0:T(8,128)(2,1)S(1)}, u32[]{:S(2)}, u32[]{:S(2)}) %collective-permute-start.9) | collective-permute-done | bytes 100384 | tf_op jit(solution)/shard_map/ppermute | solution.py:520
  47.3 2.3 %collective-permute-start.18 = (bf16[2,256,256]{2,1,0:T(8,128)(2,1)S(1)}, bf16[2,256,256]{2,1,0:T(8,128)(2,1)S(1)}, u32[]{:S(2)}, u32[]{:S(2)}) collective-permute-start(bf16[2,256,256]{2,1,0:T(8,128)(2,1)S(1)} %get-tuple-element.95), channel_id=1, source_target_pairs={{0,4},{4,0},{8,12},{12,8},{16,20},{20,16},{24,28},{28,24},{1,5},{5... | collective-permute-start | bytes 786440 | tf_op jit(solution)/shard_map/ppermute | solution.py:520
  49.6 1.6 %collective-permute-start.12 = (bf16[392,128]{1,0:T(8,128)(2,1)S(1)}, bf16[392,128]{1,0:T(8,128)(2,1)S(1)}, u32[]{:S(2)}, u32[]{:S(2)}) collective-permute-start(bf16[392,128]{1,0:T(8,128)(2,1)S(1)} %fusion.2), channel_id=1, source_target_pairs={{0,8},{4,12},{8,0},{12,4},{16,24},{20,28},{24,16},{28,20},{1,9},{5... | collective-permute-start | bytes 301064 | tf_op jit(solution)/shard_map/ppermute | solution.py:520
  51.3 0.1 slice_bitcast_fusion.4
  51.4 2.1 %shard_map.102 = (bf16[1024,256]{1,0:T(8,128)(2,1)}, f32[1024,256]{1,0:T(8,128)S(1)}, f32[1024,256]{1,0:T(8,128)S(1)}) custom-call(f32[8,128]{1,0:T(8,128)S(1)} %shard_map.101.early_ref, bf16[1024,256]{1,0:T(8,128)(2,1)S(1)} %copy-done.2, bf16[1024,256]{1,0:T(8,128)(2,1)S(1)} %copy-done.3, bf16[1024,256]{1,0:T(8,128)(2,1)S(1)} %shard_map.99.do_ref, ...), custom_call_target="tpu_custom_call" | custom-call | flops 2000000000 | bytes 6000000 | tf_op jit(solution)/shard_map/pallas_call | solution.py:335
  53.5 0.1 pad_maximum_fusion
  53.5 0.8 %collective-permute-done.12.refs_1_ = bf16[392,128]{1,0:T(8,128)(2,1)S(1)} collective-permute-done((bf16[392,128]{1,0:T(8,128)(2,1)S(1)}, bf16[392,128]{1,0:T(8,128)(2,1)S(1)}, u32[]{:S(2)}, u32[]{:S(2)}) %collective-permute-start.12) | collective-permute-done | bytes 100384 | tf_op jit(solution)/shard_map/ppermute | solution.py:520
  54.4 4.4 %collective-permute-done.18 = bf16[2,256,256]{2,1,0:T(8,128)(2,1)S(1)} collective-permute-done((bf16[2,256,256]{2,1,0:T(8,128)(2,1)S(1)}, bf16[2,256,256]{2,1,0:T(8,128)(2,1)S(1)}, u32[]{:S(2)}, u32[]{:S(2)}) %collective-permute-start.18) | collective-permute-done | bytes 262176 | tf_op jit(solution)/shard_map/ppermute | solution.py:520
  58.7 2.6 %collective-permute-start.16 = (bf16[392,128]{1,0:T(8,128)(2,1)S(1)}, bf16[392,128]{1,0:T(8,128)(2,1)S(1)}, u32[]{:S(2)}, u32[]{:S(2)}) collective-permute-start(bf16[392,128]{1,0:T(8,128)(2,1)S(1)} %add_convert_fusion), channel_id=1, source_target_pairs={{0,16},{4,20},{8,24},{12,28},{16,0},{20,4},{24,8},{28,12},{1,17},{... | collective-permute-start | bytes 301064 | tf_op jit(solution)/shard_map/ppermute | solution.py:520
  61.3 0.1 convert_add_fusion
  61.4 1.6 %collective-permute-start.19 = (bf16[256,256]{1,0:T(8,128)(2,1)S(1)}, bf16[256,256]{1,0:T(8,128)(2,1)S(1)}, u32[]{:S(2)}, u32[]{:S(2)}) collective-permute-start(bf16[256,256]{1,0:T(8,128)(2,1)S(1)} %fusion.3), channel_id=1, source_target_pairs={{0,8},{4,12},{8,0},{12,4},{16,24},{20,28},{24,16},{28,20},{1,9},{5... | collective-permute-start | bytes 393224 | tf_op jit(solution)/shard_map/ppermute | solution.py:520
  63.1 0.1 convert_add_fusion.1
  63.2 0.1 collective-permute-start.13
  63.3 4.0 %collective-permute-done.19 = bf16[256,256]{1,0:T(8,128)(2,1)S(1)} collective-permute-done((bf16[256,256]{1,0:T(8,128)(2,1)S(1)}, bf16[256,256]{1,0:T(8,128)(2,1)S(1)}, u32[]{:S(2)}, u32[]{:S(2)}) %collective-permute-start.19) | collective-permute-done | bytes 131104 | tf_op jit(solution)/shard_map/ppermute | solution.py:520
  67.3 1.5 %collective-permute-start.21 = (bf16[256,256]{1,0:T(8,128)(2,1)S(1)}, bf16[256,256]{1,0:T(8,128)(2,1)S(1)}, u32[]{:S(2)}, u32[]{:S(2)}) collective-permute-start(bf16[256,256]{1,0:T(8,128)(2,1)S(1)} %fusion.4), channel_id=1, source_target_pairs={{0,8},{4,12},{8,0},{12,4},{16,24},{20,28},{24,16},{28,20},{1,9},{5... | collective-permute-start | bytes 393224 | tf_op jit(solution)/shard_map/ppermute | solution.py:520
  68.8 1.9 %collective-permute-start.20 = (bf16[256,256]{1,0:T(8,128)(2,1)S(1)}, bf16[256,256]{1,0:T(8,128)(2,1)S(1)}, u32[]{:S(2)}, u32[]{:S(2)}) collective-permute-start(bf16[256,256]{1,0:T(8,128)(2,1)S(1)} %fusion.1), channel_id=1, source_target_pairs={{0,16},{4,20},{8,24},{12,28},{16,0},{20,4},{24,8},{28,12},{1,17},{... | collective-permute-start | bytes 393224 | tf_op jit(solution)/shard_map/ppermute | solution.py:520
  70.8 2.0 %shard_map.105 = bf16[1024,512]{1,0:T(8,128)(2,1)} custom-call(f32[8,128]{1,0:T(8,128)S(1)} %shard_map.103.mark_ref, bf16[1024,256]{1,0:T(8,128)(2,1)S(1)} %get-tuple-element.80.h_ref.refs_0_, bf16[1024,256]{1,0:T(8,128)(2,1)S(1)} %collective-permute-done.10.refs_1_, bf16[1024,256]{1,0:T(8,128)(2,1)S(1)} %collective-permute-done.11.refs_2_, ...), custom_call_target="tpu_custom_call" | custom-call | flops 1073741824 | bytes 6000000 | tf_op jit(solution)/shard_map/pallas_call | solution.py:507
  72.8 0.1 collective-permute-done.21.refs_5_
  72.9 3.9 %collective-permute-done.20.refs_4_ = bf16[256,256]{1,0:T(8,128)(2,1)S(1)} collective-permute-done((bf16[256,256]{1,0:T(8,128)(2,1)S(1)}, bf16[256,256]{1,0:T(8,128)(2,1)S(1)}, u32[]{:S(2)}, u32[]{:S(2)}) %collective-permute-start.20) | collective-permute-done | bytes 131104 | tf_op jit(solution)/shard_map/ppermute | solution.py:520
  76.8 1.5 %shard_map.106 = (bf16[1024,256]{1,0:T(8,128)(2,1)}, bf16[1024,256]{1,0:T(8,128)(2,1)}, f32[256,256]{1,0:T(8,128)}) custom-call(bf16[1024,256]{1,0:T(8,128)(2,1)S(1)} %copy-done.2, bf16[1024,256]{1,0:T(8,128)(2,1)S(1)} %copy-done.3, f32[1024,256]{1,0:T(8,128)S(1)} %get-tuple-element.79.refs_0_.dk_ref, f32[1024,256]{1,0:T(8,128)S(1)} %get-tuple-element.90.dv_ref, ...), custom_call_target="tpu_custom_call" | custom-call | flops 1000000000 | bytes 6000000 | tf_op jit(solution)/shard_map/pallas_call | solution.py:383
  (37 shorter events, 0.3 us)
Async XLA Ops:
  0.6 1.0 %copy-start.2 = (bf16[1024,256]{1,0:T(8,128)(2,1)S(1)}, bf16[1024,256]{1,0:T(8,128)(2,1)}, u32[]{:S(2)}) copy-start(bf16[1024,256]{1,0:T(8,128)(2,1)} %k_ref.11) | copy-start | bytes 1572868
  0.6 1.2 %copy-start.3 = (bf16[1024,256]{1,0:T(8,128)(2,1)S(1)}, bf16[1024,256]{1,0:T(8,128)(2,1)}, u32[]{:S(2)}) copy-start(bf16[1024,256]{1,0:T(8,128)(2,1)} %v_ref.9) | copy-start | bytes 1572868
  0.7 1.5 %copy-start.1 = (bf16[1024,512]{1,0:T(8,128)(2,1)S(1)}, bf16[1024,512]{1,0:T(8,128)(2,1)}, u32[]{:S(2)}) copy-start(bf16[1024,512]{1,0:T(8,128)(2,1)} %refs_0_.3) | copy-start | bytes 3145732
  0.7 22.3 %copy-start = (bf16[256,2048]{1,0:T(8,128)(2,1)S(1)}, bf16[256,2048]{1,0:T(8,128)(2,1)}, u32[]{:S(2)}) copy-start(bf16[256,2048]{1,0:T(8,128)(2,1)} %w_ref.4) | copy-start | bytes 3145732
  2.2 20.8 %collective-permute-start = (bf16[1024,512]{1,0:T(8,128)(2,1)S(1)}, bf16[1024,512]{1,0:T(8,128)(2,1)S(1)}, u32[]{:S(2)}, u32[]{:S(2)}) collective-permute-start(bf16[1024,512]{1,0:T(8,128)(2,1)S(1)} %copy-done.1), channel_id=1, source_target_pairs={{0,1},{1,0},{2,3},{3,2},{4,5},{5,4},{6,7},{7,6},{8,9},{9,8},{10,11... | collective-permute-start | bytes 3145736 | tf_op jit(solution)/shard_map/ppermute | solution.py:520
  2.7 26.3 %collective-permute-start.7 = (bf16[1024,512]{1,0:T(8,128)(2,1)S(1)}, bf16[1024,512]{1,0:T(8,128)(2,1)S(1)}, u32[]{:S(2)}, u32[]{:S(2)}) collective-permute-start(bf16[1024,512]{1,0:T(8,128)(2,1)S(1)} %copy-done.1), channel_id=1, source_target_pairs={{0,2},{1,3},{2,0},{3,1},{4,6},{5,7},{6,4},{7,5},{8,10},{9,11},{10,... | collective-permute-start | bytes 3145736 | tf_op jit(solution)/shard_map/ppermute | solution.py:520
  5.3 4.3 %collective-permute-start.1 = (f32[136,128]{1,0:T(8,128)S(1)}, f32[136,128]{1,0:T(8,128)S(1)}, u32[]{:S(2)}, u32[]{:S(2)}) collective-permute-start(f32[136,128]{1,0:T(8,128)S(1)} %get-tuple-element.54), channel_id=1, source_target_pairs={{0,4},{4,0},{8,12},{12,8},{16,20},{20,16},{24,28},{28,24},{1,5},{5... | collective-permute-start | bytes 208904 | tf_op jit(solution)/shard_map/ppermute | solution.py:520
  9.6 4.4 %collective-permute-start.2 = (f32[136,128]{1,0:T(8,128)S(1)}, f32[136,128]{1,0:T(8,128)S(1)}, u32[]{:S(2)}, u32[]{:S(2)}) collective-permute-start(f32[136,128]{1,0:T(8,128)S(1)} %add.27), channel_id=1, source_target_pairs={{0,8},{4,12},{8,0},{12,4},{16,24},{20,28},{24,16},{28,20},{1,9},{5... | collective-permute-start | bytes 208904 | tf_op jit(solution)/shard_map/ppermute | solution.py:520
  11.3 4.3 %collective-permute-start.4 = (bf16[256,128]{1,0:T(8,128)(2,1)S(1)}, bf16[256,128]{1,0:T(8,128)(2,1)S(1)}, u32[]{:S(2)}, u32[]{:S(2)}) collective-permute-start(bf16[256,128]{1,0:T(8,128)(2,1)S(1)} %convert_element_type.53), channel_id=1, source_target_pairs={{0,4},{4,0},{8,12},{12,8},{16,20},{20,16},{24,28},{28,24},{1,5},{5... | collective-permute-start | bytes 196616 | tf_op jit(solution)/shard_map/ppermute | solution.py:520
  15.6 4.3 %collective-permute-start.5 = (bf16[256,128]{1,0:T(8,128)(2,1)S(1)}, bf16[256,128]{1,0:T(8,128)(2,1)S(1)}, u32[]{:S(2)}, u32[]{:S(2)}) collective-permute-start(bf16[256,128]{1,0:T(8,128)(2,1)S(1)} %fusion.5), channel_id=1, source_target_pairs={{0,8},{4,12},{8,0},{12,4},{16,24},{20,28},{24,16},{28,20},{1,9},{5... | collective-permute-start | bytes 196616 | tf_op jit(solution)/shard_map/ppermute | solution.py:520
  16.1 7.6 %collective-permute-start.3 = (f32[136,128]{1,0:T(8,128)S(1)}, f32[136,128]{1,0:T(8,128)S(1)}, u32[]{:S(2)}, u32[]{:S(2)}) collective-permute-start(f32[136,128]{1,0:T(8,128)S(1)} %add.28), channel_id=1, source_target_pairs={{0,16},{4,20},{8,24},{12,28},{16,0},{20,4},{24,8},{28,12},{1,17},{... | collective-permute-start | bytes 208904 | tf_op jit(solution)/shard_map/ppermute | solution.py:520
  20.0 8.0 %collective-permute-start.6 = (bf16[256,128]{1,0:T(8,128)(2,1)S(1)}, bf16[256,128]{1,0:T(8,128)(2,1)S(1)}, u32[]{:S(2)}, u32[]{:S(2)}) collective-permute-start(bf16[256,128]{1,0:T(8,128)(2,1)S(1)} %add_convert_fusion.1), channel_id=1, source_target_pairs={{0,16},{4,20},{8,24},{12,28},{16,0},{20,4},{24,8},{28,12},{1,17},{... | collective-permute-start | bytes 196616 | tf_op jit(solution)/shard_map/ppermute | solution.py:520
  23.8 7.2 %copy-start.4 = (bf16[1024,256]{1,0:T(8,128)(2,1)S(1)}, bf16[1024,256]{1,0:T(8,128)(2,1)}, u32[]{:S(2)}) copy-start(bf16[1024,256]{1,0:T(8,128)(2,1)} %q_ref.3) | copy-start | bytes 1572868
  29.0 4.3 %collective-permute-start.8 = (bf16[1024,512]{1,0:T(8,128)(2,1)S(1)}, bf16[1024,512]{1,0:T(8,128)(2,1)S(1)}, u32[]{:S(2)}, u32[]{:S(2)}) collective-permute-start(bf16[1024,512]{1,0:T(8,128)(2,1)S(1)} %collective-permute-done.7.refs_2_.refs_1_), channel_id=1, source_target_pairs={{0,1},{1,0},{2,3},{3,2},{4,5},{5,4},{6,7},{7,6},{8,9},{9,8},{10,11... | collective-permute-start | bytes 3145736 | tf_op jit(solution)/shard_map/ppermute | solution.py:520
  29.1 20.5 %collective-permute-start.14 = (bf16[2,256,512]{2,1,0:T(8,128)(2,1)S(1)}, bf16[2,256,512]{2,1,0:T(8,128)(2,1)S(1)}, u32[]{:S(2)}, u32[]{:S(2)}) collective-permute-start(bf16[2,256,512]{2,1,0:T(8,128)(2,1)S(1)} %get-tuple-element.87), channel_id=1, source_target_pairs={{0,2},{1,3},{2,0},{3,1},{4,6},{5,7},{6,4},{7,5},{8,10},{9,11},{10,... | collective-permute-start | bytes 1572872 | tf_op jit(solution)/shard_map/ppermute | solution.py:520
  42.3 5.0 %collective-permute-start.9 = (bf16[392,128]{1,0:T(8,128)(2,1)S(1)}, bf16[392,128]{1,0:T(8,128)(2,1)S(1)}, u32[]{:S(2)}, u32[]{:S(2)}) collective-permute-start(bf16[392,128]{1,0:T(8,128)(2,1)S(1)} %get-tuple-element.71.refs_0_), channel_id=1, source_target_pairs={{0,4},{4,0},{8,12},{12,8},{16,20},{20,16},{24,28},{28,24},{1,5},{5... | collective-permute-start | bytes 301064 | tf_op jit(solution)/shard_map/ppermute | solution.py:520
  43.9 19.3 %collective-permute-start.11 = (bf16[1024,256]{1,0:T(8,128)(2,1)S(1)}, bf16[1024,256]{1,0:T(8,128)(2,1)S(1)}, u32[]{:S(2)}, u32[]{:S(2)}) collective-permute-start(bf16[1024,256]{1,0:T(8,128)(2,1)S(1)} %get-tuple-element.80.h_ref.refs_0_), channel_id=1, source_target_pairs={{0,2},{1,3},{2,0},{3,1},{4,6},{5,7},{6,4},{7,5},{8,10},{9,11},{10,... | collective-permute-start | bytes 1572872 | tf_op jit(solution)/shard_map/ppermute | solution.py:520
  44.4 26.4 %collective-permute-start.10 = (bf16[1024,256]{1,0:T(8,128)(2,1)S(1)}, bf16[1024,256]{1,0:T(8,128)(2,1)S(1)}, u32[]{:S(2)}, u32[]{:S(2)}) collective-permute-start(bf16[1024,256]{1,0:T(8,128)(2,1)S(1)} %get-tuple-element.80.h_ref.refs_0_), channel_id=1, source_target_pairs={{0,1},{1,0},{2,3},{3,2},{4,5},{5,4},{6,7},{7,6},{8,9},{9,8},{10,11... | collective-permute-start | bytes 1572872 | tf_op jit(solution)/shard_map/ppermute | solution.py:520
  44.4 17.0 %collective-permute-start.17 = (bf16[2,256,256]{2,1,0:T(8,128)(2,1)S(1)}, bf16[2,256,256]{2,1,0:T(8,128)(2,1)S(1)}, u32[]{:S(2)}, u32[]{:S(2)}) collective-permute-start(bf16[2,256,256]{2,1,0:T(8,128)(2,1)S(1)} %get-tuple-element.92), channel_id=1, source_target_pairs={{0,4},{4,0},{8,12},{12,8},{16,20},{20,16},{24,28},{28,24},{1,5},{5... | collective-permute-start | bytes 786440 | tf_op jit(solution)/shard_map/ppermute | solution.py:520
  47.3 11.4 %collective-permute-start.18 = (bf16[2,256,256]{2,1,0:T(8,128)(2,1)S(1)}, bf16[2,256,256]{2,1,0:T(8,128)(2,1)S(1)}, u32[]{:S(2)}, u32[]{:S(2)}) collective-permute-start(bf16[2,256,256]{2,1,0:T(8,128)(2,1)S(1)} %get-tuple-element.95), channel_id=1, source_target_pairs={{0,4},{4,0},{8,12},{12,8},{16,20},{20,16},{24,28},{28,24},{1,5},{5... | collective-permute-start | bytes 786440 | tf_op jit(solution)/shard_map/ppermute | solution.py:520
  49.6 4.7 %collective-permute-start.12 = (bf16[392,128]{1,0:T(8,128)(2,1)S(1)}, bf16[392,128]{1,0:T(8,128)(2,1)S(1)}, u32[]{:S(2)}, u32[]{:S(2)}) collective-permute-start(bf16[392,128]{1,0:T(8,128)(2,1)S(1)} %fusion.2), channel_id=1, source_target_pairs={{0,8},{4,12},{8,0},{12,4},{16,24},{20,28},{24,16},{28,20},{1,9},{5... | collective-permute-start | bytes 301064 | tf_op jit(solution)/shard_map/ppermute | solution.py:520
  54.3 14.5 %collective-permute-start.15 = (bf16[2,256,512]{2,1,0:T(8,128)(2,1)S(1)}, bf16[2,256,512]{2,1,0:T(8,128)(2,1)S(1)}, u32[]{:S(2)}, u32[]{:S(2)}) collective-permute-start(bf16[2,256,512]{2,1,0:T(8,128)(2,1)S(1)} %pad_maximum_fusion), channel_id=1, source_target_pairs={{0,1},{1,0},{2,3},{3,2},{4,5},{5,4},{6,7},{7,6},{8,9},{9,8},{10,11... | collective-permute-start | bytes 1572872 | tf_op jit(solution)/shard_map/ppermute | solution.py:520
  58.7 18.1 %collective-permute-start.16 = (bf16[392,128]{1,0:T(8,128)(2,1)S(1)}, bf16[392,128]{1,0:T(8,128)(2,1)S(1)}, u32[]{:S(2)}, u32[]{:S(2)}) collective-permute-start(bf16[392,128]{1,0:T(8,128)(2,1)S(1)} %add_convert_fusion), channel_id=1, source_target_pairs={{0,16},{4,20},{8,24},{12,28},{16,0},{20,4},{24,8},{28,12},{1,17},{... | collective-permute-start | bytes 301064 | tf_op jit(solution)/shard_map/ppermute | solution.py:520
  61.4 5.9 %collective-permute-start.19 = (bf16[256,256]{1,0:T(8,128)(2,1)S(1)}, bf16[256,256]{1,0:T(8,128)(2,1)S(1)}, u32[]{:S(2)}, u32[]{:S(2)}) collective-permute-start(bf16[256,256]{1,0:T(8,128)(2,1)S(1)} %fusion.3), channel_id=1, source_target_pairs={{0,8},{4,12},{8,0},{12,4},{16,24},{20,28},{24,16},{28,20},{1,9},{5... | collective-permute-start | bytes 393224 | tf_op jit(solution)/shard_map/ppermute | solution.py:520
  63.2 7.6 %collective-permute-start.13 = (bf16[1024,256]{1,0:T(8,128)(2,1)S(1)}, bf16[1024,256]{1,0:T(8,128)(2,1)S(1)}, u32[]{:S(2)}, u32[]{:S(2)}) collective-permute-start(bf16[1024,256]{1,0:T(8,128)(2,1)S(1)} %collective-permute-done.11.refs_2_), channel_id=1, source_target_pairs={{0,1},{1,0},{2,3},{3,2},{4,5},{5,4},{6,7},{7,6},{8,9},{9,8},{10,11... | collective-permute-start | bytes 1572872 | tf_op jit(solution)/shard_map/ppermute | solution.py:520
  67.3 5.6 %collective-permute-start.21 = (bf16[256,256]{1,0:T(8,128)(2,1)S(1)}, bf16[256,256]{1,0:T(8,128)(2,1)S(1)}, u32[]{:S(2)}, u32[]{:S(2)}) collective-permute-start(bf16[256,256]{1,0:T(8,128)(2,1)S(1)} %fusion.4), channel_id=1, source_target_pairs={{0,8},{4,12},{8,0},{12,4},{16,24},{20,28},{24,16},{28,20},{1,9},{5... | collective-permute-start | bytes 393224 | tf_op jit(solution)/shard_map/ppermute | solution.py:520
  68.8 8.0 %collective-permute-start.20 = (bf16[256,256]{1,0:T(8,128)(2,1)S(1)}, bf16[256,256]{1,0:T(8,128)(2,1)S(1)}, u32[]{:S(2)}, u32[]{:S(2)}) collective-permute-start(bf16[256,256]{1,0:T(8,128)(2,1)S(1)} %fusion.1), channel_id=1, source_target_pairs={{0,16},{4,20},{8,24},{12,28},{16,0},{20,4},{24,8},{28,12},{1,17},{... | collective-permute-start | bytes 393224 | tf_op jit(solution)/shard_map/ppermute | solution.py:520

commit v13 on v12

--- a/solution.py
+++ b/solution.py
@@ -206,7 +206,7 @@
         scores = jnp.where(keep, scores, 0.0).astype(BF16)
         w_ref[i] = scores
         nh, nl = split(pairs[h])
-        pre_ref[i] = cat([nh, nl], 1)
+        pre_ref[i] = cat([nh.T, nl.T], 0)
         state = dot(both, cat([cat([nh, nl], 1), cat([nh, nil], 1)], 0))
         out = dot(scores, v) + state[:, :HDIM] + state[:, HDIM:]
         out_ref[rows, cols] = out.astype(BF16)
@@ -219,7 +219,7 @@
         functools.partial(outputs_kernel, len(pairs)),
         out_shape=(
             shape(queries.shape, BF16),
-            shape((count, HDIM, 2 * HDIM), BF16),
+            shape((count, 2 * HDIM, HDIM), BF16),
             shape((count, SPAN, 2 * HDIM), BF16),
             shape((count, SPAN, SPAN), BF16),
         ),
@@ -241,7 +241,7 @@
         q, k, v, do = q_ref[rows, cols], k_ref[rows, cols], v_ref[rows, cols], do_ref[rows, cols]
         weights = jnp.where(keep, dot(do, v, (1, 1)), 0.0).astype(BF16)
         p_ref[i] = weights
-        ds = dot(weights, k) + dot(cat([do, do], 1), pre_ref[i], (1, 1))
+        ds = dot(weights, k) + dot(cat([do, do], 1), pre_ref[i])
         ds = ds.astype(BF16)
         ds_ref[rows, cols] = ds
         state = dot(s_ref[i], do, (0, 0))

time: 78.5 us -> 78.5 us (level)
  no operation moved by 1% of the time
where the time goes in v13:
time: 78.5 us; the launch traced here: 78.3 us
  starting transfers between devices  29.8 us (38%)
  waiting for transfers between devices  23.7 us (30%)
  Pallas kernels  22.3 us (28%)
  local copies, waits for them, and re-layouts  1.35 us (2%)
  between operations  0.92 us (1%)
    ppermute x22, starting transfers between devices, swap(): return lax.ppermute(value, axis, [(i, i ^ distance) for i in range(count)])  29.8 us
    ppermute x22, waiting for transfers between devices, swap(): return lax.ppermute(value, axis, [(i, i ^ distance) for i in range(count)])  23.7 us
    pallas_call x1, Pallas kernels, tangent(): pl.pallas_call(tangent_kernel, out_shape=(shape((count, SPAN, SPAN), BF16...  6.81 us
    pallas_call x1, Pallas kernels, inverses(): pl.pallas_call(functools.partial(inverse_kernel, len(grams)), out_shape=(...  4.23 us
    pallas_call x1, Pallas kernels, outputs(): pl.pallas_call(functools.partial(outputs_kernel, len(pairs)), out_shape=(...  2.4 us
    pallas_call x1, Pallas kernels, rest(): pl.pallas_call(rest_kernel, out_shape=(shape(keys.shape, BF16), wide, wid...  2.09 us
    pallas_call x1, Pallas kernels, layer(): pl.pallas_call(layer_kernel, out_shape=shape((rows, cols), BF16), in_spec...  1.99 us
  transfers between devices with their start and end apart: 22, of which 11 were waited for; matrix products, arithmetic and copies ran while one was open for 1% of the time, Pallas kernels for 26%

profile of v13, /device:TPU:0, one launch (start us, length us, event | category | flops | bytes accessed | tf_op | source)
XLA Modules:
  0.0 78.3 jit_solution(16249922710473865563)
XLA Ops:
  0.7 1.0 %copy-done.2 = bf16[1024,256]{1,0:T(8,128)(2,1)S(1)} copy-done((bf16[1024,256]{1,0:T(8,128)(2,1)S(1)}, bf16[1024,256]{1,0:T(8,128)(2,1)}, u32[]{:S(2)}) %copy-start.2) | copy-done | bytes 524312
  1.7 0.2 copy-done.3
  1.8 0.3 shard_map.93
  2.2 0.0 copy-done.1
  2.2 0.6 collective-permute-start
  2.7 2.6 %collective-permute-start.7 = (bf16[1024,512]{1,0:T(8,128)(2,1)S(1)}, bf16[1024,512]{1,0:T(8,128)(2,1)S(1)}, u32[]{:S(2)}, u32[]{:S(2)}) collective-permute-start(bf16[1024,512]{1,0:T(8,128)(2,1)S(1)} %copy-done.1), channel_id=1, source_target_pairs={{0,2},{1,3},{2,0},{3,1},{4,6},{5,7},{6,4},{7,5},{8,10},{9,11},{10,... | collective-permute-start | bytes 3145736 | tf_op jit(solution)/shard_map/ppermute | solution.py:520
  5.3 1.5 %collective-permute-start.1 = (f32[136,128]{1,0:T(8,128)S(1)}, f32[136,128]{1,0:T(8,128)S(1)}, u32[]{:S(2)}, u32[]{:S(2)}) collective-permute-start(f32[136,128]{1,0:T(8,128)S(1)} %get-tuple-element.54), channel_id=1, source_target_pairs={{0,4},{4,0},{8,12},{12,8},{16,20},{20,16},{24,28},{28,24},{1,5},{5... | collective-permute-start | bytes 208904 | tf_op jit(solution)/shard_map/ppermute | solution.py:520
  6.8 2.8 %collective-permute-done.1.refs_0_ = f32[136,128]{1,0:T(8,128)S(1)} collective-permute-done((f32[136,128]{1,0:T(8,128)S(1)}, f32[136,128]{1,0:T(8,128)S(1)}, u32[]{:S(2)}, u32[]{:S(2)}) %collective-permute-start.1) | collective-permute-done | bytes 69664 | tf_op jit(solution)/shard_map/ppermute | solution.py:520
  9.6 1.6 %collective-permute-start.2 = (f32[136,128]{1,0:T(8,128)S(1)}, f32[136,128]{1,0:T(8,128)S(1)}, u32[]{:S(2)}, u32[]{:S(2)}) collective-permute-start(f32[136,128]{1,0:T(8,128)S(1)} %add.27), channel_id=1, source_target_pairs={{0,8},{4,12},{8,0},{12,4},{16,24},{20,28},{24,16},{28,20},{1,9},{5... | collective-permute-start | bytes 208904 | tf_op jit(solution)/shard_map/ppermute | solution.py:520
  11.3 1.6 %collective-permute-start.4 = (bf16[256,128]{1,0:T(8,128)(2,1)S(1)}, bf16[256,128]{1,0:T(8,128)(2,1)S(1)}, u32[]{:S(2)}, u32[]{:S(2)}) collective-permute-start(bf16[256,128]{1,0:T(8,128)(2,1)S(1)} %convert_element_type.53), channel_id=1, source_target_pairs={{0,4},{4,0},{8,12},{12,8},{16,20},{20,16},{24,28},{28,24},{1,5},{5... | collective-permute-start | bytes 196616 | tf_op jit(solution)/shard_map/ppermute | solution.py:520
  12.9 1.1 %collective-permute-done.2.refs_1_ = f32[136,128]{1,0:T(8,128)S(1)} collective-permute-done((f32[136,128]{1,0:T(8,128)S(1)}, f32[136,128]{1,0:T(8,128)S(1)}, u32[]{:S(2)}, u32[]{:S(2)}) %collective-permute-start.2) | collective-permute-done | bytes 69664 | tf_op jit(solution)/shard_map/ppermute | solution.py:520
  14.0 1.6 %collective-permute-done.4.refs_0_ = bf16[256,128]{1,0:T(8,128)(2,1)S(1)} collective-permute-done((bf16[256,128]{1,0:T(8,128)(2,1)S(1)}, bf16[256,128]{1,0:T(8,128)(2,1)S(1)}, u32[]{:S(2)}, u32[]{:S(2)}) %collective-permute-start.4) | collective-permute-done | bytes 65568 | tf_op jit(solution)/shard_map/ppermute | solution.py:520
  15.6 0.5 collective-permute-start.5
  16.1 2.6 %collective-permute-start.3 = (f32[136,128]{1,0:T(8,128)S(1)}, f32[136,128]{1,0:T(8,128)S(1)}, u32[]{:S(2)}, u32[]{:S(2)}) collective-permute-start(f32[136,128]{1,0:T(8,128)S(1)} %add.28), channel_id=1, source_target_pairs={{0,16},{4,20},{8,24},{12,28},{16,0},{20,4},{24,8},{28,12},{1,17},{... | collective-permute-start | bytes 208904 | tf_op jit(solution)/shard_map/ppermute | solution.py:520
  18.7 1.2 %collective-permute-done.5.refs_1_ = bf16[256,128]{1,0:T(8,128)(2,1)S(1)} collective-permute-done((bf16[256,128]{1,0:T(8,128)(2,1)S(1)}, bf16[256,128]{1,0:T(8,128)(2,1)S(1)}, u32[]{:S(2)}, u32[]{:S(2)}) %collective-permute-start.5) | collective-permute-done | bytes 65568 | tf_op jit(solution)/shard_map/ppermute | solution.py:520
  20.0 3.0 %collective-permute-start.6 = (bf16[256,128]{1,0:T(8,128)(2,1)S(1)}, bf16[256,128]{1,0:T(8,128)(2,1)S(1)}, u32[]{:S(2)}, u32[]{:S(2)}) collective-permute-start(bf16[256,128]{1,0:T(8,128)(2,1)S(1)} %add_convert_fusion.1), channel_id=1, source_target_pairs={{0,16},{4,20},{8,24},{12,28},{16,0},{20,4},{24,8},{28,12},{1,17},{... | collective-permute-start | bytes 196616 | tf_op jit(solution)/shard_map/ppermute | solution.py:520
  23.0 0.7 shard_map.94.refs_0_
  23.8 4.2 %shard_map.95 = (bf16[8,8,128,128]{3,2,1,0:T(8,128)(2,1)S(1)}, bf16[8,8,128,128]{3,2,1,0:T(8,128)(2,1)S(1)}, f32[8,128,128]{2,1,0:T(8,128)S(1)}, f32[8,128,128]{2,1,0:T(8,128)S(1)}) custom-call(bf16[1024,256]{1,0:T(8,128)(2,1)S(1)} %copy-done.2, f32[136,128]{1,0:T(8,128)S(1)} %collective-permute-done.1.refs_0_, ...), custom_call_target="tpu_custom_call" | custom-call | flops 2000000000 | bytes 8000000 | tf_op jit(solution)/shard_map/pallas_call | solution.py:181
  28.0 1.0 %collective-permute-done.7.refs_2_.refs_1_ = bf16[1024,512]{1,0:T(8,128)(2,1)S(1)} collective-permute-done((bf16[1024,512]{1,0:T(8,128)(2,1)S(1)}, bf16[1024,512]{1,0:T(8,128)(2,1)S(1)}, u32[]{:S(2)}, u32[]{:S(2)}) %collective-permute-start.7) | collective-permute-done | bytes 1048608 | tf_op jit(solution)/shard_map/ppermute | solution.py:520
  29.0 0.1 shard_map.104
  29.1 1.8 %collective-permute-start.14 = (bf16[2,256,512]{2,1,0:T(8,128)(2,1)S(1)}, bf16[2,256,512]{2,1,0:T(8,128)(2,1)S(1)}, u32[]{:S(2)}, u32[]{:S(2)}) collective-permute-start(bf16[2,256,512]{2,1,0:T(8,128)(2,1)S(1)} %get-tuple-element.87), channel_id=1, source_target_pairs={{0,2},{1,3},{2,0},{3,1},{4,6},{5,7},{6,4},{7,5},{8,10},{9,11},{10,... | collective-permute-start | bytes 1572872 | tf_op jit(solution)/shard_map/ppermute | solution.py:520
  30.9 2.4 %shard_map.97 = (bf16[1024,256]{1,0:T(8,128)(2,1)S(1)}, bf16[8,256,128]{2,1,0:T(8,128)(2,1)S(1)}, bf16[8,256,256]{2,1,0:T(8,128)(2,1)S(1)}, bf16[8,256,256]{2,1,0:T(8,128)(2,1)S(1)}) custom-call(f32[8,128]{1,0:T(8,128)S(1)} %shard_map.96.mark_ref, bf16[1024,256]{1,0:T(8,128)(2,1)S(1)} %copy-done.4, bf16[1024,256]{1,0:T(8,128)(2,1)S(1)} %copy-done.2, ...), custom_call_target="tpu_custom_call" | custom-call | flops 2000000000 | bytes 8000000 | tf_op jit(solution)/shard_map/pallas_call | solution.py:218
  33.4 1.4 %shard_map.98 = (bf16[2,256,256]{2,1,0:T(8,128)(2,1)S(1)}, bf16[2,256,256]{2,1,0:T(8,128)(2,1)S(1)}, bf16[2,256,256]{2,1,0:T(8,128)(2,1)S(1)}, bf16[2,256,256]{2,1,0:T(8,128)(2,1)S(1)}) custom-call(bf16[1024,256]{1,0:T(8,128)(2,1)S(1)} %get-tuple-element.80.h_ref.refs_0_, bf16[1024,512]{1,0:T(8,128)(2,1)S(1)} %copy-done.1, ...), custom_call_target="tpu_custom_call" | custom-call | flops 1073741824 | bytes 6000000 | tf_op jit(solution)/shard_map/pallas_call | solution.py:476
  34.7 0.7 shard_map.99.do_ref
  35.5 6.8 %shard_map.100 = (bf16[8,256,256]{2,1,0:T(8,128)(2,1)S(1)}, bf16[1024,256]{1,0:T(8,128)(2,1)S(1)}, f32[8,128,128]{2,1,0:T(8,128)S(1)}, f32[8,128,128]{2,1,0:T(8,...) custom-call(bf16[1024,256]{1,0:T(8,128)(2,1)S(1)} %copy-done.4, bf16[1024,256]{1,0:T(8,128)(2,1)S(1)} %copy-done.2, ...), custom_call_target="tpu_custom_call" | custom-call | flops 4000000000 | bytes 8000000 | tf_op jit(solution)/shard_map/pallas_call | solution.py:290
  42.3 1.6 %collective-permute-start.9 = (bf16[392,128]{1,0:T(8,128)(2,1)S(1)}, bf16[392,128]{1,0:T(8,128)(2,1)S(1)}, u32[]{:S(2)}, u32[]{:S(2)}) collective-permute-start(bf16[392,128]{1,0:T(8,128)(2,1)S(1)} %get-tuple-element.71.refs_0_), channel_id=1, source_target_pairs={{0,4},{4,0},{8,12},{12,8},{16,20},{20,16},{24,28},{28,24},{1,5},{5... | collective-permute-start | bytes 301064 | tf_op jit(solution)/shard_map/ppermute | solution.py:520
  43.9 0.5 collective-permute-start.11
  44.4 0.3 collective-permute-start.17
  44.7 2.7 %collective-permute-done.9.refs_0_ = bf16[392,128]{1,0:T(8,128)(2,1)S(1)} collective-permute-done((bf16[392,128]{1,0:T(8,128)(2,1)S(1)}, bf16[392,128]{1,0:T(8,128)(2,1)S(1)}, u32[]{:S(2)}, u32[]{:S(2)}) %collective-permute-start.9) | collective-permute-done | bytes 100384 | tf_op jit(solution)/shard_map/ppermute | solution.py:520
  47.3 2.3 %collective-permute-start.18 = (bf16[2,256,256]{2,1,0:T(8,128)(2,1)S(1)}, bf16[2,256,256]{2,1,0:T(8,128)(2,1)S(1)}, u32[]{:S(2)}, u32[]{:S(2)}) collective-permute-start(bf16[2,256,256]{2,1,0:T(8,128)(2,1)S(1)} %get-tuple-element.95), channel_id=1, source_target_pairs={{0,4},{4,0},{8,12},{12,8},{16,20},{20,16},{24,28},{28,24},{1,5},{5... | collective-permute-start | bytes 786440 | tf_op jit(solution)/shard_map/ppermute | solution.py:520
  49.6 1.6 %collective-permute-start.12 = (bf16[392,128]{1,0:T(8,128)(2,1)S(1)}, bf16[392,128]{1,0:T(8,128)(2,1)S(1)}, u32[]{:S(2)}, u32[]{:S(2)}) collective-permute-start(bf16[392,128]{1,0:T(8,128)(2,1)S(1)} %fusion.2), channel_id=1, source_target_pairs={{0,8},{4,12},{8,0},{12,4},{16,24},{20,28},{24,16},{28,20},{1,9},{5... | collective-permute-start | bytes 301064 | tf_op jit(solution)/shard_map/ppermute | solution.py:520
  51.3 0.1 slice_bitcast_fusion.4
  51.4 2.1 %shard_map.102 = (bf16[1024,256]{1,0:T(8,128)(2,1)}, f32[1024,256]{1,0:T(8,128)S(1)}, f32[1024,256]{1,0:T(8,128)S(1)}) custom-call(f32[8,128]{1,0:T(8,128)S(1)} %shard_map.101.early_ref, bf16[1024,256]{1,0:T(8,128)(2,1)S(1)} %copy-done.2, bf16[1024,256]{1,0:T(8,128)(2,1)S(1)} %copy-done.3, bf16[1024,256]{1,0:T(8,128)(2,1)S(1)} %shard_map.99.do_ref, ...), custom_call_target="tpu_custom_call" | custom-call | flops 2000000000 | bytes 6000000 | tf_op jit(solution)/shard_map/pallas_call | solution.py:335
  53.5 0.1 pad_maximum_fusion
  53.5 0.8 %collective-permute-done.12.refs_1_ = bf16[392,128]{1,0:T(8,128)(2,1)S(1)} collective-permute-done((bf16[392,128]{1,0:T(8,128)(2,1)S(1)}, bf16[392,128]{1,0:T(8,128)(2,1)S(1)}, u32[]{:S(2)}, u32[]{:S(2)}) %collective-permute-start.12) | collective-permute-done | bytes 100384 | tf_op jit(solution)/shard_map/ppermute | solution.py:520
  54.4 4.4 %collective-permute-done.18 = bf16[2,256,256]{2,1,0:T(8,128)(2,1)S(1)} collective-permute-done((bf16[2,256,256]{2,1,0:T(8,128)(2,1)S(1)}, bf16[2,256,256]{2,1,0:T(8,128)(2,1)S(1)}, u32[]{:S(2)}, u32[]{:S(2)}) %collective-permute-start.18) | collective-permute-done | bytes 262176 | tf_op jit(solution)/shard_map/ppermute | solution.py:520
  58.8 2.6 %collective-permute-start.16 = (bf16[392,128]{1,0:T(8,128)(2,1)S(1)}, bf16[392,128]{1,0:T(8,128)(2,1)S(1)}, u32[]{:S(2)}, u32[]{:S(2)}) collective-permute-start(bf16[392,128]{1,0:T(8,128)(2,1)S(1)} %add_convert_fusion), channel_id=1, source_target_pairs={{0,16},{4,20},{8,24},{12,28},{16,0},{20,4},{24,8},{28,12},{1,17},{... | collective-permute-start | bytes 301064 | tf_op jit(solution)/shard_map/ppermute | solution.py:520
  61.3 0.1 convert_add_fusion
  61.4 1.6 %collective-permute-start.19 = (bf16[256,256]{1,0:T(8,128)(2,1)S(1)}, bf16[256,256]{1,0:T(8,128)(2,1)S(1)}, u32[]{:S(2)}, u32[]{:S(2)}) collective-permute-start(bf16[256,256]{1,0:T(8,128)(2,1)S(1)} %fusion.3), channel_id=1, source_target_pairs={{0,8},{4,12},{8,0},{12,4},{16,24},{20,28},{24,16},{28,20},{1,9},{5... | collective-permute-start | bytes 393224 | tf_op jit(solution)/shard_map/ppermute | solution.py:520
  63.1 0.1 convert_add_fusion.1
  63.2 0.1 collective-permute-start.13
  63.3 4.0 %collective-permute-done.19 = bf16[256,256]{1,0:T(8,128)(2,1)S(1)} collective-permute-done((bf16[256,256]{1,0:T(8,128)(2,1)S(1)}, bf16[256,256]{1,0:T(8,128)(2,1)S(1)}, u32[]{:S(2)}, u32[]{:S(2)}) %collective-permute-start.19) | collective-permute-done | bytes 131104 | tf_op jit(solution)/shard_map/ppermute | solution.py:520
  67.3 1.5 %collective-permute-start.21 = (bf16[256,256]{1,0:T(8,128)(2,1)S(1)}, bf16[256,256]{1,0:T(8,128)(2,1)S(1)}, u32[]{:S(2)}, u32[]{:S(2)}) collective-permute-start(bf16[256,256]{1,0:T(8,128)(2,1)S(1)} %fusion.4), channel_id=1, source_target_pairs={{0,8},{4,12},{8,0},{12,4},{16,24},{20,28},{24,16},{28,20},{1,9},{5... | collective-permute-start | bytes 393224 | tf_op jit(solution)/shard_map/ppermute | solution.py:520
  68.8 1.9 %collective-permute-start.20 = (bf16[256,256]{1,0:T(8,128)(2,1)S(1)}, bf16[256,256]{1,0:T(8,128)(2,1)S(1)}, u32[]{:S(2)}, u32[]{:S(2)}) collective-permute-start(bf16[256,256]{1,0:T(8,128)(2,1)S(1)} %fusion.1), channel_id=1, source_target_pairs={{0,16},{4,20},{8,24},{12,28},{16,0},{20,4},{24,8},{28,12},{1,17},{... | collective-permute-start | bytes 393224 | tf_op jit(solution)/shard_map/ppermute | solution.py:520
  70.8 2.0 %shard_map.105 = bf16[1024,512]{1,0:T(8,128)(2,1)} custom-call(f32[8,128]{1,0:T(8,128)S(1)} %shard_map.103.mark_ref, bf16[1024,256]{1,0:T(8,128)(2,1)S(1)} %get-tuple-element.80.h_ref.refs_0_, bf16[1024,256]{1,0:T(8,128)(2,1)S(1)} %collective-permute-done.10.refs_1_, bf16[1024,256]{1,0:T(8,128)(2,1)S(1)} %collective-permute-done.11.refs_2_, ...), custom_call_target="tpu_custom_call" | custom-call | flops 1073741824 | bytes 6000000 | tf_op jit(solution)/shard_map/pallas_call | solution.py:507
  72.8 0.2 collective-permute-done.21.refs_5_
  73.0 3.9 %collective-permute-done.20.refs_4_ = bf16[256,256]{1,0:T(8,128)(2,1)S(1)} collective-permute-done((bf16[256,256]{1,0:T(8,128)(2,1)S(1)}, bf16[256,256]{1,0:T(8,128)(2,1)S(1)}, u32[]{:S(2)}, u32[]{:S(2)}) %collective-permute-start.20) | collective-permute-done | bytes 131104 | tf_op jit(solution)/shard_map/ppermute | solution.py:520
  76.8 1.5 %shard_map.106 = (bf16[1024,256]{1,0:T(8,128)(2,1)}, bf16[1024,256]{1,0:T(8,128)(2,1)}, f32[256,256]{1,0:T(8,128)}) custom-call(bf16[1024,256]{1,0:T(8,128)(2,1)S(1)} %copy-done.2, bf16[1024,256]{1,0:T(8,128)(2,1)S(1)} %copy-done.3, f32[1024,256]{1,0:T(8,128)S(1)} %get-tuple-element.79.refs_0_.dk_ref, f32[1024,256]{1,0:T(8,128)S(1)} %get-tuple-element.90.dv_ref, ...), custom_call_target="tpu_custom_call" | custom-call | flops 1000000000 | bytes 6000000 | tf_op jit(solution)/shard_map/pallas_call | solution.py:383
  (37 shorter events, 0.3 us)
Async XLA Ops:
  0.6 1.0 %copy-start.2 = (bf16[1024,256]{1,0:T(8,128)(2,1)S(1)}, bf16[1024,256]{1,0:T(8,128)(2,1)}, u32[]{:S(2)}) copy-start(bf16[1024,256]{1,0:T(8,128)(2,1)} %k_ref.11) | copy-start | bytes 1572868
  0.6 1.2 %copy-start.3 = (bf16[1024,256]{1,0:T(8,128)(2,1)S(1)}, bf16[1024,256]{1,0:T(8,128)(2,1)}, u32[]{:S(2)}) copy-start(bf16[1024,256]{1,0:T(8,128)(2,1)} %v_ref.9) | copy-start | bytes 1572868
  0.7 1.5 %copy-start.1 = (bf16[1024,512]{1,0:T(8,128)(2,1)S(1)}, bf16[1024,512]{1,0:T(8,128)(2,1)}, u32[]{:S(2)}) copy-start(bf16[1024,512]{1,0:T(8,128)(2,1)} %refs_0_.3) | copy-start | bytes 3145732
  0.7 22.3 %copy-start = (bf16[256,2048]{1,0:T(8,128)(2,1)S(1)}, bf16[256,2048]{1,0:T(8,128)(2,1)}, u32[]{:S(2)}) copy-start(bf16[256,2048]{1,0:T(8,128)(2,1)} %w_ref.4) | copy-start | bytes 3145732
  2.2 20.8 %collective-permute-start = (bf16[1024,512]{1,0:T(8,128)(2,1)S(1)}, bf16[1024,512]{1,0:T(8,128)(2,1)S(1)}, u32[]{:S(2)}, u32[]{:S(2)}) collective-permute-start(bf16[1024,512]{1,0:T(8,128)(2,1)S(1)} %copy-done.1), channel_id=1, source_target_pairs={{0,1},{1,0},{2,3},{3,2},{4,5},{5,4},{6,7},{7,6},{8,9},{9,8},{10,11... | collective-permute-start | bytes 3145736 | tf_op jit(solution)/shard_map/ppermute | solution.py:520
  2.7 26.3 %collective-permute-start.7 = (bf16[1024,512]{1,0:T(8,128)(2,1)S(1)}, bf16[1024,512]{1,0:T(8,128)(2,1)S(1)}, u32[]{:S(2)}, u32[]{:S(2)}) collective-permute-start(bf16[1024,512]{1,0:T(8,128)(2,1)S(1)} %copy-done.1), channel_id=1, source_target_pairs={{0,2},{1,3},{2,0},{3,1},{4,6},{5,7},{6,4},{7,5},{8,10},{9,11},{10,... | collective-permute-start | bytes 3145736 | tf_op jit(solution)/shard_map/ppermute | solution.py:520
  5.3 4.3 %collective-permute-start.1 = (f32[136,128]{1,0:T(8,128)S(1)}, f32[136,128]{1,0:T(8,128)S(1)}, u32[]{:S(2)}, u32[]{:S(2)}) collective-permute-start(f32[136,128]{1,0:T(8,128)S(1)} %get-tuple-element.54), channel_id=1, source_target_pairs={{0,4},{4,0},{8,12},{12,8},{16,20},{20,16},{24,28},{28,24},{1,5},{5... | collective-permute-start | bytes 208904 | tf_op jit(solution)/shard_map/ppermute | solution.py:520
  9.6 4.4 %collective-permute-start.2 = (f32[136,128]{1,0:T(8,128)S(1)}, f32[136,128]{1,0:T(8,128)S(1)}, u32[]{:S(2)}, u32[]{:S(2)}) collective-permute-start(f32[136,128]{1,0:T(8,128)S(1)} %add.27), channel_id=1, source_target_pairs={{0,8},{4,12},{8,0},{12,4},{16,24},{20,28},{24,16},{28,20},{1,9},{5... | collective-permute-start | bytes 208904 | tf_op jit(solution)/shard_map/ppermute | solution.py:520
  11.3 4.3 %collective-permute-start.4 = (bf16[256,128]{1,0:T(8,128)(2,1)S(1)}, bf16[256,128]{1,0:T(8,128)(2,1)S(1)}, u32[]{:S(2)}, u32[]{:S(2)}) collective-permute-start(bf16[256,128]{1,0:T(8,128)(2,1)S(1)} %convert_element_type.53), channel_id=1, source_target_pairs={{0,4},{4,0},{8,12},{12,8},{16,20},{20,16},{24,28},{28,24},{1,5},{5... | collective-permute-start | bytes 196616 | tf_op jit(solution)/shard_map/ppermute | solution.py:520
  15.6 4.3 %collective-permute-start.5 = (bf16[256,128]{1,0:T(8,128)(2,1)S(1)}, bf16[256,128]{1,0:T(8,128)(2,1)S(1)}, u32[]{:S(2)}, u32[]{:S(2)}) collective-permute-start(bf16[256,128]{1,0:T(8,128)(2,1)S(1)} %fusion.5), channel_id=1, source_target_pairs={{0,8},{4,12},{8,0},{12,4},{16,24},{20,28},{24,16},{28,20},{1,9},{5... | collective-permute-start | bytes 196616 | tf_op jit(solution)/shard_map/ppermute | solution.py:520
  16.1 7.6 %collective-permute-start.3 = (f32[136,128]{1,0:T(8,128)S(1)}, f32[136,128]{1,0:T(8,128)S(1)}, u32[]{:S(2)}, u32[]{:S(2)}) collective-permute-start(f32[136,128]{1,0:T(8,128)S(1)} %add.28), channel_id=1, source_target_pairs={{0,16},{4,20},{8,24},{12,28},{16,0},{20,4},{24,8},{28,12},{1,17},{... | collective-permute-start | bytes 208904 | tf_op jit(solution)/shard_map/ppermute | solution.py:520
  20.0 8.0 %collective-permute-start.6 = (bf16[256,128]{1,0:T(8,128)(2,1)S(1)}, bf16[256,128]{1,0:T(8,128)(2,1)S(1)}, u32[]{:S(2)}, u32[]{:S(2)}) collective-permute-start(bf16[256,128]{1,0:T(8,128)(2,1)S(1)} %add_convert_fusion.1), channel_id=1, source_target_pairs={{0,16},{4,20},{8,24},{12,28},{16,0},{20,4},{24,8},{28,12},{1,17},{... | collective-permute-start | bytes 196616 | tf_op jit(solution)/shard_map/ppermute | solution.py:520
  23.8 7.2 %copy-start.4 = (bf16[1024,256]{1,0:T(8,128)(2,1)S(1)}, bf16[1024,256]{1,0:T(8,128)(2,1)}, u32[]{:S(2)}) copy-start(bf16[1024,256]{1,0:T(8,128)(2,1)} %q_ref.3) | copy-start | bytes 1572868
  29.0 4.3 %collective-permute-start.8 = (bf16[1024,512]{1,0:T(8,128)(2,1)S(1)}, bf16[1024,512]{1,0:T(8,128)(2,1)S(1)}, u32[]{:S(2)}, u32[]{:S(2)}) collective-permute-start(bf16[1024,512]{1,0:T(8,128)(2,1)S(1)} %collective-permute-done.7.refs_2_.refs_1_), channel_id=1, source_target_pairs={{0,1},{1,0},{2,3},{3,2},{4,5},{5,4},{6,7},{7,6},{8,9},{9,8},{10,11... | collective-permute-start | bytes 3145736 | tf_op jit(solution)/shard_map/ppermute | solution.py:520
  29.1 20.5 %collective-permute-start.14 = (bf16[2,256,512]{2,1,0:T(8,128)(2,1)S(1)}, bf16[2,256,512]{2,1,0:T(8,128)(2,1)S(1)}, u32[]{:S(2)}, u32[]{:S(2)}) collective-permute-start(bf16[2,256,512]{2,1,0:T(8,128)(2,1)S(1)} %get-tuple-element.87), channel_id=1, source_target_pairs={{0,2},{1,3},{2,0},{3,1},{4,6},{5,7},{6,4},{7,5},{8,10},{9,11},{10,... | collective-permute-start | bytes 1572872 | tf_op jit(solution)/shard_map/ppermute | solution.py:520
  42.3 5.0 %collective-permute-start.9 = (bf16[392,128]{1,0:T(8,128)(2,1)S(1)}, bf16[392,128]{1,0:T(8,128)(2,1)S(1)}, u32[]{:S(2)}, u32[]{:S(2)}) collective-permute-start(bf16[392,128]{1,0:T(8,128)(2,1)S(1)} %get-tuple-element.71.refs_0_), channel_id=1, source_target_pairs={{0,4},{4,0},{8,12},{12,8},{16,20},{20,16},{24,28},{28,24},{1,5},{5... | collective-permute-start | bytes 301064 | tf_op jit(solution)/shard_map/ppermute | solution.py:520
  43.9 19.3 %collective-permute-start.11 = (bf16[1024,256]{1,0:T(8,128)(2,1)S(1)}, bf16[1024,256]{1,0:T(8,128)(2,1)S(1)}, u32[]{:S(2)}, u32[]{:S(2)}) collective-permute-start(bf16[1024,256]{1,0:T(8,128)(2,1)S(1)} %get-tuple-element.80.h_ref.refs_0_), channel_id=1, source_target_pairs={{0,2},{1,3},{2,0},{3,1},{4,6},{5,7},{6,4},{7,5},{8,10},{9,11},{10,... | collective-permute-start | bytes 1572872 | tf_op jit(solution)/shard_map/ppermute | solution.py:520
  44.4 26.4 %collective-permute-start.10 = (bf16[1024,256]{1,0:T(8,128)(2,1)S(1)}, bf16[1024,256]{1,0:T(8,128)(2,1)S(1)}, u32[]{:S(2)}, u32[]{:S(2)}) collective-permute-start(bf16[1024,256]{1,0:T(8,128)(2,1)S(1)} %get-tuple-element.80.h_ref.refs_0_), channel_id=1, source_target_pairs={{0,1},{1,0},{2,3},{3,2},{4,5},{5,4},{6,7},{7,6},{8,9},{9,8},{10,11... | collective-permute-start | bytes 1572872 | tf_op jit(solution)/shard_map/ppermute | solution.py:520
  44.4 17.0 %collective-permute-start.17 = (bf16[2,256,256]{2,1,0:T(8,128)(2,1)S(1)}, bf16[2,256,256]{2,1,0:T(8,128)(2,1)S(1)}, u32[]{:S(2)}, u32[]{:S(2)}) collective-permute-start(bf16[2,256,256]{2,1,0:T(8,128)(2,1)S(1)} %get-tuple-element.92), channel_id=1, source_target_pairs={{0,4},{4,0},{8,12},{12,8},{16,20},{20,16},{24,28},{28,24},{1,5},{5... | collective-permute-start | bytes 786440 | tf_op jit(solution)/shard_map/ppermute | solution.py:520
  47.3 11.4 %collective-permute-start.18 = (bf16[2,256,256]{2,1,0:T(8,128)(2,1)S(1)}, bf16[2,256,256]{2,1,0:T(8,128)(2,1)S(1)}, u32[]{:S(2)}, u32[]{:S(2)}) collective-permute-start(bf16[2,256,256]{2,1,0:T(8,128)(2,1)S(1)} %get-tuple-element.95), channel_id=1, source_target_pairs={{0,4},{4,0},{8,12},{12,8},{16,20},{20,16},{24,28},{28,24},{1,5},{5... | collective-permute-start | bytes 786440 | tf_op jit(solution)/shard_map/ppermute | solution.py:520
  49.6 4.7 %collective-permute-start.12 = (bf16[392,128]{1,0:T(8,128)(2,1)S(1)}, bf16[392,128]{1,0:T(8,128)(2,1)S(1)}, u32[]{:S(2)}, u32[]{:S(2)}) collective-permute-start(bf16[392,128]{1,0:T(8,128)(2,1)S(1)} %fusion.2), channel_id=1, source_target_pairs={{0,8},{4,12},{8,0},{12,4},{16,24},{20,28},{24,16},{28,20},{1,9},{5... | collective-permute-start | bytes 301064 | tf_op jit(solution)/shard_map/ppermute | solution.py:520
  54.3 14.5 %collective-permute-start.15 = (bf16[2,256,512]{2,1,0:T(8,128)(2,1)S(1)}, bf16[2,256,512]{2,1,0:T(8,128)(2,1)S(1)}, u32[]{:S(2)}, u32[]{:S(2)}) collective-permute-start(bf16[2,256,512]{2,1,0:T(8,128)(2,1)S(1)} %pad_maximum_fusion), channel_id=1, source_target_pairs={{0,1},{1,0},{2,3},{3,2},{4,5},{5,4},{6,7},{7,6},{8,9},{9,8},{10,11... | collective-permute-start | bytes 1572872 | tf_op jit(solution)/shard_map/ppermute | solution.py:520
  58.8 18.1 %collective-permute-start.16 = (bf16[392,128]{1,0:T(8,128)(2,1)S(1)}, bf16[392,128]{1,0:T(8,128)(2,1)S(1)}, u32[]{:S(2)}, u32[]{:S(2)}) collective-permute-start(bf16[392,128]{1,0:T(8,128)(2,1)S(1)} %add_convert_fusion), channel_id=1, source_target_pairs={{0,16},{4,20},{8,24},{12,28},{16,0},{20,4},{24,8},{28,12},{1,17},{... | collective-permute-start | bytes 301064 | tf_op jit(solution)/shard_map/ppermute | solution.py:520
  61.4 5.9 %collective-permute-start.19 = (bf16[256,256]{1,0:T(8,128)(2,1)S(1)}, bf16[256,256]{1,0:T(8,128)(2,1)S(1)}, u32[]{:S(2)}, u32[]{:S(2)}) collective-permute-start(bf16[256,256]{1,0:T(8,128)(2,1)S(1)} %fusion.3), channel_id=1, source_target_pairs={{0,8},{4,12},{8,0},{12,4},{16,24},{20,28},{24,16},{28,20},{1,9},{5... | collective-permute-start | bytes 393224 | tf_op jit(solution)/shard_map/ppermute | solution.py:520
  63.2 7.6 %collective-permute-start.13 = (bf16[1024,256]{1,0:T(8,128)(2,1)S(1)}, bf16[1024,256]{1,0:T(8,128)(2,1)S(1)}, u32[]{:S(2)}, u32[]{:S(2)}) collective-permute-start(bf16[1024,256]{1,0:T(8,128)(2,1)S(1)} %collective-permute-done.11.refs_2_), channel_id=1, source_target_pairs={{0,1},{1,0},{2,3},{3,2},{4,5},{5,4},{6,7},{7,6},{8,9},{9,8},{10,11... | collective-permute-start | bytes 1572872 | tf_op jit(solution)/shard_map/ppermute | solution.py:520
  67.3 5.6 %collective-permute-start.21 = (bf16[256,256]{1,0:T(8,128)(2,1)S(1)}, bf16[256,256]{1,0:T(8,128)(2,1)S(1)}, u32[]{:S(2)}, u32[]{:S(2)}) collective-permute-start(bf16[256,256]{1,0:T(8,128)(2,1)S(1)} %fusion.4), channel_id=1, source_target_pairs={{0,8},{4,12},{8,0},{12,4},{16,24},{20,28},{24,16},{28,20},{1,9},{5... | collective-permute-start | bytes 393224 | tf_op jit(solution)/shard_map/ppermute | solution.py:520
  68.8 8.0 %collective-permute-start.20 = (bf16[256,256]{1,0:T(8,128)(2,1)S(1)}, bf16[256,256]{1,0:T(8,128)(2,1)S(1)}, u32[]{:S(2)}, u32[]{:S(2)}) collective-permute-start(bf16[256,256]{1,0:T(8,128)(2,1)S(1)} %fusion.1), channel_id=1, source_target_pairs={{0,16},{4,20},{8,24},{12,28},{16,0},{20,4},{24,8},{28,12},{1,17},{... | collective-permute-start | bytes 393224 | tf_op jit(solution)/shard_map/ppermute | solution.py:520
